TPU v7x, 32 devices: a whole 2x2x4 slice. The times are simulated.
32 devices in a mesh: fsdp: 2 (over x), ctx: 4 (over y, core), tp: 4 (over z).
Axes of the slice: x: 2, y: 2, z: 4, core: 2. Of those that a mesh axis runs over, the one named last changes fastest.
Arguments:
- tokens: bfloat16 [8192, 1024], P(('fsdp', 'ctx', 'tp')), may hold values from -6 to 6
- out_grad: bfloat16 [8192, 1024], P(('fsdp', 'ctx', 'tp')), may hold values from -6 to 6
- routes: int32 [8192, 8], P(('fsdp', 'ctx', 'tp')), may hold values from 0 to 31, all different within a row; in each aligned block of 256 rows (0 to 255, 256 to 511, ...) at most 96 rows name the same one
- parents: int32 [64], replicated, may hold values from -1 to 30, as said below
- adapter_set: int32 [2], replicated, may hold values from 0 to 7
- gain_a: bfloat16 [1024], replicated, may hold values from 0.5 to 1.5
- gain_b: bfloat16 [1024], replicated, may hold values from 0.5 to 1.5
- w_query: bfloat16 [1024, 1024], P('fsdp', 'tp'), may hold values from -0.75 to 0.75
- key_projection_matrix: bfloat16 [1024, 512], P('fsdp', 'tp'), may hold values from -0.75 to 0.75
- value_projection_matrix: bfloat16 [1024, 512], P('fsdp', 'tp'), may hold values from -0.1875 to 0.1875
- w_output: bfloat16 [1024, 1024], P('tp', 'fsdp'), may hold values from -3 to 3
- w_router: bfloat16 [1024, 32], replicated, may hold values from -0.09375 to 0.09375
- w_gate: bfloat16 [32, 1024, 512], P('ctx', 'fsdp'), may hold values from -0.1875 to 0.1875
- w_up: bfloat16 [32, 1024, 512], P('ctx', 'fsdp'), may hold values from -0.1875 to 0.1875
- w_down: bfloat16 [32, 512, 1024], P('ctx', 'fsdp'), may hold values from -4 to 4
- query_in: bfloat16 [1024, 128], replicated, may hold values from -0.1875 to 0.1875
- query_out: bfloat16 [128, 1024], replicated, may hold values from -1.5 to 1.5
- key_in: bfloat16 [1024, 128], replicated, may hold values from -0.1875 to 0.1875
- key_second_factor: bfloat16 [128, 512], replicated, may hold values from -1.5 to 1.5
- value_in: bfloat16 [1024, 128], replicated, may hold values from -0.1875 to 0.1875
- value_second_factor: bfloat16 [128, 512], replicated, may hold values from -1.5 to 1.5
- out_in: bfloat16 [1024, 128], replicated, may hold values from -0.1875 to 0.1875
- out_out: bfloat16 [128, 1024], replicated, may hold values from -6 to 6
- gate_in: bfloat16 [32, 1024, 128], P('ctx'), may hold values from -0.1875 to 0.1875
- gate_out: bfloat16 [32, 128, 512], P('ctx'), may hold values from -1.5 to 1.5
- up_in: bfloat16 [32, 1024, 128], P('ctx'), may hold values from -0.1875 to 0.1875
- up_out: bfloat16 [32, 128, 512], P('ctx'), may hold values from -1.5 to 1.5
- down_in: bfloat16 [32, 512, 128], P('ctx'), may hold values from -0.25 to 0.25
- down_out: bfloat16 [32, 128, 1024], P('ctx'), may hold values from -6 to 6
Outputs:
- output: bfloat16 [8192, 1024], P(('fsdp', 'ctx', 'tp'))
- input_grad: bfloat16 [8192, 1024], P(('fsdp', 'ctx', 'tp'))
- query_in_grad: float32 [1024, 128], replicated
- query_out_grad: float32 [128, 1024], replicated
- key_in_grad: float32 [1024, 128], replicated
- key_out_grad: float32 [128, 512], replicated
- value_in_grad: float32 [1024, 128], replicated
- value_out_grad: float32 [128, 512], replicated
- out_in_grad: float32 [1024, 128], replicated
- out_out_grad: float32 [128, 1024], replicated
- gate_in_grad: float32 [32, 1024, 128], P('ctx')
- gate_out_grad: float32 [32, 128, 512], P('ctx')
- up_in_grad: float32 [32, 1024, 128], P('ctx')
- up_out_grad: float32 [32, 128, 512], P('ctx')
- down_in_grad: float32 [32, 512, 128], P('ctx')
- down_out_grad: float32 [32, 128, 1024], P('ctx')
Inputs may be any that keep to these rules, and one draw needn't show every extreme that they name: `parents`: entry s is the index within its tree of segment s's parent; the first segment of every tree has -1 and no other segment has; every other segment's parent has a lower index in the same tree. `routes`: of the rows of one device (aligned blocks of 256 rows), at most 96 name one expert, and some block reaches 96.
All inputs are finite; a program needn't handle non-finite values.
Results may differ from a plain program's by a relative error of at most 0.029.
Values may be sent and summed in bfloat16 or wider, within the bound.
A program may use at most 320 MiB of HBM per device.

v0:
```python
import math

import jax
import jax.numpy as jnp
from jax import lax
from jax.sharding import PartitionSpec as P

HEAD_DIMENSION = 64
TOP = 8
ADAPTER_RANK = 16
SEG = 128
SEGS_DEV = 8
TREE_SEGS = 32


RESIDUAL_SCALE = 0.22
SCORE_SCALE = 0.015625
EPSILON = 1e-06
ROPE_BASE = 10000.0
MASKED = -1e30


def shifted(block, axis, distance):
    devices = range(lax.axis_size(axis))
    route = [(i - distance, i) for i in devices if i - distance in devices]
    return lax.ppermute(block, axis, route)


def rms_scale(values, gain_row):
    return (
        values * lax.rsqrt(jnp.mean(values * values, axis=-1, keepdims=True) + EPSILON) * gain_row
    )


def rms_back(values, gain_row, grad_in):

    def scaled(inner_arg):
        return rms_scale(inner_arg, gain_row)

    result, pullback = jax.vjp(scaled, values)
    return pullback(grad_in)[0]


def apply_rotary(values, token_positions):
    half_width = values.shape[-1] // 2
    freqs = ROPE_BASE ** (-(jnp.arange(half_width, dtype=jnp.float32) * 2.0) / values.shape[-1])
    angles = token_positions[:, None] * freqs[None, :]
    cosine = jnp.cos(angles)[:, None, :]
    sine = jnp.sin(angles)[:, None, :]
    first_half = values[..., :half_width]
    second_half = values[..., half_width:]
    return jnp.concatenate(
        [first_half * cosine - second_half * sine, second_half * cosine + first_half * sine],
        axis=-1,
    )


def rotate_back(grad_in, token_positions):

    def turned(inner_arg):
        return apply_rotary(inner_arg, token_positions)

    result, pullback = jax.vjp(turned, jnp.zeros_like(grad_in))
    return pullback(grad_in)[0]


def tree_links(tree_parents):
    seg_count = tree_parents.shape[0]
    columns = jnp.arange(seg_count, dtype=jnp.int32)

    def climb(loop_index, carried):
        current, ancestors = carried
        hit_table = current[:, None] == columns[None, :]
        ancestors = ancestors + hit_table.astype(jnp.float32)
        current = jnp.sum(hit_table.astype(jnp.int32) * (tree_parents[None, :] + 1), axis=1) - 1
        return (current, ancestors)

    current, ancestors = lax.fori_loop(
        0, seg_count, climb, (tree_parents, jnp.zeros((seg_count, seg_count), jnp.float32))
    )
    return (ancestors, jnp.sum(ancestors, axis=1))


def expert_dot(pattern, left_arg, right_arg):
    return jnp.einsum(pattern, left_arg, right_arg, preferred_element_type=jnp.float32)


def per_device(
    tokens,
    out_grad,
    routes,
    parents,
    adapter_set,
    gain_a,
    gain_b,
    w_query,
    key_projection_matrix,
    value_projection_matrix,
    w_output,
    w_router,
    w_gate,
    w_up,
    w_down,
    query_in,
    query_out,
    key_in,
    key_second_factor,
    value_in,
    value_second_factor,
    out_in,
    out_out,
    gate_in,
    gate_out,
    up_in,
    up_out,
    down_in,
    down_out,
):
    query_full, key_full, value_complete, output_full, gate_full, up_full, down_full = (
        lax.all_gather(w_query, "fsdp", axis=0, tiled=True),
        lax.all_gather(key_projection_matrix, "fsdp", axis=0, tiled=True),
        lax.all_gather(value_projection_matrix, "fsdp", axis=0, tiled=True),
        lax.all_gather(w_output, "fsdp", axis=1, tiled=True),
        lax.all_gather(w_gate, "fsdp", axis=1, tiled=True),
        lax.all_gather(w_up, "fsdp", axis=1, tiled=True),
        lax.all_gather(w_down, "fsdp", axis=1, tiled=True),
    )
    tp_rank = lax.axis_index("tp")
    ctx_rank = lax.axis_index("ctx")
    ctx_count = lax.axis_size("ctx")
    fsdp_rank = lax.axis_index("fsdp")
    tok_rows, model_width = tokens.shape
    query_cols = query_full.shape[1]
    pair_cols = key_full.shape[1]
    query_heads = query_cols // HEAD_DIMENSION
    pair_heads = pair_cols // HEAD_DIMENSION
    group_size = query_heads // pair_heads
    reduced_rank_update = query_in.shape[1]
    inputs = tokens.astype(jnp.float32)
    gain_one = gain_a.astype(jnp.float32)
    gain_two = gain_b.astype(jnp.float32)
    seg_start = (fsdp_rank * ctx_count + ctx_rank) * SEGS_DEV
    tree_index = seg_start // TREE_SEGS
    local_start = seg_start % TREE_SEGS
    tree_parents = lax.dynamic_slice_in_dim(parents, tree_index * TREE_SEGS, TREE_SEGS, 0)
    ancestors, seg_depth = tree_links(tree_parents)
    chosen = lax.dynamic_slice_in_dim(adapter_set, tree_index, 1, 0)[0]
    mask_columns = (
        jnp.arange(reduced_rank_update, dtype=jnp.int32) // ADAPTER_RANK == chosen
    ).astype(jnp.float32)
    mask_cubic = jnp.concatenate([mask_columns, mask_columns, mask_columns])
    incoming_rows = jnp.concatenate([query_in, key_in, value_in], axis=1)
    normalized_rows = rms_scale(inputs, gain_one).astype(jnp.bfloat16)
    tree_adapter = jnp.dot(
        normalized_rows, incoming_rows, preferred_element_type=jnp.float32
    ).astype(jnp.bfloat16) * mask_cubic.astype(jnp.bfloat16)
    grouped_heads, adapter_rows = (
        lax.all_gather(normalized_rows, "tp", axis=0, tiled=True),
        lax.all_gather(tree_adapter, "tp", axis=0, tiled=True),
    )
    group_rows = grouped_heads.shape[0]
    seg_local = local_start + jnp.arange(group_rows, dtype=jnp.int32) // SEG
    offset = jnp.arange(group_rows, dtype=jnp.int32) % SEG
    tree_cols = jnp.arange(TREE_SEGS, dtype=jnp.int32)
    query_onehot = (seg_local[:, None] == tree_cols[None, :]).astype(jnp.float32)
    token_positions = jnp.dot(
        query_onehot, seg_depth, precision=lax.Precision.HIGHEST
    ) * SEG + offset.astype(jnp.float32)
    query_links = jnp.dot(query_onehot, ancestors, precision=lax.Precision.HIGHEST)
    query_out_cols = lax.dynamic_slice_in_dim(query_out, tp_rank * query_cols, query_cols, 1)
    key_out_cols = lax.dynamic_slice_in_dim(key_second_factor, tp_rank * pair_cols, pair_cols, 1)
    value_out_cols = lax.dynamic_slice_in_dim(
        value_second_factor, tp_rank * pair_cols, pair_cols, 1
    )
    query_reduced = adapter_rows[:, :reduced_rank_update]
    key_reduced = adapter_rows[:, reduced_rank_update : 2 * reduced_rank_update]
    value_reduced = adapter_rows[:, 2 * reduced_rank_update :]
    query_pre = jnp.dot(grouped_heads, query_full, preferred_element_type=jnp.float32) + jnp.dot(
        query_reduced, query_out_cols, preferred_element_type=jnp.float32
    )
    key_unrotated = jnp.dot(grouped_heads, key_full, preferred_element_type=jnp.float32) + jnp.dot(
        key_reduced, key_out_cols, preferred_element_type=jnp.float32
    )
    value_pre = jnp.dot(
        grouped_heads, value_complete, preferred_element_type=jnp.float32
    ) + jnp.dot(value_reduced, value_out_cols, preferred_element_type=jnp.float32)
    query_rot = apply_rotary(
        query_pre.reshape(group_rows, query_heads, HEAD_DIMENSION), token_positions
    ).astype(jnp.bfloat16)
    key_rot = apply_rotary(
        key_unrotated.reshape(group_rows, pair_heads, HEAD_DIMENSION), token_positions
    ).astype(jnp.bfloat16)
    value_cast = value_pre.astype(jnp.bfloat16).reshape(group_rows, pair_heads, HEAD_DIMENSION)
    tree_span = TREE_SEGS // SEGS_DEV
    key_parts = [key_rot]
    value_parts = [value_cast]
    for distance in range(1, tree_span):
        far_key, far_value = shifted((key_rot, value_cast), "ctx", distance)
        key_parts.append(far_key)
        value_parts.append(far_value)
    keys_all = jnp.concatenate(key_parts, axis=0)
    every_value = jnp.concatenate(value_parts, axis=0)
    key_seg = jnp.concatenate([seg_local - distance * SEGS_DEV for distance in range(tree_span)])
    key_off = jnp.tile(offset, tree_span)
    key_onehot = (key_seg[:, None] == tree_cols[None, :]).astype(jnp.float32)
    block_rows = math.gcd(group_rows, 512)
    starts = jnp.arange(group_rows // block_rows, dtype=jnp.int32) * block_rows

    def block_scores(row_start, key_table):
        link_block = lax.dynamic_slice_in_dim(query_links, row_start, block_rows, 0)
        seg_block = lax.dynamic_slice_in_dim(seg_local, row_start, block_rows, 0)
        off_block = lax.dynamic_slice_in_dim(offset, row_start, block_rows, 0)
        linked = (
            jnp.einsum("rt,nt->rn", link_block, key_onehot, precision=lax.Precision.HIGHEST) > 0.5
        )
        same_seg = (seg_block[:, None] == key_seg[None, :]) & (
            key_off[None, :] <= off_block[:, None]
        )
        allowed = linked | same_seg
        query_block = lax.dynamic_slice_in_dim(query_rot, row_start, block_rows, 0).reshape(
            block_rows, pair_heads, group_size, HEAD_DIMENSION
        )
        raw_scores = (
            jnp.einsum("bkgd,nkd->kgbn", query_block, key_table, preferred_element_type=jnp.float32)
            * SCORE_SCALE
        )
        return (jnp.where(allowed[None, None], raw_scores, MASKED), query_block)

    def attend(row_start):
        scores, query_block = block_scores(row_start, keys_all)
        top_score = jnp.max(scores, axis=-1, keepdims=True)
        weights = jnp.exp(scores - top_score)
        prob_total = jnp.sum(weights, axis=-1, keepdims=True)
        prob_table = weights / prob_total
        mixed_rows = jnp.einsum(
            "kgbn,nkd->bkgd",
            prob_table.astype(jnp.bfloat16),
            every_value,
            preferred_element_type=jnp.float32,
        )
        return (
            mixed_rows.reshape(block_rows, query_cols),
            (top_score + jnp.log(prob_total))[..., 0],
        )

    attended_blocks, log_totals = lax.map(attend, starts)
    attention_result = attended_blocks.reshape(group_rows, query_cols).astype(jnp.bfloat16)
    output_rows = lax.dynamic_slice_in_dim(out_in, tp_rank * query_cols, query_cols, 0)
    head_part = jnp.dot(attention_result, output_full, preferred_element_type=jnp.float32)
    adapter_piece = jnp.dot(attention_result, output_rows, preferred_element_type=jnp.float32)
    summed_heads, adapter_total = (
        lax.psum_scatter(
            head_part.astype(jnp.bfloat16), "tp", scatter_dimension=0, tiled=True
        ).astype(jnp.float32),
        lax.psum_scatter(
            adapter_piece.astype(jnp.bfloat16), "tp", scatter_dimension=0, tiled=True
        ).astype(jnp.float32),
    )
    output_reduced = adapter_total.astype(jnp.bfloat16) * mask_columns.astype(jnp.bfloat16)
    branch = summed_heads + jnp.dot(output_reduced, out_out, preferred_element_type=jnp.float32)
    middle = inputs + RESIDUAL_SCALE * branch
    experts = w_router.shape[1]
    local_experts = w_gate.shape[0]
    capacity = tok_rows * TOP * 3 // (2 * experts)
    normed_two = rms_scale(middle, gain_two).astype(jnp.bfloat16)
    logits = jnp.dot(normed_two, w_router, preferred_element_type=jnp.float32)
    pick_table = (routes[:, :, None] == jnp.arange(experts, dtype=jnp.int32)[None, None, :]).astype(
        jnp.float32
    )
    picked = jnp.sum(pick_table * logits[:, None, :], axis=2)

    def gate_soft(values):
        return jax.nn.softmax(values, axis=-1)

    gate_weights, gate_pull = jax.vjp(gate_soft, picked)
    flat_routes = routes.reshape(-1)
    hit_table = (flat_routes[:, None] == jnp.arange(experts, dtype=jnp.int32)[None, :]).astype(
        jnp.int32
    )
    slot_rank = jnp.sum((jnp.cumsum(hit_table, axis=0) - 1) * hit_table, axis=1)
    owner_rank = flat_routes // local_experts
    within = flat_routes % local_experts
    slot_index = (within * ctx_count + owner_rank) * capacity + slot_rank
    send_rows = (
        jnp.zeros((experts * capacity, model_width), jnp.bfloat16)
        .at[slot_index]
        .set(jnp.repeat(normed_two, TOP, axis=0))
    )
    parcel = send_rows.reshape(local_experts, ctx_count * capacity, model_width)
    set_tags = jnp.full((1, ctx_count), chosen, jnp.int32)
    arrived, arrived_tags = (
        lax.all_to_all(parcel, "ctx", split_axis=1, concat_axis=1, tiled=True),
        lax.all_to_all(set_tags, "ctx", split_axis=1, concat_axis=1, tiled=True),
    )
    row_sets = jnp.repeat(arrived_tags[0], capacity)
    row_mask = (
        jnp.arange(reduced_rank_update, dtype=jnp.int32)[None, :] // ADAPTER_RANK
        == row_sets[:, None]
    ).astype(jnp.float32)
    row_mask_half = row_mask.astype(jnp.bfloat16)
    gate_inner = expert_dot("erd,eds->ers", arrived, gate_in).astype(jnp.bfloat16) * row_mask_half
    up_inner = expert_dot("erd,eds->ers", arrived, up_in).astype(jnp.bfloat16) * row_mask_half
    gate_value = expert_dot("erd,edf->erf", arrived, gate_full) + expert_dot(
        "ers,esf->erf", gate_inner, gate_out
    )
    up_value = expert_dot("erd,edf->erf", arrived, up_full) + expert_dot(
        "ers,esf->erf", up_inner, up_out
    )

    def swiglu(gate_arg, up_arg):
        return jax.nn.silu(gate_arg) * up_arg

    active_full, act_pull = jax.vjp(swiglu, gate_value, up_value)
    active = active_full.astype(jnp.bfloat16)
    down_inner = expert_dot("erf,efs->ers", active, down_in).astype(jnp.bfloat16) * row_mask_half
    produced = (
        expert_dot("erf,efd->erd", active, down_full)
        + expert_dot("ers,esd->erd", down_inner, down_out)
    ).astype(jnp.bfloat16)
    returned = lax.all_to_all(produced, "ctx", split_axis=1, concat_axis=1, tiled=True)
    slot_rows = returned.reshape(experts * capacity, model_width)[slot_index].reshape(
        tok_rows, TOP, model_width
    )
    mixture = jnp.sum(gate_weights[:, :, None] * slot_rows.astype(jnp.float32), axis=1)
    output = (middle + RESIDUAL_SCALE * mixture).astype(jnp.bfloat16)
    upstream = out_grad.astype(jnp.float32)
    mixture_grad = RESIDUAL_SCALE * upstream
    gate_grads = jnp.sum(mixture_grad[:, None, :] * slot_rows.astype(jnp.float32), axis=2)
    slot_grads = (
        (gate_weights[:, :, None] * mixture_grad[:, None, :])
        .astype(jnp.bfloat16)
        .reshape(tok_rows * TOP, model_width)
    )
    back_rows = (
        jnp.zeros((experts * capacity, model_width), jnp.bfloat16).at[slot_index].set(slot_grads)
    )
    produced_grad = lax.all_to_all(
        back_rows.reshape(local_experts, ctx_count * capacity, model_width),
        "ctx",
        split_axis=1,
        concat_axis=1,
        tiled=True,
    )
    down_out_grad = expert_dot("ers,erd->esd", down_inner, produced_grad)
    down_inner_grad = (expert_dot("erd,esd->ers", produced_grad, down_out) * row_mask).astype(
        jnp.bfloat16
    )
    down_in_grad = expert_dot("erf,ers->efs", active, down_inner_grad)
    active_grad = (
        expert_dot("erd,efd->erf", produced_grad, down_full)
        + expert_dot("ers,efs->erf", down_inner_grad, down_in)
    ).astype(jnp.bfloat16)
    gate_value_grad, up_value_grad = act_pull(active_grad.astype(jnp.float32))
    gate_value_grad = gate_value_grad.astype(jnp.bfloat16)
    up_value_grad = up_value_grad.astype(jnp.bfloat16)
    gate_out_grad = expert_dot("ers,erf->esf", gate_inner, gate_value_grad)
    up_out_grad = expert_dot("ers,erf->esf", up_inner, up_value_grad)
    gate_inner_grad = (expert_dot("erf,esf->ers", gate_value_grad, gate_out) * row_mask).astype(
        jnp.bfloat16
    )
    up_inner_grad = (expert_dot("erf,esf->ers", up_value_grad, up_out) * row_mask).astype(
        jnp.bfloat16
    )
    gate_in_grad = expert_dot("erd,ers->eds", arrived, gate_inner_grad)
    up_in_grad = expert_dot("erd,ers->eds", arrived, up_inner_grad)
    rows_grad = (
        expert_dot("erf,edf->erd", gate_value_grad, gate_full)
        + expert_dot("erf,edf->erd", up_value_grad, up_full)
        + expert_dot("ers,eds->erd", gate_inner_grad, gate_in)
        + expert_dot("ers,eds->erd", up_inner_grad, up_in)
    ).astype(jnp.bfloat16)
    returned_grad = lax.all_to_all(rows_grad, "ctx", split_axis=1, concat_axis=1, tiled=True)
    normed_two_grad = jnp.sum(
        returned_grad.reshape(experts * capacity, model_width)[slot_index]
        .reshape(tok_rows, TOP, model_width)
        .astype(jnp.float32),
        axis=1,
    )
    picked_grad = gate_pull(gate_grads)[0]
    logits_grad = jnp.sum(pick_table * picked_grad[:, :, None], axis=1)
    normed_two_grad = normed_two_grad + jnp.einsum(
        "te,de->td", logits_grad, w_router.astype(jnp.float32), precision=lax.Precision.HIGHEST
    )
    middle_grad = upstream + rms_back(middle, gain_two, normed_two_grad)
    branch_grad = (RESIDUAL_SCALE * middle_grad).astype(jnp.bfloat16)
    out_low_grad = (
        jnp.einsum("td,sd->ts", branch_grad, out_out, preferred_element_type=jnp.float32)
        * mask_columns
    ).astype(jnp.bfloat16)
    out_out_grad = jnp.einsum(
        "ts,td->sd", output_reduced, branch_grad, preferred_element_type=jnp.float32
    )
    branch_all, out_low_all = (
        lax.all_gather(branch_grad, "tp", axis=0, tiled=True),
        lax.all_gather(out_low_grad, "tp", axis=0, tiled=True),
    )
    attended_grad = (
        jnp.einsum("rd,cd->rc", branch_all, output_full, preferred_element_type=jnp.float32)
        + jnp.einsum("rs,cs->rc", out_low_all, output_rows, preferred_element_type=jnp.float32)
    ).astype(jnp.bfloat16)
    out_in_part = jnp.einsum(
        "rc,rs->cs", attention_result, out_low_all, preferred_element_type=jnp.float32
    )
    out_in_grad = lax.dynamic_update_slice_in_dim(
        jnp.zeros(out_in.shape, jnp.float32), out_in_part, tp_rank * query_cols, 0
    )
    grad_blocks = attended_grad.reshape(
        group_rows // block_rows, block_rows, pair_heads, group_size, HEAD_DIMENSION
    )

    def retrace(carried, packed):
        key_acc, value_acc = carried
        row_start, lse_block, grad_block = packed
        scores, query_block = block_scores(row_start, keys_all)
        prob_table = jnp.exp(scores - lse_block[..., None])
        prob_grad = jnp.einsum(
            "bkgd,nkd->kgbn", grad_block, every_value, preferred_element_type=jnp.float32
        )
        inner_sum = jnp.sum(prob_table * prob_grad, axis=-1, keepdims=True)
        score_grad = (prob_table * (prob_grad - inner_sum)).astype(jnp.bfloat16)
        query_grad = (
            jnp.einsum("kgbn,nkd->bkgd", score_grad, keys_all, preferred_element_type=jnp.float32)
            * SCORE_SCALE
        )
        key_acc = (
            key_acc
            + jnp.einsum(
                "kgbn,bkgd->nkd", score_grad, query_block, preferred_element_type=jnp.float32
            )
            * SCORE_SCALE
        )
        value_acc = value_acc + jnp.einsum(
            "kgbn,bkgd->nkd",
            prob_table.astype(jnp.bfloat16),
            grad_block,
            preferred_element_type=jnp.float32,
        )
        return ((key_acc, value_acc), query_grad.reshape(block_rows, query_heads, HEAD_DIMENSION))

    zero_keys = jnp.zeros(keys_all.shape, jnp.float32)
    (key_acc, value_acc), query_grads = lax.scan(
        retrace, (zero_keys, zero_keys), (starts, log_totals, grad_blocks)
    )
    key_grad = key_acc[:group_rows]
    value_grad = value_acc[:group_rows]
    for distance in range(1, tree_span):
        far_key_grad, far_value_grad = (
            shifted(
                key_acc[distance * group_rows : (distance + 1) * group_rows].astype(jnp.bfloat16),
                "ctx",
                -distance,
            ).astype(jnp.float32),
            shifted(
                value_acc[distance * group_rows : (distance + 1) * group_rows].astype(jnp.bfloat16),
                "ctx",
                -distance,
            ).astype(jnp.float32),
        )
        key_grad = key_grad + far_key_grad
        value_grad = value_grad + far_value_grad
    query_pre_grad = (
        rotate_back(query_grads.reshape(group_rows, query_heads, HEAD_DIMENSION), token_positions)
        .reshape(group_rows, query_cols)
        .astype(jnp.bfloat16)
    )
    key_pre_grad = (
        rotate_back(key_grad, token_positions).reshape(group_rows, pair_cols).astype(jnp.bfloat16)
    )
    value_pre_grad = value_grad.reshape(group_rows, pair_cols).astype(jnp.bfloat16)
    normed_part = (
        jnp.einsum("rc,dc->rd", query_pre_grad, query_full, preferred_element_type=jnp.float32)
        + jnp.einsum("rc,dc->rd", key_pre_grad, key_full, preferred_element_type=jnp.float32)
        + jnp.einsum(
            "rc,dc->rd", value_pre_grad, value_complete, preferred_element_type=jnp.float32
        )
    )
    adapter_piece_gradient = jnp.concatenate(
        [
            jnp.einsum(
                "rc,sc->rs", query_pre_grad, query_out_cols, preferred_element_type=jnp.float32
            ),
            jnp.einsum("rc,sc->rs", key_pre_grad, key_out_cols, preferred_element_type=jnp.float32),
            jnp.einsum(
                "rc,sc->rs", value_pre_grad, value_out_cols, preferred_element_type=jnp.float32
            ),
        ],
        axis=1,
    )
    query_out_part = jnp.einsum(
        "rs,rc->sc", query_reduced, query_pre_grad, preferred_element_type=jnp.float32
    )
    key_out_part = jnp.einsum(
        "rs,rc->sc", key_reduced, key_pre_grad, preferred_element_type=jnp.float32
    )
    value_out_part = jnp.einsum(
        "rs,rc->sc", value_reduced, value_pre_grad, preferred_element_type=jnp.float32
    )
    query_out_grad = lax.dynamic_update_slice_in_dim(
        jnp.zeros(query_out.shape, jnp.float32), query_out_part, tp_rank * query_cols, 1
    )
    key_out_grad = lax.dynamic_update_slice_in_dim(
        jnp.zeros(key_second_factor.shape, jnp.float32), key_out_part, tp_rank * pair_cols, 1
    )
    value_out_grad = lax.dynamic_update_slice_in_dim(
        jnp.zeros(value_second_factor.shape, jnp.float32), value_out_part, tp_rank * pair_cols, 1
    )
    local_normalized_gradient, tree_adapter_gradient = (
        lax.psum_scatter(
            normed_part.astype(jnp.bfloat16), "tp", scatter_dimension=0, tiled=True
        ).astype(jnp.float32),
        lax.psum_scatter(
            adapter_piece_gradient.astype(jnp.bfloat16), "tp", scatter_dimension=0, tiled=True
        ).astype(jnp.float32),
    )
    tree_adapter_reduced = (tree_adapter_gradient * mask_cubic).astype(jnp.bfloat16)
    local_normalized_gradient = local_normalized_gradient + jnp.einsum(
        "oy,ky->ok", tree_adapter_reduced, incoming_rows, preferred_element_type=jnp.float32
    )
    incoming_rows_gradient = jnp.einsum(
        "zu,zp->up", normalized_rows, tree_adapter_reduced, preferred_element_type=jnp.float32
    )
    input_grad = (middle_grad + rms_back(inputs, gain_one, local_normalized_gradient)).astype(
        jnp.bfloat16
    )
    adapter_totals = lax.psum(
        (
            incoming_rows_gradient[:, :reduced_rank_update],
            query_out_grad,
            incoming_rows_gradient[:, reduced_rank_update : 2 * reduced_rank_update],
            key_out_grad,
            incoming_rows_gradient[:, 2 * reduced_rank_update :],
            value_out_grad,
            out_in_grad,
            out_out_grad,
        ),
        ("fsdp", "ctx", "tp"),
    )
    expert_totals = (
        lax.psum(gate_in_grad.astype(jnp.bfloat16), ("fsdp", "tp")).astype(jnp.float32),
        lax.psum(gate_out_grad.astype(jnp.bfloat16), ("fsdp", "tp")).astype(jnp.float32),
        lax.psum(up_in_grad.astype(jnp.bfloat16), ("fsdp", "tp")).astype(jnp.float32),
        lax.psum(up_out_grad.astype(jnp.bfloat16), ("fsdp", "tp")).astype(jnp.float32),
        lax.psum(down_in_grad.astype(jnp.bfloat16), ("fsdp", "tp")).astype(jnp.float32),
        lax.psum(down_out_grad.astype(jnp.bfloat16), ("fsdp", "tp")).astype(jnp.float32),
    )
    return (
        output,
        input_grad,
        adapter_totals[0],
        adapter_totals[1],
        adapter_totals[2],
        adapter_totals[3],
        adapter_totals[4],
        adapter_totals[5],
        adapter_totals[6],
        adapter_totals[7],
        expert_totals[0],
        expert_totals[1],
        expert_totals[2],
        expert_totals[3],
        expert_totals[4],
        expert_totals[5],
    )


def solution(mesh):
    in_specs = (
        P(("fsdp", "ctx", "tp"), None),
        P(("fsdp", "ctx", "tp"), None),
        P(("fsdp", "ctx", "tp"), None),
        P(),
        P(),
        P(),
        P(),
        P("fsdp", "tp"),
        P("fsdp", "tp"),
        P("fsdp", "tp"),
        P("tp", "fsdp"),
        P(),
        P("ctx", "fsdp", None),
        P("ctx", "fsdp", None),
        P("ctx", "fsdp", None),
        P(),
        P(),
        P(),
        P(),
        P(),
        P(),
        P(),
        P(),
        P("ctx", None, None),
        P("ctx", None, None),
        P("ctx", None, None),
        P("ctx", None, None),
        P("ctx", None, None),
        P("ctx", None, None),
    )
    out_specs = (
        P(("fsdp", "ctx", "tp"), None),
        P(("fsdp", "ctx", "tp"), None),
        P(),
        P(),
        P(),
        P(),
        P(),
        P(),
        P(),
        P(),
        P("ctx", None, None),
        P("ctx", None, None),
        P("ctx", None, None),
        P("ctx", None, None),
        P("ctx", None, None),
        P("ctx", None, None),
    )
    return jax.shard_map(
        per_device, mesh=mesh, in_specs=in_specs, out_specs=out_specs, check_vma=False
    )
```

profile of v0, /device:TPU:13, one launch (start us, length us, event | category | flops | bytes accessed | tf_op | source)
XLA Modules:
  0.0 1682.5 jit_solution(2573971728114249958)
XLA Ops:
  52.7 16.5 all_gather.35
  104.4 121.9 %while.47 = (s32[]{:T(128)}, bf16[2,512,256]{2,1,0:T(8,128)(2,1)}, f32[2,2,2,512]{3,2,1,0:T(2,128)}, s32[2]{0:T(128)}, f32[1024,32]{1,0:T(8,128)}, /*index=5*/s3...) while((s32[]{:T(128)}, bf16[2,512,256]{2,1,0:T(8,128)(2,1)}, ...), condition=%wide.region_8.9_spmd.clone.clone, body=%wide.region_5.8_spmd.clone.clone.sunk | while | flops 3064199168 | bytes 124306240 | solution.py:246
  117.7 14.0 bitcast_reduce_fusion.2
  131.7 15.1 fusion.293
  146.8 16.6 fusion.294
  178.2 14.0 bitcast_reduce_fusion.2
  192.2 15.1 fusion.293
  207.3 16.6 fusion.294
  256.7 35.2 %reduce-scatter.5.cloned.1.call-done = bf16[256,1024]{1,0:T(8,128)(2,1)} async-done(((bf16[1024,1024]{1,0:T(8,128)(2,1)}), bf16[256,1024]{1,0:T(8,128)(2,1)}) %reduce-scatter.5.cloned.1.call-update) | async-done | bytes 524304 | tf_op jit(solution)/shard_map/reduce_scatter | solution.py:252
  294.8 13.6 scatter_custom_fusion
  328.0 14.3 scatter_custom_fusion.1
  351.3 41.2 %all-to-all-done = bf16[8,384,1024]{2,0,1:T(8,128)(2,1)} async-done(((bf16[8,384,1024]{2,0,1:T(8,128)(2,1)}), bf16[8,384,1024]{2,0,1:T(8,128)(2,1)}, u32[]{:S(2)}, u32[]{:S(2)}) %all-to-all-start) | async-done | bytes 6291488 | tf_op jit(solution)/shard_map/all_to_all | solution.py:292
  463.7 93.1 %all-gather.12.cloned.1.call-done = bf16[8,512,1024]{2,1,0:T(8,128)(2,1)} async-done(((bf16[8,256,1024]{2,1,0:T(8,128)(2,1)}), bf16[8,512,1024]{2,1,0:T(8,128)(2,1)}) %all-gather.12.cloned.1.call-update) | async-done | bytes 8388624 | tf_op jit(solution)/shard_map/all_gather | solution.py:126
  556.8 15.7 fusion.72
  579.3 15.2 fusion.66
  653.5 15.8 add_convert_fusion
  703.0 14.8 gather_fusion
  724.2 38.7 %all-to-all-done.4 = bf16[8,384,1024]{2,0,1:T(8,128)(2,1)} async-done(((bf16[8,384,1024]{2,0,1:T(8,128)(2,1)}), bf16[8,384,1024]{2,0,1:T(8,128)(2,1)}, u32[]{:S(2)}, u32[]{:S(2)}) %all-to-all-start.4) | async-done | bytes 6291488 | tf_op jit(solution)/shard_map/all_to_all | solution.py:372
  771.7 15.1 gather_fusion.1
  807.5 13.8 all_gather.43
  821.3 22.4 %all-gather.14.cloned.1.call-done = bf16[1024,1024]{1,0:T(8,128)(2,1)} async-done(((bf16[256,1024]{1,0:T(8,128)(2,1)}), bf16[1024,1024]{1,0:T(8,128)(2,1)}) %all-gather.14.cloned.1.call-update) | async-done | bytes 2097168 | tf_op jit(solution)/shard_map/all_gather | solution.py:394
  850.0 253.0 %while.48 = (s32[]{:T(128)}, f32[4096,2,64]{0,2,1:T(8,128)}, f32[4096,2,64]{0,2,1:T(8,128)}, f32[2,512,4,64]{1,0,3,2:T(2,128)}, s32[2]{0:T(128)}, /*index=5*/bf1...) while((s32[]{:T(128)}, f32[4096,2,64]{0,2,1:T(8,128)}, ...), condition=%wide.region_28.29_spmd.clone.clone.clone, body=%wide.region_26.28_spmd.clone.clone.clone.sunk | while | flops 6313342976 | bytes 284664640 | solution.py:441
  876.3 25.1 %fusion.306 = (f32[2,2,512]{2,1,0:T(2,128)}, f32[2,512,2,4096]{3,1,2,0:T(8,128)}) fusion(f32[2,512,2,4096]{3,1,2,0:T(8,128)} %fusion.305, f32[2,2,512]{2,1,0:T(2,128)S(1)} %dynamic-slice_bitcast_fusion.2, pred[512,4096]{1,0:T(8,128)(4,1)S(1)} %and_or_fusion.5, bf16[4096,2,64]{0,2,1:T(8,128)(2,1)S(1)} %copy-done.6, ...), kind=kOutput, calls=%fused_computation.41.clone.1 | convolution fusion | flops 1115682816 | bytes 70533120 | tf_op jit(solution)/shard_map/while/body/eval_jaxpr/bkgd,nkd->kgbn/dot_general | solution.py:416
  901.4 27.7 %fusion.307 = bf16[2,2,512,4096]{3,2,1,0:T(8,128)(2,1)} fusion(f32[2,512,2,4096]{3,1,2,0:T(8,128)} %get-tuple-element.913, f32[2,512,2,4096]{3,1,2,0:T(8,128)} %fusion.305, f32[2,2,512]{2,1,0:T(2,128)} %get-tuple-element.914, f32[2,2,512]{2,1,0:T(2,128)S(1)} %dynamic-slice_bitcast_fusion.2, pred[512,4096]{1,0:T(8,128)(4,1)S(1)} %and_or_fusion.5), kind=kLoop, calls=%fused_computation.43.clone.1 | loop fusion | flops 50331648 | bytes 85999616 | tf_op jit(solution)/shard_map/while/body/eval_jaxpr/convert_element_type | solution.py:420
  959.7 16.1 fusion.309
  988.8 13.1 fusion.305
  1002.0 25.1 %fusion.306 = (f32[2,2,512]{2,1,0:T(2,128)}, f32[2,512,2,4096]{3,1,2,0:T(8,128)}) fusion(f32[2,512,2,4096]{3,1,2,0:T(8,128)} %fusion.305, f32[2,2,512]{2,1,0:T(2,128)S(1)} %dynamic-slice_bitcast_fusion.2, pred[512,4096]{1,0:T(8,128)(4,1)S(1)} %and_or_fusion.5, bf16[4096,2,64]{0,2,1:T(8,128)(2,1)S(1)} %copy-done.6, ...), kind=kOutput, calls=%fused_computation.41.clone.1 | convolution fusion | flops 1115682816 | bytes 70533120 | tf_op jit(solution)/shard_map/while/body/eval_jaxpr/bkgd,nkd->kgbn/dot_general | solution.py:416
  1027.1 27.7 %fusion.307 = bf16[2,2,512,4096]{3,2,1,0:T(8,128)(2,1)} fusion(f32[2,512,2,4096]{3,1,2,0:T(8,128)} %get-tuple-element.913, f32[2,512,2,4096]{3,1,2,0:T(8,128)} %fusion.305, f32[2,2,512]{2,1,0:T(2,128)} %get-tuple-element.914, f32[2,2,512]{2,1,0:T(2,128)S(1)} %dynamic-slice_bitcast_fusion.2, pred[512,4096]{1,0:T(8,128)(4,1)S(1)} %and_or_fusion.5), kind=kLoop, calls=%fused_computation.43.clone.1 | loop fusion | flops 50331648 | bytes 85999616 | tf_op jit(solution)/shard_map/while/body/eval_jaxpr/convert_element_type | solution.py:420
  1086.0 16.6 fusion.309
  1168.8 296.5 %all-reduce.11.cloned.1.call-done = (bf16[8,1024,128]{2,1,0:T(8,128)(2,1)}, bf16[8,128,512]{2,1,0:T(8,128)(2,1)}, bf16[8,1024,128]{2,1,0:T(8,128)(2,1)}, bf16[8,...) async-done(((bf16[8,1024,128]{2,1,0:T(8,128)(2,1)}, bf16[8,128,512]{2,1,0:T(8,128)(2,1)}, bf16[8,1024,128]{2,1,0:T(8,128)(2,1)}, ...) | async-done | bytes 9437200 | tf_op jit(solution)/shard_map/psum | solution.py:539
  1478.9 31.3 %reduce-scatter.9.cloned.1.call-done = bf16[256,1024]{1,0:T(8,128)(2,1)} async-done(((bf16[1024,1024]{1,0:T(8,128)(2,1)}), bf16[256,1024]{1,0:T(8,128)(2,1)}) %reduce-scatter.9.cloned.1.call-update) | async-done | bytes 524304 | tf_op jit(solution)/shard_map/reduce_scatter | solution.py:508
  1515.4 145.8 %all-reduce.9.cloned.1.call-done = (f32[1024,128]{1,0:T(8,128)}, f32[128,1024]{1,0:T(8,128)}, f32[1024,128]{1,0:T(8,128)}, f32[128,512]{1,0:T(8,128)}, f32[1024,...) async-done(((f32[1024,128]{1,0:T(8,128)}, f32[128,1024]{1,0:T(8,128)}, f32[1024,128]{1,0:T(8,128)}, f32[128,512]{1,0:T(8,128)}, ...) | async-done | bytes 3670032 | tf_op jit(solution)/shard_map/psum | solution.py:525
  (651 shorter events, 582.2 us)
Async XLA Ops:
  8.0 564.5 %copy-start = (bf16[8,128,1024]{2,1,0:T(8,128)(2,1)S(1)}, bf16[8,128,1024]{2,1,0:T(8,128)(2,1)}, u32[]{:S(2)}) copy-start(bf16[8,128,1024]{2,1,0:T(8,128)(2,1)} %param.63) | copy-start | bytes 6291460
  8.0 61.1 %all-gather.6.cloned.1.call-start = ((), (), s32[]{:S(2)}) async-start(), calls=%async_computation.9 | async-start | bytes 2621440 | tf_op jit(solution)/shard_map/all_gather | solution.py:158
  13.3 243.4 %reduce-scatter.7.cloned.1.call-start = ((), (), s32[]{:S(2)}) async-start(), calls=%async_computation.11 | async-start | bytes 327680 | tf_op jit(solution)/shard_map/reduce_scatter | solution.py:255
  73.0 13.1 collective-permute-start.3
  74.3 16.2 collective-permute-start.4
  75.6 20.4 %collective-permute-start.5 = (bf16[1024,2,64]{0,2,1:T(8,128)(2,1)S(1)}, bf16[1024,2,64]{0,2,1:T(8,128)(2,1)S(1)}, u32[]{:S(2)}, u32[]{:S(2)}) collective-permute-start(bf16[1024,2,64]{0,2,1:T(8,128)(2,1)S(1)} %bitcast.351), channel_id=1, source_target_pairs={{0,12},{1,13},{2,14},{3,15},{16,28},{17,29},{18,30},{19,31}} | collective-permute-start | bytes 786440 | tf_op jit(solution)/shard_map/ppermute | solution.py:26
  80.4 16.5 collective-permute-start
  81.7 20.0 %collective-permute-start.1 = (bf16[1024,2,64]{0,2,1:T(8,128)(2,1)S(1)}, bf16[1024,2,64]{0,2,1:T(8,128)(2,1)S(1)}, u32[]{:S(2)}, u32[]{:S(2)}) collective-permute-start(bf16[1024,2,64]{0,2,1:T(8,128)(2,1)S(1)} %pad_maximum_fusion.4), channel_id=1, source_target_pairs={{0,8},{4,12},{1,9},{5,13},{2,10},{6,14},{3,11},{7,15},{16,24},{20,... | collective-permute-start | bytes 786440 | tf_op jit(solution)/shard_map/ppermute | solution.py:26
  86.0 18.3 %collective-permute-start.2 = (bf16[1024,2,64]{0,2,1:T(8,128)(2,1)S(1)}, bf16[1024,2,64]{0,2,1:T(8,128)(2,1)S(1)}, u32[]{:S(2)}, u32[]{:S(2)}) collective-permute-start(bf16[1024,2,64]{0,2,1:T(8,128)(2,1)S(1)} %pad_maximum_fusion.4), channel_id=1, source_target_pairs={{0,12},{1,13},{2,14},{3,15},{16,28},{17,29},{18,30},{19,31}} | collective-permute-start | bytes 786440 | tf_op jit(solution)/shard_map/ppermute | solution.py:26
  228.8 63.2 %reduce-scatter.5.cloned.1.call-start = ((), (), s32[]{:S(2)}) async-start(), calls=%async_computation.10 | async-start | bytes 2621440 | tf_op jit(solution)/shard_map/reduce_scatter | solution.py:252
  239.8 187.5 %all-gather.8.cloned.1.call-start = ((), (), s32[]{:S(2)}) async-start(), calls=%async_computation.12 | async-start | bytes 12582912 | tf_op jit(solution)/shard_map/all_gather | solution.py:124
  240.3 211.1 %all-gather.10.cloned.1.call-start = ((), (), s32[]{:S(2)}) async-start(), calls=%async_computation.13 | async-start | bytes 12582912 | tf_op jit(solution)/shard_map/all_gather | solution.py:125
  242.2 75.2 %all-to-all-start.1 = ((s32[1,4,1]{2,0,1:T(1,128)}), s32[1,4,1]{2,0,1:T(1,128)S(1)}, u32[]{:S(2)}, u32[]{:S(2)}) async-start(s32[1,4,1]{2,0,1:T(1,128)} %broadcast_in_dim.70), calls=%async_computation.3 | async-start | bytes 4096 | tf_op jit(solution)/shard_map/all_to_all | solution.py:293
  317.4 75.1 %all-to-all-start = ((bf16[8,384,1024]{2,0,1:T(8,128)(2,1)}), bf16[8,384,1024]{2,0,1:T(8,128)(2,1)}, u32[]{:S(2)}, u32[]{:S(2)}) async-start(bf16[8,384,1024]{2,0,1:T(8,128)(2,1)} %copy.211), calls=%async_computation.2 | async-start | bytes 12582912 | tf_op jit(solution)/shard_map/all_to_all | solution.py:292
  323.7 233.1 %all-gather.12.cloned.1.call-start = ((), (), s32[]{:S(2)}) async-start(), calls=%async_computation.14 | async-start | bytes 12582912 | tf_op jit(solution)/shard_map/all_gather | solution.py:126
  392.5 164.3 %all-to-all-start.3 = ((bf16[8,384,1024]{2,0,1:T(8,128)(2,1)}), bf16[8,384,1024]{2,0,1:T(8,128)(2,1)}, u32[]{:S(2)}, u32[]{:S(2)}) async-start(bf16[8,384,1024]{2,0,1:T(8,128)(2,1)} %copy.219), calls=%async_computation.5 | async-start | bytes 12582912 | tf_op jit(solution)/shard_map/all_to_all | solution.py:337
  400.2 172.3 %copy-start.79 = (f32[384,128]{1,0:T(8,128)}, f32[384,128]{1,0:T(8,128)S(1)}, u32[]{:S(2)}) copy-start(f32[384,128]{1,0:T(8,128)S(1)} %get-tuple-element.720) | copy-start | bytes 589828
  611.4 75.5 %all-to-all-start.2 = ((bf16[8,384,1024]{2,0,1:T(8,128)(2,1)}), bf16[8,384,1024]{2,0,1:T(8,128)(2,1)}, u32[]{:S(2)}, u32[]{:S(2)}) async-start(bf16[8,384,1024]{2,0,1:T(8,128)(2,1)} %copy.216), calls=%async_computation.4 | async-start | bytes 12582912 | tf_op jit(solution)/shard_map/all_to_all | solution.py:320
  686.9 75.9 %all-to-all-start.4 = ((bf16[8,384,1024]{2,0,1:T(8,128)(2,1)}), bf16[8,384,1024]{2,0,1:T(8,128)(2,1)}, u32[]{:S(2)}, u32[]{:S(2)}) async-start(bf16[8,384,1024]{2,0,1:T(8,128)(2,1)} %copy.222), calls=%async_computation.6 | async-start | bytes 12582912 | tf_op jit(solution)/shard_map/all_to_all | solution.py:372
  694.0 149.7 %all-gather.14.cloned.1.call-start = ((), (), s32[]{:S(2)}) async-start(), calls=%async_computation.15 | async-start | bytes 2621440 | tf_op jit(solution)/shard_map/all_gather | solution.py:394
  795.1 371.0 %reduce-scatter.11.cloned.1.call-start = ((), (), s32[]{:S(2)}) async-start(), calls=%async_computation.17 | async-start | bytes 983040 | tf_op jit(solution)/shard_map/reduce_scatter | solution.py:511
  849.9 255.2 %copy-start.30 = (f32[1024,32]{0,1:T(8,128)S(1)}, f32[1024,32]{0,1:T(8,128)}, u32[]{:S(2)}) copy-start(f32[1024,32]{0,1:T(8,128)} %copy-done.29) | copy-start | bytes 393220
  1108.1 10.6 collective-permute-start.6
  1111.0 9.0 collective-permute-start.7
  1113.2 11.8 collective-permute-start.8
  1114.8 15.9 collective-permute-start.10
  1116.2 18.0 %collective-permute-start.11 = (bf16[1024,2,64]{0,2,1:T(8,128)(2,1)S(1)}, bf16[1024,2,64]{0,2,1:T(8,128)(2,1)S(1)}, u32[]{:S(2)}, u32[]{:S(2)}) collective-permute-start(bf16[1024,2,64]{0,2,1:T(8,128)(2,1)S(1)} %get-tuple-element.709), channel_id=1, source_target_pairs={{12,0},{13,1},{14,2},{15,3},{28,16},{29,17},{30,18},{31,19}} | collective-permute-start | bytes 786440 | tf_op jit(solution)/shard_map/ppermute | solution.py:26
  1118.7 15.5 collective-permute-start.9
  1136.3 329.0 %all-reduce.11.cloned.1.call-start = ((), (), s32[]{:S(2)}) async-start(), calls=%async_computation.19 | async-start | bytes 18874368 | tf_op jit(solution)/shard_map/psum | solution.py:539
  1157.4 352.8 %reduce-scatter.9.cloned.1.call-start = ((), (), s32[]{:S(2)}) async-start(), calls=%async_computation.16 | async-start | bytes 2621440 | tf_op jit(solution)/shard_map/reduce_scatter | solution.py:508
  1162.1 499.1 %all-reduce.9.cloned.1.call-start = ((), (), s32[]{:S(2)}) async-start(), calls=%async_computation.18 | async-start | bytes 7340032 | tf_op jit(solution)/shard_map/psum | solution.py:525
  1511.9 162.9 %copy-start.1 = (bf16[8,128,1024]{2,1,0:T(8,128)(2,1)S(1)}, bf16[8,128,1024]{2,1,0:T(8,128)(2,1)}, u32[]{:S(2)}) copy-start(bf16[8,128,1024]{2,1,0:T(8,128)(2,1)} %param.63) | copy-start | bytes 6291460
  (118 other events, 1704.1 us)
Sparse Core Ops, SparseCore 0:
  13.4 45.6 all-gather.5
  228.9 16.0 reduce-scatter.6
  248.0 43.9 reduce-scatter.4
  795.2 48.4 all-gather.13
  1136.4 22.2 reduce-scatter.10
  1164.2 301.0 all-reduce.10
  1467.6 42.4 reduce-scatter.8
  1518.8 142.3 all-reduce.8
Sparse Core Ops, SparseCore 1:
  241.8 104.3 all-gather.7
  347.6 103.8 all-gather.9
  452.9 103.8 all-gather.11
where the time goes:
time: 1700 us; the launch traced here: 1680 us
  waiting for transfers between devices  755 us (44%)
  matrix products  456 us (27%)
  local copies, waits for them, and re-layouts  173 us (10%)
  other arithmetic  165 us (10%)
  blocking collectives  56 us (3%)
  starting transfers between devices  49.3 us (3%)
  between operations  17.7 us (1%)
    psum x1, waiting for transfers between devices, per_device(): lax.psum(gate_in_grad.astype(jnp.bfloat16), ('fsdp', 'tp'))  296 us
    dot_general x24, matrix products, expert_dot(): jnp.einsum(pattern, left_arg, right_arg, preferred_element_type=jnp.float32)  170 us
    psum x1, waiting for transfers between devices, per_device(): lax.psum((incoming_rows_gradient[:, :reduced_rank_update], query_out_grad...  146 us
    all_gather x1, waiting for transfers between devices, per_device(): lax.all_gather(w_down, 'fsdp', axis=1, tiled=True)  93.1 us
    convert_element_type x2, other arithmetic, retrace(): score_grad = (prob_table * (prob_grad - inner_sum)).astype(jnp.bfloat16)  55.4 us
    dot_general x4, matrix products, block_scores(): jnp.einsum('bkgd,nkd->kgbn', query_block, key_table, preferred_element_ty...  54.3 us
    dot_general x2, matrix products, retrace(): jnp.einsum('bkgd,nkd->kgbn', grad_block, every_value, preferred_element_t...  50.2 us
    all_to_all x1, waiting for transfers between devices, per_device(): lax.all_to_all(parcel, 'ctx', split_axis=1, concat_axis=1, tiled=True)  41.2 us
  transfers between devices with their start and end apart: 28, of which 17 were waited for; matrix products, arithmetic and copies ran while one was open for 18% of the time, Pallas kernels for 0%

commit v1 on v0

v1 whole, which is shorter than its diff:
```python
import functools
import math

import jax
import jax.numpy as jnp
from jax import lax
from jax.experimental import pallas as pl
from jax.experimental.pallas import tpu as pltpu
from jax.sharding import PartitionSpec as P

HEAD = 64
TOP = 8
RANK = 16
SEG = 128
SEGS_DEV = 8
TREE_SEGS = 32
SPAN = TREE_SEGS // SEGS_DEV
LANES = 128

RESIDUAL_SCALE = 0.22
SCORE_SCALE = 0.015625
EPSILON = 1e-06
ROPE_BASE = 10000.0
MASKED = -1e30

F32 = jnp.float32
BF16 = jnp.bfloat16

CODE = HEAD
LSE = CODE + TREE_SEGS + 1
ONES = HEAD

VMEM_LIMIT = 56 * 1024 * 1024


def dot(a, b):
    return lax.dot_general(a, b, (((1,), (0,)), ((), ())), preferred_element_type=F32)


def dot_nt(a, b):
    return lax.dot_general(a, b, (((1,), (1,)), ((), ())), preferred_element_type=F32)


def dot_tn(a, b):
    return lax.dot_general(a, b, (((0,), (0,)), ((), ())), preferred_element_type=F32)


def iota(shape, dim):
    return lax.broadcasted_iota(jnp.int32, shape, dim)


def shifted(block, axis, distance):
    devices = range(lax.axis_size(axis))
    route = [(i - distance, i) for i in devices if i - distance in devices]
    return lax.ppermute(block, axis, route)


def rms_scale(values, gain_row):
    return (
        values * lax.rsqrt(jnp.mean(values * values, axis=-1, keepdims=True) + EPSILON) * gain_row
    )


def rms_back(values, gain_row, grad):
    inv = lax.rsqrt(jnp.mean(values * values, axis=-1, keepdims=True) + EPSILON)
    scaled = grad * gain_row
    inner = jnp.mean(scaled * values, axis=-1, keepdims=True)
    return inv * scaled - values * (inv * inv * inv * inner)


def tree_links(tree_parents):
    count = tree_parents.shape[0]
    columns = jnp.arange(count, dtype=jnp.int32)
    reach = (
        (tree_parents[:, None] == columns[None, :]) | (columns[:, None] == columns[None, :])
    ).astype(BF16)
    for _ in range(max(1, (count - 1).bit_length())):
        reach = jnp.minimum(dot(reach, reach), 1.0).astype(BF16)
    reach = reach.astype(F32)
    return reach, jnp.sum(reach, axis=1) - 1.0


def swap_halves(values):
    width = values.shape[-1]
    lane = iota(values.shape, 1) % HEAD
    ahead = pltpu.roll(values, width - HEAD // 2, 1)
    behind = pltpu.roll(values, HEAD // 2, 1)
    return jnp.where(lane < HEAD // 2, -ahead, behind)


def place_table(rows, source, target):
    r, c = iota((rows, LANES), 0), iota((rows, LANES), 1)
    return ((r - source == c - target) & (c >= target) & (c < target + HEAD)).astype(BF16)


def project_kernel(normed, weights, first, second, cos, sin, codes, q_out, kv_out, lora_out):
    rows = normed[...]
    half = weights.shape[1]
    lora = dot(rows, first[...]).astype(BF16)
    lora_out[...] = lora
    pre = (
        dot(rows[:, :half], weights[0])
        + dot(rows[:, half:], weights[1])
        + dot(lora, second[...])
    )
    turn = cos.shape[1]
    parts = []
    for start in range(0, pre.shape[1] // 4 * 3, turn):
        piece = pre[:, start : start + turn]
        parts.append(piece * cos[...] + swap_halves(piece) * sin[...])
    heads = q_out.shape[0]
    width = heads * HEAD
    queries = (jnp.concatenate(parts[: width // turn], axis=1) * SCORE_SCALE).astype(BF16)
    for head in range(heads):
        place = place_table(width, head * HEAD, 0)
        q_out[head] = (dot(queries, place) + codes[...].astype(F32)).astype(BF16)
    keys = jnp.concatenate(parts[width // turn :], axis=1).astype(BF16)
    kv_out[:, : keys.shape[1]] = keys
    kv_out[:, keys.shape[1] :] = pre[:, width + keys.shape[1] :].astype(BF16)


def project(normed, weights, first, second, cos, sin, codes, heads, pairs):
    rows, width = normed.shape
    block = 256
    cols = (heads + 2 * pairs) * HEAD
    return pl.pallas_call(
        project_kernel,
        grid=(rows // block,),
        in_specs=[
            pl.BlockSpec((block, width), lambda i: (i, 0)),
            pl.BlockSpec((2, width // 2, cols), lambda i: (0, 0, 0)),
            pl.BlockSpec((width, LANES), lambda i: (0, 0)),
            pl.BlockSpec((LANES, cols), lambda i: (0, 0)),
            pl.BlockSpec((block, LANES), lambda i: (i, 0)),
            pl.BlockSpec((block, LANES), lambda i: (i, 0)),
            pl.BlockSpec((block, LANES), lambda i: (i, 0)),
        ],
        out_specs=[
            pl.BlockSpec((heads, block, LANES), lambda i: (0, i, 0)),
            pl.BlockSpec((block, 2 * pairs * HEAD), lambda i: (i, 0)),
            pl.BlockSpec((block, LANES), lambda i: (i, 0)),
        ],
        out_shape=[
            jax.ShapeDtypeStruct((heads, rows, LANES), BF16),
            jax.ShapeDtypeStruct((rows, 2 * pairs * HEAD), BF16),
            jax.ShapeDtypeStruct((rows, LANES), BF16),
        ],
        compiler_params=pltpu.CompilerParams(vmem_limit_bytes=VMEM_LIMIT),
        name="project",
    )(normed, weights, first, second, cos, sin, codes)


def build_tables(rank, kv_refs, k_aug, v_aug):
    pairs = k_aug.shape[0]
    for distance, kv in enumerate(kv_refs):

        @pl.when(distance <= rank)
        def _(distance=distance, kv=kv):
            rows, width = kv.shape
            values = kv[...]
            lane = iota((rows, LANES), 1)
            seg = (rank - distance) * SEGS_DEV + iota((rows, LANES), 0) // SEG
            key_code = ((lane - CODE == seg) | ((lane >= LSE) & (lane < LSE + 3))).astype(F32)
            one_code = ((lane == ONES) | (lane == ONES + 1)).astype(F32)
            for pair in range(pairs):
                k_place = place_table(width, pair * HEAD, 0)
                v_place = place_table(width, (pairs + pair) * HEAD, 0)
                span = pl.ds(distance * rows, rows)
                k_aug[pair, span, :] = (dot(values, k_place) + key_code).astype(BF16)
                v_aug[pair, span, :] = (dot(values, v_place) + one_code).astype(BF16)


def attend_kernel(
    rank_ref, q_ref, kv0, kv1, kv2, kv3, w_out, out_in, att_out, q_out, part_out,
    k_aug, v_aug, top, acc,
):
    step = pl.program_id(0)
    rank = rank_ref[0]
    heads, block, _ = q_ref.shape
    pairs = k_aug.shape[0]
    group = heads // pairs
    rows = kv0.shape[0]
    tall = group * block

    @pl.when(step == 0)
    def _():
        build_tables(rank, (kv0, kv1, kv2, kv3), k_aug, v_aug)

    for pair in range(pairs):
        queries = q_ref[pl.ds(pair * group, group)].reshape(tall, LANES)
        top[...] = jnp.full(top.shape, MASKED, F32)
        acc[...] = jnp.zeros(acc.shape, F32)

        def tile(start, size, causal, queries=queries, pair=pair):
            span = pl.ds(start, size)
            scores = dot_nt(queries, k_aug[pair, span, :])
            if causal:
                q_row = iota(scores.shape, 0) % block
                scores = jnp.where(iota(scores.shape, 1) <= q_row, scores, MASKED)
            before = top[...]
            now = jnp.maximum(before, jnp.max(scores, axis=1, keepdims=True))
            top[...] = now
            probs = jnp.exp(scores - now[:, :1]).astype(BF16)
            acc[...] = acc[...] * jnp.exp(before - now) + dot(probs, v_aug[pair, span, :])

        tile(pl.multiple_of(step * block, block), block, True)

        @pl.loop(0, step)
        def _(j, tile=tile):
            tile(pl.multiple_of(j * block, block), block, False)

        for distance in range(1, SPAN):

            @pl.when(distance <= rank)
            def _(distance=distance, tile=tile):
                tile(distance * rows, rows, False)

        total = acc[:, ONES : ONES + 1]
        result = (acc[...] / total).astype(BF16)
        for member in range(group):
            head = pair * group + member
            att_out[:, pl.ds(head * HEAD, HEAD)] = result[member * block : (member + 1) * block, :HEAD]
        minus = -(top[...] + jnp.log(total))
        high = minus.astype(BF16).astype(F32)
        middle = (minus - high).astype(BF16).astype(F32)
        low = minus - high - middle
        lane = iota(minus.shape, 1)
        coded = jnp.where(
            lane == LSE,
            high,
            jnp.where(
                lane == LSE + 1, middle, jnp.where(lane == LSE + 2, low, queries.astype(F32))
            ),
        )
        q_out[pl.ds(pair * group, group)] = coded.astype(BF16).reshape(group, block, LANES)

    mixed = att_out[...]
    half = w_out.shape[2]
    part_out[:, :half] = dot(mixed, w_out[0]).astype(BF16)
    part_out[:, half : 2 * half] = dot(mixed, w_out[1]).astype(BF16)
    part_out[:, 2 * half :] = dot(mixed, out_in[...]).astype(BF16)


def attend(rank, queries, kv_parts, w_out, out_in):
    heads, rows, _ = queries.shape
    block = 256
    kv_width = kv_parts[0].shape[1]
    pairs = kv_width // (2 * HEAD)
    tall = heads // pairs * block
    cols = 2 * w_out.shape[2] + LANES
    whole = lambda i, r: (0, 0)
    return pl.pallas_call(
        attend_kernel,
        grid_spec=pltpu.PrefetchScalarGridSpec(
            num_scalar_prefetch=1,
            grid=(rows // block,),
            in_specs=[pl.BlockSpec((heads, block, LANES), lambda i, r: (0, i, 0))]
            + [pl.BlockSpec((rows, kv_width), whole)] * SPAN
            + [
                pl.BlockSpec(w_out.shape, lambda i, r: (0, 0, 0)),
                pl.BlockSpec(out_in.shape, whole),
            ],
            out_specs=[
                pl.BlockSpec((block, heads * HEAD), lambda i, r: (i, 0)),
                pl.BlockSpec((heads, block, LANES), lambda i, r: (0, i, 0)),
                pl.BlockSpec((block, cols), lambda i, r: (i, 0)),
            ],
            scratch_shapes=[
                pltpu.VMEM((pairs, SPAN * rows, LANES), BF16),
                pltpu.VMEM((pairs, SPAN * rows, LANES), BF16),
                pltpu.VMEM((tall, LANES), F32),
                pltpu.VMEM((tall, LANES), F32),
            ],
        ),
        out_shape=[
            jax.ShapeDtypeStruct((rows, heads * HEAD), BF16),
            jax.ShapeDtypeStruct((heads, rows, LANES), BF16),
            jax.ShapeDtypeStruct((rows, cols), BF16),
        ],
        compiler_params=pltpu.CompilerParams(vmem_limit_bytes=VMEM_LIMIT),
        name="attend",
    )(rank, queries, *kv_parts, w_out, out_in)


def retrace_kernel(
    rank_ref, q_ref, kv0, kv1, kv2, kv3, att, branch, w_out, out_in, out_out, cos, sin,
    dq_out, own_out, far_out, in_grad,
    k_aug, v_aug, dk, dv, dq,
):
    step = pl.program_id(0)
    rank = rank_ref[0]
    heads, block, _ = q_ref.shape
    pairs = k_aug.shape[0]
    group = heads // pairs
    rows = kv0.shape[0]
    tall = group * block
    width = heads * HEAD

    @pl.when(step == 0)
    def _():
        build_tables(rank, (kv0, kv1, kv2, kv3), k_aug, v_aug)
        dk[...] = jnp.zeros(dk.shape, F32)
        dv[...] = jnp.zeros(dv.shape, F32)
        in_grad[...] = jnp.zeros(in_grad.shape, F32)

    half = w_out.shape[2]
    low_grad = dot_nt(branch[...], out_out[...]).astype(BF16)
    grads = (
        dot_nt(branch[:, :half], w_out[0])
        + dot_nt(branch[:, half:], w_out[1])
        + dot_nt(low_grad, out_in[...])
    ).astype(BF16)
    mixed = att[...]
    in_grad[...] += dot_tn(mixed, low_grad)
    product = grads.astype(F32) * mixed.astype(F32)
    wide = heads * LANES
    r, c = iota((width, wide), 0), iota((width, wide), 1)
    same = r // HEAD == c // LANES
    place = (same & (r % HEAD == c % LANES)).astype(BF16)
    spread = (same & (c % LANES >= ONES) & (c % LANES < ONES + 2)).astype(F32)
    minus = -lax.dot_general(
        product, spread, (((1,), (0,)), ((), ())),
        precision=lax.Precision.HIGHEST, preferred_element_type=F32,
    )
    high = minus.astype(BF16).astype(F32)
    lane = iota(minus.shape, 1) % LANES
    coded = dot(grads, place) + jnp.where(
        lane == ONES, high, jnp.where(lane == ONES + 1, minus - high, 0.0)
    )
    coded = coded.astype(BF16)

    pieces = []
    for pair in range(pairs):
        queries = q_ref[pl.ds(pair * group, group)].reshape(tall, LANES)
        upstream = jnp.concatenate(
            [
                coded[:, (pair * group + member) * LANES : (pair * group + member + 1) * LANES]
                for member in range(group)
            ],
            axis=0,
        )
        dq[...] = jnp.zeros(dq.shape, F32)

        def tile(start, size, causal, queries=queries, upstream=upstream, pair=pair):
            span = pl.ds(start, size)
            keys = k_aug[pair, span, :]
            probs = jnp.exp(dot_nt(keys, queries))
            if causal:
                q_row = iota(probs.shape, 1) % block
                probs = jnp.where(iota(probs.shape, 0) <= q_row, probs, 0.0)
            slopes = (probs * dot_nt(v_aug[pair, span, :], upstream)).astype(BF16)
            dv[pair, span, :] += dot(probs.astype(BF16), upstream)
            dk[pair, span, :] += dot(slopes, queries)
            dq[...] += dot_tn(slopes, keys)

        tile(pl.multiple_of(step * block, block), block, True)

        @pl.loop(0, step)
        def _(j, tile=tile):
            tile(pl.multiple_of(j * block, block), block, False)

        for distance in range(1, SPAN):

            @pl.when(distance <= rank)
            def _(distance=distance, tile=tile):
                for part in range(0, rows, rows // 2):
                    tile(distance * rows + part, rows // 2, False)

        for member in range(group):
            pieces.append(dq[member * block : (member + 1) * block, :HEAD] * SCORE_SCALE)

    for pair in range(pairs):
        turned = jnp.concatenate(pieces[pair * group : (pair + 1) * group], axis=1)
        turned = turned * cos[...] - swap_halves(turned) * sin[...]
        dq_out[:, pl.ds(pair * group * HEAD, group * HEAD)] = turned.astype(BF16)

    @pl.when(step == pl.num_programs(0) - 1)
    def _():
        for distance in range(SPAN):
            span = pl.ds(distance * rows, rows)
            joined = jnp.concatenate(
                [dk[pair, span, :HEAD] for pair in range(pairs)]
                + [dv[pair, span, :HEAD] for pair in range(pairs)],
                axis=1,
            )
            if distance == 0:
                own_out[...] = joined
            else:
                far_out[distance - 1] = joined.astype(BF16)


def retrace(rank, queries, kv_parts, att, branch, w_out, out_in, out_out, cos, sin):
    heads, rows, _ = queries.shape
    block = 256
    kv_width = kv_parts[0].shape[1]
    pairs = kv_width // (2 * HEAD)
    tall = heads // pairs * block
    width = heads * HEAD
    whole = lambda i, r: (0, 0)
    row = lambda i, r: (i, 0)
    return pl.pallas_call(
        retrace_kernel,
        grid_spec=pltpu.PrefetchScalarGridSpec(
            num_scalar_prefetch=1,
            grid=(rows // block,),
            in_specs=[pl.BlockSpec((heads, block, LANES), lambda i, r: (0, i, 0))]
            + [pl.BlockSpec((rows, kv_width), whole)] * SPAN
            + [
                pl.BlockSpec((block, width), row),
                pl.BlockSpec((block, branch.shape[1]), row),
                pl.BlockSpec(w_out.shape, lambda i, r: (0, 0, 0)),
                pl.BlockSpec(out_in.shape, whole),
                pl.BlockSpec(out_out.shape, whole),
                pl.BlockSpec((block, LANES), row),
                pl.BlockSpec((block, LANES), row),
            ],
            out_specs=[
                pl.BlockSpec((block, width), row),
                pl.BlockSpec((rows, kv_width), whole),
                pl.BlockSpec((SPAN - 1, rows, kv_width), lambda i, r: (0, 0, 0)),
                pl.BlockSpec((width, LANES), whole),
            ],
            scratch_shapes=[
                pltpu.VMEM((pairs, SPAN * rows, LANES), BF16),
                pltpu.VMEM((pairs, SPAN * rows, LANES), BF16),
                pltpu.VMEM((pairs, SPAN * rows, LANES), F32),
                pltpu.VMEM((pairs, SPAN * rows, LANES), F32),
                pltpu.VMEM((tall, LANES), F32),
            ],
        ),
        out_shape=[
            jax.ShapeDtypeStruct((rows, width), BF16),
            jax.ShapeDtypeStruct((rows, kv_width), F32),
            jax.ShapeDtypeStruct((SPAN - 1, rows, kv_width), BF16),
            jax.ShapeDtypeStruct((width, LANES), F32),
        ],
        compiler_params=pltpu.CompilerParams(vmem_limit_bytes=VMEM_LIMIT),
        name="retrace",
    )(rank, queries, *kv_parts, att, branch, w_out, out_in, out_out, cos, sin)


def unproject_kernel(
    dq, own, far1, far2, far3, lora, weights, second, cos, sin, part_out, grad_out
):
    step = pl.program_id(0)
    total = own[...] + far1[...].astype(F32) + far2[...].astype(F32) + far3[...].astype(F32)
    split = total.shape[1] // 2
    keys = total[:, :split]
    keys = keys * cos[...] - swap_halves(keys) * sin[...]
    grads = jnp.concatenate(
        [dq[...], keys.astype(BF16), total[:, split:].astype(BF16)], axis=1
    )
    half = weights.shape[1]
    part_out[:, :half] = dot_nt(grads, weights[0]).astype(BF16)
    part_out[:, half : 2 * half] = dot_nt(grads, weights[1]).astype(BF16)
    part_out[:, 2 * half :] = dot_nt(grads, second[...]).astype(BF16)

    @pl.when(step == 0)
    def _():
        grad_out[...] = jnp.zeros(grad_out.shape, F32)

    grad_out[...] += dot_tn(lora[...], grads)


def unproject(dq, own, fars, lora, weights, second, cos, sin):
    rows, width = dq.shape
    kv_width = own.shape[1]
    block = 256
    cols = weights.shape[2]
    model = 2 * weights.shape[1]
    row = lambda i: (i, 0)
    return pl.pallas_call(
        unproject_kernel,
        grid=(rows // block,),
        in_specs=[pl.BlockSpec((block, width), row)]
        + [pl.BlockSpec((block, kv_width), row)] * SPAN
        + [
            pl.BlockSpec((block, LANES), row),
            pl.BlockSpec((2, model // 2, cols), lambda i: (0, 0, 0)),
            pl.BlockSpec((LANES, cols), lambda i: (0, 0)),
            pl.BlockSpec((block, LANES), row),
            pl.BlockSpec((block, LANES), row),
        ],
        out_specs=[
            pl.BlockSpec((block, model + LANES), row),
            pl.BlockSpec((LANES, cols), lambda i: (0, 0)),
        ],
        out_shape=[
            jax.ShapeDtypeStruct((rows, model + LANES), BF16),
            jax.ShapeDtypeStruct((LANES, cols), F32),
        ],
        compiler_params=pltpu.CompilerParams(vmem_limit_bytes=VMEM_LIMIT),
        name="unproject",
    )(dq, own, *fars, lora, weights, second, cos, sin)


def expert_kernel(
    sets, base, x_ref, g_ref, routes, router, w_gate, w_up, w_down,
    gate_in, up_in, gate_out, up_out, down_in, down_out,
    mixed_out, grad_out,
    rank_rows, gate_rows, slope_rows, mix, back, xs, firsts, tall_grad,
    *, slots, sources,
):
    chunk, expert = pl.program_id(0), pl.program_id(1)
    experts = router.shape[0]
    tokens, model = x_ref.shape
    each = tokens // sources
    hidden = w_gate.shape[3]
    lanes = gate_in.shape[2]
    chosen = sets[chunk]

    @pl.when(expert == 0)
    def _():
        logits = dot_nt(router[...], x_ref[...])
        number = iota((experts, tokens), 0)
        hit = jnp.zeros((experts, tokens), F32)
        for k in range(routes.shape[0]):
            hit += (routes[k : k + 1, :] == number).astype(F32)
        kept = jnp.where(hit > 0.5, logits, MASKED)
        weights = jnp.exp(kept - jnp.max(kept, axis=0, keepdims=True)) * hit
        gate_rows[...] = weights / jnp.sum(weights, axis=0, keepdims=True)
        earlier = (iota((each, each), 0) < iota((each, each), 1)).astype(BF16)
        for s in range(sources):
            span = slice(s * each, (s + 1) * each)
            order = dot(hit[:, span].astype(BF16), earlier)
            rank_rows[:, span] = jnp.where(hit[:, span] > 0.5, order, -1.0)
        mix[...] = jnp.zeros(mix.shape, F32)
        back[...] = jnp.zeros(back.shape, F32)
        slope_rows[...] = jnp.zeros(slope_rows.shape, F32)

    row = base[0] + expert
    ranks = rank_rows[pl.ds(row, 1), :]
    gates = gate_rows[pl.ds(row, 1), :]
    slot_number = iota((slots, each), 0).astype(F32)
    picks, columns, upstreams = [], [], []
    for s in range(sources):
        span = slice(s * each, (s + 1) * each)
        pick = ranks[:, span] == slot_number
        columns.append(jnp.sum(jnp.where(pick, gates[:, span], 0.0), axis=1, keepdims=True))
        pick = pick.astype(BF16)
        picks.append(pick)
        xs[pl.ds(s * slots, slots), :] = dot(pick, x_ref[pl.ds(s * each, each), :]).astype(BF16)
        upstreams.append(dot(pick, g_ref[pl.ds(s * each, each), :]))
    gate_column = jnp.concatenate(columns, axis=0)
    upstream = RESIDUAL_SCALE * jnp.concatenate(upstreams, axis=0)

    firsts[:, :lanes] = gate_in[0]
    firsts[:, lanes:] = up_in[0]
    keep = (iota((1, 2 * lanes), 1) % lanes // RANK == chosen).astype(BF16)
    rows = xs[...]
    inner = dot(rows, firsts[...]).astype(BF16) * keep
    half = w_gate.shape[2]
    gate_value = (
        dot(rows[:, :half], w_gate[0, 0])
        + dot(rows[:, half:], w_gate[1, 0])
        + dot(inner[:, :lanes], gate_out[0])
    )
    up_value = (
        dot(rows[:, :half], w_up[0, 0])
        + dot(rows[:, half:], w_up[1, 0])
        + dot(inner[:, lanes:], up_out[0])
    )
    sigmoid = 1.0 / (1.0 + jnp.exp(-gate_value))
    silu = gate_value * sigmoid
    active = (silu * up_value).astype(BF16)
    down_inner = dot(active, down_in[0]).astype(BF16) * keep[:, :lanes]
    down_half = w_down.shape[2]
    produced = (
        dot(active[:, :down_half], w_down[0, 0])
        + dot(active[:, down_half:], w_down[1, 0])
        + dot(down_inner, down_out[0])
    ).astype(BF16).astype(F32)
    slope = jnp.sum(upstream * produced, axis=1, keepdims=True)
    sent = (gate_column * produced).astype(BF16)
    slot_grad = (gate_column * upstream).astype(BF16)

    down_inner_grad = dot_nt(slot_grad, down_out[0]).astype(BF16) * keep[:, :lanes]
    active_grad = (
        jnp.concatenate(
            [dot_nt(slot_grad, w_down[0, 0]), dot_nt(slot_grad, w_down[1, 0])], axis=1
        )
        + dot_nt(down_inner_grad, down_in[0])
    ).astype(BF16).astype(F32)
    gate_grad = (active_grad * up_value * (sigmoid + silu * (1.0 - sigmoid))).astype(BF16)
    up_grad = (active_grad * silu).astype(BF16)
    inner_grad = (
        jnp.concatenate([dot_nt(gate_grad, gate_out[0]), dot_nt(up_grad, up_out[0])], axis=1)
    ).astype(BF16) * keep
    row_grad = jnp.concatenate(
        [dot_nt(gate_grad, w_gate[h, 0]) + dot_nt(up_grad, w_up[h, 0]) for h in range(2)], axis=1
    )
    row_grad = (row_grad + dot_nt(inner_grad, firsts[...])).astype(BF16)

    for s in range(sources):
        span = slice(s * slots, (s + 1) * slots)
        spot = pl.ds(s * each, each)
        mix[spot, :] += dot_tn(picks[s], sent[span, :])
        back[spot, :] += dot_tn(picks[s], row_grad[span, :])
        slope_rows[pl.ds(expert, 1), spot] = jnp.sum(
            jnp.where(picks[s] > 0.5, slope[span, :], 0.0), axis=0, keepdims=True
        )

    own = pl.multiple_of(chosen * RANK, RANK)
    tall_grad[...] = dot_tn(inner_grad, rows)
    grad_out[0, 0, pl.ds(0, RANK), :] = tall_grad[pl.ds(own, RANK), :].astype(BF16)
    grad_out[0, 0, pl.ds(RANK, RANK), :] = tall_grad[pl.ds(lanes + own, RANK), :].astype(BF16)
    tall_grad[pl.ds(0, lanes), :hidden] = dot_tn(inner[:, :lanes], gate_grad)
    tall_grad[pl.ds(0, lanes), hidden:] = dot_tn(inner[:, lanes:], up_grad)
    grad_out[0, 0, pl.ds(2 * RANK, RANK), :] = tall_grad[pl.ds(own, RANK), :].astype(BF16)
    tall_grad[pl.ds(0, lanes), :] = dot_tn(down_inner, slot_grad)
    grad_out[0, 0, pl.ds(3 * RANK, RANK), :] = tall_grad[pl.ds(own, RANK), :].astype(BF16)
    tall_grad[pl.ds(0, lanes), :hidden] = dot_tn(down_inner_grad, active)
    tall_grad[pl.ds(0, lanes), hidden:] = jnp.zeros((lanes, model - hidden), F32)
    grad_out[0, 0, pl.ds(4 * RANK, RANK), :] = tall_grad[pl.ds(own, RANK), :].astype(BF16)

    @pl.when(expert == pl.num_programs(1) - 1)
    def _():
        mixed_out[:, :model] = mix[...].astype(BF16)
        mixed_out[:, model : 2 * model] = back[...].astype(BF16)
        turned = slope_rows[...].T
        high = turned.astype(BF16)
        low = (turned - high.astype(F32)).astype(BF16)
        local, lane = iota((LANES, LANES), 0), iota((LANES, LANES), 1)
        inside = local < pl.num_programs(1)
        first = (inside & (lane == local + base[0])).astype(BF16)
        later = (inside & (lane == local + base[0] + experts)).astype(BF16)
        mixed_out[:, 2 * model :] = (dot(high, first) + dot(low, later)).astype(BF16)


def run_experts(
    sets, base, rows, upstream, routes, router, weights, adapters, slots, sources
):
    total, model = rows.shape
    experts = router.shape[0]
    w_gate, w_up, w_down = weights
    local = w_gate.shape[1]
    trees = sets.shape[0]
    tokens = total // trees
    hidden = w_gate.shape[3]
    lanes = adapters[0].shape[2]
    cols = 2 * model + LANES
    tall = sources * slots
    piece = lambda c, e, *_: (c, 0)
    fixed = lambda c, e, *_: (0, 0)
    expert = lambda c, e, *_: (e, 0, 0)
    return pl.pallas_call(
        functools.partial(expert_kernel, slots=slots, sources=sources),
        grid_spec=pltpu.PrefetchScalarGridSpec(
            num_scalar_prefetch=2,
            grid=(trees, local),
            in_specs=[
                pl.BlockSpec((tokens, model), piece),
                pl.BlockSpec((tokens, model), piece),
                pl.BlockSpec((routes.shape[0], tokens), lambda c, e, *_: (0, c)),
                pl.BlockSpec(router.shape, fixed),
                *[
                    pl.BlockSpec((2, 1) + w.shape[2:], lambda c, e, *_: (0, e, 0, 0))
                    for w in weights
                ],
                *[pl.BlockSpec((1,) + a.shape[1:], expert) for a in adapters],
            ],
            out_specs=[
                pl.BlockSpec((tokens, cols), piece),
                pl.BlockSpec((1, 1, 5 * RANK, model), lambda c, e, *_: (c, e, 0, 0)),
            ],
            scratch_shapes=[
                pltpu.VMEM((experts, tokens), F32),
                pltpu.VMEM((experts, tokens), F32),
                pltpu.VMEM((LANES, tokens), F32),
                pltpu.VMEM((tokens, model), F32),
                pltpu.VMEM((tokens, model), F32),
                pltpu.VMEM((tall, model), BF16),
                pltpu.VMEM((model, 2 * lanes), BF16),
                pltpu.VMEM((2 * lanes, model), F32),
            ],
        ),
        out_shape=[
            jax.ShapeDtypeStruct((total, cols), BF16),
            jax.ShapeDtypeStruct((trees, local, 5 * RANK, model), BF16),
        ],
        compiler_params=pltpu.CompilerParams(vmem_limit_bytes=60 * 1024 * 1024),
        name="experts",
    )(sets, base, rows, upstream, routes, router, *weights, *adapters)


def take_set(table, chosen, axis):
    return lax.dynamic_slice_in_dim(table, chosen * RANK, RANK, axis)


def per_device(
    tokens,
    out_grad,
    routes,
    parents,
    adapter_set,
    gain_a,
    gain_b,
    w_query,
    key_projection_matrix,
    value_projection_matrix,
    w_output,
    w_router,
    w_gate,
    w_up,
    w_down,
    query_in,
    query_out,
    key_in,
    key_second_factor,
    value_in,
    value_second_factor,
    out_in,
    out_out,
    gate_in,
    gate_out,
    up_in,
    up_out,
    down_in,
    down_out,
):
    tp_rank = lax.axis_index("tp")
    ctx_rank = lax.axis_index("ctx")
    fsdp_rank = lax.axis_index("fsdp")
    ctx_count = lax.axis_size("ctx")
    tp_count = lax.axis_size("tp")
    fsdp_count = lax.axis_size("fsdp")
    tok_rows, model = tokens.shape
    q_cols = w_query.shape[1]
    kv_cols = key_projection_matrix.shape[1]
    heads, pairs = q_cols // HEAD, kv_cols // HEAD
    experts = w_router.shape[1]
    local_experts = w_gate.shape[0]
    sets = query_in.shape[1] // RANK
    slots = tok_rows * TOP * 3 // (2 * experts)
    trees = ctx_count // SPAN

    attention_shard = jnp.concatenate(
        [
            jnp.concatenate([w_query, key_projection_matrix, value_projection_matrix], axis=1),
            w_output,
        ],
        axis=0,
    )
    attention_weights = lax.all_gather(attention_shard, "fsdp")
    project_weights = attention_weights[:, : w_query.shape[0]]
    output_weights = attention_weights[:, w_query.shape[0] :]

    seg_start = (fsdp_rank * ctx_count + ctx_rank) * SEGS_DEV
    tree_index = seg_start // TREE_SEGS
    local_start = seg_start % TREE_SEGS
    rank = (local_start // SEGS_DEV).astype(jnp.int32).reshape(1)
    tree_parents = lax.dynamic_slice_in_dim(parents, tree_index * TREE_SEGS, TREE_SEGS, 0)
    reach, depth = tree_links(tree_parents)
    chosen = lax.dynamic_slice_in_dim(adapter_set, tree_index, 1, 0)[0]

    inputs = tokens.astype(F32)
    gain_one = gain_a.astype(F32)
    gain_two = gain_b.astype(F32)
    normed = rms_scale(inputs, gain_one).astype(BF16)
    normed_all = lax.all_gather(normed, "tp", axis=0, tiled=True)
    group_rows = normed_all.shape[0]

    own_reach = lax.dynamic_slice_in_dim(reach, local_start, SEGS_DEV, 0)
    codes = jnp.pad(
        jnp.where(own_reach > 0.5, 0.0, MASKED), ((0, 0), (CODE, LANES - CODE - TREE_SEGS))
    )
    codes = jnp.repeat(codes.astype(BF16), SEG, axis=0)
    own_depth = lax.dynamic_slice_in_dim(depth, local_start, SEGS_DEV, 0)
    positions = (
        own_depth[:, None] * SEG + jnp.arange(SEG, dtype=jnp.int32).astype(F32)[None, :]
    ).reshape(-1)
    half_head = HEAD // 2
    freqs = ROPE_BASE ** (-(jnp.arange(half_head, dtype=jnp.int32).astype(F32) * 2.0) / HEAD)
    angles = positions[:, None] * jnp.tile(freqs, LANES // half_head)[None, :]
    cos, sin = jnp.cos(angles), jnp.sin(angles)

    first = jnp.pad(
        jnp.concatenate(
            [take_set(t, chosen, 1) for t in (query_in, key_in, value_in)], axis=1
        ),
        ((0, 0), (0, LANES - 3 * RANK)),
    )
    q_second = lax.dynamic_slice(query_out, (chosen * RANK, tp_rank * q_cols), (RANK, q_cols))
    k_second = lax.dynamic_slice(
        key_second_factor, (chosen * RANK, tp_rank * kv_cols), (RANK, kv_cols)
    )
    v_second = lax.dynamic_slice(
        value_second_factor, (chosen * RANK, tp_rank * kv_cols), (RANK, kv_cols)
    )
    second = jnp.concatenate(
        [
            jnp.pad(q_second, ((0, 0), (0, 2 * kv_cols))),
            jnp.pad(k_second, ((0, 0), (q_cols, kv_cols))),
            jnp.pad(v_second, ((0, 0), (q_cols + kv_cols, 0))),
            jnp.zeros((LANES - 3 * RANK, q_cols + 2 * kv_cols), BF16),
        ],
        axis=0,
    )
    o_first = jnp.pad(
        lax.dynamic_slice(out_in, (tp_rank * q_cols, chosen * RANK), (q_cols, RANK)),
        ((0, 0), (0, LANES - RANK)),
    )
    o_second = jnp.pad(take_set(out_out, chosen, 0), ((0, LANES - RANK), (0, 0)))

    queries, kv, lora = project(
        normed_all, project_weights, first, second, cos, sin, codes, heads, pairs
    )
    kv_parts = [kv] + [shifted(kv, "ctx", distance) for distance in range(1, SPAN)]
    attended, queries, part = attend(rank, queries, kv_parts, output_weights, o_first)
    summed = lax.psum_scatter(part, "tp", scatter_dimension=0, tiled=True)
    o_reduced = summed[:, model:]
    middle = inputs + RESIDUAL_SCALE * (
        summed[:, :model].astype(F32)
        + jnp.dot(o_reduced, o_second, preferred_element_type=F32)
    )

    upstream_all = lax.all_gather(out_grad, "ctx", axis=0, tiled=True)
    routes_all = lax.all_gather(routes, "ctx", axis=0, tiled=True).T
    gate_full = lax.all_gather(w_gate, "fsdp")
    up_full = lax.all_gather(w_up, "fsdp")
    down_full = lax.all_gather(w_down, "fsdp")
    normed_two = rms_scale(middle, gain_two).astype(BF16)
    rows_all = lax.all_gather(normed_two, "ctx", axis=0, tiled=True)
    tree_sets = lax.dynamic_slice_in_dim(adapter_set, fsdp_rank * trees, trees, 0)
    base = (ctx_rank * local_experts).astype(jnp.int32).reshape(1)
    mixed, expert_part = run_experts(
        tree_sets,
        base,
        rows_all,
        upstream_all,
        routes_all,
        w_router.T,
        (gate_full, up_full, down_full),
        (gate_in, up_in, gate_out, up_out, down_in, down_out),
        slots,
        SPAN,
    )
    combined = lax.psum_scatter(mixed, "ctx", scatter_dimension=0, tiled=True).astype(F32)
    mixture = combined[:, :model]
    output = (middle + RESIDUAL_SCALE * mixture).astype(BF16)

    logits = jnp.dot(normed_two, w_router, preferred_element_type=F32)
    hits = jnp.sum(
        (routes[:, :, None] == jnp.arange(experts, dtype=jnp.int32)[None, None, :]).astype(F32),
        axis=1,
    )
    kept = jnp.where(hits > 0.5, logits, MASKED)
    gates = jnp.exp(kept - jnp.max(kept, axis=1, keepdims=True)) * hits
    gates = gates / jnp.sum(gates, axis=1, keepdims=True)
    slopes = (
        combined[:, 2 * model : 2 * model + experts]
        + combined[:, 2 * model + experts : 2 * model + 2 * experts]
    )
    logits_grad = gates * (slopes - jnp.sum(gates * slopes, axis=1, keepdims=True))
    normed_two_grad = combined[:, model : 2 * model] + jnp.einsum(
        "te,de->td", logits_grad, w_router.astype(F32), precision=lax.Precision.HIGHEST
    )
    upstream = out_grad.astype(F32)
    middle_grad = upstream + rms_back(middle, gain_two, normed_two_grad)
    branch_grad = (RESIDUAL_SCALE * middle_grad).astype(BF16)
    out_out_part = jnp.einsum(
        "ts,td->sd", o_reduced, branch_grad, preferred_element_type=F32
    )[:RANK]
    branch_all = lax.all_gather(branch_grad, "tp", axis=0, tiled=True)
    dq, own_grad, far_grad, out_in_part = retrace(
        rank, queries, kv_parts, attended, branch_all, output_weights, o_first, o_second, cos, sin
    )
    fars = [shifted(far_grad[d - 1], "ctx", -d) for d in range(1, SPAN)]
    part, second_part = unproject(
        dq, own_grad, fars, lora, project_weights, second, cos, sin
    )
    summed = lax.psum_scatter(part, "tp", scatter_dimension=0, tiled=True)
    reduced_grad = summed[:, model:]
    normed_grad = summed[:, :model].astype(F32) + jnp.einsum(
        "ts,ds->td", reduced_grad, first, preferred_element_type=F32
    )
    first_part = jnp.einsum(
        "ts,td->sd", reduced_grad, normed, preferred_element_type=F32
    )[: 3 * RANK]
    input_grad = (middle_grad + rms_back(inputs, gain_one, normed_grad)).astype(BF16)

    full_q = q_cols * tp_count
    full_kv = kv_cols * tp_count

    def widen(part, cols, axis, start):
        shape = list(part.shape)
        shape[axis] = cols
        return lax.dynamic_update_slice_in_dim(jnp.zeros(shape, F32), part, start, axis)

    packed = jnp.concatenate(
        [
            first_part,
            widen(out_in_part[:, :RANK].T, full_q, 1, tp_rank * q_cols),
            out_out_part,
            widen(second_part[:RANK, :q_cols], full_q, 1, tp_rank * q_cols),
            jnp.concatenate(
                [
                    widen(
                        second_part[RANK : 2 * RANK, q_cols : q_cols + kv_cols],
                        full_kv, 1, tp_rank * kv_cols,
                    ),
                    widen(
                        second_part[2 * RANK : 3 * RANK, q_cols + kv_cols :],
                        full_kv, 1, tp_rank * kv_cols,
                    ),
                ],
                axis=1,
            ),
        ],
        axis=0,
    )
    all_trees = fsdp_count * trees
    if trees > 1:
        packed = lax.psum(
            jnp.where(
                (jnp.arange(all_trees) == tree_index)[:, None, None], packed[None], 0.0
            ),
            ("fsdp", "ctx", "tp"),
        )
    else:
        packed = lax.all_gather(lax.psum(packed, ("ctx", "tp")), "fsdp")
    place = (
        adapter_set[:, None] == jnp.arange(sets, dtype=jnp.int32)[None, :]
    ).astype(F32)

    def in_rows(part):
        spread = jnp.einsum("ts,trd->srd", place, part, precision=lax.Precision.HIGHEST)
        return spread.reshape(sets * RANK, part.shape[2])

    def in_columns(part):
        return in_rows(part).T

    adapter_totals = (
        in_columns(packed[:, :RANK]),
        in_rows(packed[:, 5 * RANK : 6 * RANK]),
        in_columns(packed[:, RANK : 2 * RANK]),
        in_rows(packed[:, 6 * RANK :, :full_kv]),
        in_columns(packed[:, 2 * RANK : 3 * RANK]),
        in_rows(packed[:, 6 * RANK :, full_kv:]),
        in_columns(packed[:, 3 * RANK : 4 * RANK]),
        in_rows(packed[:, 4 * RANK : 5 * RANK]),
    )

    expert_part = lax.all_gather(lax.psum(expert_part, "tp"), "fsdp")
    expert_part = expert_part.reshape(all_trees, local_experts, 5 * RANK, model)
    hidden = w_gate.shape[2]

    def expert_rows(part):
        spread = jnp.einsum(
            "ts,terd->esrd", place.astype(BF16), part, preferred_element_type=F32
        )
        return spread.reshape(local_experts, sets * RANK, part.shape[3])

    def expert_columns(part):
        return expert_rows(part).transpose(0, 2, 1)

    return (
        output,
        input_grad,
        *adapter_totals,
        expert_columns(expert_part[:, :, :RANK]),
        expert_rows(expert_part[:, :, 2 * RANK : 3 * RANK, :hidden]),
        expert_columns(expert_part[:, :, RANK : 2 * RANK]),
        expert_rows(expert_part[:, :, 2 * RANK : 3 * RANK, hidden:]),
        expert_columns(expert_part[:, :, 4 * RANK :, :hidden]),
        expert_rows(expert_part[:, :, 3 * RANK : 4 * RANK]),
    )


def solution(mesh):
    in_specs = (
        P(("fsdp", "ctx", "tp"), None),
        P(("fsdp", "ctx", "tp"), None),
        P(("fsdp", "ctx", "tp"), None),
        P(),
        P(),
        P(),
        P(),
        P("fsdp", "tp"),
        P("fsdp", "tp"),
        P("fsdp", "tp"),
        P("tp", "fsdp"),
        P(),
        P("ctx", "fsdp", None),
        P("ctx", "fsdp", None),
        P("ctx", "fsdp", None),
        P(),
        P(),
        P(),
        P(),
        P(),
        P(),
        P(),
        P(),
        P("ctx", None, None),
        P("ctx", None, None),
        P("ctx", None, None),
        P("ctx", None, None),
        P("ctx", None, None),
        P("ctx", None, None),
    )
    out_specs = (
        P(("fsdp", "ctx", "tp"), None),
        P(("fsdp", "ctx", "tp"), None),
        P(),
        P(),
        P(),
        P(),
        P(),
        P(),
        P(),
        P(),
        P("ctx", None, None),
        P("ctx", None, None),
        P("ctx", None, None),
        P("ctx", None, None),
        P("ctx", None, None),
        P("ctx", None, None),
    )
    return jax.shard_map(
        per_device, mesh=mesh, in_specs=in_specs, out_specs=out_specs, check_vma=False
    )
```

time: 1700 us -> 993 us (0.58)
  matrix products: 456 us -> 22.8 us
  Pallas kernels: 0 us -> 195 us
  other arithmetic: 165 us -> 15.5 us
  waiting for transfers between devices: 755 us -> 633 us
  local copies, waits for them, and re-layouts: 173 us -> 72 us
  starting transfers between devices: 49.3 us -> 8.99 us
  blocking collectives: 56 us -> 18.3 us
    dot_general x72 -> x23, matrix products: 456 us -> 22.8 us  [the longest x6 9.33 us: expert_rows(): jnp.einsum('ts,terd->esrd', place.astype(BF16), part, preferred_element_t...]
    psum x2, waiting for transfers between devices: 442 us -> 98.5 us  [the longest x1 86.1 us: per_device(): packed = lax.all_gather(lax.psum(packed, ('ctx', 'tp')), 'fsdp')]
    all_gather x5 -> x9, waiting for transfers between devices: 128 us -> 415 us  [the longest x1 105 us: per_device(): up_full = lax.all_gather(w_up, 'fsdp')]
    pallas_call x0 -> x5, Pallas kernels: none -> 195 us  [the longest x1 64.1 us: run_experts(): pl.pallas_call(functools.partial(expert_kernel, slots=slots, sources=sour...]
    all_to_all x5 -> x0, waiting for transfers between devices: 88.7 us -> none  [the longest x1 41.2 us: per_device(): lax.all_to_all(parcel, 'ctx', split_axis=1, concat_axis=1, tiled=True)]
    convert_element_type x22 -> x8, other arithmetic: 78.1 us -> 7.29 us  [the longest x1 2.87 us: per_device(): (middle_grad + rms_back(inputs, gain_one, normed_grad)).astype(BF16)]
    reduce_sum x42 -> x3, other arithmetic: 47.9 us -> 0.44 us  [the longest x1 0.22 us: per_device(): jnp.sum(gates * slopes, axis=1, keepdims=True)]
    all_gather x6 -> x2, blocking collectives: 56 us -> 18.3 us  [the longest x1 10.9 us: per_device(): packed = lax.all_gather(lax.psum(packed, ('ctx', 'tp')), 'fsdp')]
  transfers between devices with their start and end apart: 28 -> 20, of which waited for: 17 -> 15; matrix products, arithmetic and copies ran while one was open for 18% -> 9% of each run, Pallas kernels for 0% -> 7%
where the time goes in v1:
time: 993 us; the launch traced here: 983 us
  waiting for transfers between devices  633 us (64%)
  Pallas kernels  195 us (20%)
  local copies, waits for them, and re-layouts  72 us (7%)
  matrix products  22.8 us (2%)
  blocking collectives  18.3 us (2%)
  between operations  17.3 us (2%)
  other arithmetic  15.5 us (2%)
    all_gather x1, waiting for transfers between devices, per_device(): up_full = lax.all_gather(w_up, 'fsdp')  105 us
    all_gather x1, waiting for transfers between devices, per_device(): gate_full = lax.all_gather(w_gate, 'fsdp')  105 us
    psum x1, waiting for transfers between devices, per_device(): packed = lax.all_gather(lax.psum(packed, ('ctx', 'tp')), 'fsdp')  86.1 us
    all_gather x1, waiting for transfers between devices, per_device(): down_full = lax.all_gather(w_down, 'fsdp')  73.8 us
    pallas_call x1, Pallas kernels, run_experts(): pl.pallas_call(functools.partial(expert_kernel, slots=slots, sources=sour...  64.1 us
    pallas_call x1, Pallas kernels, retrace(): pl.pallas_call(retrace_kernel, grid_spec=pltpu.PrefetchScalarGridSpec(num...  63.4 us
    pallas_call x1, Pallas kernels, attend(): pl.pallas_call(attend_kernel, grid_spec=pltpu.PrefetchScalarGridSpec(num_...  54.2 us
    all_gather x1, waiting for transfers between devices, per_device(): branch_all = lax.all_gather(branch_grad, 'tp', axis=0, tiled=True)  44.7 us
  transfers between devices with their start and end apart: 20, of which 15 were waited for; matrix products, arithmetic and copies ran while one was open for 9% of the time, Pallas kernels for 7%

profile of v1, /device:TPU:13, one launch (start us, length us, event | category | flops | bytes accessed | tf_op | source)
XLA Modules:
  0.0 982.6 jit_solution(11485745054383980704)
XLA Ops:
  18.8 3.0 multiply_sine_fusion
  21.9 17.6 %all-gather.24.cloned.1.call-done = bf16[1536,512]{1,0:T(8,128)(2,1)} async-done(((bf16[768,512]{1,0:T(8,128)(2,1)}), bf16[1536,512]{1,0:T(8,128)(2,1)}) %all-gather.24.cloned.1.call-update) | async-done | bytes 1572880 | tf_op jit(solution)/shard_map/all_gather | solution.py:744
  41.7 44.0 %all-gather.14.cloned.1.call-done.normed = bf16[1024,1024]{1,0:T(8,128)(2,1)} async-done(((bf16[256,1024]{1,0:T(8,128)(2,1)}), bf16[1024,1024]{1,0:T(8,128)(2,1)}) %all-gather.14.cloned.1.call-update) | async-done | bytes 2097168 | tf_op jit(solution)/shard_map/all_gather | solution.py:760
  86.4 6.8 project.1
  100.8 17.7 %collective-permute-done.1.kv2 = bf16[1024,256]{1,0:T(8,128)(2,1)S(1)} collective-permute-done((bf16[1024,256]{1,0:T(8,128)(2,1)}, bf16[1024,256]{1,0:T(8,128)(2,1)S(1)}, u32[]{:S(2)}, u32[]{:S(2)}) %collective-permute-start.1) | collective-permute-done | bytes 524320 | tf_op jit(solution)/shard_map/ppermute | solution.py:55
  118.4 2.6 collective-permute-done.2.kv3
  121.8 54.2 %attend.1 = (bf16[1024,256]{1,0:T(8,128)(2,1)}, bf16[4,1024,128]{2,1,0:T(8,128)(2,1)}, bf16[1024,1152]{1,0:T(8,128)(2,1)}) custom-call(s32[1]{0:T(128)} %bitcast.rank_ref, bf16[4,1024,128]{2,1,0:T(8,128)(2,1)} %get-tuple-element.30.q_ref, bf16[1024,256]{1,0:T(8,128)(2,1)} %get-tuple-element.31.kv0, bf16[1024,256]{1,0:T(8,128)(2,1)} %copy-done.9, ...), custom_call_target="tpu_custom_call" | custom-call | tf_op jit(solution)/shard_map/attend/pallas_call | solution.py:252
  179.3 42.3 %reduce-scatter.4.cloned.1.call-done = bf16[256,1152]{1,0:T(8,128)(2,1)} async-done(((bf16[1024,1152]{1,0:T(8,128)(2,1)}), bf16[256,1152]{1,0:T(8,128)(2,1)}) %reduce-scatter.4.cloned.1.call-update) | async-done | bytes 589840 | tf_op jit(solution)/shard_map/reduce_scatter | solution.py:810
  224.2 7.4 all_gather.56
  231.6 73.8 %all-gather.30.cloned.1.call-done = bf16[16,256,1024]{2,1,0:T(8,128)(2,1)} async-done(((bf16[8,256,1024]{2,1,0:T(8,128)(2,1)}), bf16[16,256,1024]{2,1,0:T(8,128)(2,1)}) %all-gather.30.cloned.1.call-update) | async-done | bytes 8388624 | tf_op jit(solution)/shard_map/all_gather | solution.py:821
  305.4 105.3 %all-gather.26.cloned.1.call-done = bf16[16,512,512]{2,1,0:T(8,128)(2,1)} async-done(((bf16[8,512,512]{2,1,0:T(8,128)(2,1)}), bf16[16,512,512]{2,1,0:T(8,128)(2,1)}) %all-gather.26.cloned.1.call-update) | async-done | bytes 8388624 | tf_op jit(solution)/shard_map/all_gather | solution.py:819
  410.7 105.4 %all-gather.28.cloned.1.call-done = bf16[16,512,512]{2,1,0:T(8,128)(2,1)} async-done(((bf16[8,512,512]{2,1,0:T(8,128)(2,1)}), bf16[16,512,512]{2,1,0:T(8,128)(2,1)}) %all-gather.28.cloned.1.call-update) | async-done | bytes 8388624 | tf_op jit(solution)/shard_map/all_gather | solution.py:820
  516.2 24.2 %all-gather.16.cloned.1.call-done.x_ref = bf16[1024,1024]{1,0:T(8,128)(2,1)} async-done(((bf16[256,1024]{1,0:T(8,128)(2,1)}), bf16[1024,1024]{1,0:T(8,128)(2,1)}) %all-gather.16.cloned.1.call-update) | async-done | bytes 2097168 | tf_op jit(solution)/shard_map/all_gather | solution.py:823
  540.4 64.1 %experts.1 = (bf16[1024,2176]{1,0:T(8,128)(2,1)}, bf16[1,8,80,1024]{3,2,1,0:T(8,128)(2,1)}) custom-call(s32[1]{0:T(128)} %get-tuple-element.109.sets, s32[1]{0:T(128)} %bitcast.5.base, bf16[1024,1024]{1,0:T(8,128)(2,1)} %all-gather.16.cloned.1.call-done.x_ref, bf16[1024,1024]{1,0:T(8,128)(2,1)} %all-gather.18.cloned.1.call-done.g_ref, s32[8,1024]{1,0:T(8,128)} %bitcast.132, ...), custom_call_target="tpu_custom_call" | custom-call | tf_op jit(solution)/shard_map/experts/pallas_call | solution.py:646
  606.1 44.2 %reduce-scatter.6.cloned.1.call-done = bf16[256,2176]{1,0:T(8,128)(2,1)} async-done(((bf16[1024,2176]{1,0:T(8,128)(2,1)}), bf16[256,2176]{1,0:T(8,128)(2,1)}) %reduce-scatter.6.cloned.1.call-update) | async-done | bytes 1114128 | tf_op jit(solution)/shard_map/reduce_scatter | solution.py:838
  656.0 12.3 %all-reduce.12.cloned.1.call-done = bf16[1,1,8,80,1024]{4,3,2,1,0:T(8,128)(2,1)} async-done(((bf16[1,1,8,80,1024]{4,3,2,1,0:T(8,128)(2,1)}), bf16[1,1,8,80,1024]{4,3,2,1,0:T(8,128)(2,1)}) %all-reduce.12.cloned.1.call-update) | async-done | bytes 1310736 | tf_op jit(solution)/shard_map/psum | solution.py:944
  669.2 44.7 %all-gather.20.cloned.1.call-done.branch = bf16[1024,1024]{1,0:T(8,128)(2,1)} async-done(((bf16[256,1024]{1,0:T(8,128)(2,1)}), bf16[1024,1024]{1,0:T(8,128)(2,1)}) %all-gather.20.cloned.1.call-update) | async-done | bytes 2097168 | tf_op jit(solution)/shard_map/all_gather | solution.py:864
  713.9 63.4 %retrace.1 = (bf16[1024,256]{1,0:T(8,128)(2,1)}, f32[1024,256]{1,0:T(8,128)}, bf16[3,1024,256]{2,1,0:T(8,128)(2,1)}, f32[256,128]{1,0:T(8,128)}) custom-call(s32[1]{0:T(128)} %bitcast.rank_ref, bf16[4,1024,128]{2,1,0:T(8,128)(2,1)} %get-tuple-element.34.q_ref, bf16[1024,256]{1,0:T(8,128)(2,1)} %get-tuple-element.31.kv0, bf16[1024,256]{1,0:T(8,128)(2,1)} %copy-done.9, ...), custom_call_target="tpu_custom_call" | custom-call | tf_op jit(solution)/shard_map/retrace/pallas_call | solution.py:401
  782.7 4.7 collective-permute-done.4.far2
  787.4 5.6 collective-permute-done.5.far3
  793.9 6.4 unproject.1
  800.4 4.4 copy.205
  806.3 4.4 copy.162
  810.7 5.3 copy.172
  817.9 4.4 copy.164
  822.3 5.3 copy.173
  829.6 4.4 copy.167
  835.5 2.5 copy.166
  838.0 3.0 copy.174
  861.9 2.9 fusion.13
  864.7 86.1 %all-reduce.10.cloned.1.call-done = f32[1,112,1024]{2,1,0:T(8,128)} async-done(((f32[1,112,1024]{2,1,0:T(8,128)}), f32[1,112,1024]{2,1,0:T(8,128)}) %all-reduce.10.cloned.1.call-update) | async-done | bytes 458768 | tf_op jit(solution)/shard_map/psum | solution.py:921
  950.9 10.9 %all_gather.65 = f32[2,112,1024]{2,1,0:T(8,128)S(1)} all-gather(f32[1,112,1024]{2,1,0:T(8,128)} %all-reduce.10.cloned.1.call-done), channel_id=1, replica_groups=mesh['fsdp'=2,'ctx'=4,'tp'=4] {'fsdp'}, dimensions={0}, use_global_device_ids=true | all-gather | bytes 1376256 | tf_op jit(solution)/shard_map/all_gather | solution.py:921
  (208 shorter events, 81.9 us)
Async XLA Ops:
  8.1 31.4 %all-gather.24.cloned.1.call-start = ((), (), s32[]{:S(2)}) async-start(), calls=%async_computation.13 | async-start | bytes 2359296 | tf_op jit(solution)/shard_map/all_gather | solution.py:744
  10.3 75.4 %all-gather.14.cloned.1.call-start = ((), (), s32[]{:S(2)}) async-start(), calls=%async_computation.3 | async-start | bytes 2621440 | tf_op jit(solution)/shard_map/all_gather | solution.py:760
  11.6 210.0 %reduce-scatter.4.cloned.1.call-start = ((), (), s32[]{:S(2)}) async-start(), calls=%async_computation.4 | async-start | bytes 2949120 | tf_op jit(solution)/shard_map/reduce_scatter | solution.py:810
  93.2 7.5 collective-permute-start
  94.5 23.9 %collective-permute-start.1 = (bf16[1024,256]{1,0:T(8,128)(2,1)}, bf16[1024,256]{1,0:T(8,128)(2,1)S(1)}, u32[]{:S(2)}, u32[]{:S(2)}) collective-permute-start(bf16[1024,256]{1,0:T(8,128)(2,1)} %get-tuple-element.31.kv0), channel_id=1, source_target_pairs={{0,8},{4,12},{1,9},{5,13},{2,10},{6,14},{3,11},{7,15},{16,24},{20,... | collective-permute-start | bytes 1572872 | tf_op jit(solution)/shard_map/ppermute | solution.py:55
  95.8 25.2 %collective-permute-start.2 = (bf16[1024,256]{1,0:T(8,128)(2,1)}, bf16[1024,256]{1,0:T(8,128)(2,1)S(1)}, u32[]{:S(2)}, u32[]{:S(2)}) collective-permute-start(bf16[1024,256]{1,0:T(8,128)(2,1)} %get-tuple-element.31.kv0), channel_id=1, source_target_pairs={{0,12},{1,13},{2,14},{3,15},{16,28},{17,29},{18,30},{19,31}} | collective-permute-start | bytes 1572872 | tf_op jit(solution)/shard_map/ppermute | solution.py:55
  100.8 20.3 %copy-start.9 = (bf16[1024,256]{1,0:T(8,128)(2,1)}, bf16[1024,256]{1,0:T(8,128)(2,1)S(1)}, u32[]{:S(2)}) copy-start(bf16[1024,256]{1,0:T(8,128)(2,1)S(1)} %collective-permute-done.kv1) | copy-start | bytes 1572868
  176.0 55.6 %all-gather.18.cloned.1.call-start = ((), (), s32[]{:S(2)}) async-start(), calls=%async_computation.6 | async-start | bytes 2621440 | tf_op jit(solution)/shard_map/all_gather | solution.py:817
  176.6 128.9 %all-gather.30.cloned.1.call-start = ((), (), s32[]{:S(2)}) async-start(), calls=%async_computation.16 | async-start | bytes 12582912 | tf_op jit(solution)/shard_map/all_gather | solution.py:821
  177.2 233.6 %all-gather.26.cloned.1.call-start = ((), (), s32[]{:S(2)}) async-start(), calls=%async_computation.14 | async-start | bytes 12582912 | tf_op jit(solution)/shard_map/all_gather | solution.py:819
  177.7 338.4 %all-gather.28.cloned.1.call-start = ((), (), s32[]{:S(2)}) async-start(), calls=%async_computation.15 | async-start | bytes 12582912 | tf_op jit(solution)/shard_map/all_gather | solution.py:820
  178.5 45.7 %copy-start.23 = (s32[256,8]{0,1:T(8,128)S(1)}, s32[256,8]{0,1:T(8,128)}, u32[]{:S(2)}) copy-start(s32[256,8]{0,1:T(8,128)} %param.31) | copy-start | bytes 24580
  178.5 361.9 %all-gather.16.cloned.1.call-start = ((), (), s32[]{:S(2)}) async-start(), calls=%async_computation.5 | async-start | bytes 2621440 | tf_op jit(solution)/shard_map/all_gather | solution.py:823
  179.3 425.2 %copy-start.18 = (bf16[16,1024]{1,0:T(8,128)(2,1)}, bf16[16,1024]{1,0:T(8,128)(2,1)S(1)}, u32[]{:S(2)}) copy-start(bf16[16,1024]{1,0:T(8,128)(2,1)S(1)} %constant_dynamic-slice_fusion) | copy-start | bytes 98308
  223.1 381.4 %copy-start.29 = (f32[256]{0:T(256)}, f32[256]{0:T(256)S(1)}, u32[]{:S(2)}) copy-start(f32[256]{0:T(256)S(1)} %get-tuple-element.113) | copy-start | bytes 3076
  224.1 426.2 %reduce-scatter.6.cloned.1.call-start = ((), (), s32[]{:S(2)}) async-start(), calls=%async_computation.7 | async-start | bytes 5570560 | tf_op jit(solution)/shard_map/reduce_scatter | solution.py:838
  604.6 63.8 %all-reduce.12.cloned.1.call-start = ((), (), s32[]{:S(2)}) async-start(), calls=%async_computation.11 | async-start | bytes 2621440 | tf_op jit(solution)/shard_map/psum | solution.py:944
  605.1 108.7 %all-gather.20.cloned.1.call-start = ((), (), s32[]{:S(2)}) async-start(), calls=%async_computation.8 | async-start | bytes 2621440 | tf_op jit(solution)/shard_map/all_gather | solution.py:864
  606.1 45.6 %copy-start.24 = (f32[256]{0:T(256)}, f32[256]{0:T(256)S(1)}, u32[]{:S(2)}) copy-start(f32[256]{0:T(256)S(1)} %get-tuple-element.92) | copy-start | bytes 3076
  606.1 48.7 %copy-start.7 = (bf16[256,1024]{1,0:T(8,128)(2,1)S(1)}, bf16[256,1024]{1,0:T(8,128)(2,1)}, u32[]{:S(2)}) copy-start(bf16[256,1024]{1,0:T(8,128)(2,1)} %param.30) | copy-start | bytes 1572868
  654.8 13.5 %copy-start.27 = (f32[256]{0:T(256)}, f32[256]{0:T(256)S(1)}, u32[]{:S(2)}) copy-start(f32[256]{0:T(256)S(1)} %fusion.70) | copy-start | bytes 3076
  654.8 13.6 %copy-start.19 = (bf16[16,1024]{1,0:T(8,128)(2,1)S(1)}, bf16[16,1024]{1,0:T(8,128)(2,1)}, u32[]{:S(2)}) copy-start(bf16[16,1024]{1,0:T(8,128)(2,1)} %copy-done.18) | copy-start | bytes 98308
  656.0 144.4 %all-gather.22.cloned.1.call-start = ((), (), s32[]{:S(2)}) async-start(), calls=%async_computation.12 | async-start | bytes 3932160 | tf_op jit(solution)/shard_map/all_gather | solution.py:944
  668.4 185.6 %reduce-scatter.8.cloned.1.call-start = ((), (), s32[]{:S(2)}) async-start(), calls=%async_computation.9 | async-start | bytes 2949120 | tf_op jit(solution)/shard_map/reduce_scatter | solution.py:872
  778.7 4.0 collective-permute-start.3
  780.0 7.4 collective-permute-start.4
  781.4 11.7 %collective-permute-start.5 = (bf16[1024,256]{1,0:T(8,128)(2,1)S(1)}, bf16[1024,256]{1,0:T(8,128)(2,1)S(1)}, u32[]{:S(2)}, u32[]{:S(2)}) collective-permute-start(bf16[1024,256]{1,0:T(8,128)(2,1)S(1)} %get-tuple-element.94), channel_id=1, source_target_pairs={{12,0},{13,1},{14,2},{15,3},{28,16},{29,17},{30,18},{31,19}} | collective-permute-start | bytes 1572872 | tf_op jit(solution)/shard_map/ppermute | solution.py:55
  782.7 10.4 %copy-start.13 = (bf16[1024,256]{1,0:T(8,128)(2,1)}, bf16[1024,256]{1,0:T(8,128)(2,1)S(1)}, u32[]{:S(2)}) copy-start(bf16[1024,256]{1,0:T(8,128)(2,1)S(1)} %collective-permute-done.3.far1) | copy-start | bytes 1572868
  800.3 150.6 %all-reduce.10.cloned.1.call-start = ((), (), s32[]{:S(2)}) async-start(), calls=%async_computation.10 | async-start | bytes 917504 | tf_op jit(solution)/shard_map/psum | solution.py:921
  846.6 7.3 copy-start.5
  849.2 12.7 %copy-start.26 = (f32[256]{0:T(256)S(1)}, f32[256]{0:T(256)}, u32[]{:S(2)}) copy-start(f32[256]{0:T(256)} %copy-done.25) | copy-start | bytes 3076
  855.7 6.2 copy-start.8
  (22 other events, 66.0 us)
Sparse Core Ops, SparseCore 0:
  11.0 28.3 all-gather.23
  41.6 44.0 all-gather.13
  176.1 45.4 reduce-scatter.3
  608.0 60.2 all-reduce.11
  669.8 43.9 all-gather.19
  715.3 39.5 all-gather.21
  800.4 47.2 reduce-scatter.7
  860.4 90.3 all-reduce.9
Sparse Core Ops, SparseCore 1:
  178.0 21.6 all-gather.17
  201.1 104.3 all-gather.29
  306.9 103.8 all-gather.25
  412.3 103.8 all-gather.27
  518.3 22.0 all-gather.15
  604.7 45.6 reduce-scatter.5

commit v2 on v1

--- a/solution.py
+++ b/solution.py
@@ -93,61 +93,401 @@
     return ((r - source == c - target) & (c >= target) & (c < target + HEAD)).astype(BF16)
 
 
-def project_kernel(normed, weights, first, second, cos, sin, codes, q_out, kv_out, lora_out):
-    rows = normed[...]
-    half = weights.shape[1]
-    lora = dot(rows, first[...]).astype(BF16)
-    lora_out[...] = lora
-    pre = (
-        dot(rows[:, :half], weights[0])
-        + dot(rows[:, half:], weights[1])
-        + dot(lora, second[...])
-    )
+def remote(src, dst, send, recv, where):
+    return pltpu.make_async_remote_copy(
+        src_ref=src,
+        dst_ref=dst,
+        send_sem=send,
+        recv_sem=recv,
+        device_id=where,
+        device_id_type=pl.DeviceIdType.MESH,
+    )
+
+
+def ring(me, step, count):
+    return lax.rem(me + (step + count), count)
+
+
+def aug_keys(kv, pair, pairs, first_seg, k_aug, v_aug, start):
+    rows, width = kv.shape
+    lane = iota((rows, LANES), 1)
+    seg = first_seg + iota((rows, LANES), 0) // SEG
+    key_code = ((lane - CODE == seg) | ((lane >= LSE) & (lane < LSE + 3))).astype(F32)
+    one_code = ((lane == ONES) | (lane == ONES + 1)).astype(F32)
+    span = pl.ds(start, rows)
+    k_aug[pair, span, :] = (dot(kv, place_table(width, pair * HEAD, 0)) + key_code).astype(BF16)
+    v_aug[pair, span, :] = (
+        dot(kv, place_table(width, (pairs + pair) * HEAD, 0)) + one_code
+    ).astype(BF16)
+
+
+def forward_kernel(
+    tokens, gain_one, gain_two, shard, first, second, o_first, o_second, cos, sin, codes,
+    w_gate, w_up, w_down, grads, routes,
+    att_out, q_out, kv_out, lora_out, middle_out, low_out, weights_out,
+    gate_far, up_far, down_far, grads_all, routes_all, rows_all,
+    normed_all, weights, q_aug, k_aug, v_aug, top, acc, parts, parts_in, rows_own,
+    shard_sem, normed_sem, kv_sem, part_sem, far_sem, grads_sem, routes_sem, rows_sem,
+    pass_sem, local_sem,
+    *, tp_count, ctx_count,
+):
+    tp, ctx, fsdp = (lax.axis_index(name) for name in ("tp", "ctx", "fsdp"))
+    rank = lax.rem(ctx, SPAN)
+    block, model = tokens.shape
+    heads = q_aug.shape[0]
+    pairs = k_aug.shape[0]
+    group = heads // pairs
+    tall = group * block
+    half = shard.shape[1]
+    q_cols = heads * HEAD
     turn = cos.shape[1]
-    parts = []
-    for start in range(0, pre.shape[1] // 4 * 3, turn):
-        piece = pre[:, start : start + turn]
-        parts.append(piece * cos[...] + swap_halves(piece) * sin[...])
-    heads = q_out.shape[0]
-    width = heads * HEAD
-    queries = (jnp.concatenate(parts[: width // turn], axis=1) * SCORE_SCALE).astype(BF16)
-    for head in range(heads):
-        place = place_table(width, head * HEAD, 0)
-        q_out[head] = (dot(queries, place) + codes[...].astype(F32)).astype(BF16)
-    keys = jnp.concatenate(parts[width // turn :], axis=1).astype(BF16)
-    kv_out[:, : keys.shape[1]] = keys
-    kv_out[:, keys.shape[1] :] = pre[:, width + keys.shape[1] :].astype(BF16)
-
-
-def project(normed, weights, first, second, cos, sin, codes, heads, pairs):
-    rows, width = normed.shape
-    block = 256
-    cols = (heads + 2 * pairs) * HEAD
+    chips = ctx_count // 2
+    partner = ctx + 1 - 2 * lax.rem(ctx, 2)
+    other = {"fsdp": 1 - fsdp}
+
+    barrier = pltpu.get_barrier_semaphore()
+    pl.semaphore_signal(barrier, 1, device_id=other, device_id_type=pl.DeviceIdType.MESH)
+    for k in range(1, tp_count):
+        pl.semaphore_signal(
+            barrier, 1, device_id={"tp": ring(tp, k, tp_count)},
+            device_id_type=pl.DeviceIdType.MESH,
+        )
+    for k in range(1, ctx_count):
+        pl.semaphore_signal(
+            barrier, 1, device_id={"ctx": ring(ctx, k, ctx_count)},
+            device_id_type=pl.DeviceIdType.MESH,
+        )
+    pl.semaphore_wait(barrier, tp_count + ctx_count - 1)
+
+    shard_copy = remote(shard, weights.at[fsdp], shard_sem.at[0], shard_sem.at[1], other)
+    shard_copy.start()
+
+    inputs = tokens[...].astype(F32)
+    normed = rms_scale(inputs, gain_one[...]).astype(BF16)
+    normed_all[tp] = normed
+
+    def normed_copy(k):
+        return remote(
+            normed_all.at[tp], normed_all.at[tp], normed_sem.at[0, k - 1], normed_sem.at[1, k - 1],
+            {"tp": ring(tp, k, tp_count)},
+        )
+
+    for k in range(1, tp_count):
+        normed_copy(k).start()
+
+    def side_copies(k):
+        where = {"ctx": ring(ctx, k, ctx_count)}
+        return (
+            remote(grads, grads_all.at[ctx], grads_sem.at[0, k], grads_sem.at[1, k], where),
+            remote(routes, routes_all.at[ctx], routes_sem.at[0, k], routes_sem.at[1, k], where),
+        )
+
+    own_copies = (
+        pltpu.make_async_copy(grads, grads_all.at[ctx], local_sem.at[0]),
+        pltpu.make_async_copy(routes, routes_all.at[ctx], local_sem.at[1]),
+    )
+    for copy in own_copies:
+        copy.start()
+    for k in range(1, ctx_count):
+        for copy in side_copies(k):
+            copy.start()
+
+    weights[fsdp] = shard[...]
+    shard_copy.wait()
+    far_copies = [
+        remote(near, far, far_sem.at[0, n], far_sem.at[1, n], other)
+        for n, (near, far) in enumerate(((w_gate, gate_far), (w_up, up_far), (w_down, down_far)))
+    ]
+    for copy in far_copies:
+        copy.start()
+    weights_out[...] = weights[...]
+
+    def kv_copy(distance, part):
+        return remote(
+            kv_out.at[0, part], kv_out.at[distance, part],
+            kv_sem.at[0, distance - 1], kv_sem.at[1, distance - 1], {"ctx": ring(ctx, distance, ctx_count)},
+        )
+
+    @pl.loop(0, tp_count)
+    def _(k):
+        @pl.when(k > 0)
+        def _():
+            normed_copy(k).wait_recv()
+
+        part = ring(tp, -k, tp_count)
+        span = pl.ds(pl.multiple_of(part * block, block), block)
+        rows = normed_all[part]
+        lora = dot(rows, first[...]).astype(BF16)
+        lora_out[span, :] = lora
+        pre = (
+            dot(rows[:, :half], weights[0, pl.ds(0, half), :])
+            + dot(rows[:, half:], weights[1, pl.ds(0, half), :])
+            + dot(lora, second[...])
+        )
+        turned = []
+        for start in range(0, pre.shape[1] // 4 * 3, turn):
+            piece = pre[:, start : start + turn]
+            turned.append(piece * cos[span, :] + swap_halves(piece) * sin[span, :])
+        queries = (
+            jnp.concatenate(turned[: q_cols // turn], axis=1) * SCORE_SCALE
+        ).astype(BF16)
+        for head in range(heads):
+            q_aug[head, span, :] = (
+                dot(queries, place_table(q_cols, head * HEAD, 0)) + codes[span, :].astype(F32)
+            ).astype(BF16)
+        keys = jnp.concatenate(turned[q_cols // turn :], axis=1)
+        kv = jnp.concatenate([keys, pre[:, q_cols + keys.shape[1] :]], axis=1).astype(BF16)
+        kv_out[0, part] = kv
+        for distance in range(1, SPAN):
+
+            @pl.when(rank + distance < SPAN)
+            def _(distance=distance):
+                kv_copy(distance, part).start()
+
+        for pair in range(pairs):
+            aug_keys(
+                kv, pair, pairs, rank * SEGS_DEV + part * (block // SEG), k_aug, v_aug,
+                pl.multiple_of(part * block, block),
+            )
+
+    def tile(part, pair, start, size, causal):
+        index = part * pairs + pair
+        rows = pl.ds(pl.multiple_of(part * block, block), block)
+        queries = q_aug[pl.ds(pair * group, group), rows, :].reshape(tall, LANES)
+        span = pl.ds(start, size)
+        scores = dot_nt(queries, k_aug[pair, span, :])
+        if causal:
+            q_row = iota(scores.shape, 0) % block
+            scores = jnp.where(iota(scores.shape, 1) <= q_row, scores, MASKED)
+            now = jnp.broadcast_to(jnp.max(scores, axis=1, keepdims=True), (tall, LANES))
+            probs = jnp.exp(scores - now[:, :1]).astype(BF16)
+            acc[index] = dot(probs, v_aug[pair, span, :])
+        else:
+            before = top[index]
+            now = jnp.maximum(before, jnp.max(scores, axis=1, keepdims=True))
+            probs = jnp.exp(scores - now[:, :1]).astype(BF16)
+            acc[index] = acc[index] * jnp.exp(before - now) + dot(probs, v_aug[pair, span, :])
+        top[index] = now
+
+    @pl.loop(0, tp_count * pairs)
+    def _(index):
+        part, pair = index // pairs, lax.rem(index, pairs)
+        tile(part, pair, pl.multiple_of(part * block, block), block, True)
+
+        @pl.loop(0, part)
+        def _(j):
+            tile(part, pair, pl.multiple_of(j * block, block), block, False)
+
+    group_rows = tp_count * block
+    for distance in range(1, SPAN):
+
+        @pl.when(distance <= rank)
+        def _(distance=distance):
+            remote(
+                kv_out.at[0], kv_out.at[distance], kv_sem.at[0, distance - 1],
+                kv_sem.at[1, distance - 1], {"ctx": ring(ctx, distance, ctx_count)},
+            ).wait_recv()
+
+            @pl.loop(0, tp_count)
+            def _(part):
+                kv = kv_out[distance, part]
+                for pair in range(pairs):
+                    aug_keys(
+                        kv, pair, pairs,
+                        (rank - distance) * SEGS_DEV + part * (block // SEG), k_aug, v_aug,
+                        pl.multiple_of(distance * group_rows + part * block, block),
+                    )
+
+        @pl.when(distance > rank)
+        def _(distance=distance):
+            kv_out[distance] = jnp.zeros(kv_out.shape[1:], BF16)
+
+    def part_copy(k):
+        return remote(
+            parts.at[k], parts_in.at[k], part_sem.at[0, k], part_sem.at[1, k],
+            {"tp": ring(tp, k + 1, tp_count)},
+        )
+
+    @pl.loop(0, tp_count)
+    def _(k):
+        part = ring(tp, k + 1, tp_count)
+        rows = pl.ds(pl.multiple_of(part * block, block), block)
+        for pair in range(pairs):
+            index = part * pairs + pair
+
+            @pl.loop(1, rank + 1)
+            def _(distance, pair=pair):
+                tile(
+                    part, pair, pl.multiple_of(distance * group_rows, group_rows), group_rows, False
+                )
+
+            summed = acc[index]
+            total = summed[:, ONES : ONES + 1]
+            result = (summed / total).astype(BF16)
+            for member in range(group):
+                head = pair * group + member
+                att_out[rows, pl.ds(head * HEAD, HEAD)] = result[
+                    member * block : (member + 1) * block, :HEAD
+                ]
+            minus = -(top[index] + jnp.log(total))
+            high = minus.astype(BF16).astype(F32)
+            middle = (minus - high).astype(BF16).astype(F32)
+            lane = iota(minus.shape, 1)
+            queries = q_aug[pl.ds(pair * group, group), rows, :].reshape(tall, LANES)
+            coded = jnp.where(
+                lane == LSE,
+                high,
+                jnp.where(
+                    lane == LSE + 1,
+                    middle,
+                    jnp.where(lane == LSE + 2, minus - high - middle, queries.astype(F32)),
+                ),
+            )
+            q_out[pl.ds(pair * group, group), rows, :] = coded.astype(BF16).reshape(
+                group, block, LANES
+            )
+        mixed = att_out[rows, :]
+        for side in range(2):
+            parts[k, :, side * half : (side + 1) * half] = dot(
+                mixed, weights[side, pl.ds(half, q_cols), :]
+            ).astype(BF16)
+        parts[k, :, model:] = dot(mixed, o_first[...]).astype(BF16)
+
+        @pl.when(k < tp_count - 1)
+        def _():
+            part_copy(k).start()
+
+    summed = parts[tp_count - 1].astype(F32)
+    for k in range(tp_count - 1):
+        part_copy(k).wait_recv()
+        summed += parts_in[k].astype(F32)
+    low = summed[:, model:].astype(BF16)
+    low_out[...] = low
+    middle = inputs + RESIDUAL_SCALE * (summed[:, :model] + dot(low, o_second[...]))
+    middle_out[...] = middle
+    rows_own[...] = rms_scale(middle, gain_two[...]).astype(BF16)
+
+    own_rows = pltpu.make_async_copy(rows_own, rows_all.at[ctx], local_sem.at[2])
+    own_rows.start()
+    to_partner = remote(
+        rows_own, rows_all.at[ctx], rows_sem.at[0, 0], rows_sem.at[1, 0], {"ctx": partner}
+    )
+    to_partner.start()
+
+    def rows_copy(k):
+        return remote(
+            rows_own, rows_all.at[ctx], rows_sem.at[0, k], rows_sem.at[1, k],
+            {"ctx": ring(ctx, 2 * k, ctx_count)},
+        )
+
+    def pass_copy(k):
+        source = ring(ctx, -2 * k, ctx_count)
+        return remote(
+            rows_all.at[source], rows_all.at[source], pass_sem.at[0, k], pass_sem.at[1, k],
+            {"ctx": partner},
+        )
+
+    for k in range(1, chips):
+        rows_copy(k).start()
+    for k in range(1, chips):
+        rows_copy(k).wait_recv()
+        pass_copy(k).start()
+
+    for k in range(1, tp_count):
+        normed_copy(k).wait_send()
+    for k in range(tp_count - 1):
+        part_copy(k).wait_send()
+    for distance in range(1, SPAN):
+
+        @pl.when(rank + distance < SPAN)
+        def _(distance=distance):
+            remote(
+                kv_out.at[0], kv_out.at[distance], kv_sem.at[0, distance - 1],
+                kv_sem.at[1, distance - 1], {"ctx": ring(ctx, distance, ctx_count)},
+            ).wait_send()
+
+    for k in range(1, ctx_count):
+        for copy in side_copies(k):
+            copy.wait()
+    for copy in own_copies:
+        copy.wait()
+    own_rows.wait()
+    to_partner.wait()
+    for k in range(1, chips):
+        rows_copy(k).wait_send()
+        pass_copy(k).wait()
+    for copy in far_copies:
+        copy.wait()
+
+
+def forward(
+    tokens, gains, shard, first, second, o_first, o_second, cos, sin, codes, weights, grads,
+    routes, tp_count, ctx_count,
+):
+    block, model = tokens.shape
+    rows = tp_count * block
+    heads = o_first.shape[0] // HEAD
+    cols = second.shape[1]
+    kv_cols = cols - heads * HEAD
+    pairs = kv_cols // (2 * HEAD)
+    tall = heads // pairs * block
+    chips = ctx_count // 2
+    vmem = pl.BlockSpec(memory_space=pltpu.VMEM)
+    hbm = pl.BlockSpec(memory_space=pl.ANY)
+    dma = pltpu.SemaphoreType.DMA
+    part = (block, model + LANES)
     return pl.pallas_call(
-        project_kernel,
-        grid=(rows // block,),
-        in_specs=[
-            pl.BlockSpec((block, width), lambda i: (i, 0)),
-            pl.BlockSpec((2, width // 2, cols), lambda i: (0, 0, 0)),
-            pl.BlockSpec((width, LANES), lambda i: (0, 0)),
-            pl.BlockSpec((LANES, cols), lambda i: (0, 0)),
-            pl.BlockSpec((block, LANES), lambda i: (i, 0)),
-            pl.BlockSpec((block, LANES), lambda i: (i, 0)),
-            pl.BlockSpec((block, LANES), lambda i: (i, 0)),
+        functools.partial(forward_kernel, tp_count=tp_count, ctx_count=ctx_count),
+        in_specs=[vmem] * 11 + [hbm] * 5,
+        out_specs=[vmem] * 7 + [hbm] * 6,
+        out_shape=[
+            jax.ShapeDtypeStruct((rows, heads * HEAD), BF16),
+            jax.ShapeDtypeStruct((heads, rows, LANES), BF16),
+            jax.ShapeDtypeStruct((SPAN, tp_count, block, kv_cols), BF16),
+            jax.ShapeDtypeStruct((rows, LANES), BF16),
+            jax.ShapeDtypeStruct((block, model), F32),
+            jax.ShapeDtypeStruct((block, LANES), BF16),
+            jax.ShapeDtypeStruct((2,) + shard.shape, BF16),
+            *[jax.ShapeDtypeStruct(w.shape, BF16) for w in weights],
+            jax.ShapeDtypeStruct((ctx_count,) + grads.shape, BF16),
+            jax.ShapeDtypeStruct((ctx_count,) + routes.shape, jnp.int32),
+            jax.ShapeDtypeStruct((ctx_count, block, model), BF16),
         ],
-        out_specs=[
-            pl.BlockSpec((heads, block, LANES), lambda i: (0, i, 0)),
-            pl.BlockSpec((block, 2 * pairs * HEAD), lambda i: (i, 0)),
-            pl.BlockSpec((block, LANES), lambda i: (i, 0)),
+        scratch_shapes=[
+            pltpu.VMEM((tp_count, block, model), BF16),
+            pltpu.VMEM((2,) + shard.shape, BF16),
+            pltpu.VMEM((heads, rows, LANES), BF16),
+            pltpu.VMEM((pairs, SPAN * rows, LANES), BF16),
+            pltpu.VMEM((pairs, SPAN * rows, LANES), BF16),
+            pltpu.VMEM((tp_count * pairs, tall, LANES), F32),
+            pltpu.VMEM((tp_count * pairs, tall, LANES), F32),
+            pltpu.VMEM((tp_count,) + part, BF16),
+            pltpu.VMEM((tp_count - 1,) + part, BF16),
+            pltpu.VMEM((block, model), BF16),
+            dma((2,)),
+            dma((2, tp_count - 1)),
+            dma((2, SPAN - 1)),
+            dma((2, tp_count - 1)),
+            dma((2, 3)),
+            dma((2, ctx_count)),
+            dma((2, ctx_count)),
+            dma((2, chips)),
+            dma((2, chips)),
+            dma((3,)),
         ],
-        out_shape=[
-            jax.ShapeDtypeStruct((heads, rows, LANES), BF16),
-            jax.ShapeDtypeStruct((rows, 2 * pairs * HEAD), BF16),
-            jax.ShapeDtypeStruct((rows, LANES), BF16),
-        ],
-        compiler_params=pltpu.CompilerParams(vmem_limit_bytes=VMEM_LIMIT),
-        name="project",
-    )(normed, weights, first, second, cos, sin, codes)
+        compiler_params=pltpu.CompilerParams(
+            vmem_limit_bytes=VMEM_LIMIT, collective_id=0, has_side_effects=True
+        ),
+        cost_estimate=pl.CostEstimate(
+            flops=16 * SPAN * rows * rows * heads * LANES,
+            bytes_accessed=32 * 1024 * 1024,
+            transcendentals=0,
+        ),
+        name="forward",
+    )(
+        tokens, *gains, shard, first, second, o_first, o_second, cos, sin, codes, *weights,
+        grads, routes,
+    )
 
 
 def build_tables(rank, kv_refs, k_aug, v_aug):
@@ -156,134 +496,16 @@
 
         @pl.when(distance <= rank)
         def _(distance=distance, kv=kv):
-            rows, width = kv.shape
             values = kv[...]
-            lane = iota((rows, LANES), 1)
-            seg = (rank - distance) * SEGS_DEV + iota((rows, LANES), 0) // SEG
-            key_code = ((lane - CODE == seg) | ((lane >= LSE) & (lane < LSE + 3))).astype(F32)
-            one_code = ((lane == ONES) | (lane == ONES + 1)).astype(F32)
             for pair in range(pairs):
-                k_place = place_table(width, pair * HEAD, 0)
-                v_place = place_table(width, (pairs + pair) * HEAD, 0)
-                span = pl.ds(distance * rows, rows)
-                k_aug[pair, span, :] = (dot(values, k_place) + key_code).astype(BF16)
-                v_aug[pair, span, :] = (dot(values, v_place) + one_code).astype(BF16)
-
-
-def attend_kernel(
-    rank_ref, q_ref, kv0, kv1, kv2, kv3, w_out, out_in, att_out, q_out, part_out,
-    k_aug, v_aug, top, acc,
-):
-    step = pl.program_id(0)
-    rank = rank_ref[0]
-    heads, block, _ = q_ref.shape
-    pairs = k_aug.shape[0]
-    group = heads // pairs
-    rows = kv0.shape[0]
-    tall = group * block
-
-    @pl.when(step == 0)
-    def _():
-        build_tables(rank, (kv0, kv1, kv2, kv3), k_aug, v_aug)
-
-    for pair in range(pairs):
-        queries = q_ref[pl.ds(pair * group, group)].reshape(tall, LANES)
-        top[...] = jnp.full(top.shape, MASKED, F32)
-        acc[...] = jnp.zeros(acc.shape, F32)
-
-        def tile(start, size, causal, queries=queries, pair=pair):
-            span = pl.ds(start, size)
-            scores = dot_nt(queries, k_aug[pair, span, :])
-            if causal:
-                q_row = iota(scores.shape, 0) % block
-                scores = jnp.where(iota(scores.shape, 1) <= q_row, scores, MASKED)
-            before = top[...]
-            now = jnp.maximum(before, jnp.max(scores, axis=1, keepdims=True))
-            top[...] = now
-            probs = jnp.exp(scores - now[:, :1]).astype(BF16)
-            acc[...] = acc[...] * jnp.exp(before - now) + dot(probs, v_aug[pair, span, :])
-
-        tile(pl.multiple_of(step * block, block), block, True)
-
-        @pl.loop(0, step)
-        def _(j, tile=tile):
-            tile(pl.multiple_of(j * block, block), block, False)
-
-        for distance in range(1, SPAN):
-
-            @pl.when(distance <= rank)
-            def _(distance=distance, tile=tile):
-                tile(distance * rows, rows, False)
-
-        total = acc[:, ONES : ONES + 1]
-        result = (acc[...] / total).astype(BF16)
-        for member in range(group):
-            head = pair * group + member
-            att_out[:, pl.ds(head * HEAD, HEAD)] = result[member * block : (member + 1) * block, :HEAD]
-        minus = -(top[...] + jnp.log(total))
-        high = minus.astype(BF16).astype(F32)
-        middle = (minus - high).astype(BF16).astype(F32)
-        low = minus - high - middle
-        lane = iota(minus.shape, 1)
-        coded = jnp.where(
-            lane == LSE,
-            high,
-            jnp.where(
-                lane == LSE + 1, middle, jnp.where(lane == LSE + 2, low, queries.astype(F32))
-            ),
-        )
-        q_out[pl.ds(pair * group, group)] = coded.astype(BF16).reshape(group, block, LANES)
-
-    mixed = att_out[...]
-    half = w_out.shape[2]
-    part_out[:, :half] = dot(mixed, w_out[0]).astype(BF16)
-    part_out[:, half : 2 * half] = dot(mixed, w_out[1]).astype(BF16)
-    part_out[:, 2 * half :] = dot(mixed, out_in[...]).astype(BF16)
-
-
-def attend(rank, queries, kv_parts, w_out, out_in):
-    heads, rows, _ = queries.shape
-    block = 256
-    kv_width = kv_parts[0].shape[1]
-    pairs = kv_width // (2 * HEAD)
-    tall = heads // pairs * block
-    cols = 2 * w_out.shape[2] + LANES
-    whole = lambda i, r: (0, 0)
-    return pl.pallas_call(
-        attend_kernel,
-        grid_spec=pltpu.PrefetchScalarGridSpec(
-            num_scalar_prefetch=1,
-            grid=(rows // block,),
-            in_specs=[pl.BlockSpec((heads, block, LANES), lambda i, r: (0, i, 0))]
-            + [pl.BlockSpec((rows, kv_width), whole)] * SPAN
-            + [
-                pl.BlockSpec(w_out.shape, lambda i, r: (0, 0, 0)),
-                pl.BlockSpec(out_in.shape, whole),
-            ],
-            out_specs=[
-                pl.BlockSpec((block, heads * HEAD), lambda i, r: (i, 0)),
-                pl.BlockSpec((heads, block, LANES), lambda i, r: (0, i, 0)),
-                pl.BlockSpec((block, cols), lambda i, r: (i, 0)),
-            ],
-            scratch_shapes=[
-                pltpu.VMEM((pairs, SPAN * rows, LANES), BF16),
-                pltpu.VMEM((pairs, SPAN * rows, LANES), BF16),
-                pltpu.VMEM((tall, LANES), F32),
-                pltpu.VMEM((tall, LANES), F32),
-            ],
-        ),
-        out_shape=[
-            jax.ShapeDtypeStruct((rows, heads * HEAD), BF16),
-            jax.ShapeDtypeStruct((heads, rows, LANES), BF16),
-            jax.ShapeDtypeStruct((rows, cols), BF16),
-        ],
-        compiler_params=pltpu.CompilerParams(vmem_limit_bytes=VMEM_LIMIT),
-        name="attend",
-    )(rank, queries, *kv_parts, w_out, out_in)
+                aug_keys(
+                    values, pair, pairs, (rank - distance) * SEGS_DEV, k_aug, v_aug,
+                    distance * values.shape[0],
+                )
 
 
 def retrace_kernel(
-    rank_ref, q_ref, kv0, kv1, kv2, kv3, att, branch, w_out, out_in, out_out, cos, sin,
+    rank_ref, q_ref, kv_ref, att, branch, w_out, out_in, out_out, cos, sin,
     dq_out, own_out, far_out, in_grad,
     k_aug, v_aug, dk, dv, dq,
 ):
@@ -292,13 +514,13 @@
     heads, block, _ = q_ref.shape
     pairs = k_aug.shape[0]
     group = heads // pairs
-    rows = kv0.shape[0]
+    rows = kv_ref.shape[1]
     tall = group * block
     width = heads * HEAD
 
     @pl.when(step == 0)
     def _():
-        build_tables(rank, (kv0, kv1, kv2, kv3), k_aug, v_aug)
+        build_tables(rank, [kv_ref.at[d] for d in range(SPAN)], k_aug, v_aug)
         dk[...] = jnp.zeros(dk.shape, F32)
         dv[...] = jnp.zeros(dv.shape, F32)
         in_grad[...] = jnp.zeros(in_grad.shape, F32)
@@ -392,7 +614,7 @@
 def retrace(rank, queries, kv_parts, att, branch, w_out, out_in, out_out, cos, sin):
     heads, rows, _ = queries.shape
     block = 256
-    kv_width = kv_parts[0].shape[1]
+    kv_width = kv_parts.shape[2]
     pairs = kv_width // (2 * HEAD)
     tall = heads // pairs * block
     width = heads * HEAD
@@ -404,8 +626,8 @@
             num_scalar_prefetch=1,
             grid=(rows // block,),
             in_specs=[pl.BlockSpec((heads, block, LANES), lambda i, r: (0, i, 0))]
-            + [pl.BlockSpec((rows, kv_width), whole)] * SPAN
             + [
+                pl.BlockSpec(kv_parts.shape, lambda i, r: (0, 0, 0)),
                 pl.BlockSpec((block, width), row),
                 pl.BlockSpec((block, branch.shape[1]), row),
                 pl.BlockSpec(w_out.shape, lambda i, r: (0, 0, 0)),
@@ -436,7 +658,12 @@
         ],
         compiler_params=pltpu.CompilerParams(vmem_limit_bytes=VMEM_LIMIT),
         name="retrace",
-    )(rank, queries, *kv_parts, att, branch, w_out, out_in, out_out, cos, sin)
+        cost_estimate=pl.CostEstimate(
+            flops=16 * SPAN * rows * rows * heads * LANES,
+            bytes_accessed=8 * 1024 * 1024,
+            transcendentals=0,
+        ),
+    )(rank, queries, kv_parts, att, branch, w_out, out_in, out_out, cos, sin)
 
 
 def unproject_kernel(
@@ -491,21 +718,27 @@
         ],
         compiler_params=pltpu.CompilerParams(vmem_limit_bytes=VMEM_LIMIT),
         name="unproject",
+        cost_estimate=pl.CostEstimate(
+            flops=2 * rows * model * (cols + 2 * LANES),
+            bytes_accessed=8 * 1024 * 1024,
+            transcendentals=0,
+        ),
     )(dq, own, *fars, lora, weights, second, cos, sin)
 
 
 def expert_kernel(
-    sets, base, x_ref, g_ref, routes, router, w_gate, w_up, w_down,
-    gate_in, up_in, gate_out, up_out, down_in, down_out,
+    sets, base, x_ref, g_ref, routes, router,
+    w_gate, w_up, w_down, w_gate_far, w_up_far, w_down_far, gate_in, up_in, gate_out, up_out, down_in, down_out,
     mixed_out, grad_out,
     rank_rows, gate_rows, slope_rows, mix, back, xs, firsts, tall_grad,
+    gate_full, up_full, down_full,
     *, slots, sources,
 ):
     chunk, expert = pl.program_id(0), pl.program_id(1)
     experts = router.shape[0]
     tokens, model = x_ref.shape
     each = tokens // sources
-    hidden = w_gate.shape[3]
+    hidden = w_gate.shape[2]
     lanes = gate_in.shape[2]
     chosen = sets[chunk]
 
@@ -549,47 +782,43 @@
     keep = (iota((1, 2 * lanes), 1) % lanes // RANK == chosen).astype(BF16)
     rows = xs[...]
     inner = dot(rows, firsts[...]).astype(BF16) * keep
-    half = w_gate.shape[2]
-    gate_value = (
-        dot(rows[:, :half], w_gate[0, 0])
-        + dot(rows[:, half:], w_gate[1, 0])
-        + dot(inner[:, :lanes], gate_out[0])
-    )
-    up_value = (
-        dot(rows[:, :half], w_up[0, 0])
-        + dot(rows[:, half:], w_up[1, 0])
-        + dot(inner[:, lanes:], up_out[0])
-    )
+    for full, near, far in (
+        (gate_full, w_gate, w_gate_far),
+        (up_full, w_up, w_up_far),
+        (down_full, w_down, w_down_far),
+    ):
+        size = near.shape[1]
+        full[pl.ds(pl.multiple_of(base[1] * size, size), size), :] = near[0]
+        full[pl.ds(pl.multiple_of((1 - base[1]) * size, size), size), :] = far[0]
+    gate_value = dot(rows, gate_full[...]) + dot(inner[:, :lanes], gate_out[0])
+    up_value = dot(rows, up_full[...]) + dot(inner[:, lanes:], up_out[0])
     sigmoid = 1.0 / (1.0 + jnp.exp(-gate_value))
     silu = gate_value * sigmoid
     active = (silu * up_value).astype(BF16)
     down_inner = dot(active, down_in[0]).astype(BF16) * keep[:, :lanes]
-    down_half = w_down.shape[2]
     produced = (
-        dot(active[:, :down_half], w_down[0, 0])
-        + dot(active[:, down_half:], w_down[1, 0])
-        + dot(down_inner, down_out[0])
-    ).astype(BF16).astype(F32)
+        (dot(active, down_full[...]) + dot(down_inner, down_out[0])).astype(BF16).astype(F32)
+    )
     slope = jnp.sum(upstream * produced, axis=1, keepdims=True)
     sent = (gate_column * produced).astype(BF16)
     slot_grad = (gate_column * upstream).astype(BF16)
 
     down_inner_grad = dot_nt(slot_grad, down_out[0]).astype(BF16) * keep[:, :lanes]
     active_grad = (
-        jnp.concatenate(
-            [dot_nt(slot_grad, w_down[0, 0]), dot_nt(slot_grad, w_down[1, 0])], axis=1
-        )
-        + dot_nt(down_inner_grad, down_in[0])
-    ).astype(BF16).astype(F32)
+        (dot_nt(slot_grad, down_full[...]) + dot_nt(down_inner_grad, down_in[0]))
+        .astype(BF16)
+        .astype(F32)
+    )
     gate_grad = (active_grad * up_value * (sigmoid + silu * (1.0 - sigmoid))).astype(BF16)
     up_grad = (active_grad * silu).astype(BF16)
     inner_grad = (
         jnp.concatenate([dot_nt(gate_grad, gate_out[0]), dot_nt(up_grad, up_out[0])], axis=1)
     ).astype(BF16) * keep
-    row_grad = jnp.concatenate(
-        [dot_nt(gate_grad, w_gate[h, 0]) + dot_nt(up_grad, w_up[h, 0]) for h in range(2)], axis=1
-    )
-    row_grad = (row_grad + dot_nt(inner_grad, firsts[...])).astype(BF16)
+    row_grad = (
+        dot_nt(gate_grad, gate_full[...])
+        + dot_nt(up_grad, up_full[...])
+        + dot_nt(inner_grad, firsts[...])
+    ).astype(BF16)
 
     for s in range(sources):
         span = slice(s * slots, (s + 1) * slots)
@@ -632,11 +861,9 @@
 ):
     total, model = rows.shape
     experts = router.shape[0]
-    w_gate, w_up, w_down = weights
-    local = w_gate.shape[1]
+    local, half, hidden = weights[0].shape
     trees = sets.shape[0]
     tokens = total // trees
-    hidden = w_gate.shape[3]
     lanes = adapters[0].shape[2]
     cols = 2 * model + LANES
     tall = sources * slots
@@ -653,11 +880,7 @@
                 pl.BlockSpec((tokens, model), piece),
                 pl.BlockSpec((routes.shape[0], tokens), lambda c, e, *_: (0, c)),
                 pl.BlockSpec(router.shape, fixed),
-                *[
-                    pl.BlockSpec((2, 1) + w.shape[2:], lambda c, e, *_: (0, e, 0, 0))
-                    for w in weights
-                ],
-                *[pl.BlockSpec((1,) + a.shape[1:], expert) for a in adapters],
+                *[pl.BlockSpec((1,) + a.shape[1:], expert) for a in (*weights, *adapters)],
             ],
             out_specs=[
                 pl.BlockSpec((tokens, cols), piece),
@@ -672,6 +895,9 @@
                 pltpu.VMEM((tall, model), BF16),
                 pltpu.VMEM((model, 2 * lanes), BF16),
                 pltpu.VMEM((2 * lanes, model), F32),
+                pltpu.VMEM((2 * half, hidden), BF16),
+                pltpu.VMEM((2 * half, hidden), BF16),
+                pltpu.VMEM((hidden, model), BF16),
             ],
         ),
         out_shape=[
@@ -680,6 +906,11 @@
         ],
         compiler_params=pltpu.CompilerParams(vmem_limit_bytes=60 * 1024 * 1024),
         name="experts",
+        cost_estimate=pl.CostEstimate(
+            flops=2 * local * total * model * model * 2,
+            bytes_accessed=8 * 1024 * 1024,
+            transcendentals=0,
+        ),
     )(sets, base, rows, upstream, routes, router, *weights, *adapters)
 
 
@@ -741,9 +972,6 @@
         ],
         axis=0,
     )
-    attention_weights = lax.all_gather(attention_shard, "fsdp")
-    project_weights = attention_weights[:, : w_query.shape[0]]
-    output_weights = attention_weights[:, w_query.shape[0] :]
 
     seg_start = (fsdp_rank * ctx_count + ctx_rank) * SEGS_DEV
     tree_index = seg_start // TREE_SEGS
@@ -757,8 +985,6 @@
     gain_one = gain_a.astype(F32)
     gain_two = gain_b.astype(F32)
     normed = rms_scale(inputs, gain_one).astype(BF16)
-    normed_all = lax.all_gather(normed, "tp", axis=0, tiled=True)
-    group_rows = normed_all.shape[0]
 
     own_reach = lax.dynamic_slice_in_dim(reach, local_start, SEGS_DEV, 0)
     codes = jnp.pad(
@@ -802,27 +1028,24 @@
     )
     o_second = jnp.pad(take_set(out_out, chosen, 0), ((0, LANES - RANK), (0, 0)))
 
-    queries, kv, lora = project(
-        normed_all, project_weights, first, second, cos, sin, codes, heads, pairs
-    )
-    kv_parts = [kv] + [shifted(kv, "ctx", distance) for distance in range(1, SPAN)]
-    attended, queries, part = attend(rank, queries, kv_parts, output_weights, o_first)
-    summed = lax.psum_scatter(part, "tp", scatter_dimension=0, tiled=True)
-    o_reduced = summed[:, model:]
-    middle = inputs + RESIDUAL_SCALE * (
-        summed[:, :model].astype(F32)
-        + jnp.dot(o_reduced, o_second, preferred_element_type=F32)
-    )
-
-    upstream_all = lax.all_gather(out_grad, "ctx", axis=0, tiled=True)
-    routes_all = lax.all_gather(routes, "ctx", axis=0, tiled=True).T
-    gate_full = lax.all_gather(w_gate, "fsdp")
-    up_full = lax.all_gather(w_up, "fsdp")
-    down_full = lax.all_gather(w_down, "fsdp")
+    (
+        attended, queries, kv_parts, lora, middle, o_reduced, attention_weights,
+        *far_weights, upstream_all, routes_all, rows_all,
+    ) = forward(
+        tokens, (gain_one[None], gain_two[None]), attention_shard, first, second,
+        o_first, o_second, cos, sin, codes, (w_gate, w_up, w_down), out_grad, routes.T,
+        tp_count, ctx_count,
+    )
+    kv_parts = kv_parts.reshape(SPAN, -1, kv_parts.shape[-1])
+    project_weights = attention_weights[:, : w_query.shape[0]]
+    output_weights = attention_weights[:, w_query.shape[0] :]
+    upstream_all = upstream_all.reshape(-1, model)
+    rows_all = rows_all.reshape(-1, model)
+    routes_all = routes_all.transpose(1, 0, 2).reshape(TOP, -1)
     normed_two = rms_scale(middle, gain_two).astype(BF16)
-    rows_all = lax.all_gather(normed_two, "ctx", axis=0, tiled=True)
+
     tree_sets = lax.dynamic_slice_in_dim(adapter_set, fsdp_rank * trees, trees, 0)
-    base = (ctx_rank * local_experts).astype(jnp.int32).reshape(1)
+    base = jnp.stack([ctx_rank * local_experts, fsdp_rank]).astype(jnp.int32)
     mixed, expert_part = run_experts(
         tree_sets,
         base,
@@ -830,7 +1053,7 @@
         upstream_all,
         routes_all,
         w_router.T,
-        (gate_full, up_full, down_full),
+        (w_gate, w_up, w_down, *far_weights),
         (gate_in, up_in, gate_out, up_out, down_in, down_out),
         slots,
         SPAN,

time: 993 us -> 780 us (0.79)
  waiting for transfers between devices: 633 us -> 199 us
  Pallas kernels: 195 us -> 432 us
    all_gather x7 -> x0, waiting for transfers between devices: 370 us -> none  [the longest x1 105 us: per_device(): up_full = lax.all_gather(w_up, 'fsdp')]
    pallas_call x2 -> x1, Pallas kernels: 60.9 us -> 295 us  [forward(): pl.pallas_call(functools.partial(forward_kernel, tp_count=tp_count, ctx_c...]
    reduce_scatter x2 -> x1, waiting for transfers between devices: 42.3 us -> 0.01 us  [per_device(): summed = lax.psum_scatter(part, 'tp', scatter_dimension=0, tiled=True)]
    ppermute x6 -> x3, waiting for transfers between devices: 30.6 us -> 9.31 us  [shifted(): return lax.ppermute(block, axis, route)]
    unnamed x80 -> x66, local copies, waits for them, and re-layouts: 23 us -> 22.4 us
  transfers between devices with their start and end apart: 20 -> 9, of which waited for: 15 -> 6; matrix products, arithmetic and copies ran while one was open for 9% -> 8% of each run, Pallas kernels for 7% -> 9%
where the time goes in v2:
time: 780 us; the launch traced here: 770 us
  Pallas kernels  432 us (55%)
  waiting for transfers between devices  199 us (26%)
  local copies, waits for them, and re-layouts  70 us (9%)
  matrix products  20.8 us (3%)
  between operations  17.3 us (2%)
  other arithmetic  15.8 us (2%)
  blocking collectives  10.9 us (1%)
    pallas_call x1, Pallas kernels, forward(): pl.pallas_call(functools.partial(forward_kernel, tp_count=tp_count, ctx_c...  295 us
    psum x1, waiting for transfers between devices, per_device(): packed = lax.all_gather(lax.psum(packed, ('ctx', 'tp')), 'fsdp')  87.1 us
    pallas_call x1, Pallas kernels, run_experts(): pl.pallas_call(functools.partial(expert_kernel, slots=slots, sources=sour...  66.7 us
    pallas_call x1, Pallas kernels, retrace(): pl.pallas_call(retrace_kernel, grid_spec=pltpu.PrefetchScalarGridSpec(num...  63.3 us
    all_gather x1, waiting for transfers between devices, per_device(): branch_all = lax.all_gather(branch_grad, 'tp', axis=0, tiled=True)  45.9 us
    reduce_scatter x1, waiting for transfers between devices, per_device(): lax.psum_scatter(mixed, 'ctx', scatter_dimension=0, tiled=True).astype(F32)  45.3 us
    unnamed x66, local copies, waits for them, and re-layouts  22.4 us
    transpose x6, local copies, waits for them, and re-layouts, expert_rows(): jnp.einsum('ts,terd->esrd', place.astype(BF16), part, preferred_element_t...  20.7 us
  transfers between devices with their start and end apart: 9, of which 6 were waited for; matrix products, arithmetic and copies ran while one was open for 8% of the time, Pallas kernels for 9%

profile of v2, /device:TPU:13, one launch (start us, length us, event | category | flops | bytes accessed | tf_op | source)
XLA Modules:
  0.0 769.7 jit_solution(5779560203648919708)
XLA Ops:
  20.0 3.0 multiply_sine_fusion
  26.0 295.2 %forward.1 = (bf16[1024,256]{1,0:T(8,128)(2,1)}, bf16[4,1024,128]{2,1,0:T(8,128)(2,1)}, bf16[4,4,256,256]{3,2,1,0:T(8,128)(2,1)}, bf16[1024,128]{1,0:T(8,128)(2,...) custom-call(bf16[256,1024]{1,0:T(8,128)(2,1)} %tokens.1, ...), custom_call_target="tpu_custom_call" | custom-call | flops 34359738368 | bytes 33554432 | tf_op jit(solution)/shard_map/forward/pallas_call | solution.py:439
  321.3 66.7 %experts.1 = (bf16[1024,2176]{1,0:T(8,128)(2,1)}, bf16[1,8,80,1024]{3,2,1,0:T(8,128)(2,1)}) custom-call(s32[1]{0:T(128)} %get-tuple-element.127.sets, s32[2]{0:T(128)} %pad_add_fusion.base, bf16[1024,1024]{1,0:T(8,128)(2,1)} %bitcast.135, bf16[1024,1024]{1,0:T(8,128)(2,1)} %bitcast.134, s32[8,1024]{1,0:T(8,128)} %bitcast.136, bf16[32,1024]{1,0:T(8,128)(2,1)} %bitcast.129, ...), custom_call_target="tpu_custom_call" | custom-call | flops 34359738368 | bytes 8388608 | tf_op jit(solution)/shard_map/experts/pallas_call | solution.py:873
  390.0 45.3 %reduce-scatter.3.cloned.1.call-done = bf16[256,2176]{1,0:T(8,128)(2,1)} async-done(((bf16[1024,2176]{1,0:T(8,128)(2,1)}), bf16[256,2176]{1,0:T(8,128)(2,1)}) %reduce-scatter.3.cloned.1.call-update) | async-done | bytes 1114128 | tf_op jit(solution)/shard_map/reduce_scatter | solution.py:1061
  440.2 1.9 slice.97.w_out
  442.1 10.7 %all-reduce.12.cloned.1.call-done = bf16[1,1,8,80,1024]{4,3,2,1,0:T(8,128)(2,1)} async-done(((bf16[1,1,8,80,1024]{4,3,2,1,0:T(8,128)(2,1)}), bf16[1,1,8,80,1024]{4,3,2,1,0:T(8,128)(2,1)}) %all-reduce.12.cloned.1.call-update) | async-done | bytes 1310736 | tf_op jit(solution)/shard_map/psum | solution.py:1167
  452.9 45.9 %all-gather.3.cloned.1.call-done.branch = bf16[1024,1024]{1,0:T(8,128)(2,1)} async-done(((bf16[256,1024]{1,0:T(8,128)(2,1)}), bf16[1024,1024]{1,0:T(8,128)(2,1)}) %all-gather.3.cloned.1.call-update) | async-done | bytes 2097168 | tf_op jit(solution)/shard_map/all_gather | solution.py:1087
  498.8 63.3 %retrace.1 = (bf16[1024,256]{1,0:T(8,128)(2,1)}, f32[1024,256]{1,0:T(8,128)}, bf16[3,1024,256]{2,1,0:T(8,128)(2,1)}, f32[256,128]{1,0:T(8,128)}) custom-call(s32[1]{0:T(128)} %bitcast.13.rank_ref, bf16[4,1024,128]{2,1,0:T(8,128)(2,1)} %get-tuple-element.45.q_ref, bf16[4,1024,256]{2,1,0:T(8,128)(2,1)} %bitcast.133, bf16[1024,256]{1,0:T(8,128)(2,1)} %get-tuple-element.47.att, ...), custom_call_target="tpu_custom_call" | custom-call | flops 34359738368 | bytes 8388608 | tf_op jit(solution)/shard_map/retrace/pallas_call | solution.py:623
  562.1 1.6 slice_bitcast_fusion
  568.7 3.7 collective-permute-done.1.far2
  572.4 5.6 collective-permute-done.2.far3
  578.9 6.4 unproject.1
  585.4 4.4 copy.205
  591.3 4.4 copy.162
  595.7 5.3 copy.172
  601.0 1.5 convolution_bitcast_fusion.5
  602.6 2.5 copy.163
  605.1 1.9 convolution_bitcast_fusion.1
  607.0 4.4 copy.164
  611.4 5.3 copy.173
  616.7 1.5 convolution_bitcast_fusion.4
  618.3 2.5 copy.165
  620.8 1.5 convolution_bitcast_fusion.3
  622.3 2.5 copy.166
  624.8 3.1 copy.174
  627.9 1.9 convolution_bitcast_fusion
  629.9 4.4 copy.167
  639.1 2.6 fusion.7
  641.7 2.1 convolution_dynamic-update-slice_fusion
  647.3 3.3 fusion.11
  650.6 87.1 %all-reduce.10.cloned.1.call-done = f32[1,112,1024]{2,1,0:T(8,128)} async-done(((f32[1,112,1024]{2,1,0:T(8,128)}), f32[1,112,1024]{2,1,0:T(8,128)}) %all-reduce.10.cloned.1.call-update) | async-done | bytes 458768 | tf_op jit(solution)/shard_map/psum | solution.py:1144
  737.7 10.9 %all_gather.17 = f32[2,112,1024]{2,1,0:T(8,128)S(1)} all-gather(f32[1,112,1024]{2,1,0:T(8,128)} %all-reduce.10.cloned.1.call-done), channel_id=1, replica_groups=mesh['fsdp'=2,'ctx'=4,'tp'=4] {'fsdp'}, dimensions={0}, use_global_device_ids=true | all-gather | bytes 1376256 | tf_op jit(solution)/shard_map/all_gather | solution.py:1144
  (162 shorter events, 49.7 us)
Async XLA Ops:
  8.0 6.2 copy-start
  8.0 10.7 %copy-start.26 = (s32[64]{0:T(128)S(1)}, s32[64]{0:T(128)}, u32[]{:S(2)}) copy-start(s32[64]{0:T(128)} %param.32) | copy-start | bytes 772
  8.0 427.3 %reduce-scatter.3.cloned.1.call-start = ((), (), s32[]{:S(2)}) async-start(), calls=%async_computation.2 | async-start | bytes 5570560 | tf_op jit(solution)/shard_map/reduce_scatter | solution.py:1061
  13.9 9.6 %copy-start.10 = (bf16[256,512]{1,0:T(8,128)(2,1)S(1)}, bf16[256,512]{1,0:T(8,128)(2,1)}, u32[]{:S(2)}) copy-start(bf16[256,512]{1,0:T(8,128)(2,1)} %param.39) | copy-start | bytes 786436
  13.9 9.6 %copy-start.11 = (bf16[512,256]{1,0:T(8,128)(2,1)S(1)}, bf16[512,256]{1,0:T(8,128)(2,1)}, u32[]{:S(2)}) copy-start(bf16[512,256]{1,0:T(8,128)(2,1)} %param.36) | copy-start | bytes 786436
  13.9 9.6 %copy-start.13 = (bf16[512,128]{1,0:T(8,128)(2,1)S(1)}, bf16[512,128]{1,0:T(8,128)(2,1)}, u32[]{:S(2)}) copy-start(bf16[512,128]{1,0:T(8,128)(2,1)} %param.38) | copy-start | bytes 393220
  14.0 9.6 %copy-start.14 = (bf16[512,128]{1,0:T(8,128)(2,1)S(1)}, bf16[512,128]{1,0:T(8,128)(2,1)}, u32[]{:S(2)}) copy-start(bf16[512,128]{1,0:T(8,128)(2,1)} %param.37) | copy-start | bytes 393220
  14.7 306.6 %copy-start.8 = (bf16[1024,48]{1,0:T(8,128)(2,1)}, bf16[1024,48]{1,0:T(8,128)(2,1)S(1)}, u32[]{:S(2)}) copy-start(bf16[1024,48]{1,0:T(8,128)(2,1)S(1)} %copy.140) | copy-start | bytes 294916
  14.7 9.9 %dynamic-slice-start = ((bf16[128,512]{1,0:T(8,128)(2,1)}, s32[]{:T(128)}, s32[]{:T(128)}), bf16[16,128]{1,0:T(8,128)(2,1)S(1)}, s32[]{:S(2)}) async-start(bf16[128,512]{1,0:T(8,128)(2,1)} %param.49, s32[]{:T(128)} %select_n.59, s32[]{:T(128)} %select_n.61), calls=%async_computation.8 | async-start | bytes 8704 | tf_op jit(solution)/shard_map/dynamic_slice | solution.py:1013
  14.7 9.8 %dynamic-slice-start.1 = ((bf16[128,512]{1,0:T(8,128)(2,1)}, s32[]{:T(128)}, s32[]{:T(128)}), bf16[16,128]{1,0:T(8,128)(2,1)S(1)}, s32[]{:S(2)}) async-start(bf16[128,512]{1,0:T(8,128)(2,1)} %param.47, s32[]{:T(128)} %select_n.59, s32[]{:T(128)} %select_n.61), calls=%async_computation.9 | async-start | bytes 8704 | tf_op jit(solution)/shard_map/dynamic_slice | solution.py:1010
  14.7 9.8 %dynamic-slice-start.2 = ((bf16[128,1024]{1,0:T(8,128)(2,1)}, s32[]{:T(128)}, s32[]{:T(128)}), bf16[16,256]{1,0:T(8,128)(2,1)S(1)}, s32[]{:S(2)}) async-start(bf16[128,1024]{1,0:T(8,128)(2,1)} %param.45, s32[]{:T(128)} %select_n.59, s32[]{:T(128)} %select_n.60), calls=%async_computation.10 | async-start | bytes 16896 | tf_op jit(solution)/shard_map/dynamic_slice | solution.py:1009
  388.0 64.8 %all-reduce.12.cloned.1.call-start = ((), (), s32[]{:S(2)}) async-start(), calls=%async_computation.6 | async-start | bytes 2621440 | tf_op jit(solution)/shard_map/psum | solution.py:1167
  388.6 110.1 %all-gather.3.cloned.1.call-start = ((), (), s32[]{:S(2)}) async-start(), calls=%async_computation.3 | async-start | bytes 2621440 | tf_op jit(solution)/shard_map/all_gather | solution.py:1087
  390.0 49.0 %copy-start.6 = (bf16[256,1024]{1,0:T(8,128)(2,1)S(1)}, bf16[256,1024]{1,0:T(8,128)(2,1)}, u32[]{:S(2)}) copy-start(bf16[256,1024]{1,0:T(8,128)(2,1)} %grads.1) | copy-start | bytes 1572868
  440.1 145.2 %all-gather.5.cloned.1.call-start = ((), (), s32[]{:S(2)}) async-start(), calls=%async_computation.7 | async-start | bytes 3932160 | tf_op jit(solution)/shard_map/all_gather | solution.py:1167
  452.8 186.2 %reduce-scatter.5.cloned.1.call-start = ((), (), s32[]{:S(2)}) async-start(), calls=%async_computation.4 | async-start | bytes 2949120 | tf_op jit(solution)/shard_map/reduce_scatter | solution.py:1095
  562.1 5.6 copy-start.7
  563.7 5.0 collective-permute-start
  565.0 7.4 collective-permute-start.1
  566.4 11.7 %collective-permute-start.2 = (bf16[1024,256]{1,0:T(8,128)(2,1)S(1)}, bf16[1024,256]{1,0:T(8,128)(2,1)S(1)}, u32[]{:S(2)}, u32[]{:S(2)}) collective-permute-start(bf16[1024,256]{1,0:T(8,128)(2,1)S(1)} %get-tuple-element.110), channel_id=1, source_target_pairs={{12,0},{13,1},{14,2},{15,3},{28,16},{29,17},{30,18},{31,19}} | collective-permute-start | bytes 1572872 | tf_op jit(solution)/shard_map/ppermute | solution.py:55
  568.7 9.3 %copy-start.23 = (bf16[1024,256]{1,0:T(8,128)(2,1)}, bf16[1024,256]{1,0:T(8,128)(2,1)S(1)}, u32[]{:S(2)}) copy-start(bf16[1024,256]{1,0:T(8,128)(2,1)S(1)} %collective-permute-done.far1) | copy-start | bytes 1572868
  572.4 5.6 copy-start.24
  585.3 4.5 copy-start.18
  585.3 152.4 %all-reduce.10.cloned.1.call-start = ((), (), s32[]{:S(2)}) async-start(), calls=%async_computation.5 | async-start | bytes 917504 | tf_op jit(solution)/shard_map/psum | solution.py:1144
  589.8 1.5 copy-start.3
  629.9 4.4 copy-start.15
  629.9 9.2 %copy-start.9 = (bf16[1024,48]{1,0:T(8,128)(2,1)S(1)}, bf16[1024,48]{1,0:T(8,128)(2,1)}, u32[]{:S(2)}) copy-start(bf16[1024,48]{1,0:T(8,128)(2,1)} %copy-done.8) | copy-start | bytes 294916
  629.9 9.2 %copy-start.21 = (f32[1024]{0:T(1024)S(1)}, f32[1024]{0:T(1024)}, u32[]{:S(2)}) copy-start(f32[1024]{0:T(1024)} %convert_element_type.96) | copy-start | bytes 12292
  634.3 10.2 %copy-start.5 = (bf16[256,1024]{1,0:T(8,128)(2,1)S(1)}, bf16[256,1024]{1,0:T(8,128)(2,1)}, u32[]{:S(2)}) copy-start(bf16[256,1024]{1,0:T(8,128)(2,1)} %multiply_convert_fusion) | copy-start | bytes 1572868
  639.1 5.4 copy-start.19
  639.1 6.8 copy-start.17
  757.5 4.3 copy-start.1
  (7 other events, 7.5 us)
Sparse Core Ops, SparseCore 0:
  388.1 47.1 reduce-scatter.2
  647.4 90.2 all-reduce.9
Sparse Core Ops, SparseCore 1:
  391.5 61.3 all-reduce.11
  454.9 43.8 all-gather.2
  500.3 39.3 all-gather.4
  585.4 48.0 reduce-scatter.4

commit v3 on v2

--- a/solution.py
+++ b/solution.py
@@ -124,9 +124,9 @@
 def forward_kernel(
     tokens, gain_one, gain_two, shard, first, second, o_first, o_second, cos, sin, codes,
     w_gate, w_up, w_down, grads, routes,
-    att_out, q_out, kv_out, lora_out, middle_out, low_out, weights_out,
+    att_out, q_out, kv_out, lora_out, middle_out, low_out, weights_out, normed_all,
     gate_far, up_far, down_far, grads_all, routes_all, rows_all,
-    normed_all, weights, q_aug, k_aug, v_aug, top, acc, parts, parts_in, rows_own,
+    weights, q_aug, k_aug, v_aug, top, acc, parts, parts_in, rows_own,
     shard_sem, normed_sem, kv_sem, part_sem, far_sem, grads_sem, routes_sem, rows_sem,
     pass_sem, local_sem,
     *, tp_count, ctx_count,
@@ -439,7 +439,7 @@
     return pl.pallas_call(
         functools.partial(forward_kernel, tp_count=tp_count, ctx_count=ctx_count),
         in_specs=[vmem] * 11 + [hbm] * 5,
-        out_specs=[vmem] * 7 + [hbm] * 6,
+        out_specs=[vmem] * 8 + [hbm] * 6,
         out_shape=[
             jax.ShapeDtypeStruct((rows, heads * HEAD), BF16),
             jax.ShapeDtypeStruct((heads, rows, LANES), BF16),
@@ -448,13 +448,13 @@
             jax.ShapeDtypeStruct((block, model), F32),
             jax.ShapeDtypeStruct((block, LANES), BF16),
             jax.ShapeDtypeStruct((2,) + shard.shape, BF16),
+            jax.ShapeDtypeStruct((tp_count, block, model), BF16),
             *[jax.ShapeDtypeStruct(w.shape, BF16) for w in weights],
             jax.ShapeDtypeStruct((ctx_count,) + grads.shape, BF16),
             jax.ShapeDtypeStruct((ctx_count,) + routes.shape, jnp.int32),
             jax.ShapeDtypeStruct((ctx_count, block, model), BF16),
         ],
         scratch_shapes=[
-            pltpu.VMEM((tp_count, block, model), BF16),
             pltpu.VMEM((2,) + shard.shape, BF16),
             pltpu.VMEM((heads, rows, LANES), BF16),
             pltpu.VMEM((pairs, SPAN * rows, LANES), BF16),
@@ -490,246 +490,566 @@
     )
 
 
-def build_tables(rank, kv_refs, k_aug, v_aug):
+def joined(dk, dv, span):
+    pairs = dk.shape[0]
+    return jnp.concatenate(
+        [dk[pair, span, :HEAD] for pair in range(pairs)]
+        + [dv[pair, span, :HEAD] for pair in range(pairs)],
+        axis=1,
+    )
+
+
+def backward_kernel(
+    tokens, upstream_ref, routes, gain_one, gain_two, router, middle_ref, low_ref, weights,
+    normed_all, lora, att, q_ref, kv_ref, first, second, o_first, o_second, cos, sin, back, mixed,
+    output, input_grad, packed_out,
+    k_aug, v_aug, up_aug, dk, dv, dq, branch_all, far_out, far_in, own_kv, parts, parts_in,
+    second_acc, first_acc, o_in_acc, packed, ctx_in, tp_in, middle_grad,
+    back_near, back_mine, back_pair, back_far, mixed_near, mixed_mine, mixed_pair, mixed_far,
+    near_sem, mine_sem, far_sem, branch_sem, kv_sem, part_sem,
+    ctx_sem, tp_sem, x_sem, tp_all_sem, ctx_all_sem,
+    *, tp_count, ctx_count, experts, direct,
+):
+    tp, ctx, fsdp = (lax.axis_index(name) for name in ("tp", "ctx", "fsdp"))
+    rank = lax.rem(ctx, SPAN)
+    block, model = tokens.shape
+    heads, rows_all, _ = q_ref.shape
     pairs = k_aug.shape[0]
-    for distance, kv in enumerate(kv_refs):
-
-        @pl.when(distance <= rank)
-        def _(distance=distance, kv=kv):
-            values = kv[...]
+    group = heads // pairs
+    tall = group * block
+    half = weights.shape[2]
+    q_cols = heads * HEAD
+    kv_cols = pairs * HEAD
+    turn = cos.shape[1]
+    partner = ctx + 1 - 2 * lax.rem(ctx, 2)
+    cross = ring(ctx, 2, ctx_count)
+    cross_partner = ring(partner, 2, ctx_count)
+    other = {"fsdp": 1 - fsdp}
+
+    barrier = pltpu.get_barrier_semaphore()
+    pl.semaphore_signal(barrier, 1, device_id=other, device_id_type=pl.DeviceIdType.MESH)
+    for k in range(1, tp_count):
+        pl.semaphore_signal(
+            barrier, 1, device_id={"tp": ring(tp, k, tp_count)},
+            device_id_type=pl.DeviceIdType.MESH,
+        )
+    for k in range(1, ctx_count):
+        pl.semaphore_signal(
+            barrier, 1, device_id={"ctx": ring(ctx, k, ctx_count)},
+            device_id_type=pl.DeviceIdType.MESH,
+        )
+    pl.semaphore_wait(barrier, tp_count + ctx_count - 1)
+
+    sums = (
+        (back, back_near, back_mine, back_pair, back_far),
+        (mixed, mixed_near, mixed_mine, mixed_pair, mixed_far),
+    )
+
+    def near_copy(n, slot):
+        source, near = sums[n][:2]
+        return remote(
+            source.at[(partner, cross_partner)[slot]], near.at[slot],
+            near_sem.at[0, 2 * n + slot], near_sem.at[1, 2 * n + slot], {"ctx": partner},
+        )
+
+    def mine_copy(n, slot):
+        return pltpu.make_async_copy(
+            sums[n][0].at[(ctx, cross)[slot]], sums[n][2].at[slot], mine_sem.at[2 * n + slot]
+        )
+
+    def pair_copy(n):
+        return remote(sums[n][3], sums[n][4], far_sem.at[0, n], far_sem.at[1, n], {"ctx": cross})
+
+    def start_sum(n):
+        for slot in (1, 0):
+            near_copy(n, slot).start()
+            mine_copy(n, slot).start()
+
+    def pass_sum(n):
+        near_copy(n, 1).wait_recv()
+        mine_copy(n, 1).wait()
+        _, near, mine, pair, _ = sums[n]
+        pair[...] = (near[1].astype(F32) + mine[1].astype(F32)).astype(BF16)
+        pair_copy(n).start()
+
+    def end_sum(n):
+        near_copy(n, 0).wait_recv()
+        mine_copy(n, 0).wait()
+        pair_copy(n).wait_recv()
+        _, near, mine, _, far = sums[n]
+        return near[0].astype(F32) + mine[0].astype(F32) + far[...].astype(F32)
+
+    if direct:
+        start_sum(0)
+        start_sum(1)
+
+    @pl.loop(0, rank + 1)
+    def _(distance):
+        @pl.loop(0, tp_count)
+        def _(part):
+            kv = kv_ref[distance, part]
             for pair in range(pairs):
                 aug_keys(
-                    values, pair, pairs, (rank - distance) * SEGS_DEV, k_aug, v_aug,
-                    distance * values.shape[0],
+                    kv, pair, pairs, (rank - distance) * SEGS_DEV + part * (block // SEG),
+                    k_aug, v_aug, pl.multiple_of(distance * rows_all + part * block, block),
                 )
 
-
-def retrace_kernel(
-    rank_ref, q_ref, kv_ref, att, branch, w_out, out_in, out_out, cos, sin,
-    dq_out, own_out, far_out, in_grad,
-    k_aug, v_aug, dk, dv, dq,
-):
-    step = pl.program_id(0)
-    rank = rank_ref[0]
-    heads, block, _ = q_ref.shape
-    pairs = k_aug.shape[0]
-    group = heads // pairs
-    rows = kv_ref.shape[1]
-    tall = group * block
-    width = heads * HEAD
-
-    @pl.when(step == 0)
-    def _():
-        build_tables(rank, [kv_ref.at[d] for d in range(SPAN)], k_aug, v_aug)
-        dk[...] = jnp.zeros(dk.shape, F32)
-        dv[...] = jnp.zeros(dv.shape, F32)
-        in_grad[...] = jnp.zeros(in_grad.shape, F32)
-
-    half = w_out.shape[2]
-    low_grad = dot_nt(branch[...], out_out[...]).astype(BF16)
-    grads = (
-        dot_nt(branch[:, :half], w_out[0])
-        + dot_nt(branch[:, half:], w_out[1])
-        + dot_nt(low_grad, out_in[...])
-    ).astype(BF16)
-    mixed = att[...]
-    in_grad[...] += dot_tn(mixed, low_grad)
-    product = grads.astype(F32) * mixed.astype(F32)
+    dk[...] = jnp.zeros(dk.shape, F32)
+    dv[...] = jnp.zeros(dv.shape, F32)
+    dq[...] = jnp.zeros(dq.shape, F32)
+    second_acc[...] = jnp.zeros(second_acc.shape, F32)
+    first_acc[...] = jnp.zeros(first_acc.shape, F32)
+    o_in_acc[...] = jnp.zeros(o_in_acc.shape, F32)
+    packed[...] = jnp.zeros(packed.shape, F32)
+
+    middle = middle_ref[...]
+    normed_two = rms_scale(middle, gain_two[...]).astype(BF16)
+    logits = dot(normed_two, router[...])
+    number = iota((block, LANES), 1)
+    hit = jnp.zeros((block, LANES), F32)
+    for k in range(routes.shape[1]):
+        hit += (routes[:, k : k + 1] == number).astype(F32)
+    kept = jnp.where(hit > 0.5, logits, MASKED)
+    gates = jnp.exp(kept - jnp.max(kept, axis=1, keepdims=True)) * hit
+    gates = gates / jnp.sum(gates, axis=1, keepdims=True)
+
+    if direct:
+        pass_sum(0)
+        back_sum = end_sum(0)
+    else:
+        back_sum = back[...].astype(F32)
+    table = back_sum[:, model:]
+    slopes = table + pltpu.roll(table, LANES - experts, 1)
+    logits_grad = gates * (slopes - jnp.sum(gates * slopes, axis=1, keepdims=True))
+    high = logits_grad.astype(BF16)
+    low = (logits_grad - high.astype(F32)).astype(BF16)
+    normed_two_grad = back_sum[:, :model] + dot_nt(high, router[...]) + dot_nt(low, router[...])
+    middle_grad[...] = upstream_ref[...].astype(F32) + rms_back(
+        middle, gain_two[...], normed_two_grad
+    )
+    branch = (RESIDUAL_SCALE * middle_grad[...]).astype(BF16)
+    branch_all[tp] = branch
+
+    def branch_copy(k):
+        return remote(
+            branch_all.at[tp], branch_all.at[tp], branch_sem.at[0, k - 1], branch_sem.at[1, k - 1],
+            {"tp": ring(tp, k, tp_count)},
+        )
+
+    for k in range(1, tp_count):
+        branch_copy(k).start()
+    packed[pl.ds(4 * RANK, RANK), :] = dot_tn(low_ref[...], branch)[:RANK]
+    if direct:
+        pass_sum(1)
+
     wide = heads * LANES
-    r, c = iota((width, wide), 0), iota((width, wide), 1)
+    r, c = iota((q_cols, wide), 0), iota((q_cols, wide), 1)
     same = r // HEAD == c // LANES
     place = (same & (r % HEAD == c % LANES)).astype(BF16)
-    spread = (same & (c % LANES >= ONES) & (c % LANES < ONES + 2)).astype(F32)
-    minus = -lax.dot_general(
-        product, spread, (((1,), (0,)), ((), ())),
-        precision=lax.Precision.HIGHEST, preferred_element_type=F32,
-    )
-    high = minus.astype(BF16).astype(F32)
-    lane = iota(minus.shape, 1) % LANES
-    coded = dot(grads, place) + jnp.where(
-        lane == ONES, high, jnp.where(lane == ONES + 1, minus - high, 0.0)
-    )
-    coded = coded.astype(BF16)
-
-    pieces = []
-    for pair in range(pairs):
-        queries = q_ref[pl.ds(pair * group, group)].reshape(tall, LANES)
-        upstream = jnp.concatenate(
-            [
-                coded[:, (pair * group + member) * LANES : (pair * group + member + 1) * LANES]
-                for member in range(group)
-            ],
-            axis=0,
-        )
-        dq[...] = jnp.zeros(dq.shape, F32)
-
-        def tile(start, size, causal, queries=queries, upstream=upstream, pair=pair):
-            span = pl.ds(start, size)
-            keys = k_aug[pair, span, :]
-            probs = jnp.exp(dot_nt(keys, queries))
-            if causal:
-                q_row = iota(probs.shape, 1) % block
-                probs = jnp.where(iota(probs.shape, 0) <= q_row, probs, 0.0)
-            slopes = (probs * dot_nt(v_aug[pair, span, :], upstream)).astype(BF16)
-            dv[pair, span, :] += dot(probs.astype(BF16), upstream)
-            dk[pair, span, :] += dot(slopes, queries)
-            dq[...] += dot_tn(slopes, keys)
-
-        tile(pl.multiple_of(step * block, block), block, True)
-
-        @pl.loop(0, step)
-        def _(j, tile=tile):
-            tile(pl.multiple_of(j * block, block), block, False)
-
-        for distance in range(1, SPAN):
-
-            @pl.when(distance <= rank)
-            def _(distance=distance, tile=tile):
-                for part in range(0, rows, rows // 2):
-                    tile(distance * rows + part, rows // 2, False)
-
-        for member in range(group):
-            pieces.append(dq[member * block : (member + 1) * block, :HEAD] * SCORE_SCALE)
-
-    for pair in range(pairs):
-        turned = jnp.concatenate(pieces[pair * group : (pair + 1) * group], axis=1)
-        turned = turned * cos[...] - swap_halves(turned) * sin[...]
-        dq_out[:, pl.ds(pair * group * HEAD, group * HEAD)] = turned.astype(BF16)
-
-    @pl.when(step == pl.num_programs(0) - 1)
-    def _():
-        for distance in range(SPAN):
-            span = pl.ds(distance * rows, rows)
-            joined = jnp.concatenate(
-                [dk[pair, span, :HEAD] for pair in range(pairs)]
-                + [dv[pair, span, :HEAD] for pair in range(pairs)],
+    spread = (same & (c % LANES >= ONES) & (c % LANES < ONES + 2)).astype(BF16)
+
+    def tile(part, pair, start, size, causal):
+        index = part * pairs + pair
+        rows = pl.ds(pl.multiple_of(part * block, block), block)
+        queries = q_ref[pl.ds(pair * group, group), rows, :].reshape(tall, LANES)
+        upstream = up_aug[pl.ds(pair * group, group), rows, :].reshape(tall, LANES)
+        span = pl.ds(start, size)
+        keys = k_aug[pair, span, :]
+        probs = jnp.exp(dot_nt(keys, queries))
+        if causal:
+            q_row = iota(probs.shape, 1) % block
+            probs = jnp.where(iota(probs.shape, 0) <= q_row, probs, 0.0)
+        steep = (probs * dot_nt(v_aug[pair, span, :], upstream)).astype(BF16)
+        dv[pair, span, :] += dot(probs.astype(BF16), upstream)
+        dk[pair, span, :] += dot(steep, queries)
+        dq[index] += dot_tn(steep, keys)
+
+    @pl.loop(0, tp_count)
+    def _(k):
+        @pl.when(k > 0)
+        def _():
+            branch_copy(k).wait_recv()
+
+        part = ring(tp, -k, tp_count)
+        rows = pl.ds(pl.multiple_of(part * block, block), block)
+        low_grad = dot_nt(branch_all[part], o_second[...]).astype(BF16)
+        grads = dot_nt(low_grad, o_first[...])
+        for side in range(2):
+            grads += dot_nt(
+                branch_all[part, :, side * half : (side + 1) * half],
+                weights[side, pl.ds(half, q_cols), :],
+            )
+        grads = grads.astype(BF16)
+        mixed_heads = att[rows, :]
+        o_in_acc[...] += dot_tn(low_grad, mixed_heads)
+        product = grads.astype(F32) * mixed_heads.astype(F32)
+        minus = jnp.zeros((block, wide), F32)
+        for _ in range(3):
+            piece = product.astype(BF16)
+            minus -= dot(piece, spread)
+            product -= piece.astype(F32)
+        top = minus.astype(BF16).astype(F32)
+        lane = iota(minus.shape, 1) % LANES
+        coded = dot(grads, place) + jnp.where(
+            lane == ONES, top, jnp.where(lane == ONES + 1, minus - top, 0.0)
+        )
+        for head in range(heads):
+            up_aug[head, rows, :] = coded[:, head * LANES : (head + 1) * LANES].astype(BF16)
+
+        @pl.loop(0, pairs)
+        def _(pair):
+            tile(part, pair, pl.multiple_of(part * block, block), block, True)
+
+            @pl.loop(0, part)
+            def _(j):
+                tile(part, pair, pl.multiple_of(j * block, block), block, False)
+
+    def far_copy(distance):
+        return remote(
+            far_out.at[distance - 1], far_in.at[distance - 1],
+            kv_sem.at[0, distance - 1], kv_sem.at[1, distance - 1],
+            {"ctx": ring(ctx, -distance, ctx_count)},
+        )
+
+    size = min(rows_all, 512)
+
+    @pl.loop(0, rank)
+    def _(step):
+        distance = rank - step
+        start = distance * rows_all
+
+        @pl.loop(0, tp_count * pairs * (rows_all // size))
+        def _(n):
+            index, piece = n // (rows_all // size), lax.rem(n, rows_all // size)
+            tile(
+                index // pairs, lax.rem(index, pairs),
+                pl.multiple_of(start + piece * size, size), size, False,
+            )
+
+        @pl.loop(0, tp_count)
+        def _(part):
+            span = pl.ds(pl.multiple_of(start + part * block, block), block)
+            far_out[distance - 1, pl.ds(pl.multiple_of(part * block, block), block), :] = joined(
+                dk, dv, span
+            ).astype(BF16)
+
+        far_copy(distance).start()
+
+    own_kv[...] = joined(dk, dv, pl.ds(0, rows_all))
+    for distance in range(1, SPAN):
+
+        @pl.when(rank + distance < SPAN)
+        def _(distance=distance):
+            far_copy(distance).wait_recv()
+            own_kv[...] += far_in[distance - 1].astype(F32)
+
+    def part_copy(k):
+        return remote(
+            parts.at[k], parts_in.at[k], part_sem.at[0, k], part_sem.at[1, k],
+            {"tp": ring(tp, k + 1, tp_count)},
+        )
+
+    @pl.loop(0, tp_count)
+    def _(k):
+        part = ring(tp, k + 1, tp_count)
+        rows = pl.ds(pl.multiple_of(part * block, block), block)
+        pieces = []
+        for pair in range(pairs):
+            held = dq[part * pairs + pair]
+            turned = SCORE_SCALE * jnp.concatenate(
+                [held[member * block : (member + 1) * block, :HEAD] for member in range(group)],
                 axis=1,
             )
-            if distance == 0:
-                own_out[...] = joined
-            else:
-                far_out[distance - 1] = joined.astype(BF16)
-
-
-def retrace(rank, queries, kv_parts, att, branch, w_out, out_in, out_out, cos, sin):
+            pieces.append(turned * cos[rows, :] - swap_halves(turned) * sin[rows, :])
+        keys = own_kv[rows, :kv_cols]
+        pieces.append(keys * cos[rows, :] - swap_halves(keys) * sin[rows, :])
+        pieces.append(own_kv[rows, kv_cols:])
+        grads = jnp.concatenate(pieces, axis=1).astype(BF16)
+        for side in range(2):
+            parts[k, :, side * half : (side + 1) * half] = dot_nt(
+                grads, weights[side, pl.ds(0, half), :]
+            ).astype(BF16)
+        low_part = dot_nt(grads, second[...]).astype(BF16)
+        parts[k, :, model:] = low_part
+
+        @pl.when(k < tp_count - 1)
+        def _():
+            part_copy(k).start()
+
+        second_acc[...] += dot_tn(lora[rows, :], grads)
+        first_acc[...] += dot_tn(low_part, normed_all[part])
+
+    packed[pl.ds(0, 3 * RANK), :] = first_acc[pl.ds(0, 3 * RANK), :]
+    lanes = pl.ds(pl.multiple_of(tp * q_cols, q_cols), q_cols)
+    packed[pl.ds(3 * RANK, RANK), lanes] = o_in_acc[pl.ds(0, RANK), :]
+    packed[pl.ds(5 * RANK, RANK), lanes] = second_acc[pl.ds(0, RANK), :q_cols]
+    lanes = pl.ds(pl.multiple_of(tp * kv_cols, kv_cols), kv_cols)
+    packed[pl.ds(6 * RANK, RANK), lanes] = second_acc[pl.ds(RANK, RANK), q_cols : q_cols + kv_cols]
+    lanes = pl.ds(pl.multiple_of(model // 2 + tp * kv_cols, kv_cols), kv_cols)
+    packed[pl.ds(6 * RANK, RANK), lanes] = second_acc[pl.ds(2 * RANK, RANK), q_cols + kv_cols :]
+
+    if direct:
+        tall_rows, few_rows = packed.shape[0] // ctx_count, packed.shape[0] // (ctx_count * tp_count)
+
+        def ctx_rows(index):
+            return pl.ds(pl.multiple_of(index * tall_rows, tall_rows), tall_rows)
+
+        def tp_rows(index):
+            start = ctx * tall_rows + index * few_rows
+            return pl.ds(pl.multiple_of(start, few_rows), few_rows)
+
+        def ctx_copy(k):
+            where = ring(ctx, k, ctx_count)
+            return remote(
+                packed.at[ctx_rows(where)], ctx_in.at[k - 1],
+                ctx_sem.at[0, k - 1], ctx_sem.at[1, k - 1], {"ctx": where},
+            )
+
+        def tp_copy(k):
+            where = ring(tp, k, tp_count)
+            return remote(
+                packed.at[tp_rows(where)], tp_in.at[k - 1],
+                tp_sem.at[0, k - 1], tp_sem.at[1, k - 1], {"tp": where},
+            )
+
+        x_copy = remote(
+            packed_out.at[fsdp, tp_rows(tp)], packed_out.at[fsdp, tp_rows(tp)],
+            x_sem.at[0], x_sem.at[1], other,
+        )
+
+        def tp_all_copy(k):
+            return remote(
+                packed_out.at[:, tp_rows(tp)], packed_out.at[:, tp_rows(tp)],
+                tp_all_sem.at[0, k - 1], tp_all_sem.at[1, k - 1], {"tp": ring(tp, k, tp_count)},
+            )
+
+        def ctx_all_copy(k):
+            return remote(
+                packed_out.at[:, ctx_rows(ctx)], packed_out.at[:, ctx_rows(ctx)],
+                ctx_all_sem.at[0, k - 1], ctx_all_sem.at[1, k - 1],
+                {"ctx": ring(ctx, k, ctx_count)},
+            )
+
+        for k in range(1, ctx_count):
+            ctx_copy(k).start()
+        for k in range(1, ctx_count):
+            ctx_copy(k).wait()
+        packed[ctx_rows(ctx), :] = packed[ctx_rows(ctx), :] + sum(
+            ctx_in[k] for k in range(ctx_count - 1)
+        )
+        for k in range(1, tp_count):
+            tp_copy(k).start()
+        for k in range(1, tp_count):
+            tp_copy(k).wait()
+        packed_out[fsdp, tp_rows(tp), :] = packed[tp_rows(tp), :] + sum(
+            tp_in[k] for k in range(tp_count - 1)
+        )
+        x_copy.start()
+        x_copy.wait()
+        for k in range(1, tp_count):
+            tp_all_copy(k).start()
+        for k in range(1, tp_count):
+            tp_all_copy(k).wait()
+        for k in range(1, ctx_count):
+            ctx_all_copy(k).start()
+    else:
+        packed_out[0] = packed[...]
+
+    summed = parts[tp_count - 1].astype(F32)
+    for k in range(tp_count - 1):
+        part_copy(k).wait_recv()
+        summed += parts_in[k].astype(F32)
+    normed_grad = summed[:, :model] + dot_nt(summed[:, model:].astype(BF16), first[...])
+    inputs = tokens[...].astype(F32)
+    input_grad[...] = (
+        middle_grad[...] + rms_back(inputs, gain_one[...], normed_grad)
+    ).astype(BF16)
+    mixture = end_sum(1) if direct else mixed[...].astype(F32)
+    output[...] = (middle_ref[...] + RESIDUAL_SCALE * mixture).astype(BF16)
+
+    if direct:
+        for k in range(1, ctx_count):
+            ctx_all_copy(k).wait()
+        for n in range(2):
+            for slot in range(2):
+                near_copy(n, slot).wait_send()
+            pair_copy(n).wait_send()
+    for k in range(1, tp_count):
+        branch_copy(k).wait_send()
+    for k in range(tp_count - 1):
+        part_copy(k).wait_send()
+    for distance in range(1, SPAN):
+
+        @pl.when(distance <= rank)
+        def _(distance=distance):
+            far_copy(distance).wait_send()
+
+
+def backward(
+    tokens, upstream, routes, gains, router, middle, low, weights, normed, lora, att, queries, kv,
+    first, second, o_first, o_second, cos, sin, back, mixed, tp_count, ctx_count, experts, direct,
+):
+    block, model = tokens.shape
     heads, rows, _ = queries.shape
-    block = 256
-    kv_width = kv_parts.shape[2]
-    pairs = kv_width // (2 * HEAD)
+    pairs = kv.shape[3] // (2 * HEAD)
     tall = heads // pairs * block
-    width = heads * HEAD
-    whole = lambda i, r: (0, 0)
-    row = lambda i, r: (i, 0)
+    cols = second.shape[1]
+    kv_width = kv.shape[3]
+    vmem = pl.BlockSpec(memory_space=pltpu.VMEM)
+    hbm = pl.BlockSpec(memory_space=pl.ANY)
+    dma = pltpu.SemaphoreType.DMA
+    part = (block, model + LANES)
+    packed = (8 * RANK, model)
+    copies = 2 if direct else 1
+    slim = (8, LANES)
+
+    def buffers(width):
+        shapes = [(2, block, width), (2, block, width), (block, width), (block, width)]
+        return [pltpu.VMEM(shape if direct else slim, BF16) for shape in shapes]
+
     return pl.pallas_call(
-        retrace_kernel,
+        functools.partial(
+            backward_kernel, tp_count=tp_count, ctx_count=ctx_count, experts=experts, direct=direct
+        ),
+        in_specs=[vmem] * 20 + [hbm if direct else vmem] * 2,
+        out_specs=[vmem] * 3,
+        out_shape=[
+            jax.ShapeDtypeStruct((block, model), BF16),
+            jax.ShapeDtypeStruct((block, model), BF16),
+            jax.ShapeDtypeStruct((copies,) + packed, F32),
+        ],
+        scratch_shapes=[
+            pltpu.VMEM((pairs, SPAN * rows, LANES), BF16),
+            pltpu.VMEM((pairs, SPAN * rows, LANES), BF16),
+            pltpu.VMEM((heads, rows, LANES), BF16),
+            pltpu.VMEM((pairs, SPAN * rows, LANES), F32),
+            pltpu.VMEM((pairs, SPAN * rows, LANES), F32),
+            pltpu.VMEM((tp_count * pairs, tall, LANES), F32),
+            pltpu.VMEM((tp_count, block, model), BF16),
+            pltpu.VMEM((SPAN - 1, rows, kv_width), BF16),
+            pltpu.VMEM((SPAN - 1, rows, kv_width), BF16),
+            pltpu.VMEM((rows, kv_width), F32),
+            pltpu.VMEM((tp_count,) + part, BF16),
+            pltpu.VMEM((tp_count - 1,) + part, BF16),
+            pltpu.VMEM((LANES, cols), F32),
+            pltpu.VMEM((LANES, model), F32),
+            pltpu.VMEM((LANES, heads * HEAD), F32),
+            pltpu.VMEM(packed, F32),
+            pltpu.VMEM((ctx_count - 1, packed[0] // ctx_count, model) if direct else slim, F32),
+            pltpu.VMEM((tp_count - 1, 8, model) if direct else slim, F32),
+            pltpu.VMEM((block, model), F32),
+            *buffers(model + LANES),
+            *buffers(model),
+            dma((2, 4)),
+            dma((4,)),
+            dma((2, 2)),
+            dma((2, tp_count - 1)),
+            dma((2, SPAN - 1)),
+            dma((2, tp_count - 1)),
+            dma((2, ctx_count - 1)),
+            dma((2, tp_count - 1)),
+            dma((2,)),
+            dma((2, tp_count - 1)),
+            dma((2, ctx_count - 1)),
+        ],
+        compiler_params=pltpu.CompilerParams(
+            vmem_limit_bytes=60 * 1024 * 1024, collective_id=1, has_side_effects=True
+        ),
+        cost_estimate=pl.CostEstimate(
+            flops=32 * SPAN * rows * rows * heads * LANES,
+            bytes_accessed=32 * 1024 * 1024,
+            transcendentals=0,
+        ),
+        name="backward",
+    )(
+        tokens, upstream, routes, *gains, router, middle, low, weights, normed, lora, att, queries,
+        kv, first, second, o_first, o_second, cos, sin, back, mixed,
+    )
+
+
+def columns_of(chosen):
+    return iota((RANK, LANES), 1) == iota((RANK, LANES), 0) + chosen * RANK
+
+
+def place_kernel(sets, packed, *outs):
+    query_in, query_out, key_in, key_out, value_in, value_out, out_in, out_out = outs
+    kv_cols = key_out.shape[1]
+    exact = dict(precision=lax.Precision.HIGHEST, preferred_element_type=F32)
+
+    def gathered(rows, lanes, turned):
+        total = None
+        for tree in range(packed.shape[0]):
+            spots = columns_of(sets[tree]).astype(F32)
+            piece = packed[tree, rows * RANK : (rows + 1) * RANK, lanes]
+            pair = (piece, spots) if turned else (spots, piece)
+            term = lax.dot_general(*pair, (((0,), (0,)), ((), ())), **exact)
+            total = term if total is None else total + term
+        return total
+
+    whole = slice(None)
+    query_in[...] = gathered(0, whole, True)
+    key_in[...] = gathered(1, whole, True)
+    value_in[...] = gathered(2, whole, True)
+    out_in[...] = gathered(3, whole, True)
+    out_out[...] = gathered(4, whole, False)
+    query_out[...] = gathered(5, whole, False)
+    key_out[...] = gathered(6, slice(0, kv_cols), False)
+    value_out[...] = gathered(6, slice(kv_cols, 2 * kv_cols), False)
+
+
+def place(sets, packed, outs):
+    vmem = pl.BlockSpec(memory_space=pltpu.VMEM)
+    return pl.pallas_call(
+        place_kernel,
+        in_specs=[pl.BlockSpec(memory_space=pltpu.SMEM), vmem],
+        out_specs=[vmem] * len(outs),
+        out_shape=[jax.ShapeDtypeStruct(o.shape, F32) for o in outs],
+        compiler_params=pltpu.CompilerParams(vmem_limit_bytes=VMEM_LIMIT),
+        name="place",
+    )(sets, packed)
+
+
+def place_experts_kernel(sets, part, gate_in, gate_out, up_in, up_out, down_in, down_out):
+    hidden = gate_out.shape[2]
+
+    def gathered(rows, lanes, turned):
+        total = None
+        for tree in range(part.shape[0]):
+            spots = columns_of(sets[tree]).astype(BF16)
+            piece = part[tree, 0, rows * RANK : (rows + 1) * RANK, lanes]
+            term = dot_tn(piece, spots) if turned else dot_tn(spots, piece)
+            total = term if total is None else total + term
+        return total
+
+    whole, left, right = slice(None), slice(0, hidden), slice(hidden, 2 * hidden)
+    gate_in[0] = gathered(0, whole, True)
+    up_in[0] = gathered(1, whole, True)
+    gate_out[0] = gathered(2, left, False)
+    up_out[0] = gathered(2, right, False)
+    down_out[0] = gathered(3, whole, False)
+    down_in[0] = gathered(4, left, True)
+
+
+def place_experts(sets, part, outs):
+    trees, local = part.shape[:2]
+    return pl.pallas_call(
+        place_experts_kernel,
         grid_spec=pltpu.PrefetchScalarGridSpec(
             num_scalar_prefetch=1,
-            grid=(rows // block,),
-            in_specs=[pl.BlockSpec((heads, block, LANES), lambda i, r: (0, i, 0))]
-            + [
-                pl.BlockSpec(kv_parts.shape, lambda i, r: (0, 0, 0)),
-                pl.BlockSpec((block, width), row),
-                pl.BlockSpec((block, branch.shape[1]), row),
-                pl.BlockSpec(w_out.shape, lambda i, r: (0, 0, 0)),
-                pl.BlockSpec(out_in.shape, whole),
-                pl.BlockSpec(out_out.shape, whole),
-                pl.BlockSpec((block, LANES), row),
-                pl.BlockSpec((block, LANES), row),
-            ],
-            out_specs=[
-                pl.BlockSpec((block, width), row),
-                pl.BlockSpec((rows, kv_width), whole),
-                pl.BlockSpec((SPAN - 1, rows, kv_width), lambda i, r: (0, 0, 0)),
-                pl.BlockSpec((width, LANES), whole),
-            ],
-            scratch_shapes=[
-                pltpu.VMEM((pairs, SPAN * rows, LANES), BF16),
-                pltpu.VMEM((pairs, SPAN * rows, LANES), BF16),
-                pltpu.VMEM((pairs, SPAN * rows, LANES), F32),
-                pltpu.VMEM((pairs, SPAN * rows, LANES), F32),
-                pltpu.VMEM((tall, LANES), F32),
-            ],
+            grid=(local,),
+            in_specs=[pl.BlockSpec((trees, 1) + part.shape[2:], lambda e, s: (0, e, 0, 0))],
+            out_specs=[pl.BlockSpec((1,) + o.shape[1:], lambda e, s: (e, 0, 0)) for o in outs],
         ),
-        out_shape=[
-            jax.ShapeDtypeStruct((rows, width), BF16),
-            jax.ShapeDtypeStruct((rows, kv_width), F32),
-            jax.ShapeDtypeStruct((SPAN - 1, rows, kv_width), BF16),
-            jax.ShapeDtypeStruct((width, LANES), F32),
-        ],
+        out_shape=[jax.ShapeDtypeStruct(o.shape, F32) for o in outs],
         compiler_params=pltpu.CompilerParams(vmem_limit_bytes=VMEM_LIMIT),
-        name="retrace",
-        cost_estimate=pl.CostEstimate(
-            flops=16 * SPAN * rows * rows * heads * LANES,
-            bytes_accessed=8 * 1024 * 1024,
-            transcendentals=0,
-        ),
-    )(rank, queries, kv_parts, att, branch, w_out, out_in, out_out, cos, sin)
-
-
-def unproject_kernel(
-    dq, own, far1, far2, far3, lora, weights, second, cos, sin, part_out, grad_out
-):
-    step = pl.program_id(0)
-    total = own[...] + far1[...].astype(F32) + far2[...].astype(F32) + far3[...].astype(F32)
-    split = total.shape[1] // 2
-    keys = total[:, :split]
-    keys = keys * cos[...] - swap_halves(keys) * sin[...]
-    grads = jnp.concatenate(
-        [dq[...], keys.astype(BF16), total[:, split:].astype(BF16)], axis=1
-    )
-    half = weights.shape[1]
-    part_out[:, :half] = dot_nt(grads, weights[0]).astype(BF16)
-    part_out[:, half : 2 * half] = dot_nt(grads, weights[1]).astype(BF16)
-    part_out[:, 2 * half :] = dot_nt(grads, second[...]).astype(BF16)
-
-    @pl.when(step == 0)
-    def _():
-        grad_out[...] = jnp.zeros(grad_out.shape, F32)
-
-    grad_out[...] += dot_tn(lora[...], grads)
-
-
-def unproject(dq, own, fars, lora, weights, second, cos, sin):
-    rows, width = dq.shape
-    kv_width = own.shape[1]
-    block = 256
-    cols = weights.shape[2]
-    model = 2 * weights.shape[1]
-    row = lambda i: (i, 0)
-    return pl.pallas_call(
-        unproject_kernel,
-        grid=(rows // block,),
-        in_specs=[pl.BlockSpec((block, width), row)]
-        + [pl.BlockSpec((block, kv_width), row)] * SPAN
-        + [
-            pl.BlockSpec((block, LANES), row),
-            pl.BlockSpec((2, model // 2, cols), lambda i: (0, 0, 0)),
-            pl.BlockSpec((LANES, cols), lambda i: (0, 0)),
-            pl.BlockSpec((block, LANES), row),
-            pl.BlockSpec((block, LANES), row),
-        ],
-        out_specs=[
-            pl.BlockSpec((block, model + LANES), row),
-            pl.BlockSpec((LANES, cols), lambda i: (0, 0)),
-        ],
-        out_shape=[
-            jax.ShapeDtypeStruct((rows, model + LANES), BF16),
-            jax.ShapeDtypeStruct((LANES, cols), F32),
-        ],
-        compiler_params=pltpu.CompilerParams(vmem_limit_bytes=VMEM_LIMIT),
-        name="unproject",
-        cost_estimate=pl.CostEstimate(
-            flops=2 * rows * model * (cols + 2 * LANES),
-            bytes_accessed=8 * 1024 * 1024,
-            transcendentals=0,
-        ),
-    )(dq, own, *fars, lora, weights, second, cos, sin)
+        name="place_experts",
+    )(sets, part)
 
 
 def expert_kernel(
     sets, base, x_ref, g_ref, routes, router,
     w_gate, w_up, w_down, w_gate_far, w_up_far, w_down_far, gate_in, up_in, gate_out, up_out, down_in, down_out,
-    mixed_out, grad_out,
+    back_out, mixed_out, grad_out,
     rank_rows, gate_rows, slope_rows, mix, back, xs, firsts, tall_grad,
     gate_full, up_full, down_full,
     *, slots, sources,
@@ -844,8 +1164,8 @@
 
     @pl.when(expert == pl.num_programs(1) - 1)
     def _():
-        mixed_out[:, :model] = mix[...].astype(BF16)
-        mixed_out[:, model : 2 * model] = back[...].astype(BF16)
+        mixed_out[...] = mix[...].astype(BF16)
+        back_out[:, :model] = back[...].astype(BF16)
         turned = slope_rows[...].T
         high = turned.astype(BF16)
         low = (turned - high.astype(F32)).astype(BF16)
@@ -853,7 +1173,7 @@
         inside = local < pl.num_programs(1)
         first = (inside & (lane == local + base[0])).astype(BF16)
         later = (inside & (lane == local + base[0] + experts)).astype(BF16)
-        mixed_out[:, 2 * model :] = (dot(high, first) + dot(low, later)).astype(BF16)
+        back_out[:, model:] = (dot(high, first) + dot(low, later)).astype(BF16)
 
 
 def run_experts(
@@ -865,7 +1185,6 @@
     trees = sets.shape[0]
     tokens = total // trees
     lanes = adapters[0].shape[2]
-    cols = 2 * model + LANES
     tall = sources * slots
     piece = lambda c, e, *_: (c, 0)
     fixed = lambda c, e, *_: (0, 0)
@@ -883,7 +1202,8 @@
                 *[pl.BlockSpec((1,) + a.shape[1:], expert) for a in (*weights, *adapters)],
             ],
             out_specs=[
-                pl.BlockSpec((tokens, cols), piece),
+                pl.BlockSpec((tokens, model + LANES), piece),
+                pl.BlockSpec((tokens, model), piece),
                 pl.BlockSpec((1, 1, 5 * RANK, model), lambda c, e, *_: (c, e, 0, 0)),
             ],
             scratch_shapes=[
@@ -901,7 +1221,8 @@
             ],
         ),
         out_shape=[
-            jax.ShapeDtypeStruct((total, cols), BF16),
+            jax.ShapeDtypeStruct((total, model + LANES), BF16),
+            jax.ShapeDtypeStruct((total, model), BF16),
             jax.ShapeDtypeStruct((trees, local, 5 * RANK, model), BF16),
         ],
         compiler_params=pltpu.CompilerParams(vmem_limit_bytes=60 * 1024 * 1024),
@@ -981,10 +1302,8 @@
     reach, depth = tree_links(tree_parents)
     chosen = lax.dynamic_slice_in_dim(adapter_set, tree_index, 1, 0)[0]
 
-    inputs = tokens.astype(F32)
     gain_one = gain_a.astype(F32)
     gain_two = gain_b.astype(F32)
-    normed = rms_scale(inputs, gain_one).astype(BF16)
 
     own_reach = lax.dynamic_slice_in_dim(reach, local_start, SEGS_DEV, 0)
     codes = jnp.pad(
@@ -1030,23 +1349,19 @@
 
     (
         attended, queries, kv_parts, lora, middle, o_reduced, attention_weights,
-        *far_weights, upstream_all, routes_all, rows_all,
+        normed_all, *far_weights, upstream_all, routes_all, rows_all,
     ) = forward(
         tokens, (gain_one[None], gain_two[None]), attention_shard, first, second,
         o_first, o_second, cos, sin, codes, (w_gate, w_up, w_down), out_grad, routes.T,
         tp_count, ctx_count,
     )
-    kv_parts = kv_parts.reshape(SPAN, -1, kv_parts.shape[-1])
-    project_weights = attention_weights[:, : w_query.shape[0]]
-    output_weights = attention_weights[:, w_query.shape[0] :]
     upstream_all = upstream_all.reshape(-1, model)
     rows_all = rows_all.reshape(-1, model)
     routes_all = routes_all.transpose(1, 0, 2).reshape(TOP, -1)
-    normed_two = rms_scale(middle, gain_two).astype(BF16)
 
     tree_sets = lax.dynamic_slice_in_dim(adapter_set, fsdp_rank * trees, trees, 0)
     base = jnp.stack([ctx_rank * local_experts, fsdp_rank]).astype(jnp.int32)
-    mixed, expert_part = run_experts(
+    back, mixed, expert_part = run_experts(
         tree_sets,
         base,
         rows_all,
@@ -1058,136 +1373,38 @@
         slots,
         SPAN,
     )
-    combined = lax.psum_scatter(mixed, "ctx", scatter_dimension=0, tiled=True).astype(F32)
-    mixture = combined[:, :model]
-    output = (middle + RESIDUAL_SCALE * mixture).astype(BF16)
-
-    logits = jnp.dot(normed_two, w_router, preferred_element_type=F32)
-    hits = jnp.sum(
-        (routes[:, :, None] == jnp.arange(experts, dtype=jnp.int32)[None, None, :]).astype(F32),
-        axis=1,
-    )
-    kept = jnp.where(hits > 0.5, logits, MASKED)
-    gates = jnp.exp(kept - jnp.max(kept, axis=1, keepdims=True)) * hits
-    gates = gates / jnp.sum(gates, axis=1, keepdims=True)
-    slopes = (
-        combined[:, 2 * model : 2 * model + experts]
-        + combined[:, 2 * model + experts : 2 * model + 2 * experts]
-    )
-    logits_grad = gates * (slopes - jnp.sum(gates * slopes, axis=1, keepdims=True))
-    normed_two_grad = combined[:, model : 2 * model] + jnp.einsum(
-        "te,de->td", logits_grad, w_router.astype(F32), precision=lax.Precision.HIGHEST
-    )
-    upstream = out_grad.astype(F32)
-    middle_grad = upstream + rms_back(middle, gain_two, normed_two_grad)
-    branch_grad = (RESIDUAL_SCALE * middle_grad).astype(BF16)
-    out_out_part = jnp.einsum(
-        "ts,td->sd", o_reduced, branch_grad, preferred_element_type=F32
-    )[:RANK]
-    branch_all = lax.all_gather(branch_grad, "tp", axis=0, tiled=True)
-    dq, own_grad, far_grad, out_in_part = retrace(
-        rank, queries, kv_parts, attended, branch_all, output_weights, o_first, o_second, cos, sin
-    )
-    fars = [shifted(far_grad[d - 1], "ctx", -d) for d in range(1, SPAN)]
-    part, second_part = unproject(
-        dq, own_grad, fars, lora, project_weights, second, cos, sin
-    )
-    summed = lax.psum_scatter(part, "tp", scatter_dimension=0, tiled=True)
-    reduced_grad = summed[:, model:]
-    normed_grad = summed[:, :model].astype(F32) + jnp.einsum(
-        "ts,ds->td", reduced_grad, first, preferred_element_type=F32
-    )
-    first_part = jnp.einsum(
-        "ts,td->sd", reduced_grad, normed, preferred_element_type=F32
-    )[: 3 * RANK]
-    input_grad = (middle_grad + rms_back(inputs, gain_one, normed_grad)).astype(BF16)
-
-    full_q = q_cols * tp_count
-    full_kv = kv_cols * tp_count
-
-    def widen(part, cols, axis, start):
-        shape = list(part.shape)
-        shape[axis] = cols
-        return lax.dynamic_update_slice_in_dim(jnp.zeros(shape, F32), part, start, axis)
-
-    packed = jnp.concatenate(
-        [
-            first_part,
-            widen(out_in_part[:, :RANK].T, full_q, 1, tp_rank * q_cols),
-            out_out_part,
-            widen(second_part[:RANK, :q_cols], full_q, 1, tp_rank * q_cols),
-            jnp.concatenate(
-                [
-                    widen(
-                        second_part[RANK : 2 * RANK, q_cols : q_cols + kv_cols],
-                        full_kv, 1, tp_rank * kv_cols,
-                    ),
-                    widen(
-                        second_part[2 * RANK : 3 * RANK, q_cols + kv_cols :],
-                        full_kv, 1, tp_rank * kv_cols,
-                    ),
-                ],
-                axis=1,
-            ),
-        ],
-        axis=0,
+    direct = ctx_count == SPAN
+    if direct:
+        back = back.reshape(ctx_count, tok_rows, -1)
+        mixed = mixed.reshape(ctx_count, tok_rows, -1)
+    else:
+        back = lax.psum_scatter(back, "ctx", scatter_dimension=0, tiled=True)
+        mixed = lax.psum_scatter(mixed, "ctx", scatter_dimension=0, tiled=True)
+    output, input_grad, packed = backward(
+        tokens, out_grad, routes, (gain_one[None], gain_two[None]),
+        jnp.pad(w_router, ((0, 0), (0, LANES - experts))), middle, o_reduced, attention_weights,
+        normed_all, lora, attended, queries, kv_parts, first, second, o_first, o_second,
+        cos, sin, back, mixed, tp_count, ctx_count, experts, direct,
     )
     all_trees = fsdp_count * trees
-    if trees > 1:
-        packed = lax.psum(
-            jnp.where(
-                (jnp.arange(all_trees) == tree_index)[:, None, None], packed[None], 0.0
-            ),
-            ("fsdp", "ctx", "tp"),
-        )
-    else:
-        packed = lax.all_gather(lax.psum(packed, ("ctx", "tp")), "fsdp")
-    place = (
-        adapter_set[:, None] == jnp.arange(sets, dtype=jnp.int32)[None, :]
-    ).astype(F32)
-
-    def in_rows(part):
-        spread = jnp.einsum("ts,trd->srd", place, part, precision=lax.Precision.HIGHEST)
-        return spread.reshape(sets * RANK, part.shape[2])
-
-    def in_columns(part):
-        return in_rows(part).T
-
-    adapter_totals = (
-        in_columns(packed[:, :RANK]),
-        in_rows(packed[:, 5 * RANK : 6 * RANK]),
-        in_columns(packed[:, RANK : 2 * RANK]),
-        in_rows(packed[:, 6 * RANK :, :full_kv]),
-        in_columns(packed[:, 2 * RANK : 3 * RANK]),
-        in_rows(packed[:, 6 * RANK :, full_kv:]),
-        in_columns(packed[:, 3 * RANK : 4 * RANK]),
-        in_rows(packed[:, 4 * RANK : 5 * RANK]),
+    if not direct:
+        mine = (jnp.arange(all_trees, dtype=jnp.int32) == tree_index)[:, None, None]
+        packed = lax.psum(jnp.where(mine, packed, 0.0), ("fsdp", "ctx", "tp"))
+    adapter_totals = place(
+        adapter_set,
+        packed,
+        (
+            query_in, query_out, key_in, key_second_factor, value_in, value_second_factor,
+            out_in, out_out,
+        ),
     )
 
     expert_part = lax.all_gather(lax.psum(expert_part, "tp"), "fsdp")
     expert_part = expert_part.reshape(all_trees, local_experts, 5 * RANK, model)
-    hidden = w_gate.shape[2]
-
-    def expert_rows(part):
-        spread = jnp.einsum(
-            "ts,terd->esrd", place.astype(BF16), part, preferred_element_type=F32
-        )
-        return spread.reshape(local_experts, sets * RANK, part.shape[3])
-
-    def expert_columns(part):
-        return expert_rows(part).transpose(0, 2, 1)
-
-    return (
-        output,
-        input_grad,
-        *adapter_totals,
-        expert_columns(expert_part[:, :, :RANK]),
-        expert_rows(expert_part[:, :, 2 * RANK : 3 * RANK, :hidden]),
-        expert_columns(expert_part[:, :, RANK : 2 * RANK]),
-        expert_rows(expert_part[:, :, 2 * RANK : 3 * RANK, hidden:]),
-        expert_columns(expert_part[:, :, 4 * RANK :, :hidden]),
-        expert_rows(expert_part[:, :, 3 * RANK : 4 * RANK]),
-    )
+    expert_totals = place_experts(
+        adapter_set, expert_part, (gate_in, gate_out, up_in, up_out, down_in, down_out)
+    )
+    return (output, input_grad, *adapter_totals, *expert_totals)
 
 
 def solution(mesh):

time: 780 us -> 679 us (0.87)
  Pallas kernels: 432 us -> 575 us
  waiting for transfers between devices: 199 us -> 59.8 us
  local copies, waits for them, and re-layouts: 70 us -> 12.4 us
  matrix products: 20.8 us -> 0.79 us
  blocking collectives: 10.9 us -> 0 us
    pallas_call x2 -> x3, Pallas kernels: 69.7 us -> 212 us  [the longest x1 193 us: backward(): pl.pallas_call(functools.partial(backward_kernel, tp_count=tp_count, ctx_...]
    psum x1 -> x0, waiting for transfers between devices: 87.1 us -> none  [per_device(): packed = lax.all_gather(lax.psum(packed, ('ctx', 'tp')), 'fsdp')]
    psum x1, waiting for transfers between devices: 10.7 us -> 59.8 us  [per_device(): expert_part = lax.all_gather(lax.psum(expert_part, 'tp'), 'fsdp')]
    all_gather x1 -> x0, waiting for transfers between devices: 45.9 us -> none  [per_device(): branch_all = lax.all_gather(branch_grad, 'tp', axis=0, tiled=True)]
    reduce_scatter x2 -> x0, waiting for transfers between devices: 45.3 us -> none  [the longest x1 45.3 us: per_device(): lax.psum_scatter(mixed, 'ctx', scatter_dimension=0, tiled=True).astype(F32)]
    transpose x8 -> x0, local copies, waits for them, and re-layouts: 21.4 us -> none  [the longest x6 20.7 us: expert_rows(): jnp.einsum('ts,terd->esrd', place.astype(BF16), part, preferred_element_t...]
    dot_general x19 -> x0, matrix products: 20 us -> none  [the longest x6 9.34 us: expert_rows(): jnp.einsum('ts,terd->esrd', place.astype(BF16), part, preferred_element_t...]
    unnamed x66 -> x27, local copies, waits for them, and re-layouts: 22.4 us -> 2.95 us
  transfers between devices with their start and end apart: 9 -> 2, of which waited for: 6 -> 1; matrix products, arithmetic and copies ran while one was open for 8% -> 0% of each run, Pallas kernels for 9% -> 30%
where the time goes in v3:
time: 679 us; the launch traced here: 671 us
  Pallas kernels  575 us (85%)
  waiting for transfers between devices  59.8 us (9%)
  between operations  15 us (2%)
  local copies, waits for them, and re-layouts  12.4 us (2%)
  other arithmetic  8.03 us (1%)
    pallas_call x1, Pallas kernels, forward(): pl.pallas_call(functools.partial(forward_kernel, tp_count=tp_count, ctx_c...  296 us
    pallas_call x1, Pallas kernels, backward(): pl.pallas_call(functools.partial(backward_kernel, tp_count=tp_count, ctx_...  193 us
    pallas_call x1, Pallas kernels, run_experts(): pl.pallas_call(functools.partial(expert_kernel, slots=slots, sources=sour...  66.7 us
    psum x1, waiting for transfers between devices, per_device(): expert_part = lax.all_gather(lax.psum(expert_part, 'tp'), 'fsdp')  59.8 us
  transfers between devices with their start and end apart: 2, of which 1 were waited for; matrix products, arithmetic and copies ran while one was open for 0% of the time, Pallas kernels for 30%

profile of v3, /device:TPU:13, one launch (start us, length us, event | category | flops | bytes accessed | tf_op | source)
XLA Modules:
  0.0 671.0 jit_solution(5835028746601220449)
XLA Ops:
  7.3 1.3 fusion.23
  9.4 1.3 broadcast_in_dim.40
  10.7 1.3 broadcast_in_dim.41
  11.9 0.7 dynamic_slice.48
  12.7 0.3 fusion.1
  13.0 0.2 fusion.3
  13.2 0.2 fusion.24
  13.6 0.9 dynamic_slice.46
  14.6 0.6 pad.38.o_first
  15.2 0.7 pad.39.o_second
  16.0 1.1 constant_dynamic-slice_fusion.3
  17.3 1.3 constant_dynamic-slice_fusion.1
  18.7 0.1 copy.54
  18.9 0.2 copy.51
  19.0 0.8 pad.34.first
  19.8 0.6 pad_add_fusion.base
  20.5 3.0 multiply_sine_fusion
  23.6 0.7 fusion.12.second
  24.3 0.9 pad_maximum_fusion.shard
  25.3 0.7 broadcast_in_dim.39
  26.0 295.9 %forward.1 = (bf16[1024,256]{1,0:T(8,128)(2,1)}, bf16[4,1024,128]{2,1,0:T(8,128)(2,1)}, bf16[4,4,256,256]{3,2,1,0:T(8,128)(2,1)}, bf16[1024,128]{1,0:T(8,128)(2,...) custom-call(bf16[256,1024]{1,0:T(8,128)(2,1)} %tokens.3, ...), custom_call_target="tpu_custom_call" | custom-call | flops 34359738368 | bytes 33554432 | tf_op jit(solution)/shard_map/forward/pallas_call | solution.py:439
  321.9 66.7 %experts.1 = (bf16[1024,1152]{1,0:T(8,128)(2,1)}, bf16[1024,1024]{1,0:T(8,128)(2,1)}, bf16[1,8,80,1024]{3,2,1,0:T(8,128)(2,1)}) custom-call(s32[1]{0:T(128)} %get-tuple-element.86.sets, s32[2]{0:T(128)} %pad_add_fusion.base, bf16[1024,1024]{1,0:T(8,128)(2,1)} %bitcast.35, bf16[1024,1024]{1,0:T(8,128)(2,1)} %bitcast.34, s32[8,1024]{1,0:T(8,128)} %bitcast.36, ...), custom_call_target="tpu_custom_call" | custom-call | flops 34359738368 | bytes 8388608 | tf_op jit(solution)/shard_map/experts/pallas_call | solution.py:1192
  388.7 0.3 all-gather.2.cloned.1.call-start
  389.0 0.8 copy.52.routes
  389.8 0.2 copy.47
  389.9 0.8 pad.33.router
  390.7 59.8 %all-reduce.10.cloned.1.call-done = bf16[1,1,8,80,1024]{4,3,2,1,0:T(8,128)(2,1)} async-done(((bf16[1,1,8,80,1024]{4,3,2,1,0:T(8,128)(2,1)}), bf16[1,1,8,80,1024]{4,3,2,1,0:T(8,128)(2,1)}) %all-reduce.10.cloned.1.call-update) | async-done | bytes 1310736 | tf_op jit(solution)/shard_map/psum | solution.py:1402
  450.5 192.6 %backward.1 = (bf16[256,1024]{1,0:T(8,128)(2,1)}, bf16[256,1024]{1,0:T(8,128)(2,1)}, f32[2,128,1024]{2,1,0:T(8,128)}) custom-call(bf16[256,1024]{1,0:T(8,128)(2,1)} %tokens.3, bf16[256,1024]{1,0:T(8,128)(2,1)} %upstream_ref.1, s32[256,8]{1,0:T(8,128)} %copy.52.routes, f32[1,1024]{1,0:T(1,128)} %bitcast.29, f32[1,1024]{1,0:T(1,128)} %bitcast.31, ...), custom_call_target="tpu_custom_call" | custom-call | flops 68719476736 | bytes 33554432 | tf_op jit(solution)/shard_map/backward/pallas_call | solution.py:910
  643.1 8.3 %place.1 = (f32[1024,128]{1,0:T(8,128)}, f32[128,1024]{1,0:T(8,128)}, f32[1024,128]{1,0:T(8,128)}, f32[128,512]{1,0:T(8,128)}, f32[1024,128]{1,0:T(8,128)}, /*in...) custom-call(s32[2]{0:T(128)} %sets.3, f32[2,128,1024]{2,1,0:T(8,128)} %get-tuple-element.68.packed), custom_call_target="tpu_custom_call" | custom-call | tf_op jit(solution)/shard_map/place/pallas_call | solution.py:1002
  651.5 11.1 %place_experts.1 = (f32[8,1024,128]{2,1,0:T(8,128)}, f32[8,128,512]{2,1,0:T(8,128)}, f32[8,1024,128]{2,1,0:T(8,128)}, f32[8,128,512]{2,1,0:T(8,128)}, f32[8,512,128]{2,1,0:T(8,128)}, /*index=5*/f32[8,128,1024]{2,1,0:T(8,128)}) custom-call(s32[2]{0:T(128)} %sets.3, bf16[2,8,80,1024]{3,2,1,0:T(8,128)(2,1)} %bitcast.23), custom_call_target="tpu_custom_call" | custom-call | tf_op jit(solution)/shard_map/place_experts/pallas_call | solution.py:1035
  662.6 0.8 copy.59
  663.4 0.8 copy.60
  (45 shorter events, 0.8 us)
Async XLA Ops:
  7.2 6.4 copy-start
  7.2 443.3 %all-reduce.10.cloned.1.call-start = ((), (), s32[]{:S(2)}) async-start(), calls=%async_computation | async-start | bytes 2621440 | tf_op jit(solution)/shard_map/psum | solution.py:1402
  17.1 6.5 dynamic-slice-start
  17.1 6.5 dynamic-slice-start.1
  17.1 6.5 dynamic-slice-start.2
  17.1 7.2 %copy-start.4 = (bf16[256,512]{1,0:T(8,128)(2,1)S(1)}, bf16[256,512]{1,0:T(8,128)(2,1)}, u32[]{:S(2)}) copy-start(bf16[256,512]{1,0:T(8,128)(2,1)} %param.39) | copy-start | bytes 786436
  17.1 7.2 %copy-start.5 = (bf16[512,256]{1,0:T(8,128)(2,1)S(1)}, bf16[512,256]{1,0:T(8,128)(2,1)}, u32[]{:S(2)}) copy-start(bf16[512,256]{1,0:T(8,128)(2,1)} %param.36) | copy-start | bytes 786436
  17.1 7.2 %copy-start.6 = (bf16[512,128]{1,0:T(8,128)(2,1)S(1)}, bf16[512,128]{1,0:T(8,128)(2,1)}, u32[]{:S(2)}) copy-start(bf16[512,128]{1,0:T(8,128)(2,1)} %param.38) | copy-start | bytes 393220
  17.2 7.2 %copy-start.7 = (bf16[512,128]{1,0:T(8,128)(2,1)S(1)}, bf16[512,128]{1,0:T(8,128)(2,1)}, u32[]{:S(2)}) copy-start(bf16[512,128]{1,0:T(8,128)(2,1)} %param.37) | copy-start | bytes 393220
  321.9 67.1 %copy-start.9 = (s32[256,8]{0,1:T(8,128)S(1)}, s32[256,8]{0,1:T(8,128)}, u32[]{:S(2)}) copy-start(s32[256,8]{0,1:T(8,128)} %param.31) | copy-start | bytes 24580
  321.9 67.9 %copy-start.8 = (bf16[1024,32]{0,1:T(8,128)(2,1)S(1)}, bf16[1024,32]{0,1:T(8,128)(2,1)}, u32[]{:S(2)}) copy-start(bf16[1024,32]{0,1:T(8,128)(2,1)} %param.40) | copy-start | bytes 196612
  388.7 262.8 %all-gather.2.cloned.1.call-start = ((), (), s32[]{:S(2)}) async-start(), calls=%async_computation.1 | async-start | bytes 3932160 | tf_op jit(solution)/shard_map/all_gather | solution.py:1402
  643.1 19.5 %copy-start.3 = (bf16[256,1024]{1,0:T(8,128)(2,1)S(1)}, bf16[256,1024]{1,0:T(8,128)(2,1)}, u32[]{:S(2)}) copy-start(bf16[256,1024]{1,0:T(8,128)(2,1)} %get-tuple-element.108) | copy-start | bytes 1572868
  651.4 12.0 %copy-start.2 = (bf16[256,1024]{1,0:T(8,128)(2,1)S(1)}, bf16[256,1024]{1,0:T(8,128)(2,1)}, u32[]{:S(2)}) copy-start(bf16[256,1024]{1,0:T(8,128)(2,1)} %get-tuple-element.109) | copy-start | bytes 1572868
  651.5 12.8 %copy-start.1 = (bf16[128,1024]{1,0:T(8,128)(2,1)S(1)}, bf16[128,1024]{1,0:T(8,128)(2,1)}, u32[]{:S(2)}) copy-start(bf16[128,1024]{1,0:T(8,128)(2,1)} %param.51) | copy-start | bytes 786436
Sparse Core Ops, SparseCore 0:
  388.8 61.6 all-reduce.9
  452.0 39.0 all-gather.1

commit v4 on v3

--- a/solution.py
+++ b/solution.py
@@ -93,6 +93,12 @@
     return ((r - source == c - target) & (c >= target) & (c < target + HEAD)).astype(BF16)
 
 
+def transfer_plan(local, tp_count):
+    if local == 8 and tp_count % 2 == 0:
+        return 5, 1, 1, 1
+    return 0, local, 0, 0
+
+
 def remote(src, dst, send, recv, where):
     return pltpu.make_async_remote_copy(
         src_ref=src,
@@ -102,6 +108,35 @@
         device_id=where,
         device_id_type=pl.DeviceIdType.MESH,
     )
+
+
+def far_moves(near, far, sems, pass_sems, shared, direct, first, land, other, tp):
+    mate = {"tp": tp + 1 - 2 * lax.rem(tp, 2)}
+    side = lax.rem(tp, 2)
+
+    def piece(ref, rows, which):
+        return ref.at[pl.ds(pl.multiple_of(which * rows, rows), rows)]
+
+    def cross(n):
+        moves = []
+        for a, (source, target) in enumerate(zip(near, far)):
+            src, dst = source.at[first + n], target.at[land + n]
+            if n < shared:
+                rows = src.shape[0] // 2
+                src, dst = piece(src, rows, side), piece(dst, rows, side)
+            moves.append(remote(src, dst, sems.at[0, n, a], sems.at[1, n, a], other))
+        return moves
+
+    def hand_on(n):
+        moves = []
+        for a, target in enumerate(far):
+            dst = target.at[land + n]
+            rows = dst.shape[0] // 2
+            dst = piece(dst, rows, side)
+            moves.append(remote(dst, dst, pass_sems.at[0, n, a], pass_sems.at[1, n, a], mate))
+        return moves
+
+    return cross, hand_on
 
 
 def ring(me, step, count):
@@ -127,9 +162,9 @@
     att_out, q_out, kv_out, lora_out, middle_out, low_out, weights_out, normed_all,
     gate_far, up_far, down_far, grads_all, routes_all, rows_all,
     weights, q_aug, k_aug, v_aug, top, acc, parts, parts_in, rows_own,
-    shard_sem, normed_sem, kv_sem, part_sem, far_sem, grads_sem, routes_sem, rows_sem,
+    shard_sem, normed_sem, kv_sem, part_sem, far_sem, pass_far_sem, grads_sem, routes_sem, rows_sem,
     pass_sem, local_sem,
-    *, tp_count, ctx_count,
+    *, tp_count, ctx_count, shared, straight,
 ):
     tp, ctx, fsdp = (lax.axis_index(name) for name in ("tp", "ctx", "fsdp"))
     rank = lax.rem(ctx, SPAN)
@@ -194,12 +229,21 @@
 
     weights[fsdp] = shard[...]
     shard_copy.wait()
-    far_copies = [
-        remote(near, far, far_sem.at[0, n], far_sem.at[1, n], other)
-        for n, (near, far) in enumerate(((w_gate, gate_far), (w_up, up_far), (w_down, down_far)))
-    ]
-    for copy in far_copies:
-        copy.start()
+    cross, hand_on = far_moves(
+        (w_gate, w_up, w_down), (gate_far, up_far, down_far), far_sem, pass_far_sem,
+        shared, straight, 0, 0, other, tp,
+    )
+    for n in range(shared + straight):
+        for copy in cross(n):
+            copy.start()
+
+    def relay(n):
+        if n < shared:
+            for copy in cross(n):
+                copy.wait_recv()
+            for copy in hand_on(n):
+                copy.start()
+
     weights_out[...] = weights[...]
 
     def kv_copy(distance, part):
@@ -249,6 +293,8 @@
                 kv, pair, pairs, rank * SEGS_DEV + part * (block // SEG), k_aug, v_aug,
                 pl.multiple_of(part * block, block),
             )
+
+    relay(0)
 
     def tile(part, pair, start, size, causal):
         index = part * pairs + pair
@@ -278,6 +324,7 @@
         def _(j):
             tile(part, pair, pl.multiple_of(j * block, block), block, False)
 
+    relay(1)
     group_rows = tp_count * block
     for distance in range(1, SPAN):
 
@@ -357,6 +404,12 @@
         def _():
             part_copy(k).start()
 
+        for n in range(2, shared):
+
+            @pl.when(k == n - 1)
+            def _(n=n):
+                relay(n)
+
     summed = parts[tp_count - 1].astype(F32)
     for k in range(tp_count - 1):
         part_copy(k).wait_recv()
@@ -416,8 +469,14 @@
     for k in range(1, chips):
         rows_copy(k).wait_send()
         pass_copy(k).wait()
-    for copy in far_copies:
-        copy.wait()
+    for n in range(shared + straight):
+        for copy in cross(n):
+            copy.wait_send()
+            if n >= shared:
+                copy.wait_recv()
+    for n in range(shared):
+        for copy in hand_on(n):
+            copy.wait()
 
 
 def forward(
@@ -432,12 +491,15 @@
     pairs = kv_cols // (2 * HEAD)
     tall = heads // pairs * block
     chips = ctx_count // 2
+    shared, straight, _, _ = transfer_plan(weights[0].shape[0], tp_count)
     vmem = pl.BlockSpec(memory_space=pltpu.VMEM)
     hbm = pl.BlockSpec(memory_space=pl.ANY)
     dma = pltpu.SemaphoreType.DMA
     part = (block, model + LANES)
     return pl.pallas_call(
-        functools.partial(forward_kernel, tp_count=tp_count, ctx_count=ctx_count),
+        functools.partial(
+            forward_kernel, tp_count=tp_count, ctx_count=ctx_count, shared=shared, straight=straight
+        ),
         in_specs=[vmem] * 11 + [hbm] * 5,
         out_specs=[vmem] * 8 + [hbm] * 6,
         out_shape=[
@@ -449,7 +511,7 @@
             jax.ShapeDtypeStruct((block, LANES), BF16),
             jax.ShapeDtypeStruct((2,) + shard.shape, BF16),
             jax.ShapeDtypeStruct((tp_count, block, model), BF16),
-            *[jax.ShapeDtypeStruct(w.shape, BF16) for w in weights],
+            *[jax.ShapeDtypeStruct((shared + straight,) + w.shape[1:], BF16) for w in weights],
             jax.ShapeDtypeStruct((ctx_count,) + grads.shape, BF16),
             jax.ShapeDtypeStruct((ctx_count,) + routes.shape, jnp.int32),
             jax.ShapeDtypeStruct((ctx_count, block, model), BF16),
@@ -468,7 +530,8 @@
             dma((2, tp_count - 1)),
             dma((2, SPAN - 1)),
             dma((2, tp_count - 1)),
-            dma((2, 3)),
+            dma((2, shared + straight, 3)),
+            dma((2, max(shared, 1), 3)),
             dma((2, ctx_count)),
             dma((2, ctx_count)),
             dma((2, chips)),
@@ -501,13 +564,13 @@
 
 def backward_kernel(
     tokens, upstream_ref, routes, gain_one, gain_two, router, middle_ref, low_ref, weights,
-    normed_all, lora, att, q_ref, kv_ref, first, second, o_first, o_second, cos, sin, back, mixed,
-    output, input_grad, packed_out,
+    normed_all, lora, att, q_ref, kv_ref, first, second, o_first, o_second, cos, sin, back, mixed, shares,
+    output, input_grad, packed_out, shares_out,
     k_aug, v_aug, up_aug, dk, dv, dq, branch_all, far_out, far_in, own_kv, parts, parts_in,
     second_acc, first_acc, o_in_acc, packed, ctx_in, tp_in, middle_grad,
     back_near, back_mine, back_pair, back_far, mixed_near, mixed_mine, mixed_pair, mixed_far,
     near_sem, mine_sem, far_sem, branch_sem, kv_sem, part_sem,
-    ctx_sem, tp_sem, x_sem, tp_all_sem, ctx_all_sem,
+    ctx_sem, tp_sem, x_sem, tp_all_sem, ctx_all_sem, share_sem, swap_sem, own_sem,
     *, tp_count, ctx_count, experts, direct,
 ):
     tp, ctx, fsdp = (lax.axis_index(name) for name in ("tp", "ctx", "fsdp"))
@@ -580,8 +643,25 @@
         return near[0].astype(F32) + mine[0].astype(F32) + far[...].astype(F32)
 
     if direct:
+        share = shares.shape[2]
+        own_lanes = pl.ds(pl.multiple_of(tp * share, share), share)
+
+        def share_copy(k):
+            return remote(
+                shares, shares_out.at[fsdp, :, :, own_lanes],
+                share_sem.at[0, k - 1], share_sem.at[1, k - 1], {"tp": ring(tp, k, tp_count)},
+            )
+
+        share_own = pltpu.make_async_copy(shares, shares_out.at[fsdp, :, :, own_lanes], own_sem.at[0])
+        swap = remote(
+            shares_out.at[fsdp], shares_out.at[fsdp], swap_sem.at[0], swap_sem.at[1], other
+        )
+
         start_sum(0)
         start_sum(1)
+        share_own.start()
+        for k in range(1, tp_count):
+            share_copy(k).start()
 
     @pl.loop(0, rank + 1)
     def _(distance):
@@ -735,6 +815,12 @@
 
         far_copy(distance).start()
 
+    if direct:
+        share_own.wait()
+        for k in range(1, tp_count):
+            share_copy(k).wait()
+        swap.start()
+
     own_kv[...] = joined(dk, dv, pl.ds(0, rows_all))
     for distance in range(1, SPAN):
 
@@ -868,6 +954,7 @@
     output[...] = (middle_ref[...] + RESIDUAL_SCALE * mixture).astype(BF16)
 
     if direct:
+        swap.wait()
         for k in range(1, ctx_count):
             ctx_all_copy(k).wait()
         for n in range(2):
@@ -887,7 +974,7 @@
 
 def backward(
     tokens, upstream, routes, gains, router, middle, low, weights, normed, lora, att, queries, kv,
-    first, second, o_first, o_second, cos, sin, back, mixed, tp_count, ctx_count, experts, direct,
+    first, second, o_first, o_second, cos, sin, back, mixed, shares, tp_count, ctx_count, experts, direct,
 ):
     block, model = tokens.shape
     heads, rows, _ = queries.shape
@@ -911,12 +998,15 @@
         functools.partial(
             backward_kernel, tp_count=tp_count, ctx_count=ctx_count, experts=experts, direct=direct
         ),
-        in_specs=[vmem] * 20 + [hbm if direct else vmem] * 2,
-        out_specs=[vmem] * 3,
+        in_specs=[vmem] * 20 + [hbm if direct else vmem] * 2 + [hbm],
+        out_specs=[vmem] * 3 + [hbm],
         out_shape=[
             jax.ShapeDtypeStruct((block, model), BF16),
             jax.ShapeDtypeStruct((block, model), BF16),
             jax.ShapeDtypeStruct((copies,) + packed, F32),
+            jax.ShapeDtypeStruct(
+                (2,) + shares.shape[:2] + (tp_count * shares.shape[2],) if direct else slim, BF16
+            ),
         ],
         scratch_shapes=[
             pltpu.VMEM((pairs, SPAN * rows, LANES), BF16),
@@ -951,6 +1041,9 @@
             dma((2,)),
             dma((2, tp_count - 1)),
             dma((2, ctx_count - 1)),
+            dma((2, tp_count - 1)),
+            dma((2,)),
+            dma((1,)),
         ],
         compiler_params=pltpu.CompilerParams(
             vmem_limit_bytes=60 * 1024 * 1024, collective_id=1, has_side_effects=True
@@ -963,7 +1056,7 @@
         name="backward",
     )(
         tokens, upstream, routes, *gains, router, middle, low, weights, normed, lora, att, queries,
-        kv, first, second, o_first, o_second, cos, sin, back, mixed,
+        kv, first, second, o_first, o_second, cos, sin, back, mixed, shares,
     )
 
 
@@ -1047,14 +1140,58 @@
 
 
 def expert_kernel(
-    sets, base, x_ref, g_ref, routes, router,
-    w_gate, w_up, w_down, w_gate_far, w_up_far, w_down_far, gate_in, up_in, gate_out, up_out, down_in, down_out,
+    sets, x_ref, g_ref, routes, router,
+    w_gate, w_up, w_down, w_gate_far, w_up_far, w_down_far, all_gate, all_up, all_down, gate_in, up_in, gate_out, up_out, down_in, down_out,
     back_out, mixed_out, grad_out,
     rank_rows, gate_rows, slope_rows, mix, back, xs, firsts, tall_grad,
-    gate_full, up_full, down_full,
-    *, slots, sources,
+    gate_full, up_full, down_full, land_gate, land_up, land_down, grads, grads_in,
+    far_sem, pass_far_sem, grads_sem, arrive_sem,
+    *, slots, sources, early, shared, straight, tp_count,
 ):
     chunk, expert = pl.program_id(0), pl.program_id(1)
+    tp, fsdp = lax.axis_index("tp"), lax.axis_index("fsdp")
+    late = shared + straight
+    gather = late > 0
+    other = {"fsdp": 1 - fsdp}
+    cross, hand_on = far_moves(
+        (all_gate, all_up, all_down), (land_gate, land_up, land_down), far_sem, pass_far_sem,
+        shared, straight, early, 0, other, tp,
+    )
+
+    if gather:
+
+        @pl.when(expert == 0)
+        def _():
+            barrier = pltpu.get_barrier_semaphore()
+            pl.semaphore_signal(
+                barrier, 1, device_id=other, device_id_type=pl.DeviceIdType.MESH
+            )
+            for k in range(1, tp_count):
+                pl.semaphore_signal(
+                    barrier, 1, device_id={"tp": ring(tp, k, tp_count)},
+                    device_id_type=pl.DeviceIdType.MESH,
+                )
+            pl.semaphore_wait(barrier, tp_count)
+            for n in range(late):
+                for copy in cross(n):
+                    copy.start()
+
+        for n in range(shared):
+
+            @pl.when(expert == 2 + n)
+            def _(n=n):
+                for copy in cross(n):
+                    copy.wait_recv()
+                for copy in hand_on(n):
+                    copy.start()
+
+        for n in range(late):
+
+            @pl.when(expert == early + n)
+            def _(n=n):
+                for copy in hand_on(n) if n < shared else cross(n):
+                    copy.wait_recv()
+
     experts = router.shape[0]
     tokens, model = x_ref.shape
     each = tokens // sources
@@ -1081,7 +1218,8 @@
         back[...] = jnp.zeros(back.shape, F32)
         slope_rows[...] = jnp.zeros(slope_rows.shape, F32)
 
-    row = base[0] + expert
+    first_row = lax.axis_index("ctx") * pl.num_programs(1)
+    row = first_row + expert
     ranks = rank_rows[pl.ds(row, 1), :]
     gates = gate_rows[pl.ds(row, 1), :]
     slot_number = iota((slots, each), 0).astype(F32)
@@ -1102,14 +1240,25 @@
     keep = (iota((1, 2 * lanes), 1) % lanes // RANK == chosen).astype(BF16)
     rows = xs[...]
     inner = dot(rows, firsts[...]).astype(BF16) * keep
-    for full, near, far in (
-        (gate_full, w_gate, w_gate_far),
-        (up_full, w_up, w_up_far),
-        (down_full, w_down, w_down_far),
+    for full, near, far, landed in (
+        (gate_full, w_gate, w_gate_far, land_gate),
+        (up_full, w_up, w_up_far, land_up),
+        (down_full, w_down, w_down_far, land_down),
     ):
         size = near.shape[1]
-        full[pl.ds(pl.multiple_of(base[1] * size, size), size), :] = near[0]
-        full[pl.ds(pl.multiple_of((1 - base[1]) * size, size), size), :] = far[0]
+        full[pl.ds(pl.multiple_of(fsdp * size, size), size), :] = near[0]
+        spot = pl.ds(pl.multiple_of((1 - fsdp) * size, size), size)
+        if not gather:
+            full[spot, :] = far[0]
+            continue
+
+        @pl.when(expert < early)
+        def _(full=full, far=far, spot=spot):
+            full[spot, :] = far[0]
+
+        @pl.when(expert >= early)
+        def _(full=full, landed=landed, spot=spot):
+            full[spot, :] = landed[jnp.maximum(expert - early, 0)]
     gate_value = dot(rows, gate_full[...]) + dot(inner[:, :lanes], gate_out[0])
     up_value = dot(rows, up_full[...]) + dot(inner[:, lanes:], up_out[0])
     sigmoid = 1.0 / (1.0 + jnp.exp(-gate_value))
@@ -1149,18 +1298,61 @@
             jnp.where(picks[s] > 0.5, slope[span, :], 0.0), axis=0, keepdims=True
         )
 
-    own = pl.multiple_of(chosen * RANK, RANK)
+    keep_at = expert if gather else 0
+
+    def folded(start, width):
+        total = tall_grad[pl.ds(start, RANK), :width]
+        for shift in range(RANK, lanes, RANK):
+            total += tall_grad[pl.ds(start + shift, RANK), :width]
+        return total.astype(BF16)
+
     tall_grad[...] = dot_tn(inner_grad, rows)
-    grad_out[0, 0, pl.ds(0, RANK), :] = tall_grad[pl.ds(own, RANK), :].astype(BF16)
-    grad_out[0, 0, pl.ds(RANK, RANK), :] = tall_grad[pl.ds(lanes + own, RANK), :].astype(BF16)
+    grads[keep_at, pl.ds(0, RANK), :] = folded(0, model)
+    grads[keep_at, pl.ds(RANK, RANK), :] = folded(lanes, model)
     tall_grad[pl.ds(0, lanes), :hidden] = dot_tn(inner[:, :lanes], gate_grad)
     tall_grad[pl.ds(0, lanes), hidden:] = dot_tn(inner[:, lanes:], up_grad)
-    grad_out[0, 0, pl.ds(2 * RANK, RANK), :] = tall_grad[pl.ds(own, RANK), :].astype(BF16)
+    grads[keep_at, pl.ds(2 * RANK, RANK), :] = folded(0, model)
     tall_grad[pl.ds(0, lanes), :] = dot_tn(down_inner, slot_grad)
-    grad_out[0, 0, pl.ds(3 * RANK, RANK), :] = tall_grad[pl.ds(own, RANK), :].astype(BF16)
+    grads[keep_at, pl.ds(3 * RANK, RANK), :] = folded(0, model)
     tall_grad[pl.ds(0, lanes), :hidden] = dot_tn(down_inner_grad, active)
-    tall_grad[pl.ds(0, lanes), hidden:] = jnp.zeros((lanes, model - hidden), F32)
-    grad_out[0, 0, pl.ds(4 * RANK, RANK), :] = tall_grad[pl.ds(own, RANK), :].astype(BF16)
+    grads[keep_at, pl.ds(4 * RANK, RANK), :hidden] = folded(0, hidden)
+    grads[keep_at, pl.ds(4 * RANK, RANK), hidden:] = jnp.zeros((RANK, model - hidden), BF16)
+
+    share = tall_grad.shape[1] // tp_count
+
+    def grads_copy(n, k):
+        where = ring(tp, k, tp_count)
+        lanes = pl.ds(pl.multiple_of(where * share, share), share)
+        return remote(
+            grads.at[n, :, lanes], grads_in.at[k - 1, n], grads_sem.at[k - 1, n],
+            arrive_sem.at[k - 1, n], {"tp": where},
+        )
+
+    if gather:
+        for k in range(1, tp_count):
+            grads_copy(expert, k).start()
+    else:
+        grad_out[0, 0] = grads[0]
+
+    if gather:
+
+        @pl.when(expert == pl.num_programs(1) - 1)
+        def _():
+            for n in range(late):
+                for copy in cross(n):
+                    copy.wait_send()
+            for n in range(shared):
+                for copy in hand_on(n):
+                    copy.wait_send()
+
+            @pl.loop(0, pl.num_programs(1))
+            def _(n):
+                lanes = pl.ds(pl.multiple_of(tp * share, share), share)
+                total = grads[n, :, lanes].astype(F32)
+                for k in range(1, tp_count):
+                    grads_copy(n, k).wait()
+                    total += grads_in[k - 1, n].astype(F32)
+                grad_out[n] = total.astype(BF16)
 
     @pl.when(expert == pl.num_programs(1) - 1)
     def _():
@@ -1171,13 +1363,13 @@
         low = (turned - high.astype(F32)).astype(BF16)
         local, lane = iota((LANES, LANES), 0), iota((LANES, LANES), 1)
         inside = local < pl.num_programs(1)
-        first = (inside & (lane == local + base[0])).astype(BF16)
-        later = (inside & (lane == local + base[0] + experts)).astype(BF16)
+        first = (inside & (lane == local + first_row)).astype(BF16)
+        later = (inside & (lane == local + first_row + experts)).astype(BF16)
         back_out[:, model:] = (dot(high, first) + dot(low, later)).astype(BF16)
 
 
 def run_experts(
-    sets, base, rows, upstream, routes, router, weights, adapters, slots, sources
+    sets, rows, upstream, routes, router, weights, far, adapters, slots, sources, tp_count
 ):
     total, model = rows.shape
     experts = router.shape[0]
@@ -1189,22 +1381,42 @@
     piece = lambda c, e, *_: (c, 0)
     fixed = lambda c, e, *_: (0, 0)
     expert = lambda c, e, *_: (e, 0, 0)
+    pairs, singles, shared, straight = transfer_plan(local, tp_count)
+    early, late = pairs + singles, shared + straight
+    arrived = lambda c, e, *_: (jnp.minimum(e, early - 1), 0, 0)
+    hbm = pl.BlockSpec(memory_space=pl.ANY)
+    dma = pltpu.SemaphoreType.DMA
+    share = (local, 5 * RANK, model // tp_count)
+    gradients = (
+        (share, pl.BlockSpec(share, lambda c, e, *_: (0, 0, 0)))
+        if late
+        else (
+            (trees, local, 5 * RANK, model),
+            pl.BlockSpec((1, 1, 5 * RANK, model), lambda c, e, *_: (c, e, 0, 0)),
+        )
+    )
     return pl.pallas_call(
-        functools.partial(expert_kernel, slots=slots, sources=sources),
+        functools.partial(
+            expert_kernel, slots=slots, sources=sources, early=early, shared=shared,
+            straight=straight, tp_count=tp_count,
+        ),
         grid_spec=pltpu.PrefetchScalarGridSpec(
-            num_scalar_prefetch=2,
+            num_scalar_prefetch=1,
             grid=(trees, local),
             in_specs=[
                 pl.BlockSpec((tokens, model), piece),
                 pl.BlockSpec((tokens, model), piece),
                 pl.BlockSpec((routes.shape[0], tokens), lambda c, e, *_: (0, c)),
                 pl.BlockSpec(router.shape, fixed),
-                *[pl.BlockSpec((1,) + a.shape[1:], expert) for a in (*weights, *adapters)],
+                *[pl.BlockSpec((1,) + w.shape[1:], expert) for w in weights],
+                *[pl.BlockSpec((1,) + w.shape[1:], arrived) for w in weights],
+                *[hbm] * len(weights),
+                *[pl.BlockSpec((1,) + a.shape[1:], expert) for a in adapters],
             ],
             out_specs=[
                 pl.BlockSpec((tokens, model + LANES), piece),
                 pl.BlockSpec((tokens, model), piece),
-                pl.BlockSpec((1, 1, 5 * RANK, model), lambda c, e, *_: (c, e, 0, 0)),
+                gradients[1],
             ],
             scratch_shapes=[
                 pltpu.VMEM((experts, tokens), F32),
@@ -1218,21 +1430,34 @@
                 pltpu.VMEM((2 * half, hidden), BF16),
                 pltpu.VMEM((2 * half, hidden), BF16),
                 pltpu.VMEM((hidden, model), BF16),
+                *[pltpu.VMEM((max(late, 1),) + w.shape[1:], BF16) for w in weights],
+                pltpu.VMEM((local if late else 1, 5 * RANK, model), BF16),
+                pltpu.VMEM((tp_count - 1,) + (share if late else (1, 16, LANES)), BF16),
+                dma((2, max(late, 1), 3)),
+                dma((2, max(shared, 1), 3)),
+                dma((tp_count - 1, local)),
+                dma((tp_count - 1, local)),
             ],
         ),
         out_shape=[
             jax.ShapeDtypeStruct((total, model + LANES), BF16),
             jax.ShapeDtypeStruct((total, model), BF16),
-            jax.ShapeDtypeStruct((trees, local, 5 * RANK, model), BF16),
+            jax.ShapeDtypeStruct(gradients[0], BF16),
         ],
-        compiler_params=pltpu.CompilerParams(vmem_limit_bytes=60 * 1024 * 1024),
+        compiler_params=(
+            pltpu.CompilerParams(
+                vmem_limit_bytes=60 * 1024 * 1024, collective_id=2, has_side_effects=True
+            )
+            if late
+            else pltpu.CompilerParams(vmem_limit_bytes=60 * 1024 * 1024)
+        ),
         name="experts",
         cost_estimate=pl.CostEstimate(
             flops=2 * local * total * model * model * 2,
             bytes_accessed=8 * 1024 * 1024,
             transcendentals=0,
         ),
-    )(sets, base, rows, upstream, routes, router, *weights, *adapters)
+    )(sets, rows, upstream, routes, router, *weights, *far, *weights, *adapters)
 
 
 def take_set(table, chosen, axis):
@@ -1360,18 +1585,18 @@
     routes_all = routes_all.transpose(1, 0, 2).reshape(TOP, -1)
 
     tree_sets = lax.dynamic_slice_in_dim(adapter_set, fsdp_rank * trees, trees, 0)
-    base = jnp.stack([ctx_rank * local_experts, fsdp_rank]).astype(jnp.int32)
     back, mixed, expert_part = run_experts(
         tree_sets,
-        base,
         rows_all,
         upstream_all,
         routes_all,
         w_router.T,
-        (w_gate, w_up, w_down, *far_weights),
+        (w_gate, w_up, w_down),
+        far_weights,
         (gate_in, up_in, gate_out, up_out, down_in, down_out),
         slots,
         SPAN,
+        tp_count,
     )
     direct = ctx_count == SPAN
     if direct:
@@ -1380,11 +1605,11 @@
     else:
         back = lax.psum_scatter(back, "ctx", scatter_dimension=0, tiled=True)
         mixed = lax.psum_scatter(mixed, "ctx", scatter_dimension=0, tiled=True)
-    output, input_grad, packed = backward(
+    output, input_grad, packed, all_shares = backward(
         tokens, out_grad, routes, (gain_one[None], gain_two[None]),
         jnp.pad(w_router, ((0, 0), (0, LANES - experts))), middle, o_reduced, attention_weights,
         normed_all, lora, attended, queries, kv_parts, first, second, o_first, o_second,
-        cos, sin, back, mixed, tp_count, ctx_count, experts, direct,
+        cos, sin, back, mixed, expert_part, tp_count, ctx_count, experts, direct,
     )
     all_trees = fsdp_count * trees
     if not direct:
@@ -1399,8 +1624,11 @@
         ),
     )
 
-    expert_part = lax.all_gather(lax.psum(expert_part, "tp"), "fsdp")
-    expert_part = expert_part.reshape(all_trees, local_experts, 5 * RANK, model)
+    if direct:
+        expert_part = all_shares
+    else:
+        expert_part = lax.all_gather(lax.psum(expert_part, "tp"), "fsdp")
+        expert_part = expert_part.reshape(all_trees, local_experts, 5 * RANK, model)
     expert_totals = place_experts(
         adapter_set, expert_part, (gate_in, gate_out, up_in, up_out, down_in, down_out)
     )

time: 679 us -> 508 us (0.75)
  Pallas kernels: 575 us -> 477 us
  waiting for transfers between devices: 59.8 us -> 0 us
  between operations: 15 us -> 1.54 us
    pallas_call x1, Pallas kernels: 296 us -> 177 us  [forward(): pl.pallas_call(functools.partial(forward_kernel, tp_count=tp_count, ctx_c...]
    psum x1 -> x0, waiting for transfers between devices: 59.8 us -> none  [per_device(): expert_part = lax.all_gather(lax.psum(expert_part, 'tp'), 'fsdp')]
    pallas_call x1, Pallas kernels: 66.7 us -> 80 us  [run_experts(): pl.pallas_call(functools.partial(expert_kernel, slots=slots, sources=sour...]
    pallas_call x1, Pallas kernels: 193 us -> 201 us  [backward(): pl.pallas_call(functools.partial(backward_kernel, tp_count=tp_count, ctx_...]
  transfers between devices with their start and end apart: 2 -> 0, of which waited for: 1 -> 0; matrix products, arithmetic and copies ran while one was open for 0% -> 0% of each run, Pallas kernels for 30% -> 0%
where the time goes in v4:
time: 508 us; the launch traced here: 499 us
  Pallas kernels  477 us (94%)
  local copies, waits for them, and re-layouts  13.6 us (3%)
  other arithmetic  6.1 us (1%)
    pallas_call x1, Pallas kernels, backward(): pl.pallas_call(functools.partial(backward_kernel, tp_count=tp_count, ctx_...  201 us
    pallas_call x1, Pallas kernels, forward(): pl.pallas_call(functools.partial(forward_kernel, tp_count=tp_count, ctx_c...  177 us
    pallas_call x1, Pallas kernels, run_experts(): pl.pallas_call(functools.partial(expert_kernel, slots=slots, sources=sour...  80 us
    pallas_call x1, Pallas kernels, place_experts(): pl.pallas_call(place_experts_kernel, grid_spec=pltpu.PrefetchScalarGridSp...  11.1 us

profile of v4, /device:TPU:13, one launch (start us, length us, event | category | flops | bytes accessed | tf_op | source)
XLA Modules:
  0.0 498.9 jit_solution(5738008172387342567)
XLA Ops:
  0.7 1.3 fusion.23
  2.7 0.7 dynamic_slice.43
  3.4 0.7 dynamic_slice.44
  4.1 0.7 dynamic_slice.45
  4.8 0.7 fusion.12.second
  5.6 1.2 constant_dynamic-slice_fusion.1
  6.8 0.1 copy.54
  7.1 0.1 constant_dynamic-slice_fusion.3
  7.4 0.2 copy.51
  7.6 0.8 pad.34.first
  8.4 0.3 fusion.1
  8.7 0.2 fusion.3
  9.0 0.2 fusion.24
  9.5 3.0 multiply_sine_fusion
  12.5 0.8 constant_dynamic-slice_fusion
  13.3 0.7 pad.39.o_second
  14.0 0.9 dynamic_slice.46
  14.9 0.6 pad.38.o_first
  15.7 0.7 broadcast_in_dim.39
  16.4 0.6 broadcast_in_dim.40
  17.0 0.6 broadcast_in_dim.41
  17.6 0.9 pad_maximum_fusion.shard
  18.6 176.9 %forward.1 = (bf16[1024,256]{1,0:T(8,128)(2,1)}, bf16[4,1024,128]{2,1,0:T(8,128)(2,1)}, bf16[4,4,256,256]{3,2,1,0:T(8,128)(2,1)}, bf16[1024,128]{1,0:T(8,128)(2,...) custom-call(bf16[256,1024]{1,0:T(8,128)(2,1)} %tokens.3, ...), custom_call_target="tpu_custom_call" | custom-call | flops 34359738368 | bytes 33554432 | tf_op jit(solution)/shard_map/forward/pallas_call | solution.py:499
  195.5 80.0 %experts.1 = (bf16[1024,1152]{1,0:T(8,128)(2,1)}, bf16[1024,1024]{1,0:T(8,128)(2,1)}, bf16[8,80,256]{2,1,0:T(8,128)(2,1)}) custom-call(s32[1]{0:T(128)} %get-tuple-element.88.sets, bf16[1024,1024]{1,0:T(8,128)(2,1)} %bitcast.29, bf16[1024,1024]{1,0:T(8,128)(2,1)} %bitcast.28, s32[8,1024]{1,0:T(8,128)} %bitcast.30, bf16[32,1024]{1,0:T(8,128)(2,1)} %bitcast.20, ...), custom_call_target="tpu_custom_call" | custom-call | flops 34359738368 | bytes 8388608 | tf_op jit(solution)/shard_map/experts/pallas_call | solution.py:1398
  275.5 0.2 copy.47
  275.7 0.8 pad.33.router
  276.5 0.8 copy.52.routes
  277.3 200.5 %backward.1 = (bf16[256,1024]{1,0:T(8,128)(2,1)}, bf16[256,1024]{1,0:T(8,128)(2,1)}, f32[2,128,1024]{2,1,0:T(8,128)}, bf16[2,8,80,1024]{3,2,1,0:T(8,128)(2,1)}) custom-call(bf16[256,1024]{1,0:T(8,128)(2,1)} %tokens.3, bf16[256,1024]{1,0:T(8,128)(2,1)} %upstream_ref.1, s32[256,8]{1,0:T(8,128)} %copy.52.routes, f32[1,1024]{1,0:T(1,128)} %bitcast.23, ...), custom_call_target="tpu_custom_call" | custom-call | flops 68719476736 | bytes 33554432 | tf_op jit(solution)/shard_map/backward/pallas_call | solution.py:997
  477.9 11.1 %place_experts.1 = (f32[8,1024,128]{2,1,0:T(8,128)}, f32[8,128,512]{2,1,0:T(8,128)}, f32[8,1024,128]{2,1,0:T(8,128)}, f32[8,128,512]{2,1,0:T(8,128)}, f32[8,512,128]{2,1,0:T(8,128)}, /*index=5*/f32[8,128,1024]{2,1,0:T(8,128)}) custom-call(s32[2]{0:T(128)} %sets.3, bf16[2,8,80,1024]{3,2,1,0:T(8,128)(2,1)} %get-tuple-element.79.part), custom_call_target="tpu_custom_call" | custom-call | tf_op jit(solution)/shard_map/place_experts/pallas_call | solution.py:1128
  489.0 8.3 %place.1 = (f32[1024,128]{1,0:T(8,128)}, f32[128,1024]{1,0:T(8,128)}, f32[1024,128]{1,0:T(8,128)}, f32[128,512]{1,0:T(8,128)}, f32[1024,128]{1,0:T(8,128)}, /*in...) custom-call(s32[2]{0:T(128)} %sets.3, f32[2,128,1024]{2,1,0:T(8,128)} %get-tuple-element.70.packed), custom_call_target="tpu_custom_call" | custom-call | tf_op jit(solution)/shard_map/place/pallas_call | solution.py:1095
  497.3 0.8 copy.58
  498.1 0.8 copy.59
  (41 shorter events, 0.8 us)
Async XLA Ops:
  0.6 6.5 %copy-start = (bf16[1024,128]{1,0:T(8,128)(2,1)S(1)}, bf16[1024,128]{1,0:T(8,128)(2,1)}, u32[]{:S(2)}) copy-start(bf16[1024,128]{1,0:T(8,128)(2,1)} %param.44) | copy-start | bytes 786436
  0.7 7.7 %copy-start.12 = (s32[64]{0:T(128)S(1)}, s32[64]{0:T(128)}, u32[]{:S(2)}) copy-start(s32[64]{0:T(128)} %param.32) | copy-start | bytes 772
  6.9 9.5 %copy-start.10 = (bf16[1024]{0:T(1024)(128)(2,1)S(1)}, bf16[1024]{0:T(1024)(128)(2,1)}, u32[]{:S(2)}) copy-start(bf16[1024]{0:T(1024)(128)(2,1)} %param.34) | copy-start | bytes 6148
  6.9 10.1 %copy-start.11 = (bf16[1024]{0:T(1024)(128)(2,1)S(1)}, bf16[1024]{0:T(1024)(128)(2,1)}, u32[]{:S(2)}) copy-start(bf16[1024]{0:T(1024)(128)(2,1)} %param.35) | copy-start | bytes 6148
  7.0 10.7 %copy-start.4 = (bf16[256,512]{1,0:T(8,128)(2,1)S(1)}, bf16[256,512]{1,0:T(8,128)(2,1)}, u32[]{:S(2)}) copy-start(bf16[256,512]{1,0:T(8,128)(2,1)} %param.39) | copy-start | bytes 786436
  7.0 10.6 %copy-start.5 = (bf16[512,256]{1,0:T(8,128)(2,1)S(1)}, bf16[512,256]{1,0:T(8,128)(2,1)}, u32[]{:S(2)}) copy-start(bf16[512,256]{1,0:T(8,128)(2,1)} %param.36) | copy-start | bytes 786436
  7.0 10.6 %copy-start.6 = (bf16[512,128]{1,0:T(8,128)(2,1)S(1)}, bf16[512,128]{1,0:T(8,128)(2,1)}, u32[]{:S(2)}) copy-start(bf16[512,128]{1,0:T(8,128)(2,1)} %param.38) | copy-start | bytes 393220
  7.0 10.6 %copy-start.7 = (bf16[512,128]{1,0:T(8,128)(2,1)S(1)}, bf16[512,128]{1,0:T(8,128)(2,1)}, u32[]{:S(2)}) copy-start(bf16[512,128]{1,0:T(8,128)(2,1)} %param.37) | copy-start | bytes 393220
  195.5 80.1 %copy-start.8 = (bf16[1024,32]{0,1:T(8,128)(2,1)S(1)}, bf16[1024,32]{0,1:T(8,128)(2,1)}, u32[]{:S(2)}) copy-start(bf16[1024,32]{0,1:T(8,128)(2,1)} %param.40) | copy-start | bytes 196612
  195.5 81.0 %copy-start.9 = (s32[256,8]{0,1:T(8,128)S(1)}, s32[256,8]{0,1:T(8,128)}, u32[]{:S(2)}) copy-start(s32[256,8]{0,1:T(8,128)} %param.31) | copy-start | bytes 24580
  477.8 19.5 %copy-start.3 = (bf16[256,1024]{1,0:T(8,128)(2,1)S(1)}, bf16[256,1024]{1,0:T(8,128)(2,1)}, u32[]{:S(2)}) copy-start(bf16[256,1024]{1,0:T(8,128)(2,1)} %get-tuple-element.110) | copy-start | bytes 1572868
  477.8 20.3 %copy-start.2 = (bf16[256,1024]{1,0:T(8,128)(2,1)S(1)}, bf16[256,1024]{1,0:T(8,128)(2,1)}, u32[]{:S(2)}) copy-start(bf16[256,1024]{1,0:T(8,128)(2,1)} %get-tuple-element.111) | copy-start | bytes 1572868
  477.8 21.0 %copy-start.1 = (bf16[1024,128]{1,0:T(8,128)(2,1)S(1)}, bf16[1024,128]{1,0:T(8,128)(2,1)}, u32[]{:S(2)}) copy-start(bf16[1024,128]{1,0:T(8,128)(2,1)} %param.44) | copy-start | bytes 786436

commit v5 on v4

--- a/solution.py
+++ b/solution.py
@@ -95,8 +95,12 @@
 
 def transfer_plan(local, tp_count):
     if local == 8 and tp_count % 2 == 0:
-        return 5, 1, 1, 1
+        return 3, 2, 2, 1
     return 0, local, 0, 0
+
+
+BEGIN = {"start": (0, 1), "proj": (2,), "own": (3,), "k1": (4,), 0: (0,), 2: (1,), 4: (2,)}
+RELAY = {"proj": (0,), "sum": (1, 2), 2: (0,), 4: (1,)}
 
 
 def remote(src, dst, send, recv, where):
@@ -137,6 +141,56 @@
         return moves
 
     return cross, hand_on
+
+
+class Line:
+    def __init__(self, buffer, sems, me, count):
+        self.buffer, self.sems, self.me, self.count = buffer, sems, me, count
+        self.turns = 2 * count - 1
+
+    def move(self, way, block):
+        where = ring(self.me, 1 if way == 0 else -1, self.count)
+        return remote(
+            self.buffer.at[block], self.buffer.at[block],
+            self.sems.at[way, 0, block], self.sems.at[way, 1, block], {"tp": where},
+        )
+
+    def goes(self, way):
+        return self.me < self.count - 1 if way == 0 else self.me > 0
+
+    def send(self, way, block):
+        @pl.when(self.goes(way))
+        def _():
+            self.move(way, block).start()
+
+    def start(self):
+        self.send(0, self.me)
+        self.send(1, self.me)
+
+    def block(self, turn):
+        step = (turn + 1) // 2
+        block = jnp.where(lax.rem(turn, 2) == 1, self.me - step, self.me + step)
+        valid = (block >= 0) & (block < self.count)
+        return jnp.clip(block, 0, self.count - 1), valid
+
+    def last(self):
+        return jnp.maximum(2 * self.me - 1, 2 * (self.count - 1 - self.me))
+
+    def arrive(self, turn, block):
+        for way, odd in ((0, 1), (1, 0)):
+
+            @pl.when((turn > 0) & (lax.rem(turn, 2) == odd))
+            def _(way=way):
+                self.move(way, block).wait_recv()
+                self.send(way, block)
+
+    def end(self):
+        for block in range(self.count):
+            for way, owned in ((0, block <= self.me), (1, block >= self.me)):
+
+                @pl.when(owned & self.goes(way))
+                def _(way=way):
+                    self.move(way, block).wait_send()
 
 
 def ring(me, step, count):
@@ -201,14 +255,8 @@
     normed = rms_scale(inputs, gain_one[...]).astype(BF16)
     normed_all[tp] = normed
 
-    def normed_copy(k):
-        return remote(
-            normed_all.at[tp], normed_all.at[tp], normed_sem.at[0, k - 1], normed_sem.at[1, k - 1],
-            {"tp": ring(tp, k, tp_count)},
-        )
-
-    for k in range(1, tp_count):
-        normed_copy(k).start()
+    line = Line(normed_all, normed_sem, tp, tp_count)
+    line.start()
 
     def side_copies(k):
         where = {"ctx": ring(ctx, k, ctx_count)}
@@ -233,17 +281,24 @@
         (w_gate, w_up, w_down), (gate_far, up_far, down_far), far_sem, pass_far_sem,
         shared, straight, 0, 0, other, tp,
     )
-    for n in range(shared + straight):
-        for copy in cross(n):
-            copy.start()
-
-    def relay(n):
-        if n < shared:
+
+    def point(name):
+        if not shared:
+            if name == "start":
+                for n in range(straight):
+                    for copy in cross(n):
+                        copy.start()
+            return
+        for n in RELAY.get(name, ()):
             for copy in cross(n):
                 copy.wait_recv()
             for copy in hand_on(n):
                 copy.start()
-
+        for n in BEGIN.get(name, ()):
+            for copy in cross(n):
+                copy.start()
+
+    point("start")
     weights_out[...] = weights[...]
 
     def kv_copy(distance, part):
@@ -252,13 +307,7 @@
             kv_sem.at[0, distance - 1], kv_sem.at[1, distance - 1], {"ctx": ring(ctx, distance, ctx_count)},
         )
 
-    @pl.loop(0, tp_count)
-    def _(k):
-        @pl.when(k > 0)
-        def _():
-            normed_copy(k).wait_recv()
-
-        part = ring(tp, -k, tp_count)
+    def project(part):
         span = pl.ds(pl.multiple_of(part * block, block), block)
         rows = normed_all[part]
         lora = dot(rows, first[...]).astype(BF16)
@@ -294,7 +343,16 @@
                 pl.multiple_of(part * block, block),
             )
 
-    relay(0)
+    @pl.loop(0, line.turns)
+    def _(turn):
+        part, valid = line.block(turn)
+
+        @pl.when(valid)
+        def _():
+            line.arrive(turn, part)
+            project(part)
+
+    point("proj")
 
     def tile(part, pair, start, size, causal):
         index = part * pairs + pair
@@ -324,7 +382,7 @@
         def _(j):
             tile(part, pair, pl.multiple_of(j * block, block), block, False)
 
-    relay(1)
+    point("own")
     group_rows = tp_count * block
     for distance in range(1, SPAN):
 
@@ -394,29 +452,31 @@
                 group, block, LANES
             )
         mixed = att_out[rows, :]
+        low = dot(mixed, o_first[...]).astype(BF16)
+        low_out[rows, :] = low
         for side in range(2):
-            parts[k, :, side * half : (side + 1) * half] = dot(
-                mixed, weights[side, pl.ds(half, q_cols), :]
+            columns = slice(side * half, (side + 1) * half)
+            parts[k, :, columns] = (
+                dot(mixed, weights[side, pl.ds(half, q_cols), :]) + dot(low, o_second[:, columns])
             ).astype(BF16)
-        parts[k, :, model:] = dot(mixed, o_first[...]).astype(BF16)
 
         @pl.when(k < tp_count - 1)
         def _():
             part_copy(k).start()
 
-        for n in range(2, shared):
-
-            @pl.when(k == n - 1)
-            def _(n=n):
-                relay(n)
+        for n in range(tp_count):
+            if f"k{n}" in BEGIN or f"k{n}" in RELAY:
+
+                @pl.when(k == n)
+                def _(n=n):
+                    point(f"k{n}")
 
     summed = parts[tp_count - 1].astype(F32)
     for k in range(tp_count - 1):
         part_copy(k).wait_recv()
         summed += parts_in[k].astype(F32)
-    low = summed[:, model:].astype(BF16)
-    low_out[...] = low
-    middle = inputs + RESIDUAL_SCALE * (summed[:, :model] + dot(low, o_second[...]))
+    point("sum")
+    middle = inputs + RESIDUAL_SCALE * summed
     middle_out[...] = middle
     rows_own[...] = rms_scale(middle, gain_two[...]).astype(BF16)
 
@@ -446,8 +506,7 @@
         rows_copy(k).wait_recv()
         pass_copy(k).start()
 
-    for k in range(1, tp_count):
-        normed_copy(k).wait_send()
+    line.end()
     for k in range(tp_count - 1):
         part_copy(k).wait_send()
     for distance in range(1, SPAN):
@@ -495,7 +554,7 @@
     vmem = pl.BlockSpec(memory_space=pltpu.VMEM)
     hbm = pl.BlockSpec(memory_space=pl.ANY)
     dma = pltpu.SemaphoreType.DMA
-    part = (block, model + LANES)
+    part = (block, model)
     return pl.pallas_call(
         functools.partial(
             forward_kernel, tp_count=tp_count, ctx_count=ctx_count, shared=shared, straight=straight
@@ -508,7 +567,7 @@
             jax.ShapeDtypeStruct((SPAN, tp_count, block, kv_cols), BF16),
             jax.ShapeDtypeStruct((rows, LANES), BF16),
             jax.ShapeDtypeStruct((block, model), F32),
-            jax.ShapeDtypeStruct((block, LANES), BF16),
+            jax.ShapeDtypeStruct((rows, LANES), BF16),
             jax.ShapeDtypeStruct((2,) + shard.shape, BF16),
             jax.ShapeDtypeStruct((tp_count, block, model), BF16),
             *[jax.ShapeDtypeStruct((shared + straight,) + w.shape[1:], BF16) for w in weights],
@@ -527,7 +586,7 @@
             pltpu.VMEM((tp_count - 1,) + part, BF16),
             pltpu.VMEM((block, model), BF16),
             dma((2,)),
-            dma((2, tp_count - 1)),
+            dma((2, 2, tp_count)),
             dma((2, SPAN - 1)),
             dma((2, tp_count - 1)),
             dma((2, shared + straight, 3)),
@@ -567,7 +626,7 @@
     normed_all, lora, att, q_ref, kv_ref, first, second, o_first, o_second, cos, sin, back, mixed, shares,
     output, input_grad, packed_out, shares_out,
     k_aug, v_aug, up_aug, dk, dv, dq, branch_all, far_out, far_in, own_kv, parts, parts_in,
-    second_acc, first_acc, o_in_acc, packed, ctx_in, tp_in, middle_grad,
+    second_acc, first_acc, o_in_acc, o_out_acc, packed, ctx_in, tp_in, middle_grad,
     back_near, back_mine, back_pair, back_far, mixed_near, mixed_mine, mixed_pair, mixed_far,
     near_sem, mine_sem, far_sem, branch_sem, kv_sem, part_sem,
     ctx_sem, tp_sem, x_sem, tp_all_sem, ctx_all_sem, share_sem, swap_sem, own_sem,
@@ -680,6 +739,7 @@
     second_acc[...] = jnp.zeros(second_acc.shape, F32)
     first_acc[...] = jnp.zeros(first_acc.shape, F32)
     o_in_acc[...] = jnp.zeros(o_in_acc.shape, F32)
+    o_out_acc[...] = jnp.zeros(o_out_acc.shape, F32)
     packed[...] = jnp.zeros(packed.shape, F32)
 
     middle = middle_ref[...]
@@ -710,15 +770,8 @@
     branch = (RESIDUAL_SCALE * middle_grad[...]).astype(BF16)
     branch_all[tp] = branch
 
-    def branch_copy(k):
-        return remote(
-            branch_all.at[tp], branch_all.at[tp], branch_sem.at[0, k - 1], branch_sem.at[1, k - 1],
-            {"tp": ring(tp, k, tp_count)},
-        )
-
-    for k in range(1, tp_count):
-        branch_copy(k).start()
-    packed[pl.ds(4 * RANK, RANK), :] = dot_tn(low_ref[...], branch)[:RANK]
+    line = Line(branch_all, branch_sem, tp, tp_count)
+    line.start()
     if direct:
         pass_sum(1)
 
@@ -744,13 +797,16 @@
         dk[pair, span, :] += dot(steep, queries)
         dq[index] += dot_tn(steep, keys)
 
-    @pl.loop(0, tp_count)
-    def _(k):
-        @pl.when(k > 0)
-        def _():
-            branch_copy(k).wait_recv()
-
-        part = ring(tp, -k, tp_count)
+    def far_copy(distance):
+        return remote(
+            far_out.at[distance - 1], far_in.at[distance - 1],
+            kv_sem.at[0, distance - 1], kv_sem.at[1, distance - 1],
+            {"ctx": ring(ctx, -distance, ctx_count)},
+        )
+
+    size = min(rows_all, 512)
+
+    def take_block(part):
         rows = pl.ds(pl.multiple_of(part * block, block), block)
         low_grad = dot_nt(branch_all[part], o_second[...]).astype(BF16)
         grads = dot_nt(low_grad, o_first[...])
@@ -762,6 +818,7 @@
         grads = grads.astype(BF16)
         mixed_heads = att[rows, :]
         o_in_acc[...] += dot_tn(low_grad, mixed_heads)
+        o_out_acc[...] += dot_tn(low_ref[rows, :], branch_all[part])
         product = grads.astype(F32) * mixed_heads.astype(F32)
         minus = jnp.zeros((block, wide), F32)
         for _ in range(3):
@@ -776,44 +833,42 @@
         for head in range(heads):
             up_aug[head, rows, :] = coded[:, head * LANES : (head + 1) * LANES].astype(BF16)
 
-        @pl.loop(0, pairs)
-        def _(pair):
-            tile(part, pair, pl.multiple_of(part * block, block), block, True)
-
-            @pl.loop(0, part)
-            def _(j):
-                tile(part, pair, pl.multiple_of(j * block, block), block, False)
-
-    def far_copy(distance):
-        return remote(
-            far_out.at[distance - 1], far_in.at[distance - 1],
-            kv_sem.at[0, distance - 1], kv_sem.at[1, distance - 1],
-            {"ctx": ring(ctx, -distance, ctx_count)},
-        )
-
-    size = min(rows_all, 512)
-
-    @pl.loop(0, rank)
-    def _(step):
-        distance = rank - step
-        start = distance * rows_all
-
-        @pl.loop(0, tp_count * pairs * (rows_all // size))
-        def _(n):
-            index, piece = n // (rows_all // size), lax.rem(n, rows_all // size)
-            tile(
-                index // pairs, lax.rem(index, pairs),
-                pl.multiple_of(start + piece * size, size), size, False,
-            )
-
-        @pl.loop(0, tp_count)
-        def _(part):
-            span = pl.ds(pl.multiple_of(start + part * block, block), block)
-            far_out[distance - 1, pl.ds(pl.multiple_of(part * block, block), block), :] = joined(
-                dk, dv, span
-            ).astype(BF16)
-
-        far_copy(distance).start()
+    @pl.loop(0, line.turns)
+    def _(turn):
+        part, valid = line.block(turn)
+
+        @pl.when(valid)
+        def _():
+            line.arrive(turn, part)
+            take_block(part)
+
+            @pl.loop(0, rank)
+            def _(step):
+                distance = rank - step
+                start = distance * rows_all
+
+                @pl.loop(0, pairs * (rows_all // size))
+                def _(n):
+                    pair, piece = n // (rows_all // size), lax.rem(n, rows_all // size)
+                    tile(part, pair, pl.multiple_of(start + piece * size, size), size, False)
+
+                @pl.when(turn == line.last())
+                def _():
+                    @pl.loop(0, tp_count)
+                    def _(spot):
+                        span = pl.ds(pl.multiple_of(start + spot * block, block), block)
+                        rows = pl.ds(pl.multiple_of(spot * block, block), block)
+                        far_out[distance - 1, rows, :] = joined(dk, dv, span).astype(BF16)
+
+                    far_copy(distance).start()
+
+            @pl.loop(0, pairs)
+            def _(pair):
+                tile(part, pair, pl.multiple_of(part * block, block), block, True)
+
+                @pl.loop(0, part)
+                def _(j):
+                    tile(part, pair, pl.multiple_of(j * block, block), block, False)
 
     if direct:
         share_own.wait()
@@ -851,12 +906,13 @@
         pieces.append(keys * cos[rows, :] - swap_halves(keys) * sin[rows, :])
         pieces.append(own_kv[rows, kv_cols:])
         grads = jnp.concatenate(pieces, axis=1).astype(BF16)
+        low_part = dot_nt(grads, second[...]).astype(BF16)
         for side in range(2):
-            parts[k, :, side * half : (side + 1) * half] = dot_nt(
-                grads, weights[side, pl.ds(0, half), :]
+            columns = slice(side * half, (side + 1) * half)
+            parts[k, :, columns] = (
+                dot_nt(grads, weights[side, pl.ds(0, half), :])
+                + dot_nt(low_part, first[columns, :])
             ).astype(BF16)
-        low_part = dot_nt(grads, second[...]).astype(BF16)
-        parts[k, :, model:] = low_part
 
         @pl.when(k < tp_count - 1)
         def _():
@@ -866,6 +922,7 @@
         first_acc[...] += dot_tn(low_part, normed_all[part])
 
     packed[pl.ds(0, 3 * RANK), :] = first_acc[pl.ds(0, 3 * RANK), :]
+    packed[pl.ds(4 * RANK, RANK), :] = o_out_acc[pl.ds(0, RANK), :]
     lanes = pl.ds(pl.multiple_of(tp * q_cols, q_cols), q_cols)
     packed[pl.ds(3 * RANK, RANK), lanes] = o_in_acc[pl.ds(0, RANK), :]
     packed[pl.ds(5 * RANK, RANK), lanes] = second_acc[pl.ds(0, RANK), :q_cols]
@@ -945,11 +1002,8 @@
     for k in range(tp_count - 1):
         part_copy(k).wait_recv()
         summed += parts_in[k].astype(F32)
-    normed_grad = summed[:, :model] + dot_nt(summed[:, model:].astype(BF16), first[...])
     inputs = tokens[...].astype(F32)
-    input_grad[...] = (
-        middle_grad[...] + rms_back(inputs, gain_one[...], normed_grad)
-    ).astype(BF16)
+    input_grad[...] = (middle_grad[...] + rms_back(inputs, gain_one[...], summed)).astype(BF16)
     mixture = end_sum(1) if direct else mixed[...].astype(F32)
     output[...] = (middle_ref[...] + RESIDUAL_SCALE * mixture).astype(BF16)
 
@@ -961,8 +1015,7 @@
             for slot in range(2):
                 near_copy(n, slot).wait_send()
             pair_copy(n).wait_send()
-    for k in range(1, tp_count):
-        branch_copy(k).wait_send()
+    line.end()
     for k in range(tp_count - 1):
         part_copy(k).wait_send()
     for distance in range(1, SPAN):
@@ -985,7 +1038,7 @@
     vmem = pl.BlockSpec(memory_space=pltpu.VMEM)
     hbm = pl.BlockSpec(memory_space=pl.ANY)
     dma = pltpu.SemaphoreType.DMA
-    part = (block, model + LANES)
+    part = (block, model)
     packed = (8 * RANK, model)
     copies = 2 if direct else 1
     slim = (8, LANES)
@@ -1024,6 +1077,7 @@
             pltpu.VMEM((LANES, cols), F32),
             pltpu.VMEM((LANES, model), F32),
             pltpu.VMEM((LANES, heads * HEAD), F32),
+            pltpu.VMEM((LANES, model), F32),
             pltpu.VMEM(packed, F32),
             pltpu.VMEM((ctx_count - 1, packed[0] // ctx_count, model) if direct else slim, F32),
             pltpu.VMEM((tp_count - 1, 8, model) if direct else slim, F32),
@@ -1033,7 +1087,7 @@
             dma((2, 4)),
             dma((4,)),
             dma((2, 2)),
-            dma((2, tp_count - 1)),
+            dma((2, 2, tp_count)),
             dma((2, SPAN - 1)),
             dma((2, tp_count - 1)),
             dma((2, ctx_count - 1)),
@@ -1172,18 +1226,23 @@
                     device_id_type=pl.DeviceIdType.MESH,
                 )
             pl.semaphore_wait(barrier, tp_count)
-            for n in range(late):
+            for n in BEGIN[0]:
                 for copy in cross(n):
                     copy.start()
 
-        for n in range(shared):
-
-            @pl.when(expert == 2 + n)
-            def _(n=n):
-                for copy in cross(n):
-                    copy.wait_recv()
-                for copy in hand_on(n):
-                    copy.start()
+        for step in range(1, early + late):
+            if step in BEGIN or step in RELAY:
+
+                @pl.when(expert == step)
+                def _(step=step):
+                    for n in RELAY.get(step, ()):
+                        for copy in cross(n):
+                            copy.wait_recv()
+                        for copy in hand_on(n):
+                            copy.start()
+                    for n in BEGIN.get(step, ()):
+                        for copy in cross(n):
+                            copy.start()
 
         for n in range(late):
 

time: 508 us -> 459 us (0.904); the launches traced: 499 us -> 456 us
  Pallas kernels: 477 us -> 434 us
    pallas_call x1, Pallas kernels: 201 us -> 163 us  [backward(): pl.pallas_call(functools.partial(backward_kernel, tp_count=tp_count, ctx_...]
    pallas_call x1, Pallas kernels: 177 us -> 156 us  [forward(): pl.pallas_call(functools.partial(forward_kernel, tp_count=tp_count, ctx_c...]
    pallas_call x1, Pallas kernels: 80 us -> 95.4 us  [run_experts(): pl.pallas_call(functools.partial(expert_kernel, slots=slots, sources=sour...]
where the time goes in v5:
time: 459 us; the launch traced here: 456 us
  Pallas kernels  434 us (95%)
  local copies, waits for them, and re-layouts  13.6 us (3%)
  other arithmetic  6.1 us (1%)
    pallas_call x1, Pallas kernels, backward(): pl.pallas_call(functools.partial(backward_kernel, tp_count=tp_count, ctx_...  163 us
    pallas_call x1, Pallas kernels, forward(): pl.pallas_call(functools.partial(forward_kernel, tp_count=tp_count, ctx_c...  156 us
    pallas_call x1, Pallas kernels, run_experts(): pl.pallas_call(functools.partial(expert_kernel, slots=slots, sources=sour...  95.4 us
    pallas_call x1, Pallas kernels, place_experts(): pl.pallas_call(place_experts_kernel, grid_spec=pltpu.PrefetchScalarGridSp...  11.1 us

profile of v5, /device:TPU:13, one launch (start us, length us, event | category | flops | bytes accessed | tf_op | source)
XLA Modules:
  0.0 455.9 jit_solution(14344390362780494043)
XLA Ops:
  0.7 1.3 fusion.23
  2.7 0.7 dynamic_slice.43
  3.4 0.7 dynamic_slice.44
  4.1 0.7 dynamic_slice.45
  4.8 0.7 fusion.12.second
  5.6 1.2 constant_dynamic-slice_fusion.1
  6.8 0.1 copy.54
  7.1 0.1 constant_dynamic-slice_fusion.3
  7.4 0.2 copy.51
  7.6 0.8 pad.34.first
  8.4 0.3 fusion.1
  8.7 0.2 fusion.3
  9.0 0.2 fusion.24
  9.5 3.0 multiply_sine_fusion
  12.5 0.8 constant_dynamic-slice_fusion
  13.3 0.7 pad.39.o_second
  14.0 0.9 dynamic_slice.46
  14.9 0.6 pad.38.o_first
  15.7 0.7 broadcast_in_dim.39
  16.4 0.6 broadcast_in_dim.40
  17.0 0.6 broadcast_in_dim.41
  17.6 0.9 pad_maximum_fusion.shard
  18.6 155.7 %forward.1 = (bf16[1024,256]{1,0:T(8,128)(2,1)}, bf16[4,1024,128]{2,1,0:T(8,128)(2,1)}, bf16[4,4,256,256]{3,2,1,0:T(8,128)(2,1)}, bf16[1024,128]{1,0:T(8,128)(2,...) custom-call(bf16[256,1024]{1,0:T(8,128)(2,1)} %tokens.3, ...), custom_call_target="tpu_custom_call" | custom-call | flops 34359738368 | bytes 33554432 | tf_op jit(solution)/shard_map/forward/pallas_call | solution.py:558
  174.3 95.4 %experts.1 = (bf16[1024,1152]{1,0:T(8,128)(2,1)}, bf16[1024,1024]{1,0:T(8,128)(2,1)}, bf16[8,80,256]{2,1,0:T(8,128)(2,1)}) custom-call(s32[1]{0:T(128)} %get-tuple-element.88.sets, bf16[1024,1024]{1,0:T(8,128)(2,1)} %bitcast.29, bf16[1024,1024]{1,0:T(8,128)(2,1)} %bitcast.28, s32[8,1024]{1,0:T(8,128)} %bitcast.30, bf16[32,1024]{1,0:T(8,128)(2,1)} %bitcast.20, ...), custom_call_target="tpu_custom_call" | custom-call | flops 34359738368 | bytes 8388608 | tf_op jit(solution)/shard_map/experts/pallas_call | solution.py:1457
  269.6 0.2 copy.47
  269.8 0.8 pad.33.router
  270.6 0.8 copy.52.routes
  271.4 163.4 %backward.1 = (bf16[256,1024]{1,0:T(8,128)(2,1)}, bf16[256,1024]{1,0:T(8,128)(2,1)}, f32[2,128,1024]{2,1,0:T(8,128)}, bf16[2,8,80,1024]{3,2,1,0:T(8,128)(2,1)}) custom-call(bf16[256,1024]{1,0:T(8,128)(2,1)} %tokens.3, bf16[256,1024]{1,0:T(8,128)(2,1)} %upstream_ref.1, s32[256,8]{1,0:T(8,128)} %copy.52.routes, f32[1,1024]{1,0:T(1,128)} %bitcast.23, ...), custom_call_target="tpu_custom_call" | custom-call | flops 68719476736 | bytes 33554432 | tf_op jit(solution)/shard_map/backward/pallas_call | solution.py:1050
  434.8 11.1 %place_experts.1 = (f32[8,1024,128]{2,1,0:T(8,128)}, f32[8,128,512]{2,1,0:T(8,128)}, f32[8,1024,128]{2,1,0:T(8,128)}, f32[8,128,512]{2,1,0:T(8,128)}, f32[8,512,128]{2,1,0:T(8,128)}, /*index=5*/f32[8,128,1024]{2,1,0:T(8,128)}) custom-call(s32[2]{0:T(128)} %sets.3, bf16[2,8,80,1024]{3,2,1,0:T(8,128)(2,1)} %get-tuple-element.79.part), custom_call_target="tpu_custom_call" | custom-call | tf_op jit(solution)/shard_map/place_experts/pallas_call | solution.py:1182
  446.0 8.3 %place.1 = (f32[1024,128]{1,0:T(8,128)}, f32[128,1024]{1,0:T(8,128)}, f32[1024,128]{1,0:T(8,128)}, f32[128,512]{1,0:T(8,128)}, f32[1024,128]{1,0:T(8,128)}, /*in...) custom-call(s32[2]{0:T(128)} %sets.3, f32[2,128,1024]{2,1,0:T(8,128)} %get-tuple-element.70.packed), custom_call_target="tpu_custom_call" | custom-call | tf_op jit(solution)/shard_map/place/pallas_call | solution.py:1149
  454.3 0.8 copy.58
  455.1 0.8 copy.59
  (41 shorter events, 0.8 us)
Async XLA Ops:
  0.6 6.5 %copy-start = (bf16[1024,128]{1,0:T(8,128)(2,1)S(1)}, bf16[1024,128]{1,0:T(8,128)(2,1)}, u32[]{:S(2)}) copy-start(bf16[1024,128]{1,0:T(8,128)(2,1)} %param.44) | copy-start | bytes 786436
  0.7 7.7 %copy-start.12 = (s32[64]{0:T(128)S(1)}, s32[64]{0:T(128)}, u32[]{:S(2)}) copy-start(s32[64]{0:T(128)} %param.32) | copy-start | bytes 772
  6.9 9.5 %copy-start.10 = (bf16[1024]{0:T(1024)(128)(2,1)S(1)}, bf16[1024]{0:T(1024)(128)(2,1)}, u32[]{:S(2)}) copy-start(bf16[1024]{0:T(1024)(128)(2,1)} %param.34) | copy-start | bytes 6148
  6.9 10.1 %copy-start.11 = (bf16[1024]{0:T(1024)(128)(2,1)S(1)}, bf16[1024]{0:T(1024)(128)(2,1)}, u32[]{:S(2)}) copy-start(bf16[1024]{0:T(1024)(128)(2,1)} %param.35) | copy-start | bytes 6148
  7.0 10.7 %copy-start.4 = (bf16[256,512]{1,0:T(8,128)(2,1)S(1)}, bf16[256,512]{1,0:T(8,128)(2,1)}, u32[]{:S(2)}) copy-start(bf16[256,512]{1,0:T(8,128)(2,1)} %param.39) | copy-start | bytes 786436
  7.0 10.6 %copy-start.5 = (bf16[512,256]{1,0:T(8,128)(2,1)S(1)}, bf16[512,256]{1,0:T(8,128)(2,1)}, u32[]{:S(2)}) copy-start(bf16[512,256]{1,0:T(8,128)(2,1)} %param.36) | copy-start | bytes 786436
  7.0 10.6 %copy-start.6 = (bf16[512,128]{1,0:T(8,128)(2,1)S(1)}, bf16[512,128]{1,0:T(8,128)(2,1)}, u32[]{:S(2)}) copy-start(bf16[512,128]{1,0:T(8,128)(2,1)} %param.38) | copy-start | bytes 393220
  7.0 10.6 %copy-start.7 = (bf16[512,128]{1,0:T(8,128)(2,1)S(1)}, bf16[512,128]{1,0:T(8,128)(2,1)}, u32[]{:S(2)}) copy-start(bf16[512,128]{1,0:T(8,128)(2,1)} %param.37) | copy-start | bytes 393220
  174.2 95.4 %copy-start.8 = (bf16[1024,32]{0,1:T(8,128)(2,1)S(1)}, bf16[1024,32]{0,1:T(8,128)(2,1)}, u32[]{:S(2)}) copy-start(bf16[1024,32]{0,1:T(8,128)(2,1)} %param.40) | copy-start | bytes 196612
  174.2 96.3 %copy-start.9 = (s32[256,8]{0,1:T(8,128)S(1)}, s32[256,8]{0,1:T(8,128)}, u32[]{:S(2)}) copy-start(s32[256,8]{0,1:T(8,128)} %param.31) | copy-start | bytes 24580
  434.8 19.5 %copy-start.3 = (bf16[256,1024]{1,0:T(8,128)(2,1)S(1)}, bf16[256,1024]{1,0:T(8,128)(2,1)}, u32[]{:S(2)}) copy-start(bf16[256,1024]{1,0:T(8,128)(2,1)} %get-tuple-element.110) | copy-start | bytes 1572868
  434.8 20.3 %copy-start.2 = (bf16[256,1024]{1,0:T(8,128)(2,1)S(1)}, bf16[256,1024]{1,0:T(8,128)(2,1)}, u32[]{:S(2)}) copy-start(bf16[256,1024]{1,0:T(8,128)(2,1)} %get-tuple-element.111) | copy-start | bytes 1572868
  434.8 21.0 %copy-start.1 = (bf16[1024,128]{1,0:T(8,128)(2,1)S(1)}, bf16[1024,128]{1,0:T(8,128)(2,1)}, u32[]{:S(2)}) copy-start(bf16[1024,128]{1,0:T(8,128)(2,1)} %param.44) | copy-start | bytes 786436

commit v6 on v5

--- a/solution.py
+++ b/solution.py
@@ -1,8 +1,8 @@
 import functools
-import math
 
 import jax
 import jax.numpy as jnp
+import numpy as np
 from jax import lax
 from jax.experimental import pallas as pl
 from jax.experimental.pallas import tpu as pltpu
@@ -49,12 +49,6 @@
     return lax.broadcasted_iota(jnp.int32, shape, dim)
 
 
-def shifted(block, axis, distance):
-    devices = range(lax.axis_size(axis))
-    route = [(i - distance, i) for i in devices if i - distance in devices]
-    return lax.ppermute(block, axis, route)
-
-
 def rms_scale(values, gain_row):
     return (
         values * lax.rsqrt(jnp.mean(values * values, axis=-1, keepdims=True) + EPSILON) * gain_row
@@ -66,18 +60,6 @@
     scaled = grad * gain_row
     inner = jnp.mean(scaled * values, axis=-1, keepdims=True)
     return inv * scaled - values * (inv * inv * inv * inner)
-
-
-def tree_links(tree_parents):
-    count = tree_parents.shape[0]
-    columns = jnp.arange(count, dtype=jnp.int32)
-    reach = (
-        (tree_parents[:, None] == columns[None, :]) | (columns[:, None] == columns[None, :])
-    ).astype(BF16)
-    for _ in range(max(1, (count - 1).bit_length())):
-        reach = jnp.minimum(dot(reach, reach), 1.0).astype(BF16)
-    reach = reach.astype(F32)
-    return reach, jnp.sum(reach, axis=1) - 1.0
 
 
 def swap_halves(values):
@@ -211,11 +193,13 @@
 
 
 def forward_kernel(
-    tokens, gain_one, gain_two, shard, first, second, o_first, o_second, cos, sin, codes,
+    parents, adapter_set, tokens, gain_one, gain_two, freqs, w_query, w_key, w_value, w_output,
+    query_in, query_out, key_in, key_out, value_in, value_out, out_in, out_out,
     w_gate, w_up, w_down, grads, routes,
-    att_out, q_out, kv_out, lora_out, middle_out, low_out, weights_out, normed_all,
+    att_out, q_out, kv_out, lora_out, middle_out, low_out, weights, normed_all,
+    first, second, o_first, o_second, cos, sin,
     gate_far, up_far, down_far, grads_all, routes_all, rows_all,
-    weights, q_aug, k_aug, v_aug, top, acc, parts, parts_in, rows_own,
+    q_aug, k_aug, v_aug, top, acc, parts, parts_in, rows_own, code_table, depth_table,
     shard_sem, normed_sem, kv_sem, part_sem, far_sem, pass_far_sem, grads_sem, routes_sem, rows_sem,
     pass_sem, local_sem,
     *, tp_count, ctx_count, shared, straight,
@@ -227,8 +211,9 @@
     pairs = k_aug.shape[0]
     group = heads // pairs
     tall = group * block
-    half = shard.shape[1]
+    half = model // 2
     q_cols = heads * HEAD
+    kv_cols = pairs * HEAD
     turn = cos.shape[1]
     chips = ctx_count // 2
     partner = ctx + 1 - 2 * lax.rem(ctx, 2)
@@ -248,11 +233,21 @@
         )
     pl.semaphore_wait(barrier, tp_count + ctx_count - 1)
 
-    shard_copy = remote(shard, weights.at[fsdp], shard_sem.at[0], shard_sem.at[1], other)
-    shard_copy.start()
+    corners = (
+        (w_query, 0, 0),
+        (w_key, 0, q_cols),
+        (w_value, 0, q_cols + kv_cols),
+        (w_output, half, 0),
+    )
+    shard_copies = []
+    for n, (source, row, column) in enumerate(corners):
+        spot = weights.at[fsdp, pl.ds(row, source.shape[0]), pl.ds(column, source.shape[1])]
+        shard_copies.append(remote(source, spot, shard_sem.at[0, n], shard_sem.at[1, n], other))
+    for copy in shard_copies:
+        copy.start()
 
     inputs = tokens[...].astype(F32)
-    normed = rms_scale(inputs, gain_one[...]).astype(BF16)
+    normed = rms_scale(inputs, gain_one[...].astype(F32).reshape(1, model)).astype(BF16)
     normed_all[tp] = normed
 
     line = Line(normed_all, normed_sem, tp, tp_count)
@@ -275,8 +270,45 @@
         for copy in side_copies(k):
             copy.start()
 
-    weights[fsdp] = shard[...]
-    shard_copy.wait()
+    for source, row, column in corners:
+        weights[fsdp, pl.ds(row, source.shape[0]), pl.ds(column, source.shape[1])] = source[...]
+
+    tree = (fsdp * ctx_count + ctx) // SPAN
+    spot_row, spot_lane = iota((LANES, LANES), 0), iota((LANES, LANES), 1)
+    linked = (spot_row == spot_lane) & (spot_row < TREE_SEGS)
+    for n in range(TREE_SEGS):
+        linked |= (spot_row == n) & (spot_lane == parents[tree * TREE_SEGS + n])
+    reach = linked.astype(F32)
+    for _ in range((TREE_SEGS - 1).bit_length()):
+        reach = jnp.minimum(dot(reach.astype(BF16), reach.astype(BF16)), 1.0)
+    depth_table[...] = jnp.broadcast_to(
+        jnp.sum(reach, axis=1, keepdims=True) - 1.0, (LANES, LANES)
+    ).astype(BF16)
+    coded = (spot_lane >= CODE) & (spot_lane < CODE + TREE_SEGS)
+    code_table[...] = jnp.where(
+        coded & (pltpu.roll(reach, CODE, 1) < 0.5), MASKED, 0.0
+    ).astype(BF16)
+
+    chosen = adapter_set[tree]
+
+    def pick(n):
+        inside = (spot_lane >= n * RANK) & (spot_lane < (n + 1) * RANK)
+        return (inside & (spot_row == spot_lane - n * RANK + chosen * RANK)).astype(BF16)
+
+    first[...] = (
+        dot(query_in[...], pick(0)) + dot(key_in[...], pick(1)) + dot(value_in[...], pick(2))
+    ).astype(BF16)
+    for n, (source, column, width) in enumerate(
+        ((query_out, 0, q_cols), (key_out, q_cols, kv_cols), (value_out, q_cols + kv_cols, kv_cols))
+    ):
+        lanes = pl.ds(pl.multiple_of(tp * width, width), width)
+        second[:, column : column + width] = dot_tn(pick(n), source[:, lanes]).astype(BF16)
+    own = pl.ds(pl.multiple_of(tp * q_cols, q_cols), q_cols)
+    o_first[...] = dot(out_in[own, :], pick(0)).astype(BF16)
+    o_second[...] = dot_tn(pick(0), out_out[...]).astype(BF16)
+
+    for copy in shard_copies:
+        copy.wait()
     cross, hand_on = far_moves(
         (w_gate, w_up, w_down), (gate_far, up_far, down_far), far_sem, pass_far_sem,
         shared, straight, 0, 0, other, tp,
@@ -299,7 +331,6 @@
                 copy.start()
 
     point("start")
-    weights_out[...] = weights[...]
 
     def kv_copy(distance, part):
         return remote(
@@ -310,6 +341,13 @@
     def project(part):
         span = pl.ds(pl.multiple_of(part * block, block), block)
         rows = normed_all[part]
+        seg = rank * SEGS_DEV + (part * block + iota((block, LANES), 0)) // SEG
+        at_seg = (seg == iota((block, LANES), 1)).astype(BF16)
+        offset = lax.rem(iota((block, LANES), 0), SEG).astype(F32)
+        angles = (dot(at_seg, depth_table[...]) * SEG + offset) * freqs[...]
+        cos[span, :] = jnp.cos(angles)
+        sin[span, :] = jnp.sin(angles)
+        codes = dot(at_seg, code_table[...])
         lora = dot(rows, first[...]).astype(BF16)
         lora_out[span, :] = lora
         pre = (
@@ -326,7 +364,7 @@
         ).astype(BF16)
         for head in range(heads):
             q_aug[head, span, :] = (
-                dot(queries, place_table(q_cols, head * HEAD, 0)) + codes[span, :].astype(F32)
+                dot(queries, place_table(q_cols, head * HEAD, 0)) + codes
             ).astype(BF16)
         keys = jnp.concatenate(turned[q_cols // turn :], axis=1)
         kv = jnp.concatenate([keys, pre[:, q_cols + keys.shape[1] :]], axis=1).astype(BF16)
@@ -478,7 +516,7 @@
     point("sum")
     middle = inputs + RESIDUAL_SCALE * summed
     middle_out[...] = middle
-    rows_own[...] = rms_scale(middle, gain_two[...]).astype(BF16)
+    rows_own[...] = rms_scale(middle, gain_two[...].astype(F32).reshape(1, model)).astype(BF16)
 
     own_rows = pltpu.make_async_copy(rows_own, rows_all.at[ctx], local_sem.at[2])
     own_rows.start()
@@ -539,44 +577,52 @@
 
 
 def forward(
-    tokens, gains, shard, first, second, o_first, o_second, cos, sin, codes, weights, grads,
-    routes, tp_count, ctx_count,
+    parents, adapter_set, tokens, gains, attention, adapters, weights, grads, routes,
+    tp_count, ctx_count,
 ):
     block, model = tokens.shape
     rows = tp_count * block
-    heads = o_first.shape[0] // HEAD
-    cols = second.shape[1]
-    kv_cols = cols - heads * HEAD
-    pairs = kv_cols // (2 * HEAD)
+    q_cols, kv_cols = attention[0].shape[1], attention[1].shape[1]
+    heads, pairs = q_cols // HEAD, kv_cols // HEAD
+    cols = q_cols + 2 * kv_cols
     tall = heads // pairs * block
     chips = ctx_count // 2
     shared, straight, _, _ = transfer_plan(weights[0].shape[0], tp_count)
     vmem = pl.BlockSpec(memory_space=pltpu.VMEM)
+    smem = pl.BlockSpec(memory_space=pltpu.SMEM)
     hbm = pl.BlockSpec(memory_space=pl.ANY)
     dma = pltpu.SemaphoreType.DMA
     part = (block, model)
+    half_head = HEAD // 2
+    freqs = np.float32(ROPE_BASE) ** (-(np.arange(half_head, dtype=np.float32) * 2) / HEAD)
+    freqs = jnp.asarray(np.tile(freqs.astype(np.float32), LANES // half_head)[None])
     return pl.pallas_call(
         functools.partial(
             forward_kernel, tp_count=tp_count, ctx_count=ctx_count, shared=shared, straight=straight
         ),
-        in_specs=[vmem] * 11 + [hbm] * 5,
-        out_specs=[vmem] * 8 + [hbm] * 6,
+        in_specs=[smem] * 2 + [vmem] * 16 + [hbm] * 5,
+        out_specs=[vmem] * 14 + [hbm] * 6,
         out_shape=[
-            jax.ShapeDtypeStruct((rows, heads * HEAD), BF16),
+            jax.ShapeDtypeStruct((rows, q_cols), BF16),
             jax.ShapeDtypeStruct((heads, rows, LANES), BF16),
-            jax.ShapeDtypeStruct((SPAN, tp_count, block, kv_cols), BF16),
+            jax.ShapeDtypeStruct((SPAN, tp_count, block, 2 * kv_cols), BF16),
             jax.ShapeDtypeStruct((rows, LANES), BF16),
             jax.ShapeDtypeStruct((block, model), F32),
             jax.ShapeDtypeStruct((rows, LANES), BF16),
-            jax.ShapeDtypeStruct((2,) + shard.shape, BF16),
+            jax.ShapeDtypeStruct((2, model // 2 + q_cols, model // 2), BF16),
             jax.ShapeDtypeStruct((tp_count, block, model), BF16),
+            jax.ShapeDtypeStruct((model, LANES), BF16),
+            jax.ShapeDtypeStruct((LANES, cols), BF16),
+            jax.ShapeDtypeStruct((q_cols, LANES), BF16),
+            jax.ShapeDtypeStruct((LANES, model), BF16),
+            jax.ShapeDtypeStruct((rows, LANES), F32),
+            jax.ShapeDtypeStruct((rows, LANES), F32),
             *[jax.ShapeDtypeStruct((shared + straight,) + w.shape[1:], BF16) for w in weights],
             jax.ShapeDtypeStruct((ctx_count,) + grads.shape, BF16),
             jax.ShapeDtypeStruct((ctx_count,) + routes.shape, jnp.int32),
             jax.ShapeDtypeStruct((ctx_count, block, model), BF16),
         ],
         scratch_shapes=[
-            pltpu.VMEM((2,) + shard.shape, BF16),
             pltpu.VMEM((heads, rows, LANES), BF16),
             pltpu.VMEM((pairs, SPAN * rows, LANES), BF16),
             pltpu.VMEM((pairs, SPAN * rows, LANES), BF16),
@@ -585,7 +631,9 @@
             pltpu.VMEM((tp_count,) + part, BF16),
             pltpu.VMEM((tp_count - 1,) + part, BF16),
             pltpu.VMEM((block, model), BF16),
-            dma((2,)),
+            pltpu.VMEM((LANES, LANES), BF16),
+            pltpu.VMEM((LANES, LANES), BF16),
+            dma((2, 4)),
             dma((2, 2, tp_count)),
             dma((2, SPAN - 1)),
             dma((2, tp_count - 1)),
@@ -607,8 +655,7 @@
         ),
         name="forward",
     )(
-        tokens, *gains, shard, first, second, o_first, o_second, cos, sin, codes, *weights,
-        grads, routes,
+        parents, adapter_set, tokens, *gains, freqs, *attention, *adapters, *weights, grads, routes,
     )
 
 
@@ -622,14 +669,14 @@
 
 
 def backward_kernel(
-    tokens, upstream_ref, routes, gain_one, gain_two, router, middle_ref, low_ref, weights,
+    tokens, upstream_ref, routes, gain_one, gain_two, w_router, middle_ref, low_ref, weights,
     normed_all, lora, att, q_ref, kv_ref, first, second, o_first, o_second, cos, sin, back, mixed, shares,
     output, input_grad, packed_out, shares_out,
-    k_aug, v_aug, up_aug, dk, dv, dq, branch_all, far_out, far_in, own_kv, parts, parts_in,
-    second_acc, first_acc, o_in_acc, o_out_acc, packed, ctx_in, tp_in, middle_grad,
+    k_aug, v_aug, up_aug, dk, dv, dq, branch_all, far_out, far_in, own_kv, row_grads, low_grads, parts, parts_in,
+    second_acc, first_acc, o_in_acc, o_out_acc, packed, ctx_in, tp_in, middle_grad, router,
     back_near, back_mine, back_pair, back_far, mixed_near, mixed_mine, mixed_pair, mixed_far,
     near_sem, mine_sem, far_sem, branch_sem, kv_sem, part_sem,
-    ctx_sem, tp_sem, x_sem, tp_all_sem, ctx_all_sem, share_sem, swap_sem, own_sem,
+    ctx_sem, tp_sem, x_sem, ctx_all_sem, share_sem, swap_sem, own_sem,
     *, tp_count, ctx_count, experts, direct,
 ):
     tp, ctx, fsdp = (lax.axis_index(name) for name in ("tp", "ctx", "fsdp"))
@@ -719,8 +766,6 @@
         start_sum(0)
         start_sum(1)
         share_own.start()
-        for k in range(1, tp_count):
-            share_copy(k).start()
 
     @pl.loop(0, rank + 1)
     def _(distance):
@@ -743,12 +788,17 @@
     packed[...] = jnp.zeros(packed.shape, F32)
 
     middle = middle_ref[...]
-    normed_two = rms_scale(middle, gain_two[...]).astype(BF16)
-    logits = dot(normed_two, router[...])
-    number = iota((block, LANES), 1)
-    hit = jnp.zeros((block, LANES), F32)
-    for k in range(routes.shape[1]):
-        hit += (routes[:, k : k + 1] == number).astype(F32)
+    scale_one = gain_one[...].astype(F32).reshape(1, model)
+    scale_two = gain_two[...].astype(F32).reshape(1, model)
+    normed_two = rms_scale(middle, scale_two).astype(BF16)
+    router[...] = jnp.zeros(router.shape, BF16)
+    router[pl.ds(0, experts), :] = w_router[...]
+    logits = dot_nt(normed_two, router[...])
+    number = iota((LANES, block), 0)
+    hit = jnp.zeros((LANES, block), F32)
+    for k in range(routes.shape[0]):
+        hit += (routes[k : k + 1, :] == number).astype(F32)
+    hit = hit.T
     kept = jnp.where(hit > 0.5, logits, MASKED)
     gates = jnp.exp(kept - jnp.max(kept, axis=1, keepdims=True)) * hit
     gates = gates / jnp.sum(gates, axis=1, keepdims=True)
@@ -763,9 +813,9 @@
     logits_grad = gates * (slopes - jnp.sum(gates * slopes, axis=1, keepdims=True))
     high = logits_grad.astype(BF16)
     low = (logits_grad - high.astype(F32)).astype(BF16)
-    normed_two_grad = back_sum[:, :model] + dot_nt(high, router[...]) + dot_nt(low, router[...])
+    normed_two_grad = back_sum[:, :model] + dot(high, router[...]) + dot(low, router[...])
     middle_grad[...] = upstream_ref[...].astype(F32) + rms_back(
-        middle, gain_two[...], normed_two_grad
+        middle, scale_two, normed_two_grad
     )
     branch = (RESIDUAL_SCALE * middle_grad[...]).astype(BF16)
     branch_all[tp] = branch
@@ -862,6 +912,13 @@
 
                     far_copy(distance).start()
 
+            if direct:
+
+                @pl.when(turn == line.last())
+                def _():
+                    for k in range(1, tp_count):
+                        share_copy(k).start()
+
             @pl.loop(0, pairs)
             def _(pair):
                 tile(part, pair, pl.multiple_of(part * block, block), block, True)
@@ -869,12 +926,6 @@
                 @pl.loop(0, part)
                 def _(j):
                     tile(part, pair, pl.multiple_of(j * block, block), block, False)
-
-    if direct:
-        share_own.wait()
-        for k in range(1, tp_count):
-            share_copy(k).wait()
-        swap.start()
 
     own_kv[...] = joined(dk, dv, pl.ds(0, rows_all))
     for distance in range(1, SPAN):
@@ -891,8 +942,7 @@
         )
 
     @pl.loop(0, tp_count)
-    def _(k):
-        part = ring(tp, k + 1, tp_count)
+    def _(part):
         rows = pl.ds(pl.multiple_of(part * block, block), block)
         pieces = []
         for pair in range(pairs):
@@ -906,18 +956,9 @@
         pieces.append(keys * cos[rows, :] - swap_halves(keys) * sin[rows, :])
         pieces.append(own_kv[rows, kv_cols:])
         grads = jnp.concatenate(pieces, axis=1).astype(BF16)
+        row_grads[rows, :] = grads
         low_part = dot_nt(grads, second[...]).astype(BF16)
-        for side in range(2):
-            columns = slice(side * half, (side + 1) * half)
-            parts[k, :, columns] = (
-                dot_nt(grads, weights[side, pl.ds(0, half), :])
-                + dot_nt(low_part, first[columns, :])
-            ).astype(BF16)
-
-        @pl.when(k < tp_count - 1)
-        def _():
-            part_copy(k).start()
-
+        low_grads[rows, :] = low_part
         second_acc[...] += dot_tn(lora[rows, :], grads)
         first_acc[...] += dot_tn(low_part, normed_all[part])
 
@@ -931,15 +972,28 @@
     lanes = pl.ds(pl.multiple_of(model // 2 + tp * kv_cols, kv_cols), kv_cols)
     packed[pl.ds(6 * RANK, RANK), lanes] = second_acc[pl.ds(2 * RANK, RANK), q_cols + kv_cols :]
 
+    def make_parts():
+        @pl.loop(0, tp_count)
+        def _(k):
+            part = ring(tp, k + 1, tp_count)
+            rows = pl.ds(pl.multiple_of(part * block, block), block)
+            grads = row_grads[rows, :]
+            for side in range(2):
+                columns = slice(side * half, (side + 1) * half)
+                parts[k, :, columns] = (
+                    dot_nt(grads, weights[side, pl.ds(0, half), :])
+                    + dot_nt(low_grads[rows, :], first[columns, :])
+                ).astype(BF16)
+
+    def send_parts():
+        for k in range(tp_count - 1):
+            part_copy(k).start()
+
     if direct:
-        tall_rows, few_rows = packed.shape[0] // ctx_count, packed.shape[0] // (ctx_count * tp_count)
+        tall_rows = packed.shape[0] // ctx_count
 
         def ctx_rows(index):
             return pl.ds(pl.multiple_of(index * tall_rows, tall_rows), tall_rows)
-
-        def tp_rows(index):
-            start = ctx * tall_rows + index * few_rows
-            return pl.ds(pl.multiple_of(start, few_rows), few_rows)
 
         def ctx_copy(k):
             where = ring(ctx, k, ctx_count)
@@ -949,22 +1003,15 @@
             )
 
         def tp_copy(k):
-            where = ring(tp, k, tp_count)
             return remote(
-                packed.at[tp_rows(where)], tp_in.at[k - 1],
-                tp_sem.at[0, k - 1], tp_sem.at[1, k - 1], {"tp": where},
+                tp_in.at[tp], tp_in.at[tp], tp_sem.at[0, k - 1], tp_sem.at[1, k - 1],
+                {"tp": ring(tp, k, tp_count)},
             )
 
         x_copy = remote(
-            packed_out.at[fsdp, tp_rows(tp)], packed_out.at[fsdp, tp_rows(tp)],
+            packed_out.at[fsdp, ctx_rows(ctx)], packed_out.at[fsdp, ctx_rows(ctx)],
             x_sem.at[0], x_sem.at[1], other,
         )
-
-        def tp_all_copy(k):
-            return remote(
-                packed_out.at[:, tp_rows(tp)], packed_out.at[:, tp_rows(tp)],
-                tp_all_sem.at[0, k - 1], tp_all_sem.at[1, k - 1], {"tp": ring(tp, k, tp_count)},
-            )
 
         def ctx_all_copy(k):
             return remote(
@@ -975,35 +1022,37 @@
 
         for k in range(1, ctx_count):
             ctx_copy(k).start()
+        make_parts()
         for k in range(1, ctx_count):
             ctx_copy(k).wait()
-        packed[ctx_rows(ctx), :] = packed[ctx_rows(ctx), :] + sum(
-            ctx_in[k] for k in range(ctx_count - 1)
+        tp_in[tp] = (packed[ctx_rows(ctx), :] + sum(ctx_in[k] for k in range(ctx_count - 1))).astype(
+            BF16
         )
         for k in range(1, tp_count):
             tp_copy(k).start()
+        send_parts()
         for k in range(1, tp_count):
             tp_copy(k).wait()
-        packed_out[fsdp, tp_rows(tp), :] = packed[tp_rows(tp), :] + sum(
-            tp_in[k] for k in range(tp_count - 1)
-        )
+        packed_out[fsdp, ctx_rows(ctx), :] = sum(tp_in[k].astype(F32) for k in range(tp_count))
         x_copy.start()
         x_copy.wait()
-        for k in range(1, tp_count):
-            tp_all_copy(k).start()
-        for k in range(1, tp_count):
-            tp_all_copy(k).wait()
         for k in range(1, ctx_count):
             ctx_all_copy(k).start()
+        share_own.wait()
+        for k in range(1, tp_count):
+            share_copy(k).wait()
+        swap.start()
     else:
         packed_out[0] = packed[...]
+        make_parts()
+        send_parts()
 
     summed = parts[tp_count - 1].astype(F32)
     for k in range(tp_count - 1):
         part_copy(k).wait_recv()
         summed += parts_in[k].astype(F32)
     inputs = tokens[...].astype(F32)
-    input_grad[...] = (middle_grad[...] + rms_back(inputs, gain_one[...], summed)).astype(BF16)
+    input_grad[...] = (middle_grad[...] + rms_back(inputs, scale_one, summed)).astype(BF16)
     mixture = end_sum(1) if direct else mixed[...].astype(F32)
     output[...] = (middle_ref[...] + RESIDUAL_SCALE * mixture).astype(BF16)
 
@@ -1072,6 +1121,8 @@
             pltpu.VMEM((SPAN - 1, rows, kv_width), BF16),
             pltpu.VMEM((SPAN - 1, rows, kv_width), BF16),
             pltpu.VMEM((rows, kv_width), F32),
+            pltpu.VMEM((rows, cols), BF16),
+            pltpu.VMEM((rows, LANES), BF16),
             pltpu.VMEM((tp_count,) + part, BF16),
             pltpu.VMEM((tp_count - 1,) + part, BF16),
             pltpu.VMEM((LANES, cols), F32),
@@ -1080,8 +1131,9 @@
             pltpu.VMEM((LANES, model), F32),
             pltpu.VMEM(packed, F32),
             pltpu.VMEM((ctx_count - 1, packed[0] // ctx_count, model) if direct else slim, F32),
-            pltpu.VMEM((tp_count - 1, 8, model) if direct else slim, F32),
+            pltpu.VMEM((tp_count, packed[0] // ctx_count, model) if direct else slim, BF16),
             pltpu.VMEM((block, model), F32),
+            pltpu.VMEM((LANES, model), BF16),
             *buffers(model + LANES),
             *buffers(model),
             dma((2, 4)),
@@ -1093,7 +1145,6 @@
             dma((2, ctx_count - 1)),
             dma((2, tp_count - 1)),
             dma((2,)),
-            dma((2, tp_count - 1)),
             dma((2, ctx_count - 1)),
             dma((2, tp_count - 1)),
             dma((2,)),
@@ -1114,83 +1165,75 @@
     )
 
 
-def columns_of(chosen):
-    return iota((RANK, LANES), 1) == iota((RANK, LANES), 0) + chosen * RANK
-
-
-def place_kernel(sets, packed, *outs):
-    query_in, query_out, key_in, key_out, value_in, value_out, out_in, out_out = outs
-    kv_cols = key_out.shape[1]
-    exact = dict(precision=lax.Precision.HIGHEST, preferred_element_type=F32)
-
-    def gathered(rows, lanes, turned):
-        total = None
-        for tree in range(packed.shape[0]):
-            spots = columns_of(sets[tree]).astype(F32)
-            piece = packed[tree, rows * RANK : (rows + 1) * RANK, lanes]
-            pair = (piece, spots) if turned else (spots, piece)
-            term = lax.dot_general(*pair, (((0,), (0,)), ((), ())), **exact)
-            total = term if total is None else total + term
-        return total
-
-    whole = slice(None)
-    query_in[...] = gathered(0, whole, True)
-    key_in[...] = gathered(1, whole, True)
-    value_in[...] = gathered(2, whole, True)
-    out_in[...] = gathered(3, whole, True)
-    out_out[...] = gathered(4, whole, False)
-    query_out[...] = gathered(5, whole, False)
-    key_out[...] = gathered(6, slice(0, kv_cols), False)
-    value_out[...] = gathered(6, slice(kv_cols, 2 * kv_cols), False)
-
-
-def place(sets, packed, outs):
-    vmem = pl.BlockSpec(memory_space=pltpu.VMEM)
+def place_kernel(sets, packed, part, *outs):
+    query_in, query_out, key_in, key_out, value_in, value_out, out_in, out_out = outs[:8]
+    gate_in, gate_out, up_in, up_out, down_in, down_out = outs[8:]
+    kv_cols, hidden = key_out.shape[1], gate_out.shape[2]
+    trees = part.shape[0]
+    spots = jnp.concatenate(
+        [
+            (iota((RANK, LANES), 1) == iota((RANK, LANES), 0) + sets[tree] * RANK).astype(BF16)
+            for tree in range(trees)
+        ],
+        axis=0,
+    )
+    spots_twice = jnp.concatenate([spots, spots], axis=0)
+
+    def block(rows):
+        return slice(rows * RANK, (rows + 1) * RANK)
+
+    @pl.when(pl.program_id(0) == 0)
+    def _():
+        def gathered(rows, lanes, turned):
+            pieces = jnp.concatenate(
+                [packed[tree, block(rows), lanes] for tree in range(trees)], axis=0
+            )
+            high = pieces.astype(BF16)
+            both = jnp.concatenate([high, (pieces - high.astype(F32)).astype(BF16)], axis=0)
+            return dot_tn(both, spots_twice) if turned else dot_tn(spots_twice, both)
+
+        whole = slice(None)
+        query_in[...] = gathered(0, whole, True)
+        key_in[...] = gathered(1, whole, True)
+        value_in[...] = gathered(2, whole, True)
+        out_in[...] = gathered(3, whole, True)
+        out_out[...] = gathered(4, whole, False)
+        query_out[...] = gathered(5, whole, False)
+        key_out[...] = gathered(6, slice(0, kv_cols), False)
+        value_out[...] = gathered(6, slice(kv_cols, 2 * kv_cols), False)
+
+    def pieces(rows, lanes):
+        return jnp.concatenate([part[tree, 0, block(rows), lanes] for tree in range(trees)], axis=0)
+
+    whole, left, right = slice(None), slice(0, hidden), slice(hidden, 2 * hidden)
+    gate_in[0] = dot_tn(pieces(0, whole), spots)
+    up_in[0] = dot_tn(pieces(1, whole), spots)
+    gate_out[0] = dot_tn(spots, pieces(2, left))
+    up_out[0] = dot_tn(spots, pieces(2, right))
+    down_out[0] = dot_tn(spots, pieces(3, whole))
+    down_in[0] = dot_tn(pieces(4, left), spots)
+
+
+def place(sets, packed, part, once, each):
+    trees, local = part.shape[:2]
     return pl.pallas_call(
         place_kernel,
-        in_specs=[pl.BlockSpec(memory_space=pltpu.SMEM), vmem],
-        out_specs=[vmem] * len(outs),
-        out_shape=[jax.ShapeDtypeStruct(o.shape, F32) for o in outs],
-        compiler_params=pltpu.CompilerParams(vmem_limit_bytes=VMEM_LIMIT),
-        name="place",
-    )(sets, packed)
-
-
-def place_experts_kernel(sets, part, gate_in, gate_out, up_in, up_out, down_in, down_out):
-    hidden = gate_out.shape[2]
-
-    def gathered(rows, lanes, turned):
-        total = None
-        for tree in range(part.shape[0]):
-            spots = columns_of(sets[tree]).astype(BF16)
-            piece = part[tree, 0, rows * RANK : (rows + 1) * RANK, lanes]
-            term = dot_tn(piece, spots) if turned else dot_tn(spots, piece)
-            total = term if total is None else total + term
-        return total
-
-    whole, left, right = slice(None), slice(0, hidden), slice(hidden, 2 * hidden)
-    gate_in[0] = gathered(0, whole, True)
-    up_in[0] = gathered(1, whole, True)
-    gate_out[0] = gathered(2, left, False)
-    up_out[0] = gathered(2, right, False)
-    down_out[0] = gathered(3, whole, False)
-    down_in[0] = gathered(4, left, True)
-
-
-def place_experts(sets, part, outs):
-    trees, local = part.shape[:2]
-    return pl.pallas_call(
-        place_experts_kernel,
         grid_spec=pltpu.PrefetchScalarGridSpec(
             num_scalar_prefetch=1,
             grid=(local,),
-            in_specs=[pl.BlockSpec((trees, 1) + part.shape[2:], lambda e, s: (0, e, 0, 0))],
-            out_specs=[pl.BlockSpec((1,) + o.shape[1:], lambda e, s: (e, 0, 0)) for o in outs],
+            in_specs=[
+                pl.BlockSpec(packed.shape, lambda e, s: (0, 0, 0)),
+                pl.BlockSpec((trees, 1) + part.shape[2:], lambda e, s: (0, e, 0, 0)),
+            ],
+            out_specs=[
+                *[pl.BlockSpec(o.shape, lambda e, s: (0, 0)) for o in once],
+                *[pl.BlockSpec((1,) + o.shape[1:], lambda e, s: (e, 0, 0)) for o in each],
+            ],
         ),
-        out_shape=[jax.ShapeDtypeStruct(o.shape, F32) for o in outs],
+        out_shape=[jax.ShapeDtypeStruct(o.shape, F32) for o in (*once, *each)],
         compiler_params=pltpu.CompilerParams(vmem_limit_bytes=VMEM_LIMIT),
-        name="place_experts",
-    )(sets, part)
+        name="place",
+    )(sets, packed, part)
 
 
 def expert_kernel(
@@ -1256,7 +1299,7 @@
     each = tokens // sources
     hidden = w_gate.shape[2]
     lanes = gate_in.shape[2]
-    chosen = sets[chunk]
+    chosen = sets[fsdp * pl.num_programs(0) + chunk]
 
     @pl.when(expert == 0)
     def _():
@@ -1433,7 +1476,7 @@
     total, model = rows.shape
     experts = router.shape[0]
     local, half, hidden = weights[0].shape
-    trees = sets.shape[0]
+    trees = sets.shape[0] // 2
     tokens = total // trees
     lanes = adapters[0].shape[2]
     tall = sources * slots
@@ -1519,10 +1562,6 @@
     )(sets, rows, upstream, routes, router, *weights, *far, *weights, *adapters)
 
 
-def take_set(table, chosen, axis):
-    return lax.dynamic_slice_in_dim(table, chosen * RANK, RANK, axis)
-
-
 def per_device(
     tokens,
     out_grad,
@@ -1554,98 +1593,37 @@
     down_in,
     down_out,
 ):
-    tp_rank = lax.axis_index("tp")
     ctx_rank = lax.axis_index("ctx")
     fsdp_rank = lax.axis_index("fsdp")
     ctx_count = lax.axis_size("ctx")
     tp_count = lax.axis_size("tp")
     fsdp_count = lax.axis_size("fsdp")
     tok_rows, model = tokens.shape
-    q_cols = w_query.shape[1]
-    kv_cols = key_projection_matrix.shape[1]
-    heads, pairs = q_cols // HEAD, kv_cols // HEAD
     experts = w_router.shape[1]
     local_experts = w_gate.shape[0]
-    sets = query_in.shape[1] // RANK
     slots = tok_rows * TOP * 3 // (2 * experts)
     trees = ctx_count // SPAN
-
-    attention_shard = jnp.concatenate(
-        [
-            jnp.concatenate([w_query, key_projection_matrix, value_projection_matrix], axis=1),
-            w_output,
-        ],
-        axis=0,
-    )
-
-    seg_start = (fsdp_rank * ctx_count + ctx_rank) * SEGS_DEV
-    tree_index = seg_start // TREE_SEGS
-    local_start = seg_start % TREE_SEGS
-    rank = (local_start // SEGS_DEV).astype(jnp.int32).reshape(1)
-    tree_parents = lax.dynamic_slice_in_dim(parents, tree_index * TREE_SEGS, TREE_SEGS, 0)
-    reach, depth = tree_links(tree_parents)
-    chosen = lax.dynamic_slice_in_dim(adapter_set, tree_index, 1, 0)[0]
-
-    gain_one = gain_a.astype(F32)
-    gain_two = gain_b.astype(F32)
-
-    own_reach = lax.dynamic_slice_in_dim(reach, local_start, SEGS_DEV, 0)
-    codes = jnp.pad(
-        jnp.where(own_reach > 0.5, 0.0, MASKED), ((0, 0), (CODE, LANES - CODE - TREE_SEGS))
-    )
-    codes = jnp.repeat(codes.astype(BF16), SEG, axis=0)
-    own_depth = lax.dynamic_slice_in_dim(depth, local_start, SEGS_DEV, 0)
-    positions = (
-        own_depth[:, None] * SEG + jnp.arange(SEG, dtype=jnp.int32).astype(F32)[None, :]
-    ).reshape(-1)
-    half_head = HEAD // 2
-    freqs = ROPE_BASE ** (-(jnp.arange(half_head, dtype=jnp.int32).astype(F32) * 2.0) / HEAD)
-    angles = positions[:, None] * jnp.tile(freqs, LANES // half_head)[None, :]
-    cos, sin = jnp.cos(angles), jnp.sin(angles)
-
-    first = jnp.pad(
-        jnp.concatenate(
-            [take_set(t, chosen, 1) for t in (query_in, key_in, value_in)], axis=1
+    tree_index = (fsdp_rank * ctx_count + ctx_rank) // SPAN
+
+    (
+        attended, queries, kv_parts, lora, middle, o_reduced, attention_weights, normed_all,
+        first, second, o_first, o_second, cos, sin,
+        *far_weights, upstream_all, routes_all, rows_all,
+    ) = forward(
+        parents, adapter_set, tokens, (gain_a, gain_b),
+        (w_query, key_projection_matrix, value_projection_matrix, w_output),
+        (
+            query_in, query_out, key_in, key_second_factor, value_in, value_second_factor,
+            out_in, out_out,
         ),
-        ((0, 0), (0, LANES - 3 * RANK)),
-    )
-    q_second = lax.dynamic_slice(query_out, (chosen * RANK, tp_rank * q_cols), (RANK, q_cols))
-    k_second = lax.dynamic_slice(
-        key_second_factor, (chosen * RANK, tp_rank * kv_cols), (RANK, kv_cols)
-    )
-    v_second = lax.dynamic_slice(
-        value_second_factor, (chosen * RANK, tp_rank * kv_cols), (RANK, kv_cols)
-    )
-    second = jnp.concatenate(
-        [
-            jnp.pad(q_second, ((0, 0), (0, 2 * kv_cols))),
-            jnp.pad(k_second, ((0, 0), (q_cols, kv_cols))),
-            jnp.pad(v_second, ((0, 0), (q_cols + kv_cols, 0))),
-            jnp.zeros((LANES - 3 * RANK, q_cols + 2 * kv_cols), BF16),
-        ],
-        axis=0,
-    )
-    o_first = jnp.pad(
-        lax.dynamic_slice(out_in, (tp_rank * q_cols, chosen * RANK), (q_cols, RANK)),
-        ((0, 0), (0, LANES - RANK)),
-    )
-    o_second = jnp.pad(take_set(out_out, chosen, 0), ((0, LANES - RANK), (0, 0)))
-
-    (
-        attended, queries, kv_parts, lora, middle, o_reduced, attention_weights,
-        normed_all, *far_weights, upstream_all, routes_all, rows_all,
-    ) = forward(
-        tokens, (gain_one[None], gain_two[None]), attention_shard, first, second,
-        o_first, o_second, cos, sin, codes, (w_gate, w_up, w_down), out_grad, routes.T,
-        tp_count, ctx_count,
+        (w_gate, w_up, w_down), out_grad, routes.T, tp_count, ctx_count,
     )
     upstream_all = upstream_all.reshape(-1, model)
     rows_all = rows_all.reshape(-1, model)
     routes_all = routes_all.transpose(1, 0, 2).reshape(TOP, -1)
 
-    tree_sets = lax.dynamic_slice_in_dim(adapter_set, fsdp_rank * trees, trees, 0)
     back, mixed, expert_part = run_experts(
-        tree_sets,
+        adapter_set,
         rows_all,
         upstream_all,
         routes_all,
@@ -1665,8 +1643,7 @@
         back = lax.psum_scatter(back, "ctx", scatter_dimension=0, tiled=True)
         mixed = lax.psum_scatter(mixed, "ctx", scatter_dimension=0, tiled=True)
     output, input_grad, packed, all_shares = backward(
-        tokens, out_grad, routes, (gain_one[None], gain_two[None]),
-        jnp.pad(w_router, ((0, 0), (0, LANES - experts))), middle, o_reduced, attention_weights,
+        tokens, out_grad, routes.T, (gain_a, gain_b), w_router.T, middle, o_reduced, attention_weights,
         normed_all, lora, attended, queries, kv_parts, first, second, o_first, o_second,
         cos, sin, back, mixed, expert_part, tp_count, ctx_count, experts, direct,
     )
@@ -1674,24 +1651,20 @@
     if not direct:
         mine = (jnp.arange(all_trees, dtype=jnp.int32) == tree_index)[:, None, None]
         packed = lax.psum(jnp.where(mine, packed, 0.0), ("fsdp", "ctx", "tp"))
-    adapter_totals = place(
-        adapter_set,
-        packed,
-        (
-            query_in, query_out, key_in, key_second_factor, value_in, value_second_factor,
-            out_in, out_out,
-        ),
-    )
-
     if direct:
         expert_part = all_shares
     else:
         expert_part = lax.all_gather(lax.psum(expert_part, "tp"), "fsdp")
         expert_part = expert_part.reshape(all_trees, local_experts, 5 * RANK, model)
-    expert_totals = place_experts(
-        adapter_set, expert_part, (gate_in, gate_out, up_in, up_out, down_in, down_out)
-    )
-    return (output, input_grad, *adapter_totals, *expert_totals)
+    adapter_grads = place(
+        adapter_set, packed, expert_part,
+        (
+            query_in, query_out, key_in, key_second_factor, value_in, value_second_factor,
+            out_in, out_out,
+        ),
+        (gate_in, gate_out, up_in, up_out, down_in, down_out),
+    )
+    return (output, input_grad, *adapter_grads)
 
 
 def solution(mesh):

time: 459 us -> 428 us (0.932)
  local copies, waits for them, and re-layouts: 13.6 us -> 1.6 us
  Pallas kernels: 434 us -> 426 us
  other arithmetic: 6.1 us -> 0 us
    pallas_call x2 -> x1, Pallas kernels: 19.4 us -> 12.4 us  [place(): pl.pallas_call(place_kernel, grid_spec=pltpu.PrefetchScalarGridSpec(num_s...]
    dynamic_slice x9 -> x0, local copies, waits for them, and re-layouts: 6.55 us -> none  [the longest x3 2.14 us: take_set(): return lax.dynamic_slice_in_dim(table, chosen * RANK, RANK, axis)]
where the time goes in v6:
time: 428 us
  Pallas kernels  426 us (100%)
    pallas_call x1, Pallas kernels, backward(): pl.pallas_call(functools.partial(backward_kernel, tp_count=tp_count, ctx_...  161 us
    pallas_call x1, Pallas kernels, forward(): pl.pallas_call(functools.partial(forward_kernel, tp_count=tp_count, ctx_c...  157 us
    pallas_call x1, Pallas kernels, run_experts(): pl.pallas_call(functools.partial(expert_kernel, slots=slots, sources=sour...  95.7 us
    pallas_call x1, Pallas kernels, place(): pl.pallas_call(place_kernel, grid_spec=pltpu.PrefetchScalarGridSpec(num_s...  12.4 us

profile of v6, /device:TPU:13, one launch (start us, length us, event | category | flops | bytes accessed | tf_op | source)
XLA Modules:
  0.0 427.8 jit_solution(15076773108816073265)
XLA Ops:
  0.7 156.5 %forward.1 = (bf16[1024,256]{1,0:T(8,128)(2,1)}, bf16[4,1024,128]{2,1,0:T(8,128)(2,1)}, bf16[4,4,256,256]{3,2,1,0:T(8,128)(2,1)}, bf16[1024,128]{1,0:T(8,128)(2,...) custom-call(s32[64]{0:T(128)} %parents.1, s32[2]{0:T(128)} %sets.3, ...), custom_call_target="tpu_custom_call" | custom-call | flops 34359738368 | bytes 33554432 | tf_op jit(solution)/shard_map/forward/pallas_call | solution.py:599
  157.2 95.7 %experts.1 = (bf16[1024,1152]{1,0:T(8,128)(2,1)}, bf16[1024,1024]{1,0:T(8,128)(2,1)}, bf16[8,80,256]{2,1,0:T(8,128)(2,1)}) custom-call(s32[2]{0:T(128)} %sets.3, bf16[1024,1024]{1,0:T(8,128)(2,1)} %bitcast.16, bf16[1024,1024]{1,0:T(8,128)(2,1)} %bitcast.15, s32[8,1024]{1,0:T(8,128)} %bitcast.17, bf16[32,1024]{1,0:T(8,128)(2,1)} %bitcast.9, ...), custom_call_target="tpu_custom_call" | custom-call | flops 34359738368 | bytes 8388608 | tf_op jit(solution)/shard_map/experts/pallas_call | solution.py:1500
  252.9 160.9 %backward.1 = (bf16[256,1024]{1,0:T(8,128)(2,1)}, bf16[256,1024]{1,0:T(8,128)(2,1)}, f32[2,128,1024]{2,1,0:T(8,128)}, bf16[2,8,80,1024]{3,2,1,0:T(8,128)(2,1)}) custom-call(bf16[256,1024]{1,0:T(8,128)(2,1)} %tokens.3, bf16[256,1024]{1,0:T(8,128)(2,1)} %upstream_ref.1, s32[8,256]{1,0:T(8,128)} %bitcast.12, bf16[1024]{0:T(1024)(128)(2,1)} %gain_one.3, ...), custom_call_target="tpu_custom_call" | custom-call | flops 68719476736 | bytes 33554432 | tf_op jit(solution)/shard_map/backward/pallas_call | solution.py:1099
  413.8 0.0 copy-start.1
  413.8 0.0 copy-start
  413.8 12.4 %place.1 = (f32[1024,128]{1,0:T(8,128)}, f32[128,1024]{1,0:T(8,128)}, f32[1024,128]{1,0:T(8,128)}, f32[128,512]{1,0:T(8,128)}, f32[1024,128]{1,0:T(8,128)}, /*in...) custom-call(s32[2]{0:T(128)} %sets.3, ...), custom_call_target="tpu_custom_call" | custom-call | tf_op jit(solution)/shard_map/place/pallas_call | solution.py:1219
  426.2 0.0 copy-done.1
  426.3 0.8 copy.48
  427.0 0.0 copy-done
  427.1 0.8 copy.49
Async XLA Ops:
  413.8 12.5 %copy-start.1 = (bf16[256,1024]{1,0:T(8,128)(2,1)S(1)}, bf16[256,1024]{1,0:T(8,128)(2,1)}, u32[]{:S(2)}) copy-start(bf16[256,1024]{1,0:T(8,128)(2,1)} %get-tuple-element.114) | copy-start | bytes 1572868
  413.8 13.3 %copy-start = (bf16[256,1024]{1,0:T(8,128)(2,1)S(1)}, bf16[256,1024]{1,0:T(8,128)(2,1)}, u32[]{:S(2)}) copy-start(bf16[256,1024]{1,0:T(8,128)(2,1)} %get-tuple-element.115) | copy-start | bytes 1572868

commit v7 on v6

--- a/solution.py
+++ b/solution.py
@@ -81,8 +81,8 @@
     return 0, local, 0, 0
 
 
-BEGIN = {"start": (0, 1), "proj": (2,), "own": (3,), "k1": (4,), 0: (0,), 2: (1,), 4: (2,)}
-RELAY = {"proj": (0,), "sum": (1, 2), 2: (0,), 4: (1,)}
+BEGIN = {'start': (0, 1), 'proj': (2,), 'own': (3,), 'k1': (4,), 0: (0,), 2: (1,), 3: (2,)}
+RELAY = {'k0': (0, 1), 'k3': (2,), 2: (0,), 4: (1,)}
 
 
 def remote(src, dst, send, recv, where):
@@ -197,10 +197,10 @@
     query_in, query_out, key_in, key_out, value_in, value_out, out_in, out_out,
     w_gate, w_up, w_down, grads, routes,
     att_out, q_out, kv_out, lora_out, middle_out, low_out, weights, normed_all,
-    first, second, o_first, o_second, cos, sin,
+    first, second, o_first, o_second, cos, sin, w_rows, att_rows,
     gate_far, up_far, down_far, grads_all, routes_all, rows_all,
-    q_aug, k_aug, v_aug, top, acc, parts, parts_in, rows_own, code_table, depth_table,
-    shard_sem, normed_sem, kv_sem, part_sem, far_sem, pass_far_sem, grads_sem, routes_sem, rows_sem,
+    q_aug, k_aug, v_aug, top, acc, rows_own, code_table, depth_table,
+    shard_sem, normed_sem, kv_sem, part_sem, w_rows_sem, far_sem, pass_far_sem, grads_sem, routes_sem, rows_sem,
     pass_sem, local_sem,
     *, tp_count, ctx_count, shared, straight,
 ):
@@ -303,8 +303,7 @@
     ):
         lanes = pl.ds(pl.multiple_of(tp * width, width), width)
         second[:, column : column + width] = dot_tn(pick(n), source[:, lanes]).astype(BF16)
-    own = pl.ds(pl.multiple_of(tp * q_cols, q_cols), q_cols)
-    o_first[...] = dot(out_in[own, :], pick(0)).astype(BF16)
+    o_first[...] = dot(out_in[...], pick(0)).astype(BF16)
     o_second[...] = dot_tn(pick(0), out_out[...]).astype(BF16)
 
     for copy in shard_copies:
@@ -390,7 +389,20 @@
             line.arrive(turn, part)
             project(part)
 
+    w_line = Line(w_rows, w_rows_sem, tp, tp_count)
+    for side in range(2):
+        w_rows[tp, side] = weights[side, pl.ds(half, q_cols), :]
+    w_line.start()
     point("proj")
+
+    def advance(step):
+        @pl.loop(2 * step - 1, 2 * step + 1)
+        def _(turn):
+            shard, valid = w_line.block(turn)
+
+            @pl.when(valid)
+            def _():
+                w_line.arrive(turn, shard)
 
     def tile(part, pair, start, size, causal):
         index = part * pairs + pair
@@ -420,6 +432,7 @@
         def _(j):
             tile(part, pair, pl.multiple_of(j * block, block), block, False)
 
+    advance(1)
     point("own")
     group_rows = tp_count * block
     for distance in range(1, SPAN):
@@ -446,9 +459,10 @@
             kv_out[distance] = jnp.zeros(kv_out.shape[1:], BF16)
 
     def part_copy(k):
+        part = ring(tp, k + 1, tp_count)
+        rows = pl.ds(pl.multiple_of(part * block, block), block)
         return remote(
-            parts.at[k], parts_in.at[k], part_sem.at[0, k], part_sem.at[1, k],
-            {"tp": ring(tp, k + 1, tp_count)},
+            att_out.at[rows], att_rows.at[tp], part_sem.at[0, k], part_sem.at[1, k], {"tp": part}
         )
 
     @pl.loop(0, tp_count)
@@ -489,19 +503,21 @@
             q_out[pl.ds(pair * group, group), rows, :] = coded.astype(BF16).reshape(
                 group, block, LANES
             )
-        mixed = att_out[rows, :]
-        low = dot(mixed, o_first[...]).astype(BF16)
-        low_out[rows, :] = low
-        for side in range(2):
-            columns = slice(side * half, (side + 1) * half)
-            parts[k, :, columns] = (
-                dot(mixed, weights[side, pl.ds(half, q_cols), :]) + dot(low, o_second[:, columns])
-            ).astype(BF16)
 
         @pl.when(k < tp_count - 1)
         def _():
             part_copy(k).start()
 
+        @pl.when(k == tp_count - 1)
+        def _():
+            att_rows[tp] = att_out[rows, :]
+
+        for step in range(2, tp_count):
+
+            @pl.when(k == step - 2)
+            def _(step=step):
+                advance(step)
+
         for n in range(tp_count):
             if f"k{n}" in BEGIN or f"k{n}" in RELAY:
 
@@ -509,12 +525,18 @@
                 def _(n=n):
                     point(f"k{n}")
 
-    summed = parts[tp_count - 1].astype(F32)
     for k in range(tp_count - 1):
         part_copy(k).wait_recv()
-        summed += parts_in[k].astype(F32)
     point("sum")
-    middle = inputs + RESIDUAL_SCALE * summed
+    low = sum(
+        dot(att_rows[t], o_first[pl.ds(t * q_cols, q_cols), :]) for t in range(tp_count)
+    ).astype(BF16)
+    low_out[...] = low
+    branch = dot(low, o_second[...]) + jnp.concatenate(
+        [sum(dot(att_rows[t], w_rows[t, side]) for t in range(tp_count)) for side in range(2)],
+        axis=1,
+    )
+    middle = inputs + RESIDUAL_SCALE * branch
     middle_out[...] = middle
     rows_own[...] = rms_scale(middle, gain_two[...].astype(F32).reshape(1, model)).astype(BF16)
 
@@ -545,6 +567,7 @@
         pass_copy(k).start()
 
     line.end()
+    w_line.end()
     for k in range(tp_count - 1):
         part_copy(k).wait_send()
     for distance in range(1, SPAN):
@@ -592,7 +615,6 @@
     smem = pl.BlockSpec(memory_space=pltpu.SMEM)
     hbm = pl.BlockSpec(memory_space=pl.ANY)
     dma = pltpu.SemaphoreType.DMA
-    part = (block, model)
     half_head = HEAD // 2
     freqs = np.float32(ROPE_BASE) ** (-(np.arange(half_head, dtype=np.float32) * 2) / HEAD)
     freqs = jnp.asarray(np.tile(freqs.astype(np.float32), LANES // half_head)[None])
@@ -601,22 +623,24 @@
             forward_kernel, tp_count=tp_count, ctx_count=ctx_count, shared=shared, straight=straight
         ),
         in_specs=[smem] * 2 + [vmem] * 16 + [hbm] * 5,
-        out_specs=[vmem] * 14 + [hbm] * 6,
+        out_specs=[vmem] * 16 + [hbm] * 6,
         out_shape=[
             jax.ShapeDtypeStruct((rows, q_cols), BF16),
             jax.ShapeDtypeStruct((heads, rows, LANES), BF16),
             jax.ShapeDtypeStruct((SPAN, tp_count, block, 2 * kv_cols), BF16),
             jax.ShapeDtypeStruct((rows, LANES), BF16),
             jax.ShapeDtypeStruct((block, model), F32),
-            jax.ShapeDtypeStruct((rows, LANES), BF16),
+            jax.ShapeDtypeStruct((block, LANES), BF16),
             jax.ShapeDtypeStruct((2, model // 2 + q_cols, model // 2), BF16),
             jax.ShapeDtypeStruct((tp_count, block, model), BF16),
             jax.ShapeDtypeStruct((model, LANES), BF16),
             jax.ShapeDtypeStruct((LANES, cols), BF16),
-            jax.ShapeDtypeStruct((q_cols, LANES), BF16),
+            jax.ShapeDtypeStruct((tp_count * q_cols, LANES), BF16),
             jax.ShapeDtypeStruct((LANES, model), BF16),
             jax.ShapeDtypeStruct((rows, LANES), F32),
             jax.ShapeDtypeStruct((rows, LANES), F32),
+            jax.ShapeDtypeStruct((tp_count, 2, q_cols, model // 2), BF16),
+            jax.ShapeDtypeStruct((tp_count, block, q_cols), BF16),
             *[jax.ShapeDtypeStruct((shared + straight,) + w.shape[1:], BF16) for w in weights],
             jax.ShapeDtypeStruct((ctx_count,) + grads.shape, BF16),
             jax.ShapeDtypeStruct((ctx_count,) + routes.shape, jnp.int32),
@@ -628,8 +652,6 @@
             pltpu.VMEM((pairs, SPAN * rows, LANES), BF16),
             pltpu.VMEM((tp_count * pairs, tall, LANES), F32),
             pltpu.VMEM((tp_count * pairs, tall, LANES), F32),
-            pltpu.VMEM((tp_count,) + part, BF16),
-            pltpu.VMEM((tp_count - 1,) + part, BF16),
             pltpu.VMEM((block, model), BF16),
             pltpu.VMEM((LANES, LANES), BF16),
             pltpu.VMEM((LANES, LANES), BF16),
@@ -637,6 +659,7 @@
             dma((2, 2, tp_count)),
             dma((2, SPAN - 1)),
             dma((2, tp_count - 1)),
+            dma((2, 2, tp_count)),
             dma((2, shared + straight, 3)),
             dma((2, max(shared, 1), 3)),
             dma((2, ctx_count)),
@@ -670,10 +693,10 @@
 
 def backward_kernel(
     tokens, upstream_ref, routes, gain_one, gain_two, w_router, middle_ref, low_ref, weights,
-    normed_all, lora, att, q_ref, kv_ref, first, second, o_first, o_second, cos, sin, back, mixed, shares,
+    normed_all, lora, att, q_ref, kv_ref, first, second, o_first, o_second, cos, sin, w_rows, att_rows, back, mixed, shares,
     output, input_grad, packed_out, shares_out,
-    k_aug, v_aug, up_aug, dk, dv, dq, branch_all, far_out, far_in, own_kv, row_grads, low_grads, parts, parts_in,
-    second_acc, first_acc, o_in_acc, o_out_acc, packed, ctx_in, tp_in, middle_grad, router,
+    k_aug, v_aug, up_aug, dk, dv, dq, do_out, do_all, far_out, far_in, own_kv, row_grads, low_grads, parts, parts_in,
+    second_acc, first_acc, packed, ctx_in, tp_in, middle_grad, router,
     back_near, back_mine, back_pair, back_far, mixed_near, mixed_mine, mixed_pair, mixed_far,
     near_sem, mine_sem, far_sem, branch_sem, kv_sem, part_sem,
     ctx_sem, tp_sem, x_sem, ctx_all_sem, share_sem, swap_sem, own_sem,
@@ -783,8 +806,6 @@
     dq[...] = jnp.zeros(dq.shape, F32)
     second_acc[...] = jnp.zeros(second_acc.shape, F32)
     first_acc[...] = jnp.zeros(first_acc.shape, F32)
-    o_in_acc[...] = jnp.zeros(o_in_acc.shape, F32)
-    o_out_acc[...] = jnp.zeros(o_out_acc.shape, F32)
     packed[...] = jnp.zeros(packed.shape, F32)
 
     middle = middle_ref[...]
@@ -818,10 +839,29 @@
         middle, scale_two, normed_two_grad
     )
     branch = (RESIDUAL_SCALE * middle_grad[...]).astype(BF16)
-    branch_all[tp] = branch
-
-    line = Line(branch_all, branch_sem, tp, tp_count)
-    line.start()
+    low_grad = dot_nt(branch, o_second[...]).astype(BF16)
+
+    def do_copy(k):
+        where = ring(tp, k, tp_count)
+        return remote(
+            do_out.at[where], do_all.at[tp], branch_sem.at[0, k - 1], branch_sem.at[1, k - 1],
+            {"tp": where},
+        )
+
+    for t in range(tp_count):
+        do_out[t] = (
+            dot_nt(branch[:, :half], w_rows[t, 0])
+            + dot_nt(branch[:, half:], w_rows[t, 1])
+            + dot_nt(low_grad, o_first[pl.ds(t * q_cols, q_cols), :])
+        ).astype(BF16)
+    for k in range(1, tp_count):
+        do_copy(k).start()
+    do_all[tp] = do_out[tp]
+    for t in range(tp_count):
+        packed[pl.ds(3 * RANK, RANK), t * q_cols : (t + 1) * q_cols] = dot_tn(
+            low_grad, att_rows[t]
+        )[:RANK]
+    packed[pl.ds(4 * RANK, RANK), :] = dot_tn(low_ref[...], branch)[:RANK]
     if direct:
         pass_sum(1)
 
@@ -854,21 +894,12 @@
             {"ctx": ring(ctx, -distance, ctx_count)},
         )
 
-    size = min(rows_all, 512)
+    size = min(rows_all, 1024)
 
     def take_block(part):
         rows = pl.ds(pl.multiple_of(part * block, block), block)
-        low_grad = dot_nt(branch_all[part], o_second[...]).astype(BF16)
-        grads = dot_nt(low_grad, o_first[...])
-        for side in range(2):
-            grads += dot_nt(
-                branch_all[part, :, side * half : (side + 1) * half],
-                weights[side, pl.ds(half, q_cols), :],
-            )
-        grads = grads.astype(BF16)
+        grads = do_all[part]
         mixed_heads = att[rows, :]
-        o_in_acc[...] += dot_tn(low_grad, mixed_heads)
-        o_out_acc[...] += dot_tn(low_ref[rows, :], branch_all[part])
         product = grads.astype(F32) * mixed_heads.astype(F32)
         minus = jnp.zeros((block, wide), F32)
         for _ in range(3):
@@ -883,13 +914,16 @@
         for head in range(heads):
             up_aug[head, rows, :] = coded[:, head * LANES : (head + 1) * LANES].astype(BF16)
 
-    @pl.loop(0, line.turns)
+    @pl.loop(0, tp_count)
     def _(turn):
-        part, valid = line.block(turn)
-
-        @pl.when(valid)
+        part = ring(tp, -turn, tp_count)
+
+        @pl.when(turn > 0)
         def _():
-            line.arrive(turn, part)
+            do_copy(turn).wait_recv()
+
+        @pl.when(turn >= 0)
+        def _():
             take_block(part)
 
             @pl.loop(0, rank)
@@ -902,7 +936,7 @@
                     pair, piece = n // (rows_all // size), lax.rem(n, rows_all // size)
                     tile(part, pair, pl.multiple_of(start + piece * size, size), size, False)
 
-                @pl.when(turn == line.last())
+                @pl.when(turn == tp_count - 1)
                 def _():
                     @pl.loop(0, tp_count)
                     def _(spot):
@@ -914,7 +948,7 @@
 
             if direct:
 
-                @pl.when(turn == line.last())
+                @pl.when(turn == tp_count - 1)
                 def _():
                     for k in range(1, tp_count):
                         share_copy(k).start()
@@ -963,9 +997,7 @@
         first_acc[...] += dot_tn(low_part, normed_all[part])
 
     packed[pl.ds(0, 3 * RANK), :] = first_acc[pl.ds(0, 3 * RANK), :]
-    packed[pl.ds(4 * RANK, RANK), :] = o_out_acc[pl.ds(0, RANK), :]
     lanes = pl.ds(pl.multiple_of(tp * q_cols, q_cols), q_cols)
-    packed[pl.ds(3 * RANK, RANK), lanes] = o_in_acc[pl.ds(0, RANK), :]
     packed[pl.ds(5 * RANK, RANK), lanes] = second_acc[pl.ds(0, RANK), :q_cols]
     lanes = pl.ds(pl.multiple_of(tp * kv_cols, kv_cols), kv_cols)
     packed[pl.ds(6 * RANK, RANK), lanes] = second_acc[pl.ds(RANK, RANK), q_cols : q_cols + kv_cols]
@@ -1064,7 +1096,8 @@
             for slot in range(2):
                 near_copy(n, slot).wait_send()
             pair_copy(n).wait_send()
-    line.end()
+    for k in range(1, tp_count):
+        do_copy(k).wait_send()
     for k in range(tp_count - 1):
         part_copy(k).wait_send()
     for distance in range(1, SPAN):
@@ -1076,7 +1109,8 @@
 
 def backward(
     tokens, upstream, routes, gains, router, middle, low, weights, normed, lora, att, queries, kv,
-    first, second, o_first, o_second, cos, sin, back, mixed, shares, tp_count, ctx_count, experts, direct,
+    first, second, o_first, o_second, cos, sin, w_rows, att_rows, back, mixed, shares,
+    tp_count, ctx_count, experts, direct,
 ):
     block, model = tokens.shape
     heads, rows, _ = queries.shape
@@ -1100,7 +1134,7 @@
         functools.partial(
             backward_kernel, tp_count=tp_count, ctx_count=ctx_count, experts=experts, direct=direct
         ),
-        in_specs=[vmem] * 20 + [hbm if direct else vmem] * 2 + [hbm],
+        in_specs=[vmem] * 22 + [hbm if direct else vmem] * 2 + [hbm],
         out_specs=[vmem] * 3 + [hbm],
         out_shape=[
             jax.ShapeDtypeStruct((block, model), BF16),
@@ -1117,7 +1151,8 @@
             pltpu.VMEM((pairs, SPAN * rows, LANES), F32),
             pltpu.VMEM((pairs, SPAN * rows, LANES), F32),
             pltpu.VMEM((tp_count * pairs, tall, LANES), F32),
-            pltpu.VMEM((tp_count, block, model), BF16),
+            pltpu.VMEM((tp_count, block, heads * HEAD), BF16),
+            pltpu.VMEM((tp_count, block, heads * HEAD), BF16),
             pltpu.VMEM((SPAN - 1, rows, kv_width), BF16),
             pltpu.VMEM((SPAN - 1, rows, kv_width), BF16),
             pltpu.VMEM((rows, kv_width), F32),
@@ -1126,8 +1161,6 @@
             pltpu.VMEM((tp_count,) + part, BF16),
             pltpu.VMEM((tp_count - 1,) + part, BF16),
             pltpu.VMEM((LANES, cols), F32),
-            pltpu.VMEM((LANES, model), F32),
-            pltpu.VMEM((LANES, heads * HEAD), F32),
             pltpu.VMEM((LANES, model), F32),
             pltpu.VMEM(packed, F32),
             pltpu.VMEM((ctx_count - 1, packed[0] // ctx_count, model) if direct else slim, F32),
@@ -1139,7 +1172,7 @@
             dma((2, 4)),
             dma((4,)),
             dma((2, 2)),
-            dma((2, 2, tp_count)),
+            dma((2, tp_count - 1)),
             dma((2, SPAN - 1)),
             dma((2, tp_count - 1)),
             dma((2, ctx_count - 1)),
@@ -1161,7 +1194,7 @@
         name="backward",
     )(
         tokens, upstream, routes, *gains, router, middle, low, weights, normed, lora, att, queries,
-        kv, first, second, o_first, o_second, cos, sin, back, mixed, shares,
+        kv, first, second, o_first, o_second, cos, sin, w_rows, att_rows, back, mixed, shares,
     )
 
 
@@ -1607,7 +1640,7 @@
 
     (
         attended, queries, kv_parts, lora, middle, o_reduced, attention_weights, normed_all,
-        first, second, o_first, o_second, cos, sin,
+        first, second, o_first, o_second, cos, sin, w_rows, att_rows,
         *far_weights, upstream_all, routes_all, rows_all,
     ) = forward(
         parents, adapter_set, tokens, (gain_a, gain_b),
@@ -1645,7 +1678,7 @@
     output, input_grad, packed, all_shares = backward(
         tokens, out_grad, routes.T, (gain_a, gain_b), w_router.T, middle, o_reduced, attention_weights,
         normed_all, lora, attended, queries, kv_parts, first, second, o_first, o_second,
-        cos, sin, back, mixed, expert_part, tp_count, ctx_count, experts, direct,
+        cos, sin, w_rows, att_rows, back, mixed, expert_part, tp_count, ctx_count, experts, direct,
     )
     all_trees = fsdp_count * trees
     if not direct:

time: 428 us -> 405 us (0.946)
  Pallas kernels: 426 us -> 401 us
    pallas_call x1, Pallas kernels: 161 us -> 148 us  [backward(): pl.pallas_call(functools.partial(backward_kernel, tp_count=tp_count, ctx_...]
    pallas_call x1, Pallas kernels: 157 us -> 146 us  [forward(): pl.pallas_call(functools.partial(forward_kernel, tp_count=tp_count, ctx_c...]
where the time goes in v7:
time: 405 us; the launch traced here: 403 us
  Pallas kernels  401 us (99%)
    pallas_call x1, Pallas kernels, backward(): pl.pallas_call(functools.partial(backward_kernel, tp_count=tp_count, ctx_...  148 us
    pallas_call x1, Pallas kernels, forward(): pl.pallas_call(functools.partial(forward_kernel, tp_count=tp_count, ctx_c...  146 us
    pallas_call x1, Pallas kernels, run_experts(): pl.pallas_call(functools.partial(expert_kernel, slots=slots, sources=sour...  93.7 us
    pallas_call x1, Pallas kernels, place(): pl.pallas_call(place_kernel, grid_spec=pltpu.PrefetchScalarGridSpec(num_s...  12.4 us

profile of v7, /device:TPU:13, one launch (start us, length us, event | category | flops | bytes accessed | tf_op | source)
XLA Modules:
  0.0 403.2 jit_solution(10853815251172160377)
XLA Ops:
  0.7 146.4 %forward.1 = (bf16[1024,256]{1,0:T(8,128)(2,1)}, bf16[4,1024,128]{2,1,0:T(8,128)(2,1)}, bf16[4,4,256,256]{3,2,1,0:T(8,128)(2,1)}, bf16[1024,128]{1,0:T(8,128)(2,...) custom-call(s32[64]{0:T(128)} %parents.1, s32[2]{0:T(128)} %sets.3, ...), custom_call_target="tpu_custom_call" | custom-call | flops 34359738368 | bytes 33554432 | tf_op jit(solution)/shard_map/forward/pallas_call | solution.py:621
  147.1 93.7 %experts.1 = (bf16[1024,1152]{1,0:T(8,128)(2,1)}, bf16[1024,1024]{1,0:T(8,128)(2,1)}, bf16[8,80,256]{2,1,0:T(8,128)(2,1)}) custom-call(s32[2]{0:T(128)} %sets.3, bf16[1024,1024]{1,0:T(8,128)(2,1)} %bitcast.16, bf16[1024,1024]{1,0:T(8,128)(2,1)} %bitcast.15, s32[8,1024]{1,0:T(8,128)} %bitcast.17, bf16[32,1024]{1,0:T(8,128)(2,1)} %bitcast.9, ...), custom_call_target="tpu_custom_call" | custom-call | flops 34359738368 | bytes 8388608 | tf_op jit(solution)/shard_map/experts/pallas_call | solution.py:1533
  240.8 148.4 %backward.1 = (bf16[256,1024]{1,0:T(8,128)(2,1)}, bf16[256,1024]{1,0:T(8,128)(2,1)}, f32[2,128,1024]{2,1,0:T(8,128)}, bf16[2,8,80,1024]{3,2,1,0:T(8,128)(2,1)}) custom-call(bf16[256,1024]{1,0:T(8,128)(2,1)} %tokens.3, bf16[256,1024]{1,0:T(8,128)(2,1)} %upstream_ref.1, s32[8,256]{1,0:T(8,128)} %bitcast.12, bf16[1024]{0:T(1024)(128)(2,1)} %gain_one.3, ...), custom_call_target="tpu_custom_call" | custom-call | flops 68719476736 | bytes 33554432 | tf_op jit(solution)/shard_map/backward/pallas_call | solution.py:1133
  389.1 0.0 copy-start.1
  389.2 0.0 copy-start
  389.2 12.4 %place.1 = (f32[1024,128]{1,0:T(8,128)}, f32[128,1024]{1,0:T(8,128)}, f32[1024,128]{1,0:T(8,128)}, f32[128,512]{1,0:T(8,128)}, f32[1024,128]{1,0:T(8,128)}, /*in...) custom-call(s32[2]{0:T(128)} %sets.3, ...), custom_call_target="tpu_custom_call" | custom-call | tf_op jit(solution)/shard_map/place/pallas_call | solution.py:1252
  401.6 0.0 copy-done.1
  401.6 0.8 copy.48
  402.4 0.0 copy-done
  402.4 0.8 copy.49
Async XLA Ops:
  389.1 12.5 %copy-start.1 = (bf16[256,1024]{1,0:T(8,128)(2,1)S(1)}, bf16[256,1024]{1,0:T(8,128)(2,1)}, u32[]{:S(2)}) copy-start(bf16[256,1024]{1,0:T(8,128)(2,1)} %get-tuple-element.118) | copy-start | bytes 1572868
  389.2 13.3 %copy-start = (bf16[256,1024]{1,0:T(8,128)(2,1)S(1)}, bf16[256,1024]{1,0:T(8,128)(2,1)}, u32[]{:S(2)}) copy-start(bf16[256,1024]{1,0:T(8,128)(2,1)} %get-tuple-element.119) | copy-start | bytes 1572868

commit v8 on v7

--- a/solution.py
+++ b/solution.py
@@ -693,13 +693,14 @@
 
 def backward_kernel(
     tokens, upstream_ref, routes, gain_one, gain_two, w_router, middle_ref, low_ref, weights,
-    normed_all, lora, att, q_ref, kv_ref, first, second, o_first, o_second, cos, sin, w_rows, att_rows, back, mixed, shares,
+    normed_all, lora, att, q_ref, kv_ref, first, second, o_first, o_second, cos, sin, w_rows, att_rows, back, mixed, shares, help_q,
     output, input_grad, packed_out, shares_out,
-    k_aug, v_aug, up_aug, dk, dv, dq, do_out, do_all, far_out, far_in, own_kv, row_grads, low_grads, parts, parts_in,
+    k_aug, v_aug, up_aug, dk, dv, dq, help_up, help_dq, help_sum, do_out, do_all, far_out, far_in, own_kv, row_grads, low_grads, parts, parts_in,
     second_acc, first_acc, packed, ctx_in, tp_in, middle_grad, router,
     back_near, back_mine, back_pair, back_far, mixed_near, mixed_mine, mixed_pair, mixed_far,
     near_sem, mine_sem, far_sem, branch_sem, kv_sem, part_sem,
     ctx_sem, tp_sem, x_sem, ctx_all_sem, share_sem, swap_sem, own_sem,
+    up_sem, sum_sem,
     *, tp_count, ctx_count, experts, direct,
 ):
     tp, ctx, fsdp = (lax.axis_index(name) for name in ("tp", "ctx", "fsdp"))
@@ -786,11 +787,19 @@
             shares_out.at[fsdp], shares_out.at[fsdp], swap_sem.at[0], swap_sem.at[1], other
         )
 
-        start_sum(0)
+        near_copy(0, 1).start()
+        for slot in (1, 0):
+            mine_copy(0, slot).start()
+        pass_sum(0)
+        near_copy(0, 0).start()
         start_sum(1)
         share_own.start()
 
-    @pl.loop(0, rank + 1)
+    last_rank, first_rank = rank == SPAN - 1, rank == 0
+    mirror = {"ctx": ctx + SPAN - 1 - 2 * rank}
+    far_count = jnp.where(last_rank, rank - 1, rank) if direct else rank
+
+    @pl.loop(0, far_count + 1)
     def _(distance):
         @pl.loop(0, tp_count)
         def _(part):
@@ -825,7 +834,6 @@
     gates = gates / jnp.sum(gates, axis=1, keepdims=True)
 
     if direct:
-        pass_sum(0)
         back_sum = end_sum(0)
     else:
         back_sum = back[...].astype(F32)
@@ -871,11 +879,11 @@
     place = (same & (r % HEAD == c % LANES)).astype(BF16)
     spread = (same & (c % LANES >= ONES) & (c % LANES < ONES + 2)).astype(BF16)
 
-    def tile(part, pair, start, size, causal):
+    def tile(part, pair, start, size, causal, from_q=q_ref, from_up=up_aug, into=dq):
         index = part * pairs + pair
         rows = pl.ds(pl.multiple_of(part * block, block), block)
-        queries = q_ref[pl.ds(pair * group, group), rows, :].reshape(tall, LANES)
-        upstream = up_aug[pl.ds(pair * group, group), rows, :].reshape(tall, LANES)
+        queries = from_q[pl.ds(pair * group, group), rows, :].reshape(tall, LANES)
+        upstream = from_up[pl.ds(pair * group, group), rows, :].reshape(tall, LANES)
         span = pl.ds(start, size)
         keys = k_aug[pair, span, :]
         probs = jnp.exp(dot_nt(keys, queries))
@@ -885,7 +893,7 @@
         steep = (probs * dot_nt(v_aug[pair, span, :], upstream)).astype(BF16)
         dv[pair, span, :] += dot(probs.astype(BF16), upstream)
         dk[pair, span, :] += dot(steep, queries)
-        dq[index] += dot_tn(steep, keys)
+        into[pair if into is help_dq else index] += dot_tn(steep, keys)
 
     def far_copy(distance):
         return remote(
@@ -914,6 +922,18 @@
         for head in range(heads):
             up_aug[head, rows, :] = coded[:, head * LANES : (head + 1) * LANES].astype(BF16)
 
+    def up_copy(part):
+        rows = pl.ds(pl.multiple_of(part * block, block), block)
+        return remote(
+            up_aug.at[:, rows], help_up.at[:, rows], up_sem.at[0, part], up_sem.at[1, part], mirror
+        )
+
+    def sum_copy(part):
+        spot = pl.ds(part * pairs, pairs)
+        return remote(
+            help_sum.at[spot], help_sum.at[spot], sum_sem.at[0, part], sum_sem.at[1, part], mirror
+        )
+
     @pl.loop(0, tp_count)
     def _(turn):
         part = ring(tp, -turn, tp_count)
@@ -925,10 +945,15 @@
         @pl.when(turn >= 0)
         def _():
             take_block(part)
-
-            @pl.loop(0, rank)
+            if direct:
+
+                @pl.when(last_rank)
+                def _():
+                    up_copy(part).start()
+
+            @pl.loop(0, far_count)
             def _(step):
-                distance = rank - step
+                distance = far_count - step
                 start = distance * rows_all
 
                 @pl.loop(0, pairs * (rows_all // size))
@@ -948,7 +973,7 @@
 
             if direct:
 
-                @pl.when(turn == tp_count - 1)
+                @pl.when(turn == 1)
                 def _():
                     for k in range(1, tp_count):
                         share_copy(k).start()
@@ -961,8 +986,34 @@
                 def _(j):
                     tile(part, pair, pl.multiple_of(j * block, block), block, False)
 
+            if direct:
+
+                @pl.when(first_rank)
+                def _():
+                    up_copy(part).wait_recv()
+                    help_dq[...] = jnp.zeros(help_dq.shape, F32)
+
+                    @pl.loop(0, pairs)
+                    def _(pair):
+                        tile(part, pair, 0, rows_all, False, help_q, help_up, help_dq)
+
+                    spot = pl.ds(part * pairs, pairs)
+                    help_sum[spot] = help_dq[...].astype(BF16)
+                    sum_copy(part).start()
+
+    if direct:
+
+        @pl.when(last_rank)
+        def _():
+            @pl.loop(0, tp_count)
+            def _(part):
+                sum_copy(part).wait_recv()
+                spot = pl.ds(part * pairs, pairs)
+                dq[spot] += help_sum[spot].astype(F32)
+
     own_kv[...] = joined(dk, dv, pl.ds(0, rows_all))
-    for distance in range(1, SPAN):
+    far_steps = far_out.shape[0] + 1
+    for distance in range(1, far_steps):
 
         @pl.when(rank + distance < SPAN)
         def _(distance=distance):
@@ -1098,18 +1149,29 @@
             pair_copy(n).wait_send()
     for k in range(1, tp_count):
         do_copy(k).wait_send()
+    if direct:
+        for part in range(tp_count):
+
+            @pl.when(last_rank)
+            def _(part=part):
+                up_copy(part).wait_send()
+
+            @pl.when(first_rank)
+            def _(part=part):
+                sum_copy(part).wait_send()
+
     for k in range(tp_count - 1):
         part_copy(k).wait_send()
-    for distance in range(1, SPAN):
-
-        @pl.when(distance <= rank)
+    for distance in range(1, far_steps):
+
+        @pl.when(distance <= far_count)
         def _(distance=distance):
             far_copy(distance).wait_send()
 
 
 def backward(
     tokens, upstream, routes, gains, router, middle, low, weights, normed, lora, att, queries, kv,
-    first, second, o_first, o_second, cos, sin, w_rows, att_rows, back, mixed, shares,
+    first, second, o_first, o_second, cos, sin, w_rows, att_rows, back, mixed, shares, help_q,
     tp_count, ctx_count, experts, direct,
 ):
     block, model = tokens.shape
@@ -1134,7 +1196,7 @@
         functools.partial(
             backward_kernel, tp_count=tp_count, ctx_count=ctx_count, experts=experts, direct=direct
         ),
-        in_specs=[vmem] * 22 + [hbm if direct else vmem] * 2 + [hbm],
+        in_specs=[vmem] * 22 + [hbm if direct else vmem] * 2 + [hbm, vmem if direct else hbm],
         out_specs=[vmem] * 3 + [hbm],
         out_shape=[
             jax.ShapeDtypeStruct((block, model), BF16),
@@ -1151,10 +1213,13 @@
             pltpu.VMEM((pairs, SPAN * rows, LANES), F32),
             pltpu.VMEM((pairs, SPAN * rows, LANES), F32),
             pltpu.VMEM((tp_count * pairs, tall, LANES), F32),
+            pltpu.VMEM((heads, rows, LANES) if direct else slim, BF16),
+            pltpu.VMEM((pairs, tall, LANES) if direct else slim, F32),
+            pltpu.VMEM((tp_count * pairs, tall, LANES) if direct else slim, BF16),
             pltpu.VMEM((tp_count, block, heads * HEAD), BF16),
             pltpu.VMEM((tp_count, block, heads * HEAD), BF16),
-            pltpu.VMEM((SPAN - 1, rows, kv_width), BF16),
-            pltpu.VMEM((SPAN - 1, rows, kv_width), BF16),
+            pltpu.VMEM((SPAN - 2 if direct else SPAN - 1, rows, kv_width), BF16),
+            pltpu.VMEM((SPAN - 2 if direct else SPAN - 1, rows, kv_width), BF16),
             pltpu.VMEM((rows, kv_width), F32),
             pltpu.VMEM((rows, cols), BF16),
             pltpu.VMEM((rows, LANES), BF16),
@@ -1182,6 +1247,8 @@
             dma((2, tp_count - 1)),
             dma((2,)),
             dma((1,)),
+            dma((2, tp_count)),
+            dma((2, tp_count)),
         ],
         compiler_params=pltpu.CompilerParams(
             vmem_limit_bytes=60 * 1024 * 1024, collective_id=1, has_side_effects=True
@@ -1194,7 +1261,7 @@
         name="backward",
     )(
         tokens, upstream, routes, *gains, router, middle, low, weights, normed, lora, att, queries,
-        kv, first, second, o_first, o_second, cos, sin, w_rows, att_rows, back, mixed, shares,
+        kv, first, second, o_first, o_second, cos, sin, w_rows, att_rows, back, mixed, shares, help_q,
     )
 
 
@@ -1235,32 +1302,37 @@
         key_out[...] = gathered(6, slice(0, kv_cols), False)
         value_out[...] = gathered(6, slice(kv_cols, 2 * kv_cols), False)
 
-    def pieces(rows, lanes):
-        return jnp.concatenate([part[tree, 0, block(rows), lanes] for tree in range(trees)], axis=0)
-
     whole, left, right = slice(None), slice(0, hidden), slice(hidden, 2 * hidden)
-    gate_in[0] = dot_tn(pieces(0, whole), spots)
-    up_in[0] = dot_tn(pieces(1, whole), spots)
-    gate_out[0] = dot_tn(spots, pieces(2, left))
-    up_out[0] = dot_tn(spots, pieces(2, right))
-    down_out[0] = dot_tn(spots, pieces(3, whole))
-    down_in[0] = dot_tn(pieces(4, left), spots)
+    for n in range(part.shape[1]):
+
+        def pieces(rows, lanes, n=n):
+            return jnp.concatenate(
+                [part[tree, n, block(rows), lanes] for tree in range(trees)], axis=0
+            )
+
+        gate_in[n] = dot_tn(pieces(0, whole), spots)
+        up_in[n] = dot_tn(pieces(1, whole), spots)
+        gate_out[n] = dot_tn(spots, pieces(2, left))
+        up_out[n] = dot_tn(spots, pieces(2, right))
+        down_out[n] = dot_tn(spots, pieces(3, whole))
+        down_in[n] = dot_tn(pieces(4, left), spots)
 
 
 def place(sets, packed, part, once, each):
     trees, local = part.shape[:2]
+    batch = 2 if local % 2 == 0 else 1
     return pl.pallas_call(
         place_kernel,
         grid_spec=pltpu.PrefetchScalarGridSpec(
             num_scalar_prefetch=1,
-            grid=(local,),
+            grid=(local // batch,),
             in_specs=[
                 pl.BlockSpec(packed.shape, lambda e, s: (0, 0, 0)),
-                pl.BlockSpec((trees, 1) + part.shape[2:], lambda e, s: (0, e, 0, 0)),
+                pl.BlockSpec((trees, batch) + part.shape[2:], lambda e, s: (0, e, 0, 0)),
             ],
             out_specs=[
                 *[pl.BlockSpec(o.shape, lambda e, s: (0, 0)) for o in once],
-                *[pl.BlockSpec((1,) + o.shape[1:], lambda e, s: (e, 0, 0)) for o in each],
+                *[pl.BlockSpec((batch,) + o.shape[1:], lambda e, s: (e, 0, 0)) for o in each],
             ],
         ),
         out_shape=[jax.ShapeDtypeStruct(o.shape, F32) for o in (*once, *each)],
@@ -1271,11 +1343,11 @@
 
 def expert_kernel(
     sets, x_ref, g_ref, routes, router,
-    w_gate, w_up, w_down, w_gate_far, w_up_far, w_down_far, all_gate, all_up, all_down, gate_in, up_in, gate_out, up_out, down_in, down_out,
-    back_out, mixed_out, grad_out,
+    w_gate, w_up, w_down, w_gate_far, w_up_far, w_down_far, all_gate, all_up, all_down, queries, gate_in, up_in, gate_out, up_out, down_in, down_out,
+    back_out, mixed_out, grad_out, help_queries,
     rank_rows, gate_rows, slope_rows, mix, back, xs, firsts, tall_grad,
     gate_full, up_full, down_full, land_gate, land_up, land_down, grads, grads_in,
-    far_sem, pass_far_sem, grads_sem, arrive_sem,
+    far_sem, pass_far_sem, grads_sem, arrive_sem, query_sem,
     *, slots, sources, early, shared, straight, tp_count,
 ):
     chunk, expert = pl.program_id(0), pl.program_id(1)
@@ -1288,20 +1360,33 @@
         shared, straight, early, 0, other, tp,
     )
 
+    ctx = lax.axis_index("ctx")
+    rank = lax.rem(ctx, SPAN)
+    mirror = {"ctx": ctx + SPAN - 1 - 2 * rank}
+
+    def query_copy():
+        return remote(queries, help_queries, query_sem.at[0], query_sem.at[1], mirror)
+
     if gather:
 
         @pl.when(expert == 0)
         def _():
             barrier = pltpu.get_barrier_semaphore()
-            pl.semaphore_signal(
-                barrier, 1, device_id=other, device_id_type=pl.DeviceIdType.MESH
-            )
+            for where in (other, mirror):
+                pl.semaphore_signal(
+                    barrier, 1, device_id=where, device_id_type=pl.DeviceIdType.MESH
+                )
             for k in range(1, tp_count):
                 pl.semaphore_signal(
                     barrier, 1, device_id={"tp": ring(tp, k, tp_count)},
                     device_id_type=pl.DeviceIdType.MESH,
                 )
-            pl.semaphore_wait(barrier, tp_count)
+            pl.semaphore_wait(barrier, tp_count + 1)
+
+            @pl.when(rank == SPAN - 1)
+            def _():
+                query_copy().start()
+
             for n in BEGIN[0]:
                 for copy in cross(n):
                     copy.start()
@@ -1463,9 +1548,22 @@
             arrive_sem.at[k - 1, n], {"tp": where},
         )
 
+    def add_up(n):
+        lanes = pl.ds(pl.multiple_of(tp * share, share), share)
+        total = grads[n, :, lanes].astype(F32)
+        for k in range(1, tp_count):
+            grads_copy(n, k).wait()
+            total += grads_in[k - 1, n].astype(F32)
+        grad_out[n] = total.astype(BF16)
+
     if gather:
         for k in range(1, tp_count):
             grads_copy(expert, k).start()
+
+        @pl.when(expert >= 2)
+        def _():
+            add_up(expert - 2)
+
     else:
         grad_out[0, 0] = grads[0]
 
@@ -1480,14 +1578,16 @@
                 for copy in hand_on(n):
                     copy.wait_send()
 
-            @pl.loop(0, pl.num_programs(1))
-            def _(n):
-                lanes = pl.ds(pl.multiple_of(tp * share, share), share)
-                total = grads[n, :, lanes].astype(F32)
-                for k in range(1, tp_count):
-                    grads_copy(n, k).wait()
-                    total += grads_in[k - 1, n].astype(F32)
-                grad_out[n] = total.astype(BF16)
+            @pl.when(rank == SPAN - 1)
+            def _():
+                query_copy().wait_send()
+
+            @pl.when(rank == 0)
+            def _():
+                query_copy().wait_recv()
+
+            for n in (2, 1):
+                add_up(expert + 1 - n)
 
     @pl.when(expert == pl.num_programs(1) - 1)
     def _():
@@ -1504,7 +1604,7 @@
 
 
 def run_experts(
-    sets, rows, upstream, routes, router, weights, far, adapters, slots, sources, tp_count
+    sets, rows, upstream, routes, router, weights, far, queries, adapters, slots, sources, tp_count
 ):
     total, model = rows.shape
     experts = router.shape[0]
@@ -1545,13 +1645,14 @@
                 pl.BlockSpec(router.shape, fixed),
                 *[pl.BlockSpec((1,) + w.shape[1:], expert) for w in weights],
                 *[pl.BlockSpec((1,) + w.shape[1:], arrived) for w in weights],
-                *[hbm] * len(weights),
+                *[hbm] * (len(weights) + 1),
                 *[pl.BlockSpec((1,) + a.shape[1:], expert) for a in adapters],
             ],
             out_specs=[
                 pl.BlockSpec((tokens, model + LANES), piece),
                 pl.BlockSpec((tokens, model), piece),
                 gradients[1],
+                hbm,
             ],
             scratch_shapes=[
                 pltpu.VMEM((experts, tokens), F32),
@@ -1572,12 +1673,14 @@
                 dma((2, max(shared, 1), 3)),
                 dma((tp_count - 1, local)),
                 dma((tp_count - 1, local)),
+                dma((2,)),
             ],
         ),
         out_shape=[
             jax.ShapeDtypeStruct((total, model + LANES), BF16),
             jax.ShapeDtypeStruct((total, model), BF16),
             jax.ShapeDtypeStruct(gradients[0], BF16),
+            jax.ShapeDtypeStruct(queries.shape, BF16),
         ],
         compiler_params=(
             pltpu.CompilerParams(
@@ -1592,7 +1695,7 @@
             bytes_accessed=8 * 1024 * 1024,
             transcendentals=0,
         ),
-    )(sets, rows, upstream, routes, router, *weights, *far, *weights, *adapters)
+    )(sets, rows, upstream, routes, router, *weights, *far, *weights, queries, *adapters)
 
 
 def per_device(
@@ -1655,7 +1758,7 @@
     rows_all = rows_all.reshape(-1, model)
     routes_all = routes_all.transpose(1, 0, 2).reshape(TOP, -1)
 
-    back, mixed, expert_part = run_experts(
+    back, mixed, expert_part, help_queries = run_experts(
         adapter_set,
         rows_all,
         upstream_all,
@@ -1663,6 +1766,7 @@
         w_router.T,
         (w_gate, w_up, w_down),
         far_weights,
+        queries,
         (gate_in, up_in, gate_out, up_out, down_in, down_out),
         slots,
         SPAN,
@@ -1678,7 +1782,7 @@
     output, input_grad, packed, all_shares = backward(
         tokens, out_grad, routes.T, (gain_a, gain_b), w_router.T, middle, o_reduced, attention_weights,
         normed_all, lora, attended, queries, kv_parts, first, second, o_first, o_second,
-        cos, sin, w_rows, att_rows, back, mixed, expert_part, tp_count, ctx_count, experts, direct,
+        cos, sin, w_rows, att_rows, back, mixed, expert_part, help_queries, tp_count, ctx_count, experts, direct,
     )
     all_trees = fsdp_count * trees
     if not direct:

time: 405 us -> 396 us (0.978)
  Pallas kernels: 401 us -> 393 us
    pallas_call x1, Pallas kernels: 148 us -> 142 us  [backward(): pl.pallas_call(functools.partial(backward_kernel, tp_count=tp_count, ctx_...]
where the time goes in v8:
time: 396 us
  Pallas kernels  393 us (99%)
    pallas_call x1, Pallas kernels, forward(): pl.pallas_call(functools.partial(forward_kernel, tp_count=tp_count, ctx_c...  146 us
    pallas_call x1, Pallas kernels, backward(): pl.pallas_call(functools.partial(backward_kernel, tp_count=tp_count, ctx_...  142 us
    pallas_call x1, Pallas kernels, run_experts(): pl.pallas_call(functools.partial(expert_kernel, slots=slots, sources=sour...  93.9 us
    pallas_call x1, Pallas kernels, place(): pl.pallas_call(place_kernel, grid_spec=pltpu.PrefetchScalarGridSpec(num_s...  11.3 us

profile of v8, /device:TPU:13, one launch (start us, length us, event | category | flops | bytes accessed | tf_op | source)
XLA Modules:
  0.0 395.7 jit_solution(6348445012625585514)
XLA Ops:
  0.7 146.4 %forward.1 = (bf16[1024,256]{1,0:T(8,128)(2,1)}, bf16[4,1024,128]{2,1,0:T(8,128)(2,1)}, bf16[4,4,256,256]{3,2,1,0:T(8,128)(2,1)}, bf16[1024,128]{1,0:T(8,128)(2,...) custom-call(s32[64]{0:T(128)} %parents.1, s32[2]{0:T(128)} %sets.3, ...), custom_call_target="tpu_custom_call" | custom-call | flops 34359738368 | bytes 33554432 | tf_op jit(solution)/shard_map/forward/pallas_call | solution.py:621
  147.1 93.9 %experts.1 = (bf16[1024,1152]{1,0:T(8,128)(2,1)}, bf16[1024,1024]{1,0:T(8,128)(2,1)}, bf16[8,80,256]{2,1,0:T(8,128)(2,1)}, bf16[4,1024,128]{2,1,0:T(8,128)(2,1)}) custom-call(s32[2]{0:T(128)} %sets.3, bf16[1024,1024]{1,0:T(8,128)(2,1)} %bitcast.16, bf16[1024,1024]{1,0:T(8,128)(2,1)} %bitcast.15, s32[8,1024]{1,0:T(8,128)} %bitcast.17, ...), custom_call_target="tpu_custom_call" | custom-call | flops 34359738368 | bytes 8388608 | tf_op jit(solution)/shard_map/experts/pallas_call | solution.py:1633
  241.0 141.9 %backward.1 = (bf16[256,1024]{1,0:T(8,128)(2,1)}, bf16[256,1024]{1,0:T(8,128)(2,1)}, f32[2,128,1024]{2,1,0:T(8,128)}, bf16[2,8,80,1024]{3,2,1,0:T(8,128)(2,1)}) custom-call(bf16[256,1024]{1,0:T(8,128)(2,1)} %tokens.3, bf16[256,1024]{1,0:T(8,128)(2,1)} %upstream_ref.1, s32[8,256]{1,0:T(8,128)} %bitcast.12, bf16[1024]{0:T(1024)(128)(2,1)} %gain_one.3, ...), custom_call_target="tpu_custom_call" | custom-call | flops 68719476736 | bytes 33554432 | tf_op jit(solution)/shard_map/backward/pallas_call | solution.py:1195
  382.9 0.0 copy-start.1
  382.9 0.0 copy-start
  382.9 11.3 %place.1 = (f32[1024,128]{1,0:T(8,128)}, f32[128,1024]{1,0:T(8,128)}, f32[1024,128]{1,0:T(8,128)}, f32[128,512]{1,0:T(8,128)}, f32[1024,128]{1,0:T(8,128)}, /*in...) custom-call(s32[2]{0:T(128)} %sets.3, ...), custom_call_target="tpu_custom_call" | custom-call | tf_op jit(solution)/shard_map/place/pallas_call | solution.py:1324
  394.1 0.0 copy-done.1
  394.1 0.8 copy.48
  394.9 0.0 copy-done
  394.9 0.8 copy.49
Async XLA Ops:
  382.9 11.3 %copy-start.1 = (bf16[256,1024]{1,0:T(8,128)(2,1)S(1)}, bf16[256,1024]{1,0:T(8,128)(2,1)}, u32[]{:S(2)}) copy-start(bf16[256,1024]{1,0:T(8,128)(2,1)} %get-tuple-element.120) | copy-start | bytes 1572868
  382.9 12.1 %copy-start = (bf16[256,1024]{1,0:T(8,128)(2,1)S(1)}, bf16[256,1024]{1,0:T(8,128)(2,1)}, u32[]{:S(2)}) copy-start(bf16[256,1024]{1,0:T(8,128)(2,1)} %get-tuple-element.121) | copy-start | bytes 1572868

commit v9 on v8

--- a/solution.py
+++ b/solution.py
@@ -126,14 +126,14 @@
 
 
 class Line:
-    def __init__(self, buffer, sems, me, count):
-        self.buffer, self.sems, self.me, self.count = buffer, sems, me, count
+    def __init__(self, view, sems, me, count):
+        self.view, self.sems, self.me, self.count = view, sems, me, count
         self.turns = 2 * count - 1
 
     def move(self, way, block):
         where = ring(self.me, 1 if way == 0 else -1, self.count)
         return remote(
-            self.buffer.at[block], self.buffer.at[block],
+            self.view(block), self.view(block),
             self.sems.at[way, 0, block], self.sems.at[way, 1, block], {"tp": where},
         )
 
@@ -200,7 +200,7 @@
     first, second, o_first, o_second, cos, sin, w_rows, att_rows,
     gate_far, up_far, down_far, grads_all, routes_all, rows_all,
     q_aug, k_aug, v_aug, top, acc, rows_own, code_table, depth_table,
-    shard_sem, normed_sem, kv_sem, part_sem, w_rows_sem, far_sem, pass_far_sem, grads_sem, routes_sem, rows_sem,
+    shard_sem, normed_sem, kv_sem, part_sem, w_rows_sem, w_pass_sem, far_sem, pass_far_sem, grads_sem, routes_sem, rows_sem,
     pass_sem, local_sem,
     *, tp_count, ctx_count, shared, straight,
 ):
@@ -240,9 +240,25 @@
         (w_output, half, 0),
     )
     shard_copies = []
+    shard_passes = []
+    core = lax.rem(ctx, 2)
     for n, (source, row, column) in enumerate(corners):
-        spot = weights.at[fsdp, pl.ds(row, source.shape[0]), pl.ds(column, source.shape[1])]
-        shard_copies.append(remote(source, spot, shard_sem.at[0, n], shard_sem.at[1, n], other))
+        size = source.shape[0] // 2
+        start = pl.multiple_of(core * size, size)
+        rows = pl.ds(pl.multiple_of(row + core * size, size), size)
+        lanes = pl.ds(column, source.shape[1])
+        shard_copies.append(
+            remote(
+                source.at[pl.ds(start, size)], weights.at[fsdp, rows, lanes],
+                shard_sem.at[0, n], shard_sem.at[1, n], other,
+            )
+        )
+        landed = weights.at[1 - fsdp, rows, lanes]
+        shard_passes.append(
+            remote(
+                landed, landed, shard_sem.at[2, n], shard_sem.at[3, n], {"ctx": partner}
+            )
+        )
     for copy in shard_copies:
         copy.start()
 
@@ -250,7 +266,7 @@
     normed = rms_scale(inputs, gain_one[...].astype(F32).reshape(1, model)).astype(BF16)
     normed_all[tp] = normed
 
-    line = Line(normed_all, normed_sem, tp, tp_count)
+    line = Line(lambda b: normed_all.at[b], normed_sem, tp, tp_count)
     line.start()
 
     def side_copies(k):
@@ -306,8 +322,9 @@
     o_first[...] = dot(out_in[...], pick(0)).astype(BF16)
     o_second[...] = dot_tn(pick(0), out_out[...]).astype(BF16)
 
-    for copy in shard_copies:
+    for copy, onward in zip(shard_copies, shard_passes):
         copy.wait()
+        onward.start()
     cross, hand_on = far_moves(
         (w_gate, w_up, w_down), (gate_far, up_far, down_far), far_sem, pass_far_sem,
         shared, straight, 0, 0, other, tp,
@@ -330,6 +347,8 @@
                 copy.start()
 
     point("start")
+    for onward in shard_passes:
+        onward.wait()
 
     def kv_copy(distance, part):
         return remote(
@@ -389,10 +408,12 @@
             line.arrive(turn, part)
             project(part)
 
-    w_line = Line(w_rows, w_rows_sem, tp, tp_count)
-    for side in range(2):
-        w_rows[tp, side] = weights[side, pl.ds(half, q_cols), :]
+    w_line = Line(lambda b: w_rows.at[b, core], w_rows_sem, tp, tp_count)
+    w_rows[tp, core] = weights[core, pl.ds(half, q_cols), :]
     w_line.start()
+    w_pass = remote(
+        w_rows.at[:, core], w_rows.at[:, core], w_pass_sem.at[0], w_pass_sem.at[1], {"ctx": partner}
+    )
     point("proj")
 
     def advance(step):
@@ -517,6 +538,8 @@
             @pl.when(k == step - 2)
             def _(step=step):
                 advance(step)
+                if step == tp_count - 1:
+                    w_pass.start()
 
         for n in range(tp_count):
             if f"k{n}" in BEGIN or f"k{n}" in RELAY:
@@ -528,6 +551,7 @@
     for k in range(tp_count - 1):
         part_copy(k).wait_recv()
     point("sum")
+    w_pass.wait_recv()
     low = sum(
         dot(att_rows[t], o_first[pl.ds(t * q_cols, q_cols), :]) for t in range(tp_count)
     ).astype(BF16)
@@ -568,6 +592,7 @@
 
     line.end()
     w_line.end()
+    w_pass.wait_send()
     for k in range(tp_count - 1):
         part_copy(k).wait_send()
     for distance in range(1, SPAN):
@@ -655,11 +680,12 @@
             pltpu.VMEM((block, model), BF16),
             pltpu.VMEM((LANES, LANES), BF16),
             pltpu.VMEM((LANES, LANES), BF16),
-            dma((2, 4)),
+            dma((4, 4)),
             dma((2, 2, tp_count)),
             dma((2, SPAN - 1)),
             dma((2, tp_count - 1)),
             dma((2, 2, tp_count)),
+            dma((2,)),
             dma((2, shared + straight, 3)),
             dma((2, max(shared, 1), 3)),
             dma((2, ctx_count)),

time: 396 us -> 388 us (0.980)
  Pallas kernels: 393 us -> 385 us
    pallas_call x1, Pallas kernels: 146 us -> 138 us  [forward(): pl.pallas_call(functools.partial(forward_kernel, tp_count=tp_count, ctx_c...]
where the time goes in v9:
time: 388 us; the launch traced here: 387 us
  Pallas kernels  385 us (99%)
    pallas_call x1, Pallas kernels, backward(): pl.pallas_call(functools.partial(backward_kernel, tp_count=tp_count, ctx_...  143 us
    pallas_call x1, Pallas kernels, forward(): pl.pallas_call(functools.partial(forward_kernel, tp_count=tp_count, ctx_c...  138 us
    pallas_call x1, Pallas kernels, run_experts(): pl.pallas_call(functools.partial(expert_kernel, slots=slots, sources=sour...  92.7 us
    pallas_call x1, Pallas kernels, place(): pl.pallas_call(place_kernel, grid_spec=pltpu.PrefetchScalarGridSpec(num_s...  11.3 us

profile of v9, /device:TPU:13, one launch (start us, length us, event | category | flops | bytes accessed | tf_op | source)
XLA Modules:
  0.0 387.1 jit_solution(4735858279593126622)
XLA Ops:
  0.7 138.3 %forward.1 = (bf16[1024,256]{1,0:T(8,128)(2,1)}, bf16[4,1024,128]{2,1,0:T(8,128)(2,1)}, bf16[4,4,256,256]{3,2,1,0:T(8,128)(2,1)}, bf16[1024,128]{1,0:T(8,128)(2,...) custom-call(s32[64]{0:T(128)} %parents.1, s32[2]{0:T(128)} %sets.3, ...), custom_call_target="tpu_custom_call" | custom-call | flops 34359738368 | bytes 33554432 | tf_op jit(solution)/shard_map/forward/pallas_call | solution.py:646
  139.0 92.7 %experts.1 = (bf16[1024,1152]{1,0:T(8,128)(2,1)}, bf16[1024,1024]{1,0:T(8,128)(2,1)}, bf16[8,80,256]{2,1,0:T(8,128)(2,1)}, bf16[4,1024,128]{2,1,0:T(8,128)(2,1)}) custom-call(s32[2]{0:T(128)} %sets.3, bf16[1024,1024]{1,0:T(8,128)(2,1)} %bitcast.16, bf16[1024,1024]{1,0:T(8,128)(2,1)} %bitcast.15, s32[8,1024]{1,0:T(8,128)} %bitcast.17, ...), custom_call_target="tpu_custom_call" | custom-call | flops 34359738368 | bytes 8388608 | tf_op jit(solution)/shard_map/experts/pallas_call | solution.py:1659
  231.6 142.6 %backward.1 = (bf16[256,1024]{1,0:T(8,128)(2,1)}, bf16[256,1024]{1,0:T(8,128)(2,1)}, f32[2,128,1024]{2,1,0:T(8,128)}, bf16[2,8,80,1024]{3,2,1,0:T(8,128)(2,1)}) custom-call(bf16[256,1024]{1,0:T(8,128)(2,1)} %tokens.3, bf16[256,1024]{1,0:T(8,128)(2,1)} %upstream_ref.1, s32[8,256]{1,0:T(8,128)} %bitcast.12, bf16[1024]{0:T(1024)(128)(2,1)} %gain_one.3, ...), custom_call_target="tpu_custom_call" | custom-call | flops 68719476736 | bytes 33554432 | tf_op jit(solution)/shard_map/backward/pallas_call | solution.py:1221
  374.2 0.0 copy-start.1
  374.2 0.0 copy-start
  374.2 11.3 %place.1 = (f32[1024,128]{1,0:T(8,128)}, f32[128,1024]{1,0:T(8,128)}, f32[1024,128]{1,0:T(8,128)}, f32[128,512]{1,0:T(8,128)}, f32[1024,128]{1,0:T(8,128)}, /*in...) custom-call(s32[2]{0:T(128)} %sets.3, ...), custom_call_target="tpu_custom_call" | custom-call | tf_op jit(solution)/shard_map/place/pallas_call | solution.py:1350
  385.5 0.0 copy-done.1
  385.5 0.8 copy.48
  386.3 0.0 copy-done
  386.3 0.8 copy.49
Async XLA Ops:
  374.2 11.3 %copy-start.1 = (bf16[256,1024]{1,0:T(8,128)(2,1)S(1)}, bf16[256,1024]{1,0:T(8,128)(2,1)}, u32[]{:S(2)}) copy-start(bf16[256,1024]{1,0:T(8,128)(2,1)} %get-tuple-element.120) | copy-start | bytes 1572868
  374.2 12.1 %copy-start = (bf16[256,1024]{1,0:T(8,128)(2,1)S(1)}, bf16[256,1024]{1,0:T(8,128)(2,1)}, u32[]{:S(2)}) copy-start(bf16[256,1024]{1,0:T(8,128)(2,1)} %get-tuple-element.121) | copy-start | bytes 1572868
